TPU v7x, 32 devices: a whole 2x2x4 slice. The times are simulated.
32 devices in a mesh: gx: 2 (over core), gy: 4 (over y, x), gz: 4 (over z).
Axes of the slice: x: 2, y: 2, z: 4, core: 2. Of those that a mesh axis runs over, the one named last changes fastest.
Arguments:
- flow: float32 [4, 64, 64, 1024], P(None, 'gx', 'gz', 'gy'), may hold values from -6 to 6
- positions: float32 [3, 3, 8, 128], P(None, None, ('gx', 'gy'), 'gz'), may hold values from 0 to 1024
- loads: float32 [3, 3, 8, 128], P(None, None, ('gx', 'gy'), 'gz'), may hold values from -120 to 120
- block_list: int32 [2, 4, 4, 2], P('gx', 'gy', 'gz'), may hold values from 0 to 8, as said below
Outputs:
- flow_out: float32 [4, 64, 64, 1024], P(None, 'gx', 'gz', 'gy')
- sampled: float32 [3, 3, 8, 128], P(None, None, ('gx', 'gy'), 'gz')
Inputs may be any that keep to these rules, and one draw needn't show every extreme that they name: `block_list`: an entry names a turbine whose rotor reaches that device's cells, or is 8 for an empty slot. No turbine appears twice in one list. Each turbine is named by exactly four devices with one gy index: two neighbours along gx, each with gz index 0 and 1; these four lists hold the same set of turbines. Every list is either full or empty.
All inputs are finite; a program needn't handle non-finite values.
Results may differ from a plain program's by a relative error of at most 0.0003.
Values sent between devices are 32-bit elements; how exact they have to be, the bound alone decides.
No kernel may reach another device: no remote copies, remote signals or barrier semaphores. Data moves between devices by JAX's collectives and lax.ppermute only.
A program may use at most 128 MiB of HBM per device.

v0:
```python
import functools
import math

import jax
import jax.numpy as jnp
from jax import lax
from jax.experimental import pallas as pl
from jax.experimental.pallas import tpu as pltpu
from jax.sharding import PartitionSpec as P

kernel_width = 2.0
kernel_norm = 1.0 / (math.pi**1.5 * kernel_width**3)
time_step = 0.1
smag_coef = 0.17
viscosity = 0.02
diffusivity = 0.02
prandtl = 0.4
vmem_limit = 48 << 20


def swap_pairs(count, first):
    pairs = []
    for low in range(first, count - 1, 2):
        pairs += [(low, low + 1), (low + 1, low)]
    return pairs


def swap(value, axis, first):
    pairs = swap_pairs(lax.axis_size(axis), first)
    if not pairs:
        return jnp.zeros_like(value)
    return lax.ppermute(value, axis, pairs)


def from_distance(value, axis, distance):
    count = lax.axis_size(axis)
    return lax.ppermute(value, axis, [(i, i ^ distance) for i in range(count)])


def gather_relative(value, axis):
    distance = 1
    while distance < lax.axis_size(axis):
        value = jnp.concatenate([value, from_distance(value, axis, distance)], axis=0)
        distance *= 2
    return value


def pick(flag, first, second):
    return jnp.where(flag, first, second)


def is_even(axis):
    return lax.rem(lax.axis_index(axis), 2) == 0


def write_faces(q_ref, face_refs, shape):
    count_x, count_z, count_y = shape
    xa_ref, xb_ref, za_ref, zb_ref, ya_ref, yb_ref = face_refs
    even_x, even_z, even_y = is_even("gx"), is_even("gz"), is_even("gy")
    low, high = q_ref[:, 0], q_ref[:, count_x - 1]
    xa_ref[...] = pick(even_x, high, low)
    xb_ref[...] = pick(even_x, low, high)
    for comp in range(4):
        low = q_ref[comp, :, 0, :]
        high = q_ref[comp, :, count_z - 1, :]
        za_ref[comp] = pick(even_z, high, low)
        zb_ref[comp] = pick(even_z, low, high)
    lane = lax.broadcasted_iota(jnp.int32, (count_z, 128), 1)
    for comp in range(4):
        low = jnp.zeros((count_z, 128), jnp.float32)
        high = jnp.zeros((count_z, 128), jnp.float32)
        for x in range(count_x):
            first = q_ref[comp, x, :, :128]
            last = q_ref[comp, x, :, count_y - 128 :]
            low = jnp.where(lane == x, pltpu.roll(first, x, 1), low)
            high = jnp.where(lane == x, pltpu.roll(last, (x + 1) % 128, 1), high)
        ya_ref[comp] = pick(even_y, high, low)
        yb_ref[comp] = pick(even_y, low, high)


def faces_body(q_ref, *face_refs, shape):
    write_faces(q_ref, face_refs, shape)


def sorted_slots(list_ref, capacity):
    slots = [list_ref[j] for j in range(capacity)]
    for first in range(capacity):
        for second in range(first + 1, capacity):
            a, b = slots[first], slots[second]
            slots[first], slots[second] = jnp.minimum(a, b), jnp.maximum(a, b)
    return slots


def plane_update(centre, minus_x, plus_x, rows_z, cols_y, pushed, shape):
    count_x, count_z, count_y = shape
    sub = lax.broadcasted_iota(jnp.int32, (count_z, count_y), 0)
    lane = lax.broadcasted_iota(jnp.int32, (count_z, count_y), 1)
    diffs, laplace = [], []
    for comp in range(4):
        c = centre[comp]
        low_z, high_z = rows_z[comp]
        low_y, high_y = cols_y[comp]
        minus_z = jnp.where(sub == 0, low_z, pltpu.roll(c, 1, 0))
        plus_z = jnp.where(sub == count_z - 1, high_z, pltpu.roll(c, count_z - 1, 0))
        minus_y = jnp.where(lane == 0, low_y, pltpu.roll(c, 1, 1))
        plus_y = jnp.where(lane == count_y - 1, high_y, pltpu.roll(c, count_y - 1, 1))
        diffs.append((plus_x[comp] - minus_x[comp], plus_y - minus_y, plus_z - minus_z))
        total = (plus_x[comp] + minus_x[comp]) + (plus_y + minus_y) + (plus_z + minus_z)
        laplace.append(total - 6.0 * c)
    diagonal = diffs[0][0] * diffs[0][0] + diffs[1][1] * diffs[1][1] + diffs[2][2] * diffs[2][2]
    xy = diffs[0][1] + diffs[1][0]
    xz = diffs[0][2] + diffs[2][0]
    yz = diffs[1][2] + diffs[2][1]
    doubled = 0.5 * diagonal + 0.25 * (xy * xy + xz * xz + yz * yz)
    eddy = smag_coef**2 * jnp.sqrt(doubled)
    half = [0.5 * time_step * centre[a] for a in range(3)]
    scale_u = time_step * (viscosity + eddy)
    scale_t = time_step * (diffusivity + eddy / prandtl)
    out = []
    for comp in range(4):
        d = diffs[comp]
        moved = half[0] * d[0] + half[1] * d[1] + half[2] * d[2]
        value = centre[comp] - moved + (scale_u if comp < 3 else scale_t) * laplace[comp]
        if comp < 3:
            value = value + time_step * pushed[comp]
        out.append(value)
    return out


def step_body(
    list_ref, table_ref, q_ref, xa_ref, xb_ref, za_ref, zb_ref, ya_ref, yb_ref, *rest, shape, points, capacity, step, last
):
    count_x, count_z, count_y = shape
    out_ref, sample_ref = rest[:2]
    face_refs = rest[2:-8]
    force_ref, rows_ref, low_ref, high_ref, low_z_ref, high_z_ref, low_y_ref, high_y_ref = rest[-8:]
    index_x, index_y, index_z = lax.axis_index("gx"), lax.axis_index("gy"), lax.axis_index("gz")
    size_x, size_y, size_z = lax.axis_size("gx"), lax.axis_size("gy"), lax.axis_size("gz")
    turbines = size_x * size_y
    slots = sorted_slots(list_ref, capacity)
    listed = slots[0] < turbines
    part = points // size_z

    @pl.when(listed)
    def _():
        for j in range(capacity):
            t = jnp.minimum(slots[j], turbines - 1)
            place_x = lax.bitwise_xor(lax.div(t, size_y), index_x)
            place_y = lax.bitwise_xor(lax.rem(t, size_y), index_y)
            for c in range(size_z):
                place_z = lax.bitwise_xor(index_z, c)
                entry = (place_x * size_y + place_y) * size_z + place_z
                offset = j * points + c * part
                rows_ref[:, offset : offset + part] = table_ref[entry, 8 * step : 8 * step + 8, :]
        rows = rows_ref[...]
        lanes = capacity * points
        start_x = (index_x * count_x).astype(jnp.float32)
        start_z = (index_z * count_z).astype(jnp.float32)
        start_y = (index_y * count_y).astype(jnp.float32)

        def factor(row, start, count):
            cells = lax.broadcasted_iota(jnp.int32, (count, lanes), 0).astype(jnp.float32) + start
            gap = cells - row
            return jnp.exp(-(gap * gap) / kernel_width**2)

        factor_x = factor(rows[0:1], start_x, count_x)
        factor_y = factor(rows[1:2], start_y, count_y)
        factor_z = factor(rows[2:3], start_z, count_z) * kernel_norm
        weights = (factor_x[:, None, :] * factor_z[None, :, :]).reshape(count_x * count_z, lanes)
        for comp in range(3):
            spread = weights * rows[3 + comp : 4 + comp]
            pushed = lax.dot_general(
                spread,
                factor_y,
                (((1,), (1,)), ((), ())),
                precision=lax.Precision.HIGHEST,
                preferred_element_type=jnp.float32,
            )
            force_ref[comp] = pushed.reshape(shape)
            along = jnp.dot(
                q_ref[comp].reshape(count_x * count_z, count_y), factor_y, precision=lax.Precision.HIGHEST, preferred_element_type=jnp.float32
            )
            sample_ref[comp : comp + 1, :] = jnp.sum(along * weights, axis=0, keepdims=True)

    @pl.when(jnp.logical_not(listed))
    def _():
        force_ref[...] = jnp.zeros(force_ref.shape, jnp.float32)
        sample_ref[...] = jnp.zeros(sample_ref.shape, jnp.float32)

    even_x, even_z, even_y = is_even("gx"), is_even("gz"), is_even("gy")
    low_ref[...] = pick(even_x, xb_ref[...], xa_ref[...])
    high_ref[...] = pick(even_x, xa_ref[...], xb_ref[...])
    low_z_ref[...] = pick(even_z, zb_ref[...], za_ref[...])
    high_z_ref[...] = pick(even_z, za_ref[...], zb_ref[...])
    low_y_ref[...] = pick(even_y, yb_ref[...], ya_ref[...])
    high_y_ref[...] = pick(even_y, ya_ref[...], yb_ref[...])

    def plane(x, minus_x, plus_x):
        centre = planes(q_ref, x)
        rows_z, cols_y = [], []
        for comp in range(4):
            rows_z.append((low_z_ref[comp, pl.ds(x, 1), :], high_z_ref[comp, pl.ds(x, 1), :]))
            low_y = pltpu.roll(low_y_ref[comp], (128 - x) % 128 if isinstance(x, int) else 128 - x, 1)
            high_y = pltpu.roll(high_y_ref[comp], 127 - x, 1)
            cols_y.append((jnp.concatenate([low_y, low_y], 1), jnp.concatenate([high_y, high_y], 1)))
        pushed = [force_ref[comp, x] for comp in range(3)]
        for comp, value in enumerate(plane_update(centre, minus_x, plus_x, rows_z, cols_y, pushed, shape)):
            out_ref[comp, x] = value

    def planes(ref, x):
        return [ref[comp, x] for comp in range(4)]

    plane(0, [low_ref[comp] for comp in range(4)], planes(q_ref, 1))

    def middle(x, carry):
        plane(x, planes(q_ref, x - 1), planes(q_ref, x + 1))
        return carry

    lax.fori_loop(1, count_x - 1, middle, 0)
    plane(count_x - 1, planes(q_ref, count_x - 2), [high_ref[comp] for comp in range(4)])
    if not last:
        write_faces(out_ref, face_refs, shape)


def face_shapes(shape):
    count_x, count_z, count_y = shape
    forms = [(4, count_z, count_y)] * 2 + [(4, count_x, count_y)] * 2 + [(4, count_z, 128)] * 2
    return [jax.ShapeDtypeStruct(form, jnp.float32) for form in forms]


def vmem_specs(count):
    return [pl.BlockSpec(memory_space=pltpu.VMEM)] * count


def exchange(faces):
    xa, xb, za, zb, ya, yb = faces
    return [
        swap(za, "gz", 0),
        swap(zb, "gz", 1),
        swap(ya, "gy", 0),
        swap(yb, "gy", 1),
        swap(xa, "gx", 0),
        swap(xb, "gx", 1),
    ]


def shards(flow, positions, loads, block_list):
    capacity = block_list.shape[-1]
    steps_count, _, _, part = positions.shape
    shape = flow.shape[1:]
    count_x, count_z, count_y = shape
    size_x, size_y, size_z = lax.axis_size("gx"), lax.axis_size("gy"), lax.axis_size("gz")
    points = part * size_z
    lanes = capacity * points
    params = pltpu.CompilerParams(vmem_limit_bytes=vmem_limit)
    q = flow
    turbines = block_list.reshape(capacity)

    own = jnp.concatenate([positions.reshape(steps_count, 3, part), loads.reshape(steps_count, 3, part)], axis=1)
    named = sorted_slots(turbines, capacity)
    lists = jnp.pad(jnp.stack(named).astype(jnp.float32), (0, part - capacity))
    own = jnp.concatenate([own, jnp.broadcast_to(lists, (steps_count, 2, part))], axis=1)
    table = own.reshape(1, 8 * steps_count, part)
    for axis in ("gz", "gy", "gx"):
        table = gather_relative(table, axis)

    faces = pl.pallas_call(
        functools.partial(faces_body, shape=shape),
        out_shape=face_shapes(shape),
        in_specs=vmem_specs(1),
        out_specs=vmem_specs(6),
        compiler_params=params,
        name="faces",
    )(q)
    sample_list = []
    for step in range(steps_count):
        last = step == steps_count - 1
        za, zb, ya, yb, xa, xb = exchange(faces)
        shapes = [
            jax.ShapeDtypeStruct(q.shape, jnp.float32),
            jax.ShapeDtypeStruct((3, lanes), jnp.float32),
        ] + ([] if last else face_shapes(shape))
        body = functools.partial(
            step_body, shape=shape, points=points, capacity=capacity, step=step, last=last
        )
        results = pl.pallas_call(
            body,
            out_shape=shapes,
            in_specs=[pl.BlockSpec(memory_space=pltpu.SMEM)] + vmem_specs(8),
            out_specs=vmem_specs(len(shapes)),
            scratch_shapes=[
                pltpu.VMEM((3,) + shape, jnp.float32),
                pltpu.VMEM((8, lanes), jnp.float32),
            ]
            + [pltpu.VMEM(form.shape, jnp.float32) for form in face_shapes(shape)],
            compiler_params=params,
            name="step",
        )(turbines, table, q, xa, xb, za, zb, ya, yb)
        q, samples, faces = results[0], results[1], results[2:]
        sample_list.append(samples)

    sums = jnp.stack(sample_list).reshape(3 * steps_count, capacity, points)
    sums = sums + from_distance(sums, "gz", 1)
    distance = 2
    while distance < size_z:
        sums = sums + from_distance(sums, "gz", distance)
        distance *= 2
    mine = lax.dynamic_slice_in_dim(sums, lax.axis_index("gz") * part, part, axis=2)[None]
    for axis in ("gy", "gx"):
        mine = gather_relative(mine, axis)
    holder = (lax.axis_index("gx") * size_y + lax.axis_index("gy")).astype(jnp.float32)
    named = table[:, 6, :capacity].reshape(-1, size_z, capacity).min(axis=1)
    match = (named == holder).astype(jnp.float32)
    returned = jnp.sum(mine * match[:, None, :, None], axis=(0, 2))
    return q, returned.reshape(positions.shape)


def solution(mesh):
    in_specs = (
        P(None, "gx", "gz", "gy"),
        P(None, None, ("gx", "gy"), "gz"),
        P(None, None, ("gx", "gy"), "gz"),
        P("gx", "gy", "gz", None),
    )
    out_specs = (P(None, "gx", "gz", "gy"), P(None, None, ("gx", "gy"), "gz"))
    return jax.shard_map(shards, mesh=mesh, in_specs=in_specs, out_specs=out_specs, check_vma=False)
```

profile of v0, /device:TPU:0, one launch (start us, length us, event | category | flops | bytes accessed | tf_op | source)
XLA Modules:
  0.0 104.8 jit_solution(12532906270796934611)
XLA Ops:
  0.6 1.3 %fusion.2 = (s32[1,1,1,1]{3,2,1,0:T(1,128)}, s32[1,1,1,1]{3,2,1,0:T(1,128)}) fusion(s32[1,1,1,2]{3,2,1,0:T(1,128)} %param.7), kind=kLoop, calls=%fused_computation.26 | loop fusion | bytes 16 | tf_op jit(solution)/shard_map/slice | solution.py:86
  4.7 0.7 copy_bitcast_fusion
  5.4 3.1 %collective-permute-start = (f32[1,24,32]{2,1,0:T(8,128)S(1)}, f32[1,24,32]{2,1,0:T(8,128)S(1)}, u32[]{:S(2)}, u32[]{:S(2)}) collective-permute-start(f32[1,24,32]{2,1,0:T(8,128)S(1)} %maximum_bitcast_fusion), channel_id=1, source_target_pairs={{0,1},{1,0},{2,3},{3,2},{4,5},{5,4},{6,7},{7,6},{8,9},{9,8},{10,11... | collective-permute-start | bytes 9224 | tf_op jit(solution)/shard_map/ppermute | solution.py:37
  8.5 1.7 %collective-permute-done = f32[1,24,32]{2,1,0:T(8,128)S(1)} collective-permute-done((f32[1,24,32]{2,1,0:T(8,128)S(1)}, f32[1,24,32]{2,1,0:T(8,128)S(1)}, u32[]{:S(2)}, u32[]{:S(2)}) %collective-permute-start) | collective-permute-done | bytes 3104 | tf_op jit(solution)/shard_map/ppermute | solution.py:37
  10.1 3.0 %collective-permute-start.1 = (f32[2,24,32]{2,1,0:T(8,128)S(1)}, f32[2,24,32]{2,1,0:T(8,128)S(1)}, u32[]{:S(2)}, u32[]{:S(2)}) collective-permute-start(f32[2,24,32]{2,1,0:T(8,128)S(1)} %pad_maximum_fusion.3), channel_id=1, source_target_pairs={{0,2},{1,3},{2,0},{3,1},{4,6},{5,7},{6,4},{7,5},{8,10},{9,11},{10,... | collective-permute-start | bytes 18440 | tf_op jit(solution)/shard_map/ppermute | solution.py:37
  13.2 1.8 %collective-permute-done.1 = f32[2,24,32]{2,1,0:T(8,128)S(1)} collective-permute-done((f32[2,24,32]{2,1,0:T(8,128)S(1)}, f32[2,24,32]{2,1,0:T(8,128)S(1)}, u32[]{:S(2)}, u32[]{:S(2)}) %collective-permute-start.1) | collective-permute-done | bytes 6176 | tf_op jit(solution)/shard_map/ppermute | solution.py:37
  15.0 1.9 %collective-permute-start.2 = (f32[4,24,32]{2,1,0:T(8,128)S(1)}, f32[4,24,32]{2,1,0:T(8,128)S(1)}, u32[]{:S(2)}, u32[]{:S(2)}) collective-permute-start(f32[4,24,32]{2,1,0:T(8,128)S(1)} %pad_maximum_fusion.1), channel_id=1, source_target_pairs={{0,4},{4,0},{8,12},{12,8},{1,5},{5,1},{9,13},{13,9},{2,6},{6,2},{1... | collective-permute-start | bytes 36872 | tf_op jit(solution)/shard_map/ppermute | solution.py:37
  16.9 2.3 %collective-permute-done.2 = f32[4,24,32]{2,1,0:T(8,128)S(1)} collective-permute-done((f32[4,24,32]{2,1,0:T(8,128)S(1)}, f32[4,24,32]{2,1,0:T(8,128)S(1)}, u32[]{:S(2)}, u32[]{:S(2)}) %collective-permute-start.2) | collective-permute-done | bytes 12320 | tf_op jit(solution)/shard_map/ppermute | solution.py:37
  19.2 1.9 %collective-permute-start.3 = (f32[8,24,32]{2,1,0:T(8,128)S(1)}, f32[8,24,32]{2,1,0:T(8,128)S(1)}, u32[]{:S(2)}, u32[]{:S(2)}) collective-permute-start(f32[8,24,32]{2,1,0:T(8,128)S(1)} %pad_maximum_fusion), channel_id=1, source_target_pairs={{0,8},{4,12},{8,0},{12,4},{1,9},{5,13},{9,1},{13,5},{2,10},{6,14},... | collective-permute-start | bytes 73736 | tf_op jit(solution)/shard_map/ppermute | solution.py:37
  21.1 2.8 %collective-permute-done.3 = f32[8,24,32]{2,1,0:T(8,128)S(1)} collective-permute-done((f32[8,24,32]{2,1,0:T(8,128)S(1)}, f32[8,24,32]{2,1,0:T(8,128)S(1)}, u32[]{:S(2)}, u32[]{:S(2)}) %collective-permute-start.3) | collective-permute-done | bytes 24608 | tf_op jit(solution)/shard_map/ppermute | solution.py:37
  23.9 1.6 %copy-done = f32[4,32,16,256]{3,2,1,0:T(8,128)S(1)} copy-done((f32[4,32,16,256]{3,2,1,0:T(8,128)S(1)}, f32[4,32,16,256]{3,2,1,0:T(8,128)}, u32[]{:S(2)}) %copy-start) | copy-done | bytes 2097176
  25.5 1.4 %faces.1 = (f32[4,16,256]{2,1,0:T(8,128)S(1)}, f32[4,16,256]{2,1,0:T(8,128)}, f32[4,32,256]{2,1,0:T(8,128)S(1)}, f32[4,32,256]{2,1,0:T(8,128)S(1)}, f32[4,16,128...) custom-call(f32[4,32,16,256]{3,2,1,0:T(8,128)S(1)} %copy-done), custom_call_target="tpu_custom_call" | custom-call | tf_op jit(solution)/shard_map/faces/pallas_call | solution.py:267
  26.9 1.9 %collective-permute-start.6 = (f32[4,32,256]{2,1,0:T(8,128)S(1)}, f32[4,32,256]{2,1,0:T(8,128)S(1)}, u32[]{:S(2)}, u32[]{:S(2)}) collective-permute-start(f32[4,32,256]{2,1,0:T(8,128)S(1)} %get-tuple-element.24), channel_id=1, source_target_pairs={{0,1},{1,0},{2,3},{3,2},{4,5},{5,4},{6,7},{7,6},{8,9},{9,8},{10,11... | collective-permute-start | bytes 393224 | tf_op jit(solution)/shard_map/ppermute | solution.py:32
  29.7 1.5 %collective-permute-start.8 = (f32[4,16,128]{2,1,0:T(8,128)S(1)}, f32[4,16,128]{2,1,0:T(8,128)S(1)}, u32[]{:S(2)}, u32[]{:S(2)}) collective-permute-start(f32[4,16,128]{2,1,0:T(8,128)S(1)} %get-tuple-element.26), channel_id=1, source_target_pairs={{0,4},{4,0},{8,12},{12,8},{1,5},{5,1},{9,13},{13,9},{2,6},{6,2},{1... | collective-permute-start | bytes 98312 | tf_op jit(solution)/shard_map/ppermute | solution.py:32
  31.9 1.7 %collective-permute-done.8.ya_ref = f32[4,16,128]{2,1,0:T(8,128)S(1)} collective-permute-done((f32[4,16,128]{2,1,0:T(8,128)S(1)}, f32[4,16,128]{2,1,0:T(8,128)S(1)}, u32[]{:S(2)}, u32[]{:S(2)}) %collective-permute-start.8) | collective-permute-done | bytes 32800 | tf_op jit(solution)/shard_map/ppermute | solution.py:32
  33.7 9.3 %step.3 = (f32[4,32,16,256]{3,2,1,0:T(8,128)S(1)}, f32[3,256]{1,0:T(4,128)S(1)}, f32[4,16,256]{2,1,0:T(8,128)S(1)}, f32[4,16,256]{2,1,0:T(8,128)}, f32[4,32,256]...) custom-call(s32[2]{0:T(128)S(1)} %bitcast.19, ...), custom_call_target="tpu_custom_call" | custom-call | tf_op jit(solution)/shard_map/step/pallas_call | solution.py:286
  43.0 4.4 %collective-permute-start.11 = (f32[4,32,256]{2,1,0:T(8,128)S(1)}, f32[4,32,256]{2,1,0:T(8,128)S(1)}, u32[]{:S(2)}, u32[]{:S(2)}) collective-permute-start(f32[4,32,256]{2,1,0:T(8,128)S(1)} %get-tuple-element.30), channel_id=1, source_target_pairs={{0,1},{1,0},{2,3},{3,2},{4,5},{5,4},{6,7},{7,6},{8,9},{9,8},{10,11... | collective-permute-start | bytes 393224 | tf_op jit(solution)/shard_map/ppermute | solution.py:32
  48.1 4.9 %collective-permute-start.13 = (f32[4,16,128]{2,1,0:T(8,128)S(1)}, f32[4,16,128]{2,1,0:T(8,128)S(1)}, u32[]{:S(2)}, u32[]{:S(2)}) collective-permute-start(f32[4,16,128]{2,1,0:T(8,128)S(1)} %get-tuple-element.32), channel_id=1, source_target_pairs={{0,4},{4,0},{8,12},{12,8},{1,5},{5,1},{9,13},{13,9},{2,6},{6,2},{1... | collective-permute-start | bytes 98312 | tf_op jit(solution)/shard_map/ppermute | solution.py:32
  53.7 1.3 %collective-permute-done.13.ya_ref = f32[4,16,128]{2,1,0:T(8,128)S(1)} collective-permute-done((f32[4,16,128]{2,1,0:T(8,128)S(1)}, f32[4,16,128]{2,1,0:T(8,128)S(1)}, u32[]{:S(2)}, u32[]{:S(2)}) %collective-permute-start.13) | collective-permute-done | bytes 32800 | tf_op jit(solution)/shard_map/ppermute | solution.py:32
  55.0 9.4 %step.4 = (f32[4,32,16,256]{3,2,1,0:T(8,128)S(1)}, f32[3,256]{1,0:T(4,128)S(1)}, f32[4,16,256]{2,1,0:T(8,128)S(1)}, f32[4,16,256]{2,1,0:T(8,128)}, f32[4,32,256]...) custom-call(s32[2]{0:T(128)S(1)} %bitcast.20, ...), custom_call_target="tpu_custom_call" | custom-call | tf_op jit(solution)/shard_map/step/pallas_call | solution.py:286
  64.5 1.3 %collective-permute-start.16 = (f32[4,32,256]{2,1,0:T(8,128)S(1)}, f32[4,32,256]{2,1,0:T(8,128)S(1)}, u32[]{:S(2)}, u32[]{:S(2)}) collective-permute-start(f32[4,32,256]{2,1,0:T(8,128)S(1)} %get-tuple-element.36), channel_id=1, source_target_pairs={{0,1},{1,0},{2,3},{3,2},{4,5},{5,4},{6,7},{7,6},{8,9},{9,8},{10,11... | collective-permute-start | bytes 393224 | tf_op jit(solution)/shard_map/ppermute | solution.py:32
  66.5 4.8 %collective-permute-start.18 = (f32[4,16,128]{2,1,0:T(8,128)S(1)}, f32[4,16,128]{2,1,0:T(8,128)S(1)}, u32[]{:S(2)}, u32[]{:S(2)}) collective-permute-start(f32[4,16,128]{2,1,0:T(8,128)S(1)} %get-tuple-element.38), channel_id=1, source_target_pairs={{0,4},{4,0},{8,12},{12,8},{1,5},{5,1},{9,13},{13,9},{2,6},{6,2},{1... | collective-permute-start | bytes 98312 | tf_op jit(solution)/shard_map/ppermute | solution.py:32
  71.9 1.3 %collective-permute-done.18.ya_ref = f32[4,16,128]{2,1,0:T(8,128)S(1)} collective-permute-done((f32[4,16,128]{2,1,0:T(8,128)S(1)}, f32[4,16,128]{2,1,0:T(8,128)S(1)}, u32[]{:S(2)}, u32[]{:S(2)}) %collective-permute-start.18) | collective-permute-done | bytes 32800 | tf_op jit(solution)/shard_map/ppermute | solution.py:32
  73.3 9.9 %step.5 = (f32[4,32,16,256]{3,2,1,0:T(8,128)}, f32[3,256]{1,0:T(4,128)S(1)}) custom-call(s32[2]{0:T(128)S(1)} %bitcast.21, f32[32,24,32]{2,1,0:T(8,128)S(1)} %constant_dynamic-update-slice_fusion.5.table_ref, f32[4,32,16,256]{3,2,1,0:T(8,128)S(1)} %get-tuple-element.34.q_ref, f32[4,16,256]{2,1,0:T(8,128)S(1)} %collective-permute-done.15.xa_ref, ...), custom_call_target="tpu_custom_call" | custom-call | tf_op jit(solution)/shard_map/step/pallas_call | solution.py:286
  83.1 2.1 %collective-permute-start.20 = (f32[9,2,128]{2,1,0:T(2,128)S(1)}, f32[9,2,128]{2,1,0:T(2,128)S(1)}, u32[]{:S(2)}, u32[]{:S(2)}) collective-permute-start(f32[9,2,128]{2,1,0:T(2,128)S(1)} %reshape.38), channel_id=1, source_target_pairs={{0,1},{1,0},{2,3},{3,2},{4,5},{5,4},{6,7},{7,6},{8,9},{9,8},{10,11... | collective-permute-start | bytes 27656 | tf_op jit(solution)/shard_map/ppermute | solution.py:37
  85.2 1.6 %collective-permute-done.20 = f32[9,2,128]{2,1,0:T(2,128)S(1)} collective-permute-done((f32[9,2,128]{2,1,0:T(2,128)S(1)}, f32[9,2,128]{2,1,0:T(2,128)S(1)}, u32[]{:S(2)}, u32[]{:S(2)}) %collective-permute-start.20) | collective-permute-done | bytes 9248 | tf_op jit(solution)/shard_map/ppermute | solution.py:37
  87.5 4.0 %collective-permute-done.21 = f32[9,2,128]{2,1,0:T(2,128)S(1)} collective-permute-done((f32[9,2,128]{2,1,0:T(2,128)S(1)}, f32[9,2,128]{2,1,0:T(2,128)S(1)}, u32[]{:S(2)}, u32[]{:S(2)}) %collective-permute-start.21) | collective-permute-done | bytes 9248 | tf_op jit(solution)/shard_map/ppermute | solution.py:37
  91.5 4.8 %collective-permute-start.22 = (f32[1,9,2,32]{3,2,1,0:T(2,128)S(1)}, f32[1,9,2,32]{3,2,1,0:T(2,128)S(1)}, u32[]{:S(2)}, u32[]{:S(2)}) collective-permute-start(f32[1,9,2,32]{3,2,1,0:T(2,128)S(1)} %fusion.1), channel_id=1, source_target_pairs={{0,4},{4,0},{8,12},{12,8},{1,5},{5,1},{9,13},{13,9},{2,6},{6,2},{1... | collective-permute-start | bytes 6920 | tf_op jit(solution)/shard_map/ppermute | solution.py:37
  96.3 1.6 %collective-permute-done.22 = f32[1,9,2,32]{3,2,1,0:T(2,128)S(1)} collective-permute-done((f32[1,9,2,32]{3,2,1,0:T(2,128)S(1)}, f32[1,9,2,32]{3,2,1,0:T(2,128)S(1)}, u32[]{:S(2)}, u32[]{:S(2)}) %collective-permute-start.22) | collective-permute-done | bytes 2336 | tf_op jit(solution)/shard_map/ppermute | solution.py:37
  98.0 3.1 %collective-permute-start.23 = (f32[2,9,2,32]{3,2,1,0:T(2,128)S(1)}, f32[2,9,2,32]{3,2,1,0:T(2,128)S(1)}, u32[]{:S(2)}, u32[]{:S(2)}) collective-permute-start(f32[2,9,2,32]{3,2,1,0:T(2,128)S(1)} %pad_maximum_fusion.4), channel_id=1, source_target_pairs={{0,8},{4,12},{8,0},{12,4},{1,9},{5,13},{9,1},{13,5},{2,10},{6,14},... | collective-permute-start | bytes 13832 | tf_op jit(solution)/shard_map/ppermute | solution.py:37
  101.2 1.6 %collective-permute-done.23 = f32[2,9,2,32]{3,2,1,0:T(2,128)S(1)} collective-permute-done((f32[2,9,2,32]{3,2,1,0:T(2,128)S(1)}, f32[2,9,2,32]{3,2,1,0:T(2,128)S(1)}, u32[]{:S(2)}, u32[]{:S(2)}) %collective-permute-start.23) | collective-permute-done | bytes 4640 | tf_op jit(solution)/shard_map/ppermute | solution.py:37
  103.0 1.1 %collective-permute-done.24 = f32[4,9,2,32]{3,2,1,0:T(2,128)S(1)} collective-permute-done((f32[4,9,2,32]{3,2,1,0:T(2,128)S(1)}, f32[4,9,2,32]{3,2,1,0:T(2,128)S(1)}, u32[]{:S(2)}, u32[]{:S(2)}) %collective-permute-start.24) | collective-permute-done | bytes 9248 | tf_op jit(solution)/shard_map/ppermute | solution.py:37
  (55 shorter events, 6.4 us)
Async XLA Ops:
  0.6 33.1 %copy-start.1 = (s32[1,1,1,2]{3,2,1,0:T(1,128)S(1)}, s32[1,1,1,2]{3,2,1,0:T(1,128)}, u32[]{:S(2)}) copy-start(s32[1,1,1,2]{3,2,1,0:T(1,128)} %param.7) | copy-start | bytes 28
  5.4 4.8 %collective-permute-start = (f32[1,24,32]{2,1,0:T(8,128)S(1)}, f32[1,24,32]{2,1,0:T(8,128)S(1)}, u32[]{:S(2)}, u32[]{:S(2)}) collective-permute-start(f32[1,24,32]{2,1,0:T(8,128)S(1)} %maximum_bitcast_fusion), channel_id=1, source_target_pairs={{0,1},{1,0},{2,3},{3,2},{4,5},{5,4},{6,7},{7,6},{8,9},{9,8},{10,11... | collective-permute-start | bytes 9224 | tf_op jit(solution)/shard_map/ppermute | solution.py:37
  10.1 4.8 %collective-permute-start.1 = (f32[2,24,32]{2,1,0:T(8,128)S(1)}, f32[2,24,32]{2,1,0:T(8,128)S(1)}, u32[]{:S(2)}, u32[]{:S(2)}) collective-permute-start(f32[2,24,32]{2,1,0:T(8,128)S(1)} %pad_maximum_fusion.3), channel_id=1, source_target_pairs={{0,2},{1,3},{2,0},{3,1},{4,6},{5,7},{6,4},{7,5},{8,10},{9,11},{10,... | collective-permute-start | bytes 18440 | tf_op jit(solution)/shard_map/ppermute | solution.py:37
  15.0 4.2 %collective-permute-start.2 = (f32[4,24,32]{2,1,0:T(8,128)S(1)}, f32[4,24,32]{2,1,0:T(8,128)S(1)}, u32[]{:S(2)}, u32[]{:S(2)}) collective-permute-start(f32[4,24,32]{2,1,0:T(8,128)S(1)} %pad_maximum_fusion.1), channel_id=1, source_target_pairs={{0,4},{4,0},{8,12},{12,8},{1,5},{5,1},{9,13},{13,9},{2,6},{6,2},{1... | collective-permute-start | bytes 36872 | tf_op jit(solution)/shard_map/ppermute | solution.py:37
  19.2 4.7 %collective-permute-start.3 = (f32[8,24,32]{2,1,0:T(8,128)S(1)}, f32[8,24,32]{2,1,0:T(8,128)S(1)}, u32[]{:S(2)}, u32[]{:S(2)}) collective-permute-start(f32[8,24,32]{2,1,0:T(8,128)S(1)} %pad_maximum_fusion), channel_id=1, source_target_pairs={{0,8},{4,12},{8,0},{12,4},{1,9},{5,13},{9,1},{13,5},{2,10},{6,14},... | collective-permute-start | bytes 73736 | tf_op jit(solution)/shard_map/ppermute | solution.py:37
  23.9 7.4 %collective-permute-start.4 = (f32[16,24,32]{2,1,0:T(8,128)S(1)}, f32[16,24,32]{2,1,0:T(8,128)S(1)}, u32[]{:S(2)}, u32[]{:S(2)}) collective-permute-start(f32[16,24,32]{2,1,0:T(8,128)S(1)} %get-tuple-element.44), channel_id=1, source_target_pairs={{0,16},{16,0},{1,17},{17,1},{2,18},{18,2},{3,19},{19,3},{4,20},{20... | collective-permute-start | bytes 147464 | tf_op jit(solution)/shard_map/ppermute | solution.py:37
  23.9 1.6 %copy-start = (f32[4,32,16,256]{3,2,1,0:T(8,128)S(1)}, f32[4,32,16,256]{3,2,1,0:T(8,128)}, u32[]{:S(2)}) copy-start(f32[4,32,16,256]{3,2,1,0:T(8,128)} %q_ref.3) | copy-start | bytes 6291460
  26.9 6.8 %collective-permute-start.6 = (f32[4,32,256]{2,1,0:T(8,128)S(1)}, f32[4,32,256]{2,1,0:T(8,128)S(1)}, u32[]{:S(2)}, u32[]{:S(2)}) collective-permute-start(f32[4,32,256]{2,1,0:T(8,128)S(1)} %get-tuple-element.24), channel_id=1, source_target_pairs={{0,1},{1,0},{2,3},{3,2},{4,5},{5,4},{6,7},{7,6},{8,9},{9,8},{10,11... | collective-permute-start | bytes 393224 | tf_op jit(solution)/shard_map/ppermute | solution.py:32
  28.8 4.9 %collective-permute-start.7 = (f32[4,32,256]{2,1,0:T(8,128)S(1)}, f32[4,32,256]{2,1,0:T(8,128)S(1)}, u32[]{:S(2)}, u32[]{:S(2)}) collective-permute-start(f32[4,32,256]{2,1,0:T(8,128)S(1)} %get-tuple-element.25), channel_id=1, source_target_pairs={{1,2},{2,1},{5,6},{6,5},{9,10},{10,9},{13,14},{14,13},{17,18},{18,... | collective-permute-start | bytes 393224 | tf_op jit(solution)/shard_map/ppermute | solution.py:32
  29.5 4.2 %collective-permute-start.5 = (f32[4,16,256]{2,1,0:T(8,128)S(1)}, f32[4,16,256]{2,1,0:T(8,128)S(1)}, u32[]{:S(2)}, u32[]{:S(2)}) collective-permute-start(f32[4,16,256]{2,1,0:T(8,128)S(1)} %get-tuple-element.23), channel_id=1, source_target_pairs={{0,16},{16,0},{1,17},{17,1},{2,18},{18,2},{3,19},{19,3},{4,20},{20... | collective-permute-start | bytes 196616 | tf_op jit(solution)/shard_map/ppermute | solution.py:32
  29.7 3.9 %collective-permute-start.8 = (f32[4,16,128]{2,1,0:T(8,128)S(1)}, f32[4,16,128]{2,1,0:T(8,128)S(1)}, u32[]{:S(2)}, u32[]{:S(2)}) collective-permute-start(f32[4,16,128]{2,1,0:T(8,128)S(1)} %get-tuple-element.26), channel_id=1, source_target_pairs={{0,4},{4,0},{8,12},{12,8},{1,5},{5,1},{9,13},{13,9},{2,6},{6,2},{1... | collective-permute-start | bytes 98312 | tf_op jit(solution)/shard_map/ppermute | solution.py:32
  31.2 2.4 %collective-permute-start.9 = (f32[4,16,128]{2,1,0:T(8,128)S(1)}, f32[4,16,128]{2,1,0:T(8,128)S(1)}, u32[]{:S(2)}, u32[]{:S(2)}) collective-permute-start(f32[4,16,128]{2,1,0:T(8,128)S(1)} %get-tuple-element.27), channel_id=1, source_target_pairs={{4,8},{8,4},{5,9},{9,5},{6,10},{10,6},{7,11},{11,7},{20,24},{24,20... | collective-permute-start | bytes 98312 | tf_op jit(solution)/shard_map/ppermute | solution.py:32
  43.0 12.0 %collective-permute-start.11 = (f32[4,32,256]{2,1,0:T(8,128)S(1)}, f32[4,32,256]{2,1,0:T(8,128)S(1)}, u32[]{:S(2)}, u32[]{:S(2)}) collective-permute-start(f32[4,32,256]{2,1,0:T(8,128)S(1)} %get-tuple-element.30), channel_id=1, source_target_pairs={{0,1},{1,0},{2,3},{3,2},{4,5},{5,4},{6,7},{7,6},{8,9},{9,8},{10,11... | collective-permute-start | bytes 393224 | tf_op jit(solution)/shard_map/ppermute | solution.py:32
  47.4 7.6 %collective-permute-start.12 = (f32[4,32,256]{2,1,0:T(8,128)S(1)}, f32[4,32,256]{2,1,0:T(8,128)S(1)}, u32[]{:S(2)}, u32[]{:S(2)}) collective-permute-start(f32[4,32,256]{2,1,0:T(8,128)S(1)} %get-tuple-element.31), channel_id=1, source_target_pairs={{1,2},{2,1},{5,6},{6,5},{9,10},{10,9},{13,14},{14,13},{17,18},{18,... | collective-permute-start | bytes 393224 | tf_op jit(solution)/shard_map/ppermute | solution.py:32
  48.1 6.9 %collective-permute-start.10 = (f32[4,16,256]{2,1,0:T(8,128)S(1)}, f32[4,16,256]{2,1,0:T(8,128)S(1)}, u32[]{:S(2)}, u32[]{:S(2)}) collective-permute-start(f32[4,16,256]{2,1,0:T(8,128)S(1)} %get-tuple-element.29), channel_id=1, source_target_pairs={{0,16},{16,0},{1,17},{17,1},{2,18},{18,2},{3,19},{19,3},{4,20},{20... | collective-permute-start | bytes 196616 | tf_op jit(solution)/shard_map/ppermute | solution.py:32
  48.1 6.8 %collective-permute-start.13 = (f32[4,16,128]{2,1,0:T(8,128)S(1)}, f32[4,16,128]{2,1,0:T(8,128)S(1)}, u32[]{:S(2)}, u32[]{:S(2)}) collective-permute-start(f32[4,16,128]{2,1,0:T(8,128)S(1)} %get-tuple-element.32), channel_id=1, source_target_pairs={{0,4},{4,0},{8,12},{12,8},{1,5},{5,1},{9,13},{13,9},{2,6},{6,2},{1... | collective-permute-start | bytes 98312 | tf_op jit(solution)/shard_map/ppermute | solution.py:32
  53.0 2.0 %collective-permute-start.14 = (f32[4,16,128]{2,1,0:T(8,128)S(1)}, f32[4,16,128]{2,1,0:T(8,128)S(1)}, u32[]{:S(2)}, u32[]{:S(2)}) collective-permute-start(f32[4,16,128]{2,1,0:T(8,128)S(1)} %get-tuple-element.33), channel_id=1, source_target_pairs={{4,8},{8,4},{5,9},{9,5},{6,10},{10,6},{7,11},{11,7},{20,24},{24,20... | collective-permute-start | bytes 98312 | tf_op jit(solution)/shard_map/ppermute | solution.py:32
  64.5 8.8 %collective-permute-start.16 = (f32[4,32,256]{2,1,0:T(8,128)S(1)}, f32[4,32,256]{2,1,0:T(8,128)S(1)}, u32[]{:S(2)}, u32[]{:S(2)}) collective-permute-start(f32[4,32,256]{2,1,0:T(8,128)S(1)} %get-tuple-element.36), channel_id=1, source_target_pairs={{0,1},{1,0},{2,3},{3,2},{4,5},{5,4},{6,7},{7,6},{8,9},{9,8},{10,11... | collective-permute-start | bytes 393224 | tf_op jit(solution)/shard_map/ppermute | solution.py:32
  65.7 7.5 %collective-permute-start.17 = (f32[4,32,256]{2,1,0:T(8,128)S(1)}, f32[4,32,256]{2,1,0:T(8,128)S(1)}, u32[]{:S(2)}, u32[]{:S(2)}) collective-permute-start(f32[4,32,256]{2,1,0:T(8,128)S(1)} %get-tuple-element.37), channel_id=1, source_target_pairs={{1,2},{2,1},{5,6},{6,5},{9,10},{10,9},{13,14},{14,13},{17,18},{18,... | collective-permute-start | bytes 393224 | tf_op jit(solution)/shard_map/ppermute | solution.py:32
  66.4 6.9 %collective-permute-start.15 = (f32[4,16,256]{2,1,0:T(8,128)S(1)}, f32[4,16,256]{2,1,0:T(8,128)S(1)}, u32[]{:S(2)}, u32[]{:S(2)}) collective-permute-start(f32[4,16,256]{2,1,0:T(8,128)S(1)} %get-tuple-element.35), channel_id=1, source_target_pairs={{0,16},{16,0},{1,17},{17,1},{2,18},{18,2},{3,19},{19,3},{4,20},{20... | collective-permute-start | bytes 196616 | tf_op jit(solution)/shard_map/ppermute | solution.py:32
  66.5 6.8 %collective-permute-start.18 = (f32[4,16,128]{2,1,0:T(8,128)S(1)}, f32[4,16,128]{2,1,0:T(8,128)S(1)}, u32[]{:S(2)}, u32[]{:S(2)}) collective-permute-start(f32[4,16,128]{2,1,0:T(8,128)S(1)} %get-tuple-element.38), channel_id=1, source_target_pairs={{0,4},{4,0},{8,12},{12,8},{1,5},{5,1},{9,13},{13,9},{2,6},{6,2},{1... | collective-permute-start | bytes 98312 | tf_op jit(solution)/shard_map/ppermute | solution.py:32
  71.2 2.0 %collective-permute-start.19 = (f32[4,16,128]{2,1,0:T(8,128)S(1)}, f32[4,16,128]{2,1,0:T(8,128)S(1)}, u32[]{:S(2)}, u32[]{:S(2)}) collective-permute-start(f32[4,16,128]{2,1,0:T(8,128)S(1)} %get-tuple-element.39), channel_id=1, source_target_pairs={{4,8},{8,4},{5,9},{9,5},{6,10},{10,6},{7,11},{11,7},{20,24},{24,20... | collective-permute-start | bytes 98312 | tf_op jit(solution)/shard_map/ppermute | solution.py:32
  83.1 3.7 %collective-permute-start.20 = (f32[9,2,128]{2,1,0:T(2,128)S(1)}, f32[9,2,128]{2,1,0:T(2,128)S(1)}, u32[]{:S(2)}, u32[]{:S(2)}) collective-permute-start(f32[9,2,128]{2,1,0:T(2,128)S(1)} %reshape.38), channel_id=1, source_target_pairs={{0,1},{1,0},{2,3},{3,2},{4,5},{5,4},{6,7},{7,6},{8,9},{9,8},{10,11... | collective-permute-start | bytes 27656 | tf_op jit(solution)/shard_map/ppermute | solution.py:37
  86.9 4.6 %collective-permute-start.21 = (f32[9,2,128]{2,1,0:T(2,128)S(1)}, f32[9,2,128]{2,1,0:T(2,128)S(1)}, u32[]{:S(2)}, u32[]{:S(2)}) collective-permute-start(f32[9,2,128]{2,1,0:T(2,128)S(1)} %add.14), channel_id=1, source_target_pairs={{0,2},{1,3},{2,0},{3,1},{4,6},{5,7},{6,4},{7,5},{8,10},{9,11},{10,... | collective-permute-start | bytes 27656 | tf_op jit(solution)/shard_map/ppermute | solution.py:37
  91.5 6.4 %collective-permute-start.22 = (f32[1,9,2,32]{3,2,1,0:T(2,128)S(1)}, f32[1,9,2,32]{3,2,1,0:T(2,128)S(1)}, u32[]{:S(2)}, u32[]{:S(2)}) collective-permute-start(f32[1,9,2,32]{3,2,1,0:T(2,128)S(1)} %fusion.1), channel_id=1, source_target_pairs={{0,4},{4,0},{8,12},{12,8},{1,5},{5,1},{9,13},{13,9},{2,6},{6,2},{1... | collective-permute-start | bytes 6920 | tf_op jit(solution)/shard_map/ppermute | solution.py:37
  98.0 4.8 %collective-permute-start.23 = (f32[2,9,2,32]{3,2,1,0:T(2,128)S(1)}, f32[2,9,2,32]{3,2,1,0:T(2,128)S(1)}, u32[]{:S(2)}, u32[]{:S(2)}) collective-permute-start(f32[2,9,2,32]{3,2,1,0:T(2,128)S(1)} %pad_maximum_fusion.4), channel_id=1, source_target_pairs={{0,8},{4,12},{8,0},{12,4},{1,9},{5,13},{9,1},{13,5},{2,10},{6,14},... | collective-permute-start | bytes 13832 | tf_op jit(solution)/shard_map/ppermute | solution.py:37
  102.8 1.3 %collective-permute-start.24 = (f32[4,9,2,32]{3,2,1,0:T(2,128)S(1)}, f32[4,9,2,32]{3,2,1,0:T(2,128)S(1)}, u32[]{:S(2)}, u32[]{:S(2)}) collective-permute-start(f32[4,9,2,32]{3,2,1,0:T(2,128)S(1)} %pad_maximum_fusion.2), channel_id=1, source_target_pairs={{0,16},{16,0},{1,17},{17,1},{2,18},{18,2},{3,19},{19,3},{4,20},{20... | collective-permute-start | bytes 27656 | tf_op jit(solution)/shard_map/ppermute | solution.py:37
where the time goes:
time: 105 us
  starting transfers between devices  43.7 us (42%)
  Pallas kernels  29.9 us (28%)
  waiting for transfers between devices  22.9 us (22%)
  local copies, waits for them, and re-layouts  4.5 us (4%)
  between operations  3.44 us (3%)
    pallas_call x3, Pallas kernels, shards(): pl.pallas_call(body, out_shape=shapes, in_specs=[pl.BlockSpec(memory_spac...  28.6 us
    ppermute x15, starting transfers between devices, swap(): return lax.ppermute(value, axis, pairs)  23.1 us
    ppermute x10, starting transfers between devices, from_distance(): return lax.ppermute(value, axis, [(i, i ^ distance) for i in range(count)])  20.6 us
    ppermute x10, waiting for transfers between devices, from_distance(): return lax.ppermute(value, axis, [(i, i ^ distance) for i in range(count)])  18.4 us
    ppermute x15, waiting for transfers between devices, swap(): return lax.ppermute(value, axis, pairs)  4.42 us
    unnamed x9, local copies, waits for them, and re-layouts  2.39 us
  transfers between devices with their start and end apart: 25, of which 12 were waited for; matrix products, arithmetic and copies ran while one was open for 0% of the time, Pallas kernels for 1%

commit v1 on v0

v1 whole, which is shorter than its diff:
```python
import functools
import math

import jax
import jax.numpy as jnp
from jax import lax
from jax.experimental import pallas as pl
from jax.experimental.pallas import tpu as pltpu
from jax.sharding import PartitionSpec as P

kernel_width = 2.0
kernel_norm = 1.0 / (math.pi**1.5 * kernel_width**3)
time_step = 0.1
smag_coef = 0.17
viscosity = 0.02
diffusivity = 0.02
prandtl = 0.4
vmem_limit = 48 << 20


def swap_pairs(count, first):
    pairs = []
    for low in range(first, count - 1, 2):
        pairs += [(low, low + 1), (low + 1, low)]
    return pairs


def swap(value, axis, first):
    pairs = swap_pairs(lax.axis_size(axis), first)
    if not pairs:
        return jnp.zeros_like(value)
    return lax.ppermute(value, axis, pairs)


def from_distance(value, axis, distance):
    count = lax.axis_size(axis)
    return lax.ppermute(value, axis, [(i, i ^ distance) for i in range(count)])


def gather_relative(value, axis):
    distance = 1
    while distance < lax.axis_size(axis):
        value = jnp.concatenate([value, from_distance(value, axis, distance)], axis=0)
        distance *= 2
    return value


def pick(flag, first, second):
    return jnp.where(flag, first, second)


def is_even(axis):
    return lax.rem(lax.axis_index(axis), 2) == 0


def write_faces(q_ref, face_refs, shape):
    count_x, count_z, count_y = shape
    za_ref, zb_ref, ya_ref, yb_ref, xa_ref, xb_ref = face_refs
    even_x, even_z, even_y = is_even("gx"), is_even("gz"), is_even("gy")
    low, high = q_ref[:, 0], q_ref[:, count_x - 1]
    xa_ref[...] = pick(even_x, high, low)
    xb_ref[...] = pick(even_x, low, high)
    for comp in range(4):
        low = q_ref[comp, :, 0, :]
        high = q_ref[comp, :, count_z - 1, :]
        za_ref[comp] = pick(even_z, high, low)
        zb_ref[comp] = pick(even_z, low, high)
    lane = lax.broadcasted_iota(jnp.int32, (count_z, 128), 1)
    for comp in range(4):
        low = jnp.zeros((count_z, 128), jnp.float32)
        high = jnp.zeros((count_z, 128), jnp.float32)
        for x in range(count_x):
            first = q_ref[comp, x, :, :128]
            last = q_ref[comp, x, :, count_y - 128 :]
            low = jnp.where(lane == x, pltpu.roll(first, x, 1), low)
            high = jnp.where(lane == x, pltpu.roll(last, (x + 1) % 128, 1), high)
        ya_ref[comp] = pick(even_y, high, low)
        yb_ref[comp] = pick(even_y, low, high)


def faces_body(q_ref, *face_refs, shape):
    write_faces(q_ref, face_refs, shape)


def sorted_slots(list_ref, capacity):
    slots = [list_ref[j] for j in range(capacity)]
    for first in range(capacity):
        for second in range(first + 1, capacity):
            a, b = slots[first], slots[second]
            slots[first], slots[second] = jnp.minimum(a, b), jnp.maximum(a, b)
    return slots


def masks_of(shape):
    count_z = shape[1]
    sub = lax.broadcasted_iota(jnp.int32, (count_z, 128), 0)
    lane = lax.broadcasted_iota(jnp.int32, (count_z, 128), 1)
    return sub == 0, sub == count_z - 1, lane == 0, lane == 127


def tile_update(shifts, pushed):
    diffs, laplace, centre = [], [], []
    for c, minus_x, plus_x, minus_y, plus_y, minus_z, plus_z in shifts:
        diffs.append((plus_x - minus_x, plus_y - minus_y, plus_z - minus_z))
        laplace.append((plus_x + minus_x) + (plus_y + minus_y) + (plus_z + minus_z) - 6.0 * c)
        centre.append(c)
    diagonal = diffs[0][0] * diffs[0][0] + diffs[1][1] * diffs[1][1] + diffs[2][2] * diffs[2][2]
    xy = diffs[0][1] + diffs[1][0]
    xz = diffs[0][2] + diffs[2][0]
    yz = diffs[1][2] + diffs[2][1]
    total = (diagonal + diagonal) + (xy * xy + xz * xz + yz * yz)
    root = total * lax.rsqrt(jnp.maximum(total, 1.1754944e-38))
    scale_u = time_step * viscosity + (0.5 * time_step * smag_coef**2) * root
    scale_t = time_step * diffusivity + (0.5 * time_step * smag_coef**2 / prandtl) * root
    half = [0.5 * time_step * centre[a] for a in range(3)]
    out = []
    for comp in range(4):
        d = diffs[comp]
        moved = half[0] * d[0] + half[1] * d[1] + half[2] * d[2]
        value = centre[comp] - moved + (scale_u if comp < 3 else scale_t) * laplace[comp]
        out.append(value + pushed[comp] if comp < 3 else value)
    return out


def split(value):
    high = value.astype(jnp.bfloat16)
    low = (value - high.astype(jnp.float32)).astype(jnp.bfloat16)
    return high, low


def turbine_rows(rows_ref, table_ref, slots, step, points):
    index_x, index_y, index_z = lax.axis_index("gx"), lax.axis_index("gy"), lax.axis_index("gz")
    size_x, size_y, size_z = lax.axis_size("gx"), lax.axis_size("gy"), lax.axis_size("gz")
    part = points // size_z
    for j, slot in enumerate(slots):
        t = jnp.minimum(slot, size_x * size_y - 1)
        place_x = lax.bitwise_xor(lax.div(t, size_y), index_x)
        place_y = lax.bitwise_xor(lax.rem(t, size_y), index_y)
        for c in range(size_z):
            entry = (place_x * size_y + place_y) * size_z + lax.bitwise_xor(index_z, c)
            offset = j * points + c * part
            rows_ref[:, offset : offset + part] = table_ref[entry, 8 * step : 8 * step + 8, :]
    return rows_ref[...]


def point_factors(rows, shape):
    lanes = rows.shape[1]

    def factor(row, axis, count):
        start = (lax.axis_index(axis) * count).astype(jnp.float32)
        cells = lax.broadcasted_iota(jnp.int32, (count, lanes), 0).astype(jnp.float32) + start
        gap = cells - row
        return jnp.exp(-(gap * gap) / kernel_width**2)

    count_x, count_z, count_y = shape
    factor_x = factor(rows[0:1], "gx", count_x)
    factor_y = factor(rows[1:2], "gy", count_y)
    factor_z = factor(rows[2:3], "gz", count_z) * kernel_norm
    weights = (factor_x[:, None, :] * factor_z[None, :, :]).reshape(count_x * count_z, lanes)
    return weights, split(factor_y)


def push(force_ref, rows, weights, factor_y, shape):
    high, low = factor_y
    right = jnp.concatenate([high, high, low], axis=1)
    for comp in range(3):
        first, second = split(weights * (rows[3 + comp : 4 + comp] * time_step))
        left = jnp.concatenate([first, second, first], axis=1)
        pushed = lax.dot_general(left, right, (((1,), (1,)), ((), ())), preferred_element_type=jnp.float32)
        force_ref[comp] = pushed.reshape(shape)


def sample(q_ref, weights, factor_y, shape):
    count_x, count_z, count_y = shape
    high, low = factor_y
    right = jnp.concatenate([high, high, low], axis=0)
    sums = []
    for comp in range(3):
        first, second = split(q_ref[comp].reshape(count_x * count_z, count_y))
        left = jnp.concatenate([first, second, first], axis=1)
        along = jnp.dot(left, right, preferred_element_type=jnp.float32)
        sums.append(jnp.sum(along * weights, axis=0, keepdims=True))
    return sums


def step_body(*refs, shape, points, capacity, step, steps):
    count_x, count_z, count_y = shape
    last, packs = step == steps - 1, step == steps - 2
    refs = list(refs)
    list_ref, table_ref, q_ref = refs[:3]
    za_ref, zb_ref, ya_ref, yb_ref, xa_ref, xb_ref = refs[3:9]
    refs = refs[9:]
    past_ref = None if step == 0 or last else refs.pop(0)
    out_ref = refs.pop(0)
    if not last:
        face_refs, refs = refs[:6], refs[6:]
        sample_ref = refs.pop(0)
    force_ref, rows_ref, low_z_ref, high_z_ref, low_y_ref, high_y_ref, low_x_ref, high_x_ref = refs
    slots = sorted_slots(list_ref, capacity)
    listed = slots[0] < lax.axis_size("gx") * lax.axis_size("gy")

    if not last:
        sample_ref[...] = jnp.zeros(sample_ref.shape, jnp.float32)
        if past_ref is not None:
            sample_ref[: 3 * step + 3] = past_ref[: 3 * step + 3]

    @pl.when(listed)
    def _():
        rows = turbine_rows(rows_ref, table_ref, slots, step, points)
        weights, factor_y = point_factors(rows, shape)
        push(force_ref, rows, weights, factor_y, shape)
        if step == 0:
            for comp, value in enumerate(sample(q_ref, weights, factor_y, shape)):
                sample_ref[comp : comp + 1] = value

    @pl.when(jnp.logical_not(listed))
    def _():
        force_ref[...] = jnp.zeros(force_ref.shape, jnp.float32)

    even_x, even_z, even_y = is_even("gx"), is_even("gz"), is_even("gy")
    index_y = lax.axis_index("gy")
    tiles = count_y // 128
    for tile in range(tiles):
        first, second = (ref[:4, :, tile * 128 : tile * 128 + 128] for ref in (za_ref, zb_ref))
        low_z_ref[:, tile] = pick(even_z, second, first)
        high_z_ref[:, tile] = pick(even_z, first, second)
    low_y_ref[...] = pick(index_y == 0, 0.0, pick(even_y, yb_ref[:4], ya_ref[:4]))
    high_y_ref[...] = pick(index_y == lax.axis_size("gy") - 1, 0.0, pick(even_y, ya_ref[:4], yb_ref[:4]))
    low_x_ref[...] = pick(even_x, xb_ref[...], xa_ref[...])
    high_x_ref[...] = pick(even_x, xa_ref[...], xb_ref[...])
    first_z, last_z, first_y, last_y = masks_of(shape)

    def plane(x, minus, plus):
        for tile in range(tiles):
            here = slice(tile * 128, tile * 128 + 128)
            shifts = []
            for comp in range(4):
                c = q_ref[comp, x, :, here]
                if tile:
                    before = pltpu.roll(q_ref[comp, x, :, tile * 128 - 128 : tile * 128], 1, 1)
                else:
                    turn = (128 - x) % 128 if isinstance(x, int) else 128 - x
                    before = pltpu.roll(low_y_ref[comp], turn, 1)
                if tile < tiles - 1:
                    after = pltpu.roll(q_ref[comp, x, :, tile * 128 + 128 : tile * 128 + 256], 127, 1)
                else:
                    after = pltpu.roll(high_y_ref[comp], 127 - x, 1)
                minus_y = jnp.where(first_y, before, pltpu.roll(c, 1, 1))
                plus_y = jnp.where(last_y, after, pltpu.roll(c, 127, 1))
                low_z = low_z_ref[comp, tile, pl.ds(x, 1), :]
                high_z = high_z_ref[comp, tile, pl.ds(x, 1), :]
                minus_z = jnp.where(first_z, low_z, pltpu.roll(c, 1, 0))
                plus_z = jnp.where(last_z, high_z, pltpu.roll(c, count_z - 1, 0))
                shifts.append((c, minus(comp, here), plus(comp, here), minus_y, plus_y, minus_z, plus_z))
            pushed = [force_ref[comp, x, :, here] for comp in range(3)]
            for comp, value in enumerate(tile_update(shifts, pushed)):
                out_ref[comp, x, :, here] = value

    def of_plane(x):
        return lambda comp, here: q_ref[comp, x, :, here]

    plane(0, lambda comp, here: low_x_ref[comp, :, here], of_plane(1))

    def middle(x, carry):
        plane(x, of_plane(x - 1), of_plane(x + 1))
        return carry

    lax.fori_loop(1, count_x - 1, middle, 0)
    plane(count_x - 1, of_plane(count_x - 2), lambda comp, here: high_x_ref[comp, :, here])

    if not last:
        za, rest = face_refs[0], face_refs[1:]
        write_faces(out_ref, [za.at[:4]] + list(rest), shape)

        @pl.when(listed)
        def _():
            rows = turbine_rows(rows_ref, table_ref, slots, step + 1, points)
            weights, factor_y = point_factors(rows, shape)
            for comp, value in enumerate(sample(out_ref, weights, factor_y, shape)):
                sample_ref[3 * step + 3 + comp : 3 * step + 4 + comp] = value

        if packs:
            count = 3 * steps
            za[4] = jnp.zeros((count_x, count_y), jnp.float32)
            for j in range(capacity):
                lane, row = (j % 2) * points, (j // 2) * count
                values = sample_ref[:count, j * points : (j + 1) * points]
                za[4, row : row + count, lane : lane + points] = values


def face_shapes(shape, extra=0):
    count_x, count_z, count_y = shape
    forms = [(4 + extra, count_x, count_y), (4, count_x, count_y)]
    forms += [(4, count_z, 128)] * 2 + [(4, count_z, count_y)] * 2
    return [jax.ShapeDtypeStruct(form, jnp.float32) for form in forms]


def vmem_specs(count):
    return [pl.BlockSpec(memory_space=pltpu.VMEM)] * count


def shards(flow, positions, loads, block_list):
    capacity = block_list.shape[-1]
    steps, _, _, part = positions.shape
    shape = flow.shape[1:]
    count_x, count_z, count_y = shape
    size_x, size_y, size_z = lax.axis_size("gx"), lax.axis_size("gy"), lax.axis_size("gz")
    points = part * size_z
    lanes = capacity * points
    params = pltpu.CompilerParams(vmem_limit_bytes=vmem_limit)
    q = flow
    turbines = block_list.reshape(capacity)
    barrier = lax.optimization_barrier

    faces = pl.pallas_call(
        functools.partial(faces_body, shape=shape),
        out_shape=face_shapes(shape),
        in_specs=vmem_specs(1),
        out_specs=vmem_specs(6),
        compiler_params=params,
        name="faces",
    )(q)

    named = block_list.reshape(1, 1, capacity).astype(jnp.float32)
    named = jnp.broadcast_to(jnp.pad(named, ((0, 0), (0, 0), (0, part - capacity))), (steps, 2, part))
    own = [positions.reshape(steps, 3, part), loads.reshape(steps, 3, part), named]
    table = jnp.concatenate(own, axis=1).reshape(1, 8 * steps, part)

    table = jnp.concatenate([table, from_distance(table, "gz", 1)], axis=0)
    waiting = list(faces)
    plan = [(0, "gz", 0), (1, "gz", 1), (2, "gy", 0), (3, "gy", 1), (4, "gx", 0), (5, "gx", 1)]
    hops = []
    for axis in ("gz", "gy", "gx"):
        distance = 2 if axis == "gz" else 1
        while distance < lax.axis_size(axis):
            hops.append((axis, distance))
            distance *= 2
    halos = [None] * 6
    for axis, distance in hops:
        table, waiting = barrier((table, waiting))
        received = from_distance(table, axis, distance)
        if plan:
            place, along, first = plan.pop(0)
            halos[place] = swap(waiting[place], along, first)
        table = jnp.concatenate([table, received], axis=0)
    for place, along, first in plan:
        halos[place] = swap(waiting[place], along, first)

    samples = None
    for step in range(steps):
        last, packs = step == steps - 1, step == steps - 2
        shapes = [jax.ShapeDtypeStruct(q.shape, jnp.float32)]
        if not last:
            shapes += face_shapes(shape, 1 if packs else 0)
            shapes += [jax.ShapeDtypeStruct((16, lanes), jnp.float32)]
        past = [] if step == 0 or last else [samples]
        results = pl.pallas_call(
            functools.partial(step_body, shape=shape, points=points, capacity=capacity, step=step, steps=steps),
            out_shape=shapes,
            in_specs=[pl.BlockSpec(memory_space=pltpu.SMEM)] + vmem_specs(8 + len(past)),
            out_specs=vmem_specs(len(shapes)),
            scratch_shapes=[pltpu.VMEM((3,) + shape, jnp.float32), pltpu.VMEM((8, lanes), jnp.float32)]
            + [pltpu.VMEM((4, count_y // 128, count_x, 128), jnp.float32)] * 2
            + [pltpu.VMEM(form.shape, jnp.float32) for form in face_shapes(shape)[2:]],
            compiler_params=params,
            name="step",
        )(turbines, table, q, *halos, *past)
        q = results[0]
        if last:
            break
        faces, samples = results[1:7], results[7]
        if not packs:
            halos = [swap(faces[place], along, first) for place, along, first in
                     [(0, "gz", 0), (1, "gz", 1), (2, "gy", 0), (3, "gy", 1), (4, "gx", 0), (5, "gx", 1)]]
            continue
        za, zb, ya, yb, xa, xb = faces
        za_in = swap(za, "gz", 0)
        zb_in = swap(zb, "gz", 1)
        sums = za[4] + za_in[4]
        row_blocks = pl.cdiv(3 * steps * pl.cdiv(capacity, 2), count_z)
        blocks = jnp.stack(
            [sums[b * count_z : (b + 1) * count_z, h * 128 : h * 128 + 128] for b in range(row_blocks) for h in range(2)]
        )
        count = blocks.shape[0]
        ya_in = swap(jnp.concatenate([ya, blocks], axis=0), "gy", 0)
        xa_in, xb_in = swap(xa, "gx", 0), swap(xb, "gx", 1)
        pieces = jnp.concatenate([blocks, ya_in[4:]], axis=0)
        yb_in = from_distance(jnp.concatenate([yb, pieces], axis=0), "gy", 3)
        pieces = jnp.concatenate([pieces, yb_in[4:]], axis=0).reshape(size_y, count, count_z, 128)
        halos = [za_in, zb_in, ya_in, yb_in, xa_in, xb_in]

    distance = 2
    while distance < size_z:
        pieces = pieces + from_distance(pieces, "gz", distance)
        distance *= 2
    mine = lax.dynamic_slice_in_dim(pieces, lax.axis_index("gz") * part, part, axis=3)[None]
    mine = gather_relative(mine, "gx")
    mine = mine.reshape(size_x * size_y, row_blocks, 2, count_z, part).transpose(0, 2, 1, 3, 4)
    mine = mine.reshape(size_x * size_y, 2, row_blocks * count_z, part)

    holder = (lax.axis_index("gx") * size_y + lax.axis_index("gy")).astype(jnp.float32)
    listed = table[:, 6, :capacity].reshape(size_x, size_y, size_z, capacity)
    slots = sorted_slots(jnp.moveaxis(listed, -1, 0), capacity)
    order = jnp.stack([jnp.min(slot, axis=2) for slot in slots])
    order = jnp.stack([order[:, :, k] for k in (0, 1, 3, 2)], axis=2).reshape(capacity, size_x * size_y)
    match = (order == holder).astype(jnp.float32)
    returned = 0.0
    for j in range(capacity):
        row = (j // 2) * 3 * steps
        values = mine[:, j % 2, row : row + 3 * steps]
        returned = returned + jnp.sum(values * match[j][:, None, None], axis=0)
    return q, returned.reshape(positions.shape)


def solution(mesh):
    in_specs = (
        P(None, "gx", "gz", "gy"),
        P(None, None, ("gx", "gy"), "gz"),
        P(None, None, ("gx", "gy"), "gz"),
        P("gx", "gy", "gz", None),
    )
    out_specs = (P(None, "gx", "gz", "gy"), P(None, None, ("gx", "gy"), "gz"))
    return jax.shard_map(shards, mesh=mesh, in_specs=in_specs, out_specs=out_specs, check_vma=False)
```

time: 105 us -> 86.7 us (0.83)
  starting transfers between devices: 43.7 us -> 31.2 us
  Pallas kernels: 29.9 us -> 26.9 us
  between operations: 3.44 us -> 0.83 us
  local copies, waits for them, and re-layouts: 4.5 us -> 3.27 us
    ppermute x10 -> x8, starting transfers between devices: 20.6 us -> 11.5 us  [from_distance(): return lax.ppermute(value, axis, [(i, i ^ distance) for i in range(count)])]
    ppermute x10 -> x8, waiting for transfers between devices: 18.4 us -> 13.3 us  [from_distance(): return lax.ppermute(value, axis, [(i, i ^ distance) for i in range(count)])]
    ppermute x15 -> x14, waiting for transfers between devices: 4.42 us -> 8.96 us  [swap(): return lax.ppermute(value, axis, pairs)]
    ppermute x15 -> x14, starting transfers between devices: 23.1 us -> 19.7 us  [swap(): return lax.ppermute(value, axis, pairs)]
    pallas_call x3, Pallas kernels: 28.6 us -> 25.5 us  [shards(): pl.pallas_call(functools.partial(step_body, shape=shape, points=points, c...]
    slice x2 -> x4, local copies, waits for them, and re-layouts: 1.35 us -> 0.02 us  [the longest x1 0.02 us: shards(): listed = table[:, 6, :capacity].reshape(size_x, size_y, size_z, capacity)]
    unnamed x9 -> x6, local copies, waits for them, and re-layouts: 2.39 us -> 2.32 us
  transfers between devices with their start and end apart: 25 -> 22, of which waited for: 12 -> 11; matrix products, arithmetic and copies ran while one was open for 0% -> 1% of each run, Pallas kernels for 1% -> 11%
where the time goes in v1:
time: 86.7 us; the launch traced here: 85.6 us
  starting transfers between devices  31.2 us (36%)
  Pallas kernels  26.9 us (31%)
  waiting for transfers between devices  22.2 us (26%)
  local copies, waits for them, and re-layouts  3.27 us (4%)
  other arithmetic  1.25 us (1%)
    pallas_call x3, Pallas kernels, shards(): pl.pallas_call(functools.partial(step_body, shape=shape, points=points, c...  25.5 us
    ppermute x14, starting transfers between devices, swap(): return lax.ppermute(value, axis, pairs)  19.7 us
    ppermute x8, waiting for transfers between devices, from_distance(): return lax.ppermute(value, axis, [(i, i ^ distance) for i in range(count)])  13.3 us
    ppermute x8, starting transfers between devices, from_distance(): return lax.ppermute(value, axis, [(i, i ^ distance) for i in range(count)])  11.5 us
    ppermute x14, waiting for transfers between devices, swap(): return lax.ppermute(value, axis, pairs)  8.96 us
    unnamed x6, local copies, waits for them, and re-layouts  2.32 us
  transfers between devices with their start and end apart: 22, of which 11 were waited for; matrix products, arithmetic and copies ran while one was open for 1% of the time, Pallas kernels for 11%

profile of v1, /device:TPU:0, one launch (start us, length us, event | category | flops | bytes accessed | tf_op | source)
XLA Modules:
  0.0 85.6 jit_solution(4300270584929277821)
XLA Ops:
  0.6 0.7 convert_bitcast_fusion
  1.4 0.7 copy_bitcast_fusion
  2.1 3.1 %collective-permute-start = (f32[1,24,32]{2,1,0:T(8,128)S(1)}, f32[1,24,32]{2,1,0:T(8,128)S(1)}, u32[]{:S(2)}, u32[]{:S(2)}) collective-permute-start(f32[1,24,32]{2,1,0:T(8,128)S(1)} %maximum_bitcast_fusion), channel_id=1, source_target_pairs={{0,1},{1,0},{2,3},{3,2},{4,5},{5,4},{6,7},{7,6},{8,9},{9,8},{10,11... | collective-permute-start | bytes 9224 | tf_op jit(solution)/shard_map/ppermute | solution.py:37
  5.2 1.6 %copy-done = f32[4,32,16,256]{3,2,1,0:T(8,128)S(1)} copy-done((f32[4,32,16,256]{3,2,1,0:T(8,128)S(1)}, f32[4,32,16,256]{3,2,1,0:T(8,128)}, u32[]{:S(2)}) %copy-start) | copy-done | bytes 2097176
  6.8 1.4 %faces.1 = (f32[4,32,256]{2,1,0:T(8,128)S(1)}, f32[4,32,256]{2,1,0:T(8,128)S(1)}, f32[4,16,128]{2,1,0:T(8,128)S(1)}, f32[4,16,128]{2,1,0:T(8,128)S(1)}, f32[4,16...) custom-call(f32[4,32,16,256]{3,2,1,0:T(8,128)S(1)} %copy-done), custom_call_target="tpu_custom_call" | custom-call | tf_op jit(solution)/shard_map/faces/pallas_call | solution.py:315
  8.1 2.7 %collective-permute-start.1 = (f32[2,24,32]{2,1,0:T(8,128)S(1)}, f32[2,24,32]{2,1,0:T(8,128)S(1)}, u32[]{:S(2)}, u32[]{:S(2)}) collective-permute-start(f32[2,24,32]{2,1,0:T(8,128)S(1)} %pad_maximum_fusion.7), channel_id=1, source_target_pairs={{0,2},{1,3},{2,0},{3,1},{4,6},{5,7},{6,4},{7,5},{8,10},{9,11},{10,... | collective-permute-start | bytes 18440 | tf_op jit(solution)/shard_map/ppermute | solution.py:37
  10.8 2.4 %collective-permute-done.1 = f32[2,24,32]{2,1,0:T(8,128)S(1)} collective-permute-done((f32[2,24,32]{2,1,0:T(8,128)S(1)}, f32[2,24,32]{2,1,0:T(8,128)S(1)}, u32[]{:S(2)}, u32[]{:S(2)}) %collective-permute-start.1) | collective-permute-done | bytes 6176 | tf_op jit(solution)/shard_map/ppermute | solution.py:37
  13.2 1.6 %collective-permute-start.2 = (f32[4,24,32]{2,1,0:T(8,128)S(1)}, f32[4,24,32]{2,1,0:T(8,128)S(1)}, u32[]{:S(2)}, u32[]{:S(2)}) collective-permute-start(f32[4,24,32]{2,1,0:T(8,128)S(1)} %pad_maximum_fusion.5), channel_id=1, source_target_pairs={{0,4},{4,0},{8,12},{12,8},{1,5},{5,1},{9,13},{13,9},{2,6},{6,2},{1... | collective-permute-start | bytes 36872 | tf_op jit(solution)/shard_map/ppermute | solution.py:37
  14.8 2.6 %collective-permute-done.2 = f32[4,24,32]{2,1,0:T(8,128)S(1)} collective-permute-done((f32[4,24,32]{2,1,0:T(8,128)S(1)}, f32[4,24,32]{2,1,0:T(8,128)S(1)}, u32[]{:S(2)}, u32[]{:S(2)}) %collective-permute-start.2) | collective-permute-done | bytes 12320 | tf_op jit(solution)/shard_map/ppermute | solution.py:37
  17.4 1.6 %collective-permute-start.3 = (f32[8,24,32]{2,1,0:T(8,128)S(1)}, f32[8,24,32]{2,1,0:T(8,128)S(1)}, u32[]{:S(2)}, u32[]{:S(2)}) collective-permute-start(f32[8,24,32]{2,1,0:T(8,128)S(1)} %pad_maximum_fusion.2), channel_id=1, source_target_pairs={{0,8},{4,12},{8,0},{12,4},{1,9},{5,13},{9,1},{13,5},{2,10},{6,14},... | collective-permute-start | bytes 73736 | tf_op jit(solution)/shard_map/ppermute | solution.py:37
  19.5 0.7 collective-permute-start.6
  20.1 1.6 %collective-permute-start.7 = (f32[4,16,128]{2,1,0:T(8,128)S(1)}, f32[4,16,128]{2,1,0:T(8,128)S(1)}, u32[]{:S(2)}, u32[]{:S(2)}) collective-permute-start(f32[4,16,128]{2,1,0:T(8,128)S(1)} %get-tuple-element.55), channel_id=1, source_target_pairs={{0,4},{4,0},{8,12},{12,8},{1,5},{5,1},{9,13},{13,9},{2,6},{6,2},{1... | collective-permute-start | bytes 98312 | tf_op jit(solution)/shard_map/ppermute | solution.py:32
  22.2 0.7 collective-permute-start.8
  22.9 0.7 collective-permute-done.4
  24.1 0.7 collective-permute-done.9.refs_7_
  24.9 9.3 %step.3 = (f32[4,32,16,256]{3,2,1,0:T(8,128)S(1)}, f32[4,32,256]{2,1,0:T(8,128)S(1)}, f32[4,32,256]{2,1,0:T(8,128)S(1)}, f32[4,16,128]{2,1,0:T(8,128)S(1)}, f32[...) custom-call(s32[2]{0:T(128)S(1)} %bitcast.37, ...), custom_call_target="tpu_custom_call" | custom-call | tf_op jit(solution)/shard_map/step/pallas_call | solution.py:357
  34.1 3.9 %collective-permute-start.10 = (f32[4,32,256]{2,1,0:T(8,128)S(1)}, f32[4,32,256]{2,1,0:T(8,128)S(1)}, u32[]{:S(2)}, u32[]{:S(2)}) collective-permute-start(f32[4,32,256]{2,1,0:T(8,128)S(1)} %get-tuple-element.62), channel_id=1, source_target_pairs={{0,1},{1,0},{2,3},{3,2},{4,5},{5,4},{6,7},{7,6},{8,9},{9,8},{10,11... | collective-permute-start | bytes 393224 | tf_op jit(solution)/shard_map/ppermute | solution.py:32
  38.0 0.7 collective-permute-start.11
  38.8 4.7 %collective-permute-start.12 = (f32[4,16,128]{2,1,0:T(8,128)S(1)}, f32[4,16,128]{2,1,0:T(8,128)S(1)}, u32[]{:S(2)}, u32[]{:S(2)}) collective-permute-start(f32[4,16,128]{2,1,0:T(8,128)S(1)} %get-tuple-element.64), channel_id=1, source_target_pairs={{0,4},{4,0},{8,12},{12,8},{1,5},{5,1},{9,13},{13,9},{2,6},{6,2},{1... | collective-permute-start | bytes 98312 | tf_op jit(solution)/shard_map/ppermute | solution.py:32
  43.4 0.7 collective-permute-start.13
  44.1 1.3 %collective-permute-done.12.refs_5_ = f32[4,16,128]{2,1,0:T(8,128)S(1)} collective-permute-done((f32[4,16,128]{2,1,0:T(8,128)S(1)}, f32[4,16,128]{2,1,0:T(8,128)S(1)}, u32[]{:S(2)}, u32[]{:S(2)}) %collective-permute-start.12) | collective-permute-done | bytes 32800 | tf_op jit(solution)/shard_map/ppermute | solution.py:32
  45.5 8.6 %step.4 = (f32[4,32,16,256]{3,2,1,0:T(8,128)S(1)}, f32[5,32,256]{2,1,0:T(8,128)S(1)}, f32[4,32,256]{2,1,0:T(8,128)S(1)}, f32[4,16,128]{2,1,0:T(8,128)S(1)}, f32[...) custom-call(s32[2]{0:T(128)S(1)} %bitcast.38, ...), custom_call_target="tpu_custom_call" | custom-call | tf_op jit(solution)/shard_map/step/pallas_call | solution.py:357
  54.1 1.3 %collective-permute-start.15 = (f32[5,32,256]{2,1,0:T(8,128)S(1)}, f32[5,32,256]{2,1,0:T(8,128)S(1)}, u32[]{:S(2)}, u32[]{:S(2)}) collective-permute-start(f32[5,32,256]{2,1,0:T(8,128)S(1)} %get-tuple-element.69), channel_id=1, source_target_pairs={{0,1},{1,0},{2,3},{3,2},{4,5},{5,4},{6,7},{7,6},{8,9},{9,8},{10,11... | collective-permute-start | bytes 491528 | tf_op jit(solution)/shard_map/ppermute | solution.py:32
  55.6 4.5 %collective-permute-done.15.refs_3_ = f32[5,32,256]{2,1,0:T(8,128)S(1)} collective-permute-done((f32[5,32,256]{2,1,0:T(8,128)S(1)}, f32[5,32,256]{2,1,0:T(8,128)S(1)}, u32[]{:S(2)}, u32[]{:S(2)}) %collective-permute-start.15) | collective-permute-done | bytes 163872 | tf_op jit(solution)/shard_map/ppermute | solution.py:32
  60.0 4.2 %collective-permute-start.17 = (f32[6,16,128]{2,1,0:T(8,128)S(1)}, f32[6,16,128]{2,1,0:T(8,128)S(1)}, u32[]{:S(2)}, u32[]{:S(2)}) collective-permute-start(f32[6,16,128]{2,1,0:T(8,128)S(1)} %pad_maximum_fusion.6), channel_id=1, source_target_pairs={{0,4},{4,0},{8,12},{12,8},{1,5},{5,1},{9,13},{13,9},{2,6},{6,2},{1... | collective-permute-start | bytes 147464 | tf_op jit(solution)/shard_map/ppermute | solution.py:32
  64.3 2.1 %collective-permute-done.17.refs_5_ = f32[6,16,128]{2,1,0:T(8,128)S(1)} collective-permute-done((f32[6,16,128]{2,1,0:T(8,128)S(1)}, f32[6,16,128]{2,1,0:T(8,128)S(1)}, u32[]{:S(2)}, u32[]{:S(2)}) %collective-permute-start.17) | collective-permute-done | bytes 49184 | tf_op jit(solution)/shard_map/ppermute | solution.py:32
  66.4 1.5 %collective-permute-start.18 = (f32[8,16,128]{2,1,0:T(8,128)S(1)}, f32[8,16,128]{2,1,0:T(8,128)S(1)}, u32[]{:S(2)}, u32[]{:S(2)}) collective-permute-start(f32[8,16,128]{2,1,0:T(8,128)S(1)} %pad_maximum_fusion.3), channel_id=1, source_target_pairs={{0,12},{4,8},{8,4},{12,0},{1,13},{5,9},{9,5},{13,1},{2,14},{6,10},... | collective-permute-start | bytes 196616 | tf_op jit(solution)/shard_map/ppermute | solution.py:37
  67.9 3.7 %collective-permute-done.18.refs_6_ = f32[8,16,128]{2,1,0:T(8,128)S(1)} collective-permute-done((f32[8,16,128]{2,1,0:T(8,128)S(1)}, f32[8,16,128]{2,1,0:T(8,128)S(1)}, u32[]{:S(2)}, u32[]{:S(2)}) %collective-permute-start.18) | collective-permute-done | bytes 65568 | tf_op jit(solution)/shard_map/ppermute | solution.py:37
  71.7 1.0 %collective-permute-start.20 = (f32[4,2,16,128]{3,2,1,0:T(8,128)S(1)}, f32[4,2,16,128]{3,2,1,0:T(8,128)S(1)}, u32[]{:S(2)}, u32[]{:S(2)}) collective-permute-start(f32[4,2,16,128]{3,2,1,0:T(8,128)S(1)} %bitcast.41), channel_id=1, source_target_pairs={{0,2},{1,3},{2,0},{3,1},{4,6},{5,7},{6,4},{7,5},{8,10},{9,11},{10,... | collective-permute-start | bytes 196616 | tf_op jit(solution)/shard_map/ppermute | solution.py:37
  72.7 0.7 collective-permute-start.16
  73.5 3.4 %collective-permute-done.20 = f32[4,2,16,128]{3,2,1,0:T(8,128)S(1)} collective-permute-done((f32[4,2,16,128]{3,2,1,0:T(8,128)S(1)}, f32[4,2,16,128]{3,2,1,0:T(8,128)S(1)}, u32[]{:S(2)}, u32[]{:S(2)}) %collective-permute-start.20) | collective-permute-done | bytes 65568 | tf_op jit(solution)/shard_map/ppermute | solution.py:37
  77.3 7.6 %step.5 = f32[4,32,16,256]{3,2,1,0:T(8,128)} custom-call(s32[2]{0:T(128)S(1)} %bitcast.39, f32[32,24,32]{2,1,0:T(8,128)S(1)} %constant_dynamic-update-slice_fusion.refs_1_, f32[4,32,16,256]{3,2,1,0:T(8,128)S(1)} %get-tuple-element.68.refs_2_, f32[5,32,256]{2,1,0:T(8,128)S(1)} %collective-permute-done.15.refs_3_, ...), custom_call_target="tpu_custom_call" | custom-call | tf_op jit(solution)/shard_map/step/pallas_call | solution.py:357
  (53 shorter events, 3.2 us)
Async XLA Ops:
  0.6 24.2 %copy-start.1 = (s32[1,1,1,2]{3,2,1,0:T(1,128)S(1)}, s32[1,1,1,2]{3,2,1,0:T(1,128)}, u32[]{:S(2)}) copy-start(s32[1,1,1,2]{3,2,1,0:T(1,128)} %param.7) | copy-start | bytes 28
  2.1 6.0 %collective-permute-start = (f32[1,24,32]{2,1,0:T(8,128)S(1)}, f32[1,24,32]{2,1,0:T(8,128)S(1)}, u32[]{:S(2)}, u32[]{:S(2)}) collective-permute-start(f32[1,24,32]{2,1,0:T(8,128)S(1)} %maximum_bitcast_fusion), channel_id=1, source_target_pairs={{0,1},{1,0},{2,3},{3,2},{4,5},{5,4},{6,7},{7,6},{8,9},{9,8},{10,11... | collective-permute-start | bytes 9224 | tf_op jit(solution)/shard_map/ppermute | solution.py:37
  5.2 1.6 %copy-start = (f32[4,32,16,256]{3,2,1,0:T(8,128)S(1)}, f32[4,32,16,256]{3,2,1,0:T(8,128)}, u32[]{:S(2)}) copy-start(f32[4,32,16,256]{3,2,1,0:T(8,128)} %refs_2_.1) | copy-start | bytes 6291460
  8.1 5.1 %collective-permute-start.1 = (f32[2,24,32]{2,1,0:T(8,128)S(1)}, f32[2,24,32]{2,1,0:T(8,128)S(1)}, u32[]{:S(2)}, u32[]{:S(2)}) collective-permute-start(f32[2,24,32]{2,1,0:T(8,128)S(1)} %pad_maximum_fusion.7), channel_id=1, source_target_pairs={{0,2},{1,3},{2,0},{3,1},{4,6},{5,7},{6,4},{7,5},{8,10},{9,11},{10,... | collective-permute-start | bytes 18440 | tf_op jit(solution)/shard_map/ppermute | solution.py:37
  13.2 4.2 %collective-permute-start.2 = (f32[4,24,32]{2,1,0:T(8,128)S(1)}, f32[4,24,32]{2,1,0:T(8,128)S(1)}, u32[]{:S(2)}, u32[]{:S(2)}) collective-permute-start(f32[4,24,32]{2,1,0:T(8,128)S(1)} %pad_maximum_fusion.5), channel_id=1, source_target_pairs={{0,4},{4,0},{8,12},{12,8},{1,5},{5,1},{9,13},{13,9},{2,6},{6,2},{1... | collective-permute-start | bytes 36872 | tf_op jit(solution)/shard_map/ppermute | solution.py:37
  17.4 4.7 %collective-permute-start.3 = (f32[8,24,32]{2,1,0:T(8,128)S(1)}, f32[8,24,32]{2,1,0:T(8,128)S(1)}, u32[]{:S(2)}, u32[]{:S(2)}) collective-permute-start(f32[8,24,32]{2,1,0:T(8,128)S(1)} %pad_maximum_fusion.2), channel_id=1, source_target_pairs={{0,8},{4,12},{8,0},{12,4},{1,9},{5,13},{9,1},{13,5},{2,10},{6,14},... | collective-permute-start | bytes 73736 | tf_op jit(solution)/shard_map/ppermute | solution.py:37
  19.0 5.9 %collective-permute-start.5 = (f32[4,32,256]{2,1,0:T(8,128)S(1)}, f32[4,32,256]{2,1,0:T(8,128)S(1)}, u32[]{:S(2)}, u32[]{:S(2)}) collective-permute-start(f32[4,32,256]{2,1,0:T(8,128)S(1)} %get-tuple-element.44), channel_id=1, source_target_pairs={{0,1},{1,0},{2,3},{3,2},{4,5},{5,4},{6,7},{7,6},{8,9},{9,8},{10,11... | collective-permute-start | bytes 393224 | tf_op jit(solution)/shard_map/ppermute | solution.py:32
  19.5 5.4 %collective-permute-start.6 = (f32[4,32,256]{2,1,0:T(8,128)S(1)}, f32[4,32,256]{2,1,0:T(8,128)S(1)}, u32[]{:S(2)}, u32[]{:S(2)}) collective-permute-start(f32[4,32,256]{2,1,0:T(8,128)S(1)} %get-tuple-element.50), channel_id=1, source_target_pairs={{1,2},{2,1},{5,6},{6,5},{9,10},{10,9},{13,14},{14,13},{17,18},{18,... | collective-permute-start | bytes 393224 | tf_op jit(solution)/shard_map/ppermute | solution.py:32
  20.1 4.0 %collective-permute-start.7 = (f32[4,16,128]{2,1,0:T(8,128)S(1)}, f32[4,16,128]{2,1,0:T(8,128)S(1)}, u32[]{:S(2)}, u32[]{:S(2)}) collective-permute-start(f32[4,16,128]{2,1,0:T(8,128)S(1)} %get-tuple-element.55), channel_id=1, source_target_pairs={{0,4},{4,0},{8,12},{12,8},{1,5},{5,1},{9,13},{13,9},{2,6},{6,2},{1... | collective-permute-start | bytes 98312 | tf_op jit(solution)/shard_map/ppermute | solution.py:32
  22.1 1.5 %collective-permute-start.4 = (f32[16,24,32]{2,1,0:T(8,128)S(1)}, f32[16,24,32]{2,1,0:T(8,128)S(1)}, u32[]{:S(2)}, u32[]{:S(2)}) collective-permute-start(f32[16,24,32]{2,1,0:T(8,128)S(1)} %pad_maximum_fusion), channel_id=1, source_target_pairs={{0,16},{16,0},{1,17},{17,1},{2,18},{18,2},{3,19},{19,3},{4,20},{20... | collective-permute-start | bytes 147464 | tf_op jit(solution)/shard_map/ppermute | solution.py:37
  22.2 1.9 %collective-permute-start.8 = (f32[4,16,128]{2,1,0:T(8,128)S(1)}, f32[4,16,128]{2,1,0:T(8,128)S(1)}, u32[]{:S(2)}, u32[]{:S(2)}) collective-permute-start(f32[4,16,128]{2,1,0:T(8,128)S(1)} %get-tuple-element.59), channel_id=1, source_target_pairs={{4,8},{8,4},{5,9},{9,5},{6,10},{10,6},{7,11},{11,7},{20,24},{24,20... | collective-permute-start | bytes 98312 | tf_op jit(solution)/shard_map/ppermute | solution.py:32
  23.6 1.3 %collective-permute-start.9 = (f32[4,16,256]{2,1,0:T(8,128)S(1)}, f32[4,16,256]{2,1,0:T(8,128)S(1)}, u32[]{:S(2)}, u32[]{:S(2)}) collective-permute-start(f32[4,16,256]{2,1,0:T(8,128)S(1)} %get-tuple-element.60), channel_id=1, source_target_pairs={{0,16},{16,0},{1,17},{17,1},{2,18},{18,2},{3,19},{19,3},{4,20},{20... | collective-permute-start | bytes 196616 | tf_op jit(solution)/shard_map/ppermute | solution.py:32
  34.1 11.3 %collective-permute-start.10 = (f32[4,32,256]{2,1,0:T(8,128)S(1)}, f32[4,32,256]{2,1,0:T(8,128)S(1)}, u32[]{:S(2)}, u32[]{:S(2)}) collective-permute-start(f32[4,32,256]{2,1,0:T(8,128)S(1)} %get-tuple-element.62), channel_id=1, source_target_pairs={{0,1},{1,0},{2,3},{3,2},{4,5},{5,4},{6,7},{7,6},{8,9},{9,8},{10,11... | collective-permute-start | bytes 393224 | tf_op jit(solution)/shard_map/ppermute | solution.py:32
  38.0 7.4 %collective-permute-start.11 = (f32[4,32,256]{2,1,0:T(8,128)S(1)}, f32[4,32,256]{2,1,0:T(8,128)S(1)}, u32[]{:S(2)}, u32[]{:S(2)}) collective-permute-start(f32[4,32,256]{2,1,0:T(8,128)S(1)} %get-tuple-element.63), channel_id=1, source_target_pairs={{1,2},{2,1},{5,6},{6,5},{9,10},{10,9},{13,14},{14,13},{17,18},{18,... | collective-permute-start | bytes 393224 | tf_op jit(solution)/shard_map/ppermute | solution.py:32
  38.7 6.7 %collective-permute-start.14 = (f32[4,16,256]{2,1,0:T(8,128)S(1)}, f32[4,16,256]{2,1,0:T(8,128)S(1)}, u32[]{:S(2)}, u32[]{:S(2)}) collective-permute-start(f32[4,16,256]{2,1,0:T(8,128)S(1)} %get-tuple-element.66), channel_id=1, source_target_pairs={{0,16},{16,0},{1,17},{17,1},{2,18},{18,2},{3,19},{19,3},{4,20},{20... | collective-permute-start | bytes 196616 | tf_op jit(solution)/shard_map/ppermute | solution.py:32
  38.8 6.6 %collective-permute-start.12 = (f32[4,16,128]{2,1,0:T(8,128)S(1)}, f32[4,16,128]{2,1,0:T(8,128)S(1)}, u32[]{:S(2)}, u32[]{:S(2)}) collective-permute-start(f32[4,16,128]{2,1,0:T(8,128)S(1)} %get-tuple-element.64), channel_id=1, source_target_pairs={{0,4},{4,0},{8,12},{12,8},{1,5},{5,1},{9,13},{13,9},{2,6},{6,2},{1... | collective-permute-start | bytes 98312 | tf_op jit(solution)/shard_map/ppermute | solution.py:32
  43.4 2.0 %collective-permute-start.13 = (f32[4,16,128]{2,1,0:T(8,128)S(1)}, f32[4,16,128]{2,1,0:T(8,128)S(1)}, u32[]{:S(2)}, u32[]{:S(2)}) collective-permute-start(f32[4,16,128]{2,1,0:T(8,128)S(1)} %get-tuple-element.65), channel_id=1, source_target_pairs={{4,8},{8,4},{5,9},{9,5},{6,10},{10,6},{7,11},{11,7},{20,24},{24,20... | collective-permute-start | bytes 98312 | tf_op jit(solution)/shard_map/ppermute | solution.py:32
  54.1 6.0 %collective-permute-start.15 = (f32[5,32,256]{2,1,0:T(8,128)S(1)}, f32[5,32,256]{2,1,0:T(8,128)S(1)}, u32[]{:S(2)}, u32[]{:S(2)}) collective-permute-start(f32[5,32,256]{2,1,0:T(8,128)S(1)} %get-tuple-element.69), channel_id=1, source_target_pairs={{0,1},{1,0},{2,3},{3,2},{4,5},{5,4},{6,7},{7,6},{8,9},{9,8},{10,11... | collective-permute-start | bytes 491528 | tf_op jit(solution)/shard_map/ppermute | solution.py:32
  60.0 6.4 %collective-permute-start.17 = (f32[6,16,128]{2,1,0:T(8,128)S(1)}, f32[6,16,128]{2,1,0:T(8,128)S(1)}, u32[]{:S(2)}, u32[]{:S(2)}) collective-permute-start(f32[6,16,128]{2,1,0:T(8,128)S(1)} %pad_maximum_fusion.6), channel_id=1, source_target_pairs={{0,4},{4,0},{8,12},{12,8},{1,5},{5,1},{9,13},{13,9},{2,6},{6,2},{1... | collective-permute-start | bytes 147464 | tf_op jit(solution)/shard_map/ppermute | solution.py:32
  66.4 5.2 %collective-permute-start.18 = (f32[8,16,128]{2,1,0:T(8,128)S(1)}, f32[8,16,128]{2,1,0:T(8,128)S(1)}, u32[]{:S(2)}, u32[]{:S(2)}) collective-permute-start(f32[8,16,128]{2,1,0:T(8,128)S(1)} %pad_maximum_fusion.3), channel_id=1, source_target_pairs={{0,12},{4,8},{8,4},{12,0},{1,13},{5,9},{9,5},{13,1},{2,14},{6,10},... | collective-permute-start | bytes 196616 | tf_op jit(solution)/shard_map/ppermute | solution.py:37
  71.7 5.2 %collective-permute-start.20 = (f32[4,2,16,128]{3,2,1,0:T(8,128)S(1)}, f32[4,2,16,128]{3,2,1,0:T(8,128)S(1)}, u32[]{:S(2)}, u32[]{:S(2)}) collective-permute-start(f32[4,2,16,128]{3,2,1,0:T(8,128)S(1)} %bitcast.41), channel_id=1, source_target_pairs={{0,2},{1,3},{2,0},{3,1},{4,6},{5,7},{6,4},{7,5},{8,10},{9,11},{10,... | collective-permute-start | bytes 196616 | tf_op jit(solution)/shard_map/ppermute | solution.py:37
  72.7 4.5 %collective-permute-start.16 = (f32[4,32,256]{2,1,0:T(8,128)S(1)}, f32[4,32,256]{2,1,0:T(8,128)S(1)}, u32[]{:S(2)}, u32[]{:S(2)}) collective-permute-start(f32[4,32,256]{2,1,0:T(8,128)S(1)} %get-tuple-element.70), channel_id=1, source_target_pairs={{1,2},{2,1},{5,6},{6,5},{9,10},{10,9},{13,14},{14,13},{17,18},{18,... | collective-permute-start | bytes 393224 | tf_op jit(solution)/shard_map/ppermute | solution.py:32
  73.4 3.9 %collective-permute-start.19 = (f32[4,16,256]{2,1,0:T(8,128)S(1)}, f32[4,16,256]{2,1,0:T(8,128)S(1)}, u32[]{:S(2)}, u32[]{:S(2)}) collective-permute-start(f32[4,16,256]{2,1,0:T(8,128)S(1)} %get-tuple-element.73), channel_id=1, source_target_pairs={{0,16},{16,0},{1,17},{17,1},{2,18},{18,2},{3,19},{19,3},{4,20},{20... | collective-permute-start | bytes 196616 | tf_op jit(solution)/shard_map/ppermute | solution.py:32
  77.0 7.9 %collective-permute-start.21 = (f32[1,4,2,16,32]{4,3,2,1,0:T(8,128)S(1)}, f32[1,4,2,16,32]{4,3,2,1,0:T(8,128)S(1)}, u32[]{:S(2)}, u32[]{:S(2)}) collective-permute-start(f32[1,4,2,16,32]{4,3,2,1,0:T(8,128)S(1)} %fusion.4), channel_id=1, source_target_pairs={{0,16},{16,0},{1,17},{17,1},{2,18},{18,2},{3,19},{19,3},{4,20},{20... | collective-permute-start | bytes 49160 | tf_op jit(solution)/shard_map/ppermute | solution.py:37

commit v2 on v1

--- a/solution.py
+++ b/solution.py
@@ -55,11 +55,12 @@
 
 def write_faces(q_ref, face_refs, shape):
     count_x, count_z, count_y = shape
-    za_ref, zb_ref, ya_ref, yb_ref, xa_ref, xb_ref = face_refs
+    za_ref, zb_ref, ya_ref, yb_ref, xa_ref = face_refs[:5]
     even_x, even_z, even_y = is_even("gx"), is_even("gz"), is_even("gy")
     low, high = q_ref[:, 0], q_ref[:, count_x - 1]
     xa_ref[...] = pick(even_x, high, low)
-    xb_ref[...] = pick(even_x, low, high)
+    for xb_ref in face_refs[5:]:
+        xb_ref[...] = pick(even_x, low, high)
     for comp in range(4):
         low = q_ref[comp, :, 0, :]
         high = q_ref[comp, :, count_z - 1, :]
@@ -129,17 +130,13 @@
 
 
 def turbine_rows(rows_ref, table_ref, slots, step, points):
-    index_x, index_y, index_z = lax.axis_index("gx"), lax.axis_index("gy"), lax.axis_index("gz")
-    size_x, size_y, size_z = lax.axis_size("gx"), lax.axis_size("gy"), lax.axis_size("gz")
-    part = points // size_z
+    size_x, size_y = lax.axis_size("gx"), lax.axis_size("gy")
     for j, slot in enumerate(slots):
         t = jnp.minimum(slot, size_x * size_y - 1)
-        place_x = lax.bitwise_xor(lax.div(t, size_y), index_x)
-        place_y = lax.bitwise_xor(lax.rem(t, size_y), index_y)
-        for c in range(size_z):
-            entry = (place_x * size_y + place_y) * size_z + lax.bitwise_xor(index_z, c)
-            offset = j * points + c * part
-            rows_ref[:, offset : offset + part] = table_ref[entry, 8 * step : 8 * step + 8, :]
+        place_x = lax.bitwise_xor(lax.div(t, size_y), lax.axis_index("gx"))
+        place_y = lax.bitwise_xor(lax.rem(t, size_y), lax.axis_index("gy"))
+        entry = place_x * size_y + lax.bitwise_xor(place_y, lax.div(place_y, 2))
+        rows_ref[:, j * points : (j + 1) * points] = table_ref[entry, 8 * step : 8 * step + 8, :]
     return rows_ref[...]
 
 
@@ -186,18 +183,23 @@
 def step_body(*refs, shape, points, capacity, step, steps):
     count_x, count_z, count_y = shape
     last, packs = step == steps - 1, step == steps - 2
+    faces = len(face_shapes(shape))
     refs = list(refs)
     list_ref, table_ref, q_ref = refs[:3]
-    za_ref, zb_ref, ya_ref, yb_ref, xa_ref, xb_ref = refs[3:9]
-    refs = refs[9:]
+    za_ref, zb_ref, ya_ref, yb_ref = refs[3:7]
+    x_refs, refs = refs[7 : 3 + faces], refs[3 + faces :]
     past_ref = None if step == 0 or last else refs.pop(0)
     out_ref = refs.pop(0)
+    sample_ref = None
     if not last:
-        face_refs, refs = refs[:6], refs[6:]
+        face_refs, refs = refs[:faces], refs[faces:]
         sample_ref = refs.pop(0)
+    else:
+        far_ref, out_ref, sems = out_ref, refs.pop(0), refs.pop(0)
     force_ref, rows_ref, low_z_ref, high_z_ref, low_y_ref, high_y_ref, low_x_ref, high_x_ref = refs
     slots = sorted_slots(list_ref, capacity)
-    listed = slots[0] < lax.axis_size("gx") * lax.axis_size("gy")
+    turbines = lax.axis_size("gx") * lax.axis_size("gy")
+    listed = slots[0] < turbines
 
     if not last:
         sample_ref[...] = jnp.zeros(sample_ref.shape, jnp.float32)
@@ -226,27 +228,27 @@
         high_z_ref[:, tile] = pick(even_z, first, second)
     low_y_ref[...] = pick(index_y == 0, 0.0, pick(even_y, yb_ref[:4], ya_ref[:4]))
     high_y_ref[...] = pick(index_y == lax.axis_size("gy") - 1, 0.0, pick(even_y, ya_ref[:4], yb_ref[:4]))
-    low_x_ref[...] = pick(even_x, xb_ref[...], xa_ref[...])
-    high_x_ref[...] = pick(even_x, xa_ref[...], xb_ref[...])
+    first = x_refs[0][...]
+    second = x_refs[1][...] if len(x_refs) > 1 else 0.0
+    low_x_ref[...] = pick(even_x, second, first)
+    high_x_ref[...] = pick(even_x, first, second)
     first_z, last_z, first_y, last_y = masks_of(shape)
 
     def plane(x, minus, plus):
+        centre, up, down = [], [], []
+        for comp in range(4):
+            row = [q_ref[comp, x, :, tile * 128 : tile * 128 + 128] for tile in range(tiles)]
+            turn = (128 - x) % 128 if isinstance(x, int) else 128 - x
+            centre.append(row)
+            up.append([pltpu.roll(low_y_ref[comp], turn, 1)] + [pltpu.roll(c, 1, 1) for c in row])
+            down.append([pltpu.roll(c, 127, 1) for c in row] + [pltpu.roll(high_y_ref[comp], 127 - x, 1)])
         for tile in range(tiles):
             here = slice(tile * 128, tile * 128 + 128)
             shifts = []
             for comp in range(4):
-                c = q_ref[comp, x, :, here]
-                if tile:
-                    before = pltpu.roll(q_ref[comp, x, :, tile * 128 - 128 : tile * 128], 1, 1)
-                else:
-                    turn = (128 - x) % 128 if isinstance(x, int) else 128 - x
-                    before = pltpu.roll(low_y_ref[comp], turn, 1)
-                if tile < tiles - 1:
-                    after = pltpu.roll(q_ref[comp, x, :, tile * 128 + 128 : tile * 128 + 256], 127, 1)
-                else:
-                    after = pltpu.roll(high_y_ref[comp], 127 - x, 1)
-                minus_y = jnp.where(first_y, before, pltpu.roll(c, 1, 1))
-                plus_y = jnp.where(last_y, after, pltpu.roll(c, 127, 1))
+                c = centre[comp][tile]
+                minus_y = jnp.where(first_y, up[comp][tile], up[comp][tile + 1])
+                plus_y = jnp.where(last_y, down[comp][tile + 1], down[comp][tile])
                 low_z = low_z_ref[comp, tile, pl.ds(x, 1), :]
                 high_z = high_z_ref[comp, tile, pl.ds(x, 1), :]
                 minus_z = jnp.where(first_z, low_z, pltpu.roll(c, 1, 0))
@@ -259,44 +261,80 @@
     def of_plane(x):
         return lambda comp, here: q_ref[comp, x, :, here]
 
+    def copy_out(number, start, count):
+        here = pl.ds(start, count)
+        return pltpu.make_async_copy(out_ref.at[:, here], far_ref.at[:, here], sems.at[number])
+
+    inner = count_x - 2
+    group = max(g for g in range(1, 11) if inner % g == 0)
+
+    def middle(trip, carry):
+        for k in range(group):
+            x = 1 + trip * group + k
+            plane(x, of_plane(x - 1), of_plane(x + 1))
+        if last:
+            copy_out(trip, 1 + trip * group, group).start()
+        return carry
+
+    lax.fori_loop(0, inner // group, middle, 0)
     plane(0, lambda comp, here: low_x_ref[comp, :, here], of_plane(1))
-
-    def middle(x, carry):
-        plane(x, of_plane(x - 1), of_plane(x + 1))
-        return carry
-
-    lax.fori_loop(1, count_x - 1, middle, 0)
     plane(count_x - 1, of_plane(count_x - 2), lambda comp, here: high_x_ref[comp, :, here])
 
-    if not last:
-        za, rest = face_refs[0], face_refs[1:]
-        write_faces(out_ref, [za.at[:4]] + list(rest), shape)
-
-        @pl.when(listed)
-        def _():
-            rows = turbine_rows(rows_ref, table_ref, slots, step + 1, points)
-            weights, factor_y = point_factors(rows, shape)
-            for comp, value in enumerate(sample(out_ref, weights, factor_y, shape)):
-                sample_ref[3 * step + 3 + comp : 3 * step + 4 + comp] = value
-
-        if packs:
-            count = 3 * steps
-            za[4] = jnp.zeros((count_x, count_y), jnp.float32)
-            for j in range(capacity):
-                lane, row = (j % 2) * points, (j // 2) * count
-                values = sample_ref[:count, j * points : (j + 1) * points]
-                za[4, row : row + count, lane : lane + points] = values
+    if last:
+        edges = [copy_out(inner // group, 0, 1), copy_out(inner // group + 1, count_x - 1, 1)]
+        for edge in edges:
+            edge.start()
+        for trip in range(inner // group):
+            copy_out(trip, 1 + trip * group, group).wait()
+        for edge in edges:
+            edge.wait()
+        return
+
+    za, others = face_refs[0], face_refs[1:]
+    write_faces(out_ref, [za.at[:4]] + list(others), shape)
+
+    @pl.when(listed)
+    def _():
+        rows = turbine_rows(rows_ref, table_ref, slots, step + 1, points)
+        weights, factor_y = point_factors(rows, shape)
+        for comp, value in enumerate(sample(out_ref, weights, factor_y, shape)):
+            sample_ref[3 * step + 3 + comp : 3 * step + 4 + comp] = value
+
+    if packs:
+        count = 3 * steps + 1
+        za[4] = jnp.zeros((count_x, count_y), jnp.float32)
+        for j, slot in enumerate(slots):
+            lane, row = (j % 2) * points, (j // 2) * count
+            values = sample_ref[: count - 1, j * points : (j + 1) * points]
+            za[4, row : row + count - 1, lane : lane + points] = values
+            name = jnp.where(listed, 0.5 * (slot + 1).astype(jnp.float32), 0.0)
+            za[4, row + count - 1 : row + count, lane : lane + points] = jnp.full((1, points), name)
 
 
 def face_shapes(shape, extra=0):
     count_x, count_z, count_y = shape
     forms = [(4 + extra, count_x, count_y), (4, count_x, count_y)]
-    forms += [(4, count_z, 128)] * 2 + [(4, count_z, count_y)] * 2
+    forms += [(4, count_z, 128)] * 2 + [(4, count_z, count_y)] * (1 if lax.axis_size("gx") == 2 else 2)
     return [jax.ShapeDtypeStruct(form, jnp.float32) for form in forms]
 
 
 def vmem_specs(count):
     return [pl.BlockSpec(memory_space=pltpu.VMEM)] * count
+
+
+def swap_faces(faces):
+    plan = [("gz", 0), ("gz", 1), ("gy", 0), ("gy", 1), ("gx", 0), ("gx", 1)]
+    return [swap(face, axis, first) for face, (axis, first) in zip(faces, plan)]
+
+
+def true_order(pieces, axis):
+    distance = 1
+    while distance < pieces.shape[0]:
+        swapped = pieces.reshape((-1, 2, distance) + pieces.shape[1:])[:, ::-1].reshape(pieces.shape)
+        odd = lax.rem(lax.div(lax.axis_index(axis), distance), 2) == 1
+        pieces = jnp.where(odd, swapped, pieces)
+        distance *= 2
+    return pieces
 
 
 def shards(flow, positions, loads, block_list):
@@ -311,104 +349,111 @@
     q = flow
     turbines = block_list.reshape(capacity)
     barrier = lax.optimization_barrier
-
+    forms = face_shapes(shape)
+
+    own = jnp.concatenate([positions.reshape(steps, 3, part), loads.reshape(steps, 3, part)], axis=1)
+    table = jnp.pad(own, ((0, 0), (0, 2), (0, 0))).reshape(1, 8 * steps, part)
+    table = jnp.concatenate([table, from_distance(table, "gz", 1)], axis=0)
     faces = pl.pallas_call(
         functools.partial(faces_body, shape=shape),
-        out_shape=face_shapes(shape),
+        out_shape=forms,
         in_specs=vmem_specs(1),
-        out_specs=vmem_specs(6),
+        out_specs=vmem_specs(len(forms)),
         compiler_params=params,
         name="faces",
     )(q)
-
-    named = block_list.reshape(1, 1, capacity).astype(jnp.float32)
-    named = jnp.broadcast_to(jnp.pad(named, ((0, 0), (0, 0), (0, part - capacity))), (steps, 2, part))
-    own = [positions.reshape(steps, 3, part), loads.reshape(steps, 3, part), named]
-    table = jnp.concatenate(own, axis=1).reshape(1, 8 * steps, part)
-
-    table = jnp.concatenate([table, from_distance(table, "gz", 1)], axis=0)
-    waiting = list(faces)
-    plan = [(0, "gz", 0), (1, "gz", 1), (2, "gy", 0), (3, "gy", 1), (4, "gx", 0), (5, "gx", 1)]
-    hops = []
-    for axis in ("gz", "gy", "gx"):
-        distance = 2 if axis == "gz" else 1
-        while distance < lax.axis_size(axis):
-            hops.append((axis, distance))
-            distance *= 2
-    halos = [None] * 6
-    for axis, distance in hops:
-        table, waiting = barrier((table, waiting))
-        received = from_distance(table, axis, distance)
-        if plan:
-            place, along, first = plan.pop(0)
-            halos[place] = swap(waiting[place], along, first)
-        table = jnp.concatenate([table, received], axis=0)
-    for place, along, first in plan:
-        halos[place] = swap(waiting[place], along, first)
+    table, faces = barrier((table, list(faces)))
+    za, zb, ya, yb = faces[:4]
+    distance = 2
+    while distance < size_z:
+        table = jnp.concatenate([table, from_distance(table, "gz", distance)], axis=0)
+        distance *= 2
+    za, zb = swap(za, "gz", 0), swap(zb, "gz", 1)
+    table = true_order(table, "gz")
+    table = jnp.concatenate([table[k] for k in range(size_z)], axis=1)
+    rows = pl.cdiv(8 * steps, 2 * count_z) * 2 * count_z
+    blocks = jnp.pad(table, ((0, rows - 8 * steps), (0, 0))).reshape(rows // count_z, count_z, points)
+    blocks, ya, yb, za = barrier((blocks, ya, yb, za))
+    ya = swap(jnp.concatenate([ya, blocks], axis=0), "gy", 0)
+    blocks = jnp.concatenate([blocks, ya[4:]], axis=0)
+    blocks, yb, zb, faces = barrier((blocks, yb, zb, list(faces)))
+    yb = from_distance(jnp.concatenate([yb, blocks], axis=0), "gy", 3)
+    x_faces = [swap(face, "gx", first) for first, face in enumerate(faces[4:])]
+    blocks = jnp.concatenate([blocks, yb[4:]], axis=0)[None]
+    table = gather_relative(blocks, "gx").reshape(size_x * size_y, rows, points)
+    halos = [za, zb, ya, yb] + x_faces
 
     samples = None
     for step in range(steps):
         last, packs = step == steps - 1, step == steps - 2
         shapes = [jax.ShapeDtypeStruct(q.shape, jnp.float32)]
-        if not last:
+        out_specs = vmem_specs(1)
+        scratch = []
+        if last:
+            out_specs = [pl.BlockSpec(memory_space=pl.ANY)]
+            scratch = [pltpu.VMEM(q.shape, jnp.float32), pltpu.SemaphoreType.DMA((count_x,))]
+        else:
             shapes += face_shapes(shape, 1 if packs else 0)
-            shapes += [jax.ShapeDtypeStruct((16, lanes), jnp.float32)]
+            if packs:
+                scratch = [pltpu.VMEM((16, lanes), jnp.float32)]
+            else:
+                shapes += [jax.ShapeDtypeStruct((16, lanes), jnp.float32)]
+            out_specs = vmem_specs(len(shapes))
         past = [] if step == 0 or last else [samples]
         results = pl.pallas_call(
             functools.partial(step_body, shape=shape, points=points, capacity=capacity, step=step, steps=steps),
             out_shape=shapes,
-            in_specs=[pl.BlockSpec(memory_space=pltpu.SMEM)] + vmem_specs(8 + len(past)),
-            out_specs=vmem_specs(len(shapes)),
-            scratch_shapes=[pltpu.VMEM((3,) + shape, jnp.float32), pltpu.VMEM((8, lanes), jnp.float32)]
+            in_specs=[pl.BlockSpec(memory_space=pltpu.SMEM)] + vmem_specs(2 + len(halos) + len(past)),
+            out_specs=out_specs,
+            scratch_shapes=scratch
+            + [pltpu.VMEM((3,) + shape, jnp.float32), pltpu.VMEM((8, lanes), jnp.float32)]
             + [pltpu.VMEM((4, count_y // 128, count_x, 128), jnp.float32)] * 2
-            + [pltpu.VMEM(form.shape, jnp.float32) for form in face_shapes(shape)[2:]],
+            + [pltpu.VMEM((4, count_z, 128), jnp.float32)] * 2
+            + [pltpu.VMEM((4, count_z, count_y), jnp.float32)] * 2,
             compiler_params=params,
             name="step",
         )(turbines, table, q, *halos, *past)
         q = results[0]
         if last:
             break
-        faces, samples = results[1:7], results[7]
+        faces = results[1 : 1 + len(forms)]
         if not packs:
-            halos = [swap(faces[place], along, first) for place, along, first in
-                     [(0, "gz", 0), (1, "gz", 1), (2, "gy", 0), (3, "gy", 1), (4, "gx", 0), (5, "gx", 1)]]
+            samples = results[-1]
+            halos = swap_faces(faces)
             continue
-        za, zb, ya, yb, xa, xb = faces
-        za_in = swap(za, "gz", 0)
-        zb_in = swap(zb, "gz", 1)
+        za, zb, ya, yb = faces[:4]
+        za_in, zb_in = swap(za, "gz", 0), swap(zb, "gz", 1)
         sums = za[4] + za_in[4]
-        row_blocks = pl.cdiv(3 * steps * pl.cdiv(capacity, 2), count_z)
+        row_blocks = pl.cdiv((3 * steps + 1) * pl.cdiv(capacity, 2), count_z)
         blocks = jnp.stack(
             [sums[b * count_z : (b + 1) * count_z, h * 128 : h * 128 + 128] for b in range(row_blocks) for h in range(2)]
         )
+        blocks, ya, zb_in = barrier((blocks, ya, zb_in))
         count = blocks.shape[0]
         ya_in = swap(jnp.concatenate([ya, blocks], axis=0), "gy", 0)
-        xa_in, xb_in = swap(xa, "gx", 0), swap(xb, "gx", 1)
+        x_faces = [swap(face, "gx", first) for first, face in enumerate(faces[4:])]
         pieces = jnp.concatenate([blocks, ya_in[4:]], axis=0)
+        pieces, yb, x_faces = barrier((pieces, yb, x_faces))
         yb_in = from_distance(jnp.concatenate([yb, pieces], axis=0), "gy", 3)
         pieces = jnp.concatenate([pieces, yb_in[4:]], axis=0).reshape(size_y, count, count_z, 128)
-        halos = [za_in, zb_in, ya_in, yb_in, xa_in, xb_in]
+        halos = [za_in, zb_in, ya_in, yb_in] + x_faces
 
     distance = 2
     while distance < size_z:
         pieces = pieces + from_distance(pieces, "gz", distance)
         distance *= 2
+    pieces, q = barrier((pieces, q))
     mine = lax.dynamic_slice_in_dim(pieces, lax.axis_index("gz") * part, part, axis=3)[None]
     mine = gather_relative(mine, "gx")
     mine = mine.reshape(size_x * size_y, row_blocks, 2, count_z, part).transpose(0, 2, 1, 3, 4)
     mine = mine.reshape(size_x * size_y, 2, row_blocks * count_z, part)
-
-    holder = (lax.axis_index("gx") * size_y + lax.axis_index("gy")).astype(jnp.float32)
-    listed = table[:, 6, :capacity].reshape(size_x, size_y, size_z, capacity)
-    slots = sorted_slots(jnp.moveaxis(listed, -1, 0), capacity)
-    order = jnp.stack([jnp.min(slot, axis=2) for slot in slots])
-    order = jnp.stack([order[:, :, k] for k in (0, 1, 3, 2)], axis=2).reshape(capacity, size_x * size_y)
-    match = (order == holder).astype(jnp.float32)
+    holder = (lax.axis_index("gx") * size_y + lax.axis_index("gy") + 1).astype(jnp.float32)
     returned = 0.0
     for j in range(capacity):
-        row = (j // 2) * 3 * steps
+        row = (j // 2) * (3 * steps + 1)
         values = mine[:, j % 2, row : row + 3 * steps]
-        returned = returned + jnp.sum(values * match[j][:, None, None], axis=0)
+        match = mine[:, j % 2, row + 3 * steps :][:, :1] == holder
+        returned = returned + jnp.sum(jnp.where(match, values, 0.0), axis=0)
     return q, returned.reshape(positions.shape)
 
 

time: 86.7 us -> 75.4 us (0.87)
  Pallas kernels: 26.9 us -> 17.6 us
  other arithmetic: 1.25 us -> 0.27 us
    pallas_call x3, Pallas kernels: 25.5 us -> 16.9 us  [shards(): pl.pallas_call(functools.partial(step_body, shape=shape, points=points, c...]
    ppermute x8 -> x7, waiting for transfers between devices: 13.3 us -> 9.08 us  [from_distance(): return lax.ppermute(value, axis, [(i, i ^ distance) for i in range(count)])]
    ppermute x14 -> x13, waiting for transfers between devices: 8.96 us -> 12.7 us  [swap(): return lax.ppermute(value, axis, pairs)]
    ppermute x8 -> x7, starting transfers between devices: 11.5 us -> 13.1 us  [from_distance(): return lax.ppermute(value, axis, [(i, i ^ distance) for i in range(count)])]
    ppermute x14 -> x13, starting transfers between devices: 19.7 us -> 18.5 us  [swap(): return lax.ppermute(value, axis, pairs)]
    unnamed x6 -> x10, local copies, waits for them, and re-layouts: 2.32 us -> 2.33 us
  transfers between devices with their start and end apart: 22 -> 20, of which waited for: 11 -> 11; matrix products, arithmetic and copies ran while one was open for 1% -> 0% of each run, Pallas kernels for 11% -> 8%
where the time goes in v2:
time: 75.4 us; the launch traced here: 75.2 us
  starting transfers between devices  31.6 us (42%)
  waiting for transfers between devices  21.8 us (29%)
  Pallas kernels  17.6 us (23%)
  local copies, waits for them, and re-layouts  3.06 us (4%)
  between operations  0.92 us (1%)
    ppermute x13, starting transfers between devices, swap(): return lax.ppermute(value, axis, pairs)  18.5 us
    pallas_call x3, Pallas kernels, shards(): pl.pallas_call(functools.partial(step_body, shape=shape, points=points, c...  16.9 us
    ppermute x7, starting transfers between devices, from_distance(): return lax.ppermute(value, axis, [(i, i ^ distance) for i in range(count)])  13.1 us
    ppermute x13, waiting for transfers between devices, swap(): return lax.ppermute(value, axis, pairs)  12.7 us
    ppermute x7, waiting for transfers between devices, from_distance(): return lax.ppermute(value, axis, [(i, i ^ distance) for i in range(count)])  9.08 us
    unnamed x10, local copies, waits for them, and re-layouts  2.33 us
  transfers between devices with their start and end apart: 20, of which 11 were waited for; matrix products, arithmetic and copies ran while one was open for 0% of the time, Pallas kernels for 8%

profile of v2, /device:TPU:0, one launch (start us, length us, event | category | flops | bytes accessed | tf_op | source)
XLA Modules:
  0.0 75.2 jit_solution(16773757673102814125)
XLA Ops:
  0.6 0.7 copy_bitcast_fusion
  1.4 3.1 %collective-permute-start = (f32[1,24,32]{2,1,0:T(8,128)S(1)}, f32[1,24,32]{2,1,0:T(8,128)S(1)}, u32[]{:S(2)}, u32[]{:S(2)}) collective-permute-start(f32[1,24,32]{2,1,0:T(8,128)S(1)} %fusion.6), channel_id=1, source_target_pairs={{0,1},{1,0},{2,3},{3,2},{4,5},{5,4},{6,7},{7,6},{8,9},{9,8},{10,11... | collective-permute-start | bytes 9224 | tf_op jit(solution)/shard_map/ppermute | solution.py:37
  4.5 1.6 %copy-done = f32[4,32,16,256]{3,2,1,0:T(8,128)S(1)} copy-done((f32[4,32,16,256]{3,2,1,0:T(8,128)S(1)}, f32[4,32,16,256]{3,2,1,0:T(8,128)}, u32[]{:S(2)}) %copy-start) | copy-done | bytes 2097176
  6.0 0.7 faces.1
  6.8 2.7 %collective-permute-start.1 = (f32[2,24,32]{2,1,0:T(8,128)S(1)}, f32[2,24,32]{2,1,0:T(8,128)S(1)}, u32[]{:S(2)}, u32[]{:S(2)}) collective-permute-start(f32[2,24,32]{2,1,0:T(8,128)S(1)} %pad_maximum_fusion.9), channel_id=1, source_target_pairs={{0,2},{1,3},{2,0},{3,1},{4,6},{5,7},{6,4},{7,5},{8,10},{9,11},{10,... | collective-permute-start | bytes 18440 | tf_op jit(solution)/shard_map/ppermute | solution.py:37
  9.4 1.3 %collective-permute-start.2 = (f32[4,32,256]{2,1,0:T(8,128)S(1)}, f32[4,32,256]{2,1,0:T(8,128)S(1)}, u32[]{:S(2)}, u32[]{:S(2)}) collective-permute-start(f32[4,32,256]{2,1,0:T(8,128)S(1)} %get-tuple-element.50), channel_id=1, source_target_pairs={{0,1},{1,0},{2,3},{3,2},{4,5},{5,4},{6,7},{7,6},{8,9},{9,8},{10,11... | collective-permute-start | bytes 393224 | tf_op jit(solution)/shard_map/ppermute | solution.py:32
  10.7 0.9 %collective-permute-done.1 = f32[2,24,32]{2,1,0:T(8,128)S(1)} collective-permute-done((f32[2,24,32]{2,1,0:T(8,128)S(1)}, f32[2,24,32]{2,1,0:T(8,128)S(1)}, u32[]{:S(2)}, u32[]{:S(2)}) %collective-permute-start.1) | collective-permute-done | bytes 6176 | tf_op jit(solution)/shard_map/ppermute | solution.py:37
  11.8 2.6 %collective-permute-done.2.refs_3_ = f32[4,32,256]{2,1,0:T(8,128)S(1)} collective-permute-done((f32[4,32,256]{2,1,0:T(8,128)S(1)}, f32[4,32,256]{2,1,0:T(8,128)S(1)}, u32[]{:S(2)}, u32[]{:S(2)}) %collective-permute-start.2) | collective-permute-done | bytes 131104 | tf_op jit(solution)/shard_map/ppermute | solution.py:32
  14.4 1.5 %collective-permute-start.3 = (f32[6,16,128]{2,1,0:T(8,128)S(1)}, f32[6,16,128]{2,1,0:T(8,128)S(1)}, u32[]{:S(2)}, u32[]{:S(2)}) collective-permute-start(f32[6,16,128]{2,1,0:T(8,128)S(1)} %pad_maximum_fusion.5), channel_id=1, source_target_pairs={{0,4},{4,0},{8,12},{12,8},{1,5},{5,1},{9,13},{13,9},{2,6},{6,2},{1... | collective-permute-start | bytes 147464 | tf_op jit(solution)/shard_map/ppermute | solution.py:32
  15.9 0.7 collective-permute-start.4
  16.6 1.9 %collective-permute-done.3.refs_5_ = f32[6,16,128]{2,1,0:T(8,128)S(1)} collective-permute-done((f32[6,16,128]{2,1,0:T(8,128)S(1)}, f32[6,16,128]{2,1,0:T(8,128)S(1)}, u32[]{:S(2)}, u32[]{:S(2)}) %collective-permute-start.3) | collective-permute-done | bytes 49184 | tf_op jit(solution)/shard_map/ppermute | solution.py:32
  18.5 2.7 %collective-permute-start.5 = (f32[8,16,128]{2,1,0:T(8,128)S(1)}, f32[8,16,128]{2,1,0:T(8,128)S(1)}, u32[]{:S(2)}, u32[]{:S(2)}) collective-permute-start(f32[8,16,128]{2,1,0:T(8,128)S(1)} %pad_maximum_fusion.2), channel_id=1, source_target_pairs={{0,12},{4,8},{8,4},{12,0},{1,13},{5,9},{9,5},{13,1},{2,14},{6,10},... | collective-permute-start | bytes 196616 | tf_op jit(solution)/shard_map/ppermute | solution.py:37
  21.3 2.5 %collective-permute-done.5.refs_6_ = f32[8,16,128]{2,1,0:T(8,128)S(1)} collective-permute-done((f32[8,16,128]{2,1,0:T(8,128)S(1)}, f32[8,16,128]{2,1,0:T(8,128)S(1)}, u32[]{:S(2)}, u32[]{:S(2)}) %collective-permute-start.5) | collective-permute-done | bytes 65568 | tf_op jit(solution)/shard_map/ppermute | solution.py:37
  24.3 0.7 collective-permute-done.6
  25.3 6.2 %step.3 = (f32[4,32,16,256]{3,2,1,0:T(8,128)S(1)}, f32[4,32,256]{2,1,0:T(8,128)S(1)}, f32[4,32,256]{2,1,0:T(8,128)S(1)}, f32[4,16,128]{2,1,0:T(8,128)S(1)}, f32[...) custom-call(s32[2]{0:T(128)S(1)} %bitcast.68, f32[8,32,128]{2,1,0:T(8,128)S(1)} %bitcast.65, ...), custom_call_target="tpu_custom_call" | custom-call | tf_op jit(solution)/shard_map/step/pallas_call | solution.py:403
  31.4 5.5 %collective-permute-start.8 = (f32[4,32,256]{2,1,0:T(8,128)S(1)}, f32[4,32,256]{2,1,0:T(8,128)S(1)}, u32[]{:S(2)}, u32[]{:S(2)}) collective-permute-start(f32[4,32,256]{2,1,0:T(8,128)S(1)} %get-tuple-element.62), channel_id=1, source_target_pairs={{0,1},{1,0},{2,3},{3,2},{4,5},{5,4},{6,7},{7,6},{8,9},{9,8},{10,11... | collective-permute-start | bytes 393224 | tf_op jit(solution)/shard_map/ppermute | solution.py:32
  37.0 0.7 collective-permute-start.9
  37.8 0.5 collective-permute-start.10
  38.3 0.7 collective-permute-start.11
  39.0 2.7 %collective-permute-done.10.refs_5_ = f32[4,16,128]{2,1,0:T(8,128)S(1)} collective-permute-done((f32[4,16,128]{2,1,0:T(8,128)S(1)}, f32[4,16,128]{2,1,0:T(8,128)S(1)}, u32[]{:S(2)}, u32[]{:S(2)}) %collective-permute-start.10) | collective-permute-done | bytes 32800 | tf_op jit(solution)/shard_map/ppermute | solution.py:32
  41.7 5.7 %step.4 = (f32[4,32,16,256]{3,2,1,0:T(8,128)S(1)}, f32[5,32,256]{2,1,0:T(8,128)S(1)}, f32[4,32,256]{2,1,0:T(8,128)S(1)}, f32[4,16,128]{2,1,0:T(8,128)S(1)}, f32[...) custom-call(s32[2]{0:T(128)S(1)} %bitcast.69, f32[8,32,128]{2,1,0:T(8,128)S(1)} %bitcast.66, ...), custom_call_target="tpu_custom_call" | custom-call | tf_op jit(solution)/shard_map/step/pallas_call | solution.py:403
  47.4 3.0 %collective-permute-start.13 = (f32[5,32,256]{2,1,0:T(8,128)S(1)}, f32[5,32,256]{2,1,0:T(8,128)S(1)}, u32[]{:S(2)}, u32[]{:S(2)}) collective-permute-start(f32[5,32,256]{2,1,0:T(8,128)S(1)} %get-tuple-element.68), channel_id=1, source_target_pairs={{0,1},{1,0},{2,3},{3,2},{4,5},{5,4},{6,7},{7,6},{8,9},{9,8},{10,11... | collective-permute-start | bytes 491528 | tf_op jit(solution)/shard_map/ppermute | solution.py:32
  50.4 0.7 collective-permute-start.14
  51.0 3.2 %collective-permute-done.13.refs_3_ = f32[5,32,256]{2,1,0:T(8,128)S(1)} collective-permute-done((f32[5,32,256]{2,1,0:T(8,128)S(1)}, f32[5,32,256]{2,1,0:T(8,128)S(1)}, u32[]{:S(2)}, u32[]{:S(2)}) %collective-permute-start.13) | collective-permute-done | bytes 163872 | tf_op jit(solution)/shard_map/ppermute | solution.py:32
  54.3 3.4 %collective-permute-start.15 = (f32[6,16,128]{2,1,0:T(8,128)S(1)}, f32[6,16,128]{2,1,0:T(8,128)S(1)}, u32[]{:S(2)}, u32[]{:S(2)}) collective-permute-start(f32[6,16,128]{2,1,0:T(8,128)S(1)} %pad_maximum_fusion.6), channel_id=1, source_target_pairs={{0,4},{4,0},{8,12},{12,8},{1,5},{5,1},{9,13},{13,9},{2,6},{6,2},{1... | collective-permute-start | bytes 147464 | tf_op jit(solution)/shard_map/ppermute | solution.py:32
  57.7 2.1 %collective-permute-done.15.refs_5_ = f32[6,16,128]{2,1,0:T(8,128)S(1)} collective-permute-done((f32[6,16,128]{2,1,0:T(8,128)S(1)}, f32[6,16,128]{2,1,0:T(8,128)S(1)}, u32[]{:S(2)}, u32[]{:S(2)}) %collective-permute-start.15) | collective-permute-done | bytes 49184 | tf_op jit(solution)/shard_map/ppermute | solution.py:32
  59.8 1.6 %collective-permute-start.17 = (f32[8,16,128]{2,1,0:T(8,128)S(1)}, f32[8,16,128]{2,1,0:T(8,128)S(1)}, u32[]{:S(2)}, u32[]{:S(2)}) collective-permute-start(f32[8,16,128]{2,1,0:T(8,128)S(1)} %pad_maximum_fusion.3), channel_id=1, source_target_pairs={{0,12},{4,8},{8,4},{12,0},{1,13},{5,9},{9,5},{13,1},{2,14},{6,10},... | collective-permute-start | bytes 196616 | tf_op jit(solution)/shard_map/ppermute | solution.py:37
  61.3 3.7 %collective-permute-done.17.refs_6_ = f32[8,16,128]{2,1,0:T(8,128)S(1)} collective-permute-done((f32[8,16,128]{2,1,0:T(8,128)S(1)}, f32[8,16,128]{2,1,0:T(8,128)S(1)}, u32[]{:S(2)}, u32[]{:S(2)}) %collective-permute-start.17) | collective-permute-done | bytes 65568 | tf_op jit(solution)/shard_map/ppermute | solution.py:37
  65.0 3.0 %collective-permute-start.18 = (f32[4,2,16,128]{3,2,1,0:T(8,128)S(1)}, f32[4,2,16,128]{3,2,1,0:T(8,128)S(1)}, u32[]{:S(2)}, u32[]{:S(2)}) collective-permute-start(f32[4,2,16,128]{3,2,1,0:T(8,128)S(1)} %bitcast.76), channel_id=1, source_target_pairs={{0,2},{1,3},{2,0},{3,1},{4,6},{5,7},{6,4},{7,5},{8,10},{9,11},{10,... | collective-permute-start | bytes 196616 | tf_op jit(solution)/shard_map/ppermute | solution.py:37
  68.0 5.0 %step.5 = f32[4,32,16,256]{3,2,1,0:T(8,128)} custom-call(s32[2]{0:T(128)S(1)} %bitcast.70, f32[8,32,128]{2,1,0:T(8,128)S(1)} %bitcast.67, f32[4,32,16,256]{3,2,1,0:T(8,128)S(1)} %get-tuple-element.77.refs_2_, f32[5,32,256]{2,1,0:T(8,128)S(1)} %collective-permute-done.13.refs_3_, f32[4,32,256]{2,1,0:T(8,128)S(1)} %collective-permute-done.14.refs_4_, ...), custom_call_target="tpu_custom_call" | custom-call | tf_op jit(solution)/shard_map/step/pallas_call | solution.py:403
  73.2 1.2 %collective-permute-done.19 = f32[1,4,2,16,32]{4,3,2,1,0:T(8,128)S(1)} collective-permute-done((f32[1,4,2,16,32]{4,3,2,1,0:T(8,128)S(1)}, f32[1,4,2,16,32]{4,3,2,1,0:T(8,128)S(1)}, u32[]{:S(2)}, u32[]{:S(2)}) %collective-permute-start.19) | collective-permute-done | bytes 16416 | tf_op jit(solution)/shard_map/ppermute | solution.py:37
  74.6 0.6 add.42
  (56 shorter events, 1.3 us)
Async XLA Ops:
  0.6 24.6 %copy-start.2 = (s32[1,1,1,2]{3,2,1,0:T(1,128)S(1)}, s32[1,1,1,2]{3,2,1,0:T(1,128)}, u32[]{:S(2)}) copy-start(s32[1,1,1,2]{3,2,1,0:T(1,128)} %param.7) | copy-start | bytes 28
  1.4 5.4 %collective-permute-start = (f32[1,24,32]{2,1,0:T(8,128)S(1)}, f32[1,24,32]{2,1,0:T(8,128)S(1)}, u32[]{:S(2)}, u32[]{:S(2)}) collective-permute-start(f32[1,24,32]{2,1,0:T(8,128)S(1)} %fusion.6), channel_id=1, source_target_pairs={{0,1},{1,0},{2,3},{3,2},{4,5},{5,4},{6,7},{7,6},{8,9},{9,8},{10,11... | collective-permute-start | bytes 9224 | tf_op jit(solution)/shard_map/ppermute | solution.py:37
  4.5 1.6 %copy-start = (f32[4,32,16,256]{3,2,1,0:T(8,128)S(1)}, f32[4,32,16,256]{3,2,1,0:T(8,128)}, u32[]{:S(2)}) copy-start(f32[4,32,16,256]{3,2,1,0:T(8,128)} %refs_2_.1) | copy-start | bytes 6291460
  6.0 19.2 %copy-start.1 = (f32[4,32,16,256]{3,2,1,0:T(8,128)S(1)}, f32[4,32,16,256]{3,2,1,0:T(8,128)}, u32[]{:S(2)}) copy-start(f32[4,32,16,256]{3,2,1,0:T(8,128)} %refs_2_.1) | copy-start | bytes 6291460
  6.8 4.9 %collective-permute-start.1 = (f32[2,24,32]{2,1,0:T(8,128)S(1)}, f32[2,24,32]{2,1,0:T(8,128)S(1)}, u32[]{:S(2)}, u32[]{:S(2)}) collective-permute-start(f32[2,24,32]{2,1,0:T(8,128)S(1)} %pad_maximum_fusion.9), channel_id=1, source_target_pairs={{0,2},{1,3},{2,0},{3,1},{4,6},{5,7},{6,4},{7,5},{8,10},{9,11},{10,... | collective-permute-start | bytes 18440 | tf_op jit(solution)/shard_map/ppermute | solution.py:37
  9.4 5.0 %collective-permute-start.2 = (f32[4,32,256]{2,1,0:T(8,128)S(1)}, f32[4,32,256]{2,1,0:T(8,128)S(1)}, u32[]{:S(2)}, u32[]{:S(2)}) collective-permute-start(f32[4,32,256]{2,1,0:T(8,128)S(1)} %get-tuple-element.50), channel_id=1, source_target_pairs={{0,1},{1,0},{2,3},{3,2},{4,5},{5,4},{6,7},{7,6},{8,9},{9,8},{10,11... | collective-permute-start | bytes 393224 | tf_op jit(solution)/shard_map/ppermute | solution.py:32
  14.4 4.1 %collective-permute-start.3 = (f32[6,16,128]{2,1,0:T(8,128)S(1)}, f32[6,16,128]{2,1,0:T(8,128)S(1)}, u32[]{:S(2)}, u32[]{:S(2)}) collective-permute-start(f32[6,16,128]{2,1,0:T(8,128)S(1)} %pad_maximum_fusion.5), channel_id=1, source_target_pairs={{0,4},{4,0},{8,12},{12,8},{1,5},{5,1},{9,13},{13,9},{2,6},{6,2},{1... | collective-permute-start | bytes 147464 | tf_op jit(solution)/shard_map/ppermute | solution.py:32
  15.9 2.6 %collective-permute-start.4 = (f32[4,32,256]{2,1,0:T(8,128)S(1)}, f32[4,32,256]{2,1,0:T(8,128)S(1)}, u32[]{:S(2)}, u32[]{:S(2)}) collective-permute-start(f32[4,32,256]{2,1,0:T(8,128)S(1)} %get-tuple-element.54), channel_id=1, source_target_pairs={{1,2},{2,1},{5,6},{6,5},{9,10},{10,9},{13,14},{14,13},{17,18},{18,... | collective-permute-start | bytes 393224 | tf_op jit(solution)/shard_map/ppermute | solution.py:32
  18.5 5.2 %collective-permute-start.5 = (f32[8,16,128]{2,1,0:T(8,128)S(1)}, f32[8,16,128]{2,1,0:T(8,128)S(1)}, u32[]{:S(2)}, u32[]{:S(2)}) collective-permute-start(f32[8,16,128]{2,1,0:T(8,128)S(1)} %pad_maximum_fusion.2), channel_id=1, source_target_pairs={{0,12},{4,8},{8,4},{12,0},{1,13},{5,9},{9,5},{13,1},{2,14},{6,10},... | collective-permute-start | bytes 196616 | tf_op jit(solution)/shard_map/ppermute | solution.py:37
  23.8 1.3 %collective-permute-start.6 = (f32[1,8,16,128]{3,2,1,0:T(8,128)S(1)}, f32[1,8,16,128]{3,2,1,0:T(8,128)S(1)}, u32[]{:S(2)}, u32[]{:S(2)}) collective-permute-start(f32[1,8,16,128]{3,2,1,0:T(8,128)S(1)} %maximum_bitcast_fusion), channel_id=1, source_target_pairs={{0,16},{16,0},{1,17},{17,1},{2,18},{18,2},{3,19},{19,3},{4,20},{20... | collective-permute-start | bytes 196616 | tf_op jit(solution)/shard_map/ppermute | solution.py:37
  23.8 1.4 %collective-permute-start.7 = (f32[4,16,256]{2,1,0:T(8,128)S(1)}, f32[4,16,256]{2,1,0:T(8,128)S(1)}, u32[]{:S(2)}, u32[]{:S(2)}) collective-permute-start(f32[4,16,256]{2,1,0:T(8,128)S(1)} %get-tuple-element.60), channel_id=1, source_target_pairs={{0,16},{16,0},{1,17},{17,1},{2,18},{18,2},{3,19},{19,3},{4,20},{20... | collective-permute-start | bytes 196616 | tf_op jit(solution)/shard_map/ppermute | solution.py:32
  31.4 10.3 %collective-permute-start.8 = (f32[4,32,256]{2,1,0:T(8,128)S(1)}, f32[4,32,256]{2,1,0:T(8,128)S(1)}, u32[]{:S(2)}, u32[]{:S(2)}) collective-permute-start(f32[4,32,256]{2,1,0:T(8,128)S(1)} %get-tuple-element.62), channel_id=1, source_target_pairs={{0,1},{1,0},{2,3},{3,2},{4,5},{5,4},{6,7},{7,6},{8,9},{9,8},{10,11... | collective-permute-start | bytes 393224 | tf_op jit(solution)/shard_map/ppermute | solution.py:32
  37.0 4.7 %collective-permute-start.9 = (f32[4,32,256]{2,1,0:T(8,128)S(1)}, f32[4,32,256]{2,1,0:T(8,128)S(1)}, u32[]{:S(2)}, u32[]{:S(2)}) collective-permute-start(f32[4,32,256]{2,1,0:T(8,128)S(1)} %get-tuple-element.63), channel_id=1, source_target_pairs={{1,2},{2,1},{5,6},{6,5},{9,10},{10,9},{13,14},{14,13},{17,18},{18,... | collective-permute-start | bytes 393224 | tf_op jit(solution)/shard_map/ppermute | solution.py:32
  37.6 4.1 %collective-permute-start.12 = (f32[4,16,256]{2,1,0:T(8,128)S(1)}, f32[4,16,256]{2,1,0:T(8,128)S(1)}, u32[]{:S(2)}, u32[]{:S(2)}) collective-permute-start(f32[4,16,256]{2,1,0:T(8,128)S(1)} %get-tuple-element.66), channel_id=1, source_target_pairs={{0,16},{16,0},{1,17},{17,1},{2,18},{18,2},{3,19},{19,3},{4,20},{20... | collective-permute-start | bytes 196616 | tf_op jit(solution)/shard_map/ppermute | solution.py:32
  37.8 3.9 %collective-permute-start.10 = (f32[4,16,128]{2,1,0:T(8,128)S(1)}, f32[4,16,128]{2,1,0:T(8,128)S(1)}, u32[]{:S(2)}, u32[]{:S(2)}) collective-permute-start(f32[4,16,128]{2,1,0:T(8,128)S(1)} %get-tuple-element.64), channel_id=1, source_target_pairs={{0,4},{4,0},{8,12},{12,8},{1,5},{5,1},{9,13},{13,9},{2,6},{6,2},{1... | collective-permute-start | bytes 98312 | tf_op jit(solution)/shard_map/ppermute | solution.py:32
  38.3 3.4 %collective-permute-start.11 = (f32[4,16,128]{2,1,0:T(8,128)S(1)}, f32[4,16,128]{2,1,0:T(8,128)S(1)}, u32[]{:S(2)}, u32[]{:S(2)}) collective-permute-start(f32[4,16,128]{2,1,0:T(8,128)S(1)} %get-tuple-element.65), channel_id=1, source_target_pairs={{4,8},{8,4},{5,9},{9,5},{6,10},{10,6},{7,11},{11,7},{20,24},{24,20... | collective-permute-start | bytes 98312 | tf_op jit(solution)/shard_map/ppermute | solution.py:32
  47.4 6.9 %collective-permute-start.13 = (f32[5,32,256]{2,1,0:T(8,128)S(1)}, f32[5,32,256]{2,1,0:T(8,128)S(1)}, u32[]{:S(2)}, u32[]{:S(2)}) collective-permute-start(f32[5,32,256]{2,1,0:T(8,128)S(1)} %get-tuple-element.68), channel_id=1, source_target_pairs={{0,1},{1,0},{2,3},{3,2},{4,5},{5,4},{6,7},{7,6},{8,9},{9,8},{10,11... | collective-permute-start | bytes 491528 | tf_op jit(solution)/shard_map/ppermute | solution.py:32
  50.4 3.9 %collective-permute-start.14 = (f32[4,32,256]{2,1,0:T(8,128)S(1)}, f32[4,32,256]{2,1,0:T(8,128)S(1)}, u32[]{:S(2)}, u32[]{:S(2)}) collective-permute-start(f32[4,32,256]{2,1,0:T(8,128)S(1)} %get-tuple-element.70), channel_id=1, source_target_pairs={{1,2},{2,1},{5,6},{6,5},{9,10},{10,9},{13,14},{14,13},{17,18},{18,... | collective-permute-start | bytes 393224 | tf_op jit(solution)/shard_map/ppermute | solution.py:32
  54.3 5.4 %collective-permute-start.15 = (f32[6,16,128]{2,1,0:T(8,128)S(1)}, f32[6,16,128]{2,1,0:T(8,128)S(1)}, u32[]{:S(2)}, u32[]{:S(2)}) collective-permute-start(f32[6,16,128]{2,1,0:T(8,128)S(1)} %pad_maximum_fusion.6), channel_id=1, source_target_pairs={{0,4},{4,0},{8,12},{12,8},{1,5},{5,1},{9,13},{13,9},{2,6},{6,2},{1... | collective-permute-start | bytes 147464 | tf_op jit(solution)/shard_map/ppermute | solution.py:32
  57.7 2.1 %collective-permute-start.16 = (f32[4,16,256]{2,1,0:T(8,128)S(1)}, f32[4,16,256]{2,1,0:T(8,128)S(1)}, u32[]{:S(2)}, u32[]{:S(2)}) collective-permute-start(f32[4,16,256]{2,1,0:T(8,128)S(1)} %get-tuple-element.74), channel_id=1, source_target_pairs={{0,16},{16,0},{1,17},{17,1},{2,18},{18,2},{3,19},{19,3},{4,20},{20... | collective-permute-start | bytes 196616 | tf_op jit(solution)/shard_map/ppermute | solution.py:32
  59.8 5.2 %collective-permute-start.17 = (f32[8,16,128]{2,1,0:T(8,128)S(1)}, f32[8,16,128]{2,1,0:T(8,128)S(1)}, u32[]{:S(2)}, u32[]{:S(2)}) collective-permute-start(f32[8,16,128]{2,1,0:T(8,128)S(1)} %pad_maximum_fusion.3), channel_id=1, source_target_pairs={{0,12},{4,8},{8,4},{12,0},{1,13},{5,9},{9,5},{13,1},{2,14},{6,10},... | collective-permute-start | bytes 196616 | tf_op jit(solution)/shard_map/ppermute | solution.py:37
  65.0 8.0 %collective-permute-start.18 = (f32[4,2,16,128]{3,2,1,0:T(8,128)S(1)}, f32[4,2,16,128]{3,2,1,0:T(8,128)S(1)}, u32[]{:S(2)}, u32[]{:S(2)}) collective-permute-start(f32[4,2,16,128]{3,2,1,0:T(8,128)S(1)} %bitcast.76), channel_id=1, source_target_pairs={{0,2},{1,3},{2,0},{3,1},{4,6},{5,7},{6,4},{7,5},{8,10},{9,11},{10,... | collective-permute-start | bytes 196616 | tf_op jit(solution)/shard_map/ppermute | solution.py:37
  73.1 1.3 %collective-permute-start.19 = (f32[1,4,2,16,32]{4,3,2,1,0:T(8,128)S(1)}, f32[1,4,2,16,32]{4,3,2,1,0:T(8,128)S(1)}, u32[]{:S(2)}, u32[]{:S(2)}) collective-permute-start(f32[1,4,2,16,32]{4,3,2,1,0:T(8,128)S(1)} %dynamic-slice_bitcast_fusion), channel_id=1, source_target_pairs={{0,16},{16,0},{1,17},{17,1},{2,18},{18,2},{3,19},{19,3},{4,20},{20... | collective-permute-start | bytes 49160 | tf_op jit(solution)/shard_map/ppermute | solution.py:37

commit v3 on v2

--- a/solution.py
+++ b/solution.py
@@ -67,16 +67,17 @@
         za_ref[comp] = pick(even_z, high, low)
         zb_ref[comp] = pick(even_z, low, high)
     lane = lax.broadcasted_iota(jnp.int32, (count_z, 128), 1)
+    low = jnp.zeros((count_z, 128), jnp.float32)
+    high = jnp.zeros((count_z, 128), jnp.float32)
     for comp in range(4):
-        low = jnp.zeros((count_z, 128), jnp.float32)
-        high = jnp.zeros((count_z, 128), jnp.float32)
         for x in range(count_x):
+            place = comp * count_x + x
             first = q_ref[comp, x, :, :128]
             last = q_ref[comp, x, :, count_y - 128 :]
-            low = jnp.where(lane == x, pltpu.roll(first, x, 1), low)
-            high = jnp.where(lane == x, pltpu.roll(last, (x + 1) % 128, 1), high)
-        ya_ref[comp] = pick(even_y, high, low)
-        yb_ref[comp] = pick(even_y, low, high)
+            low = jnp.where(lane == place, pltpu.roll(first, place, 1), low)
+            high = jnp.where(lane == place, pltpu.roll(last, (place + 1) % 128, 1), high)
+    ya_ref[0] = pick(even_y, high, low)
+    yb_ref[0] = pick(even_y, low, high)
 
 
 def faces_body(q_ref, *face_refs, shape):
@@ -226,8 +227,8 @@
         first, second = (ref[:4, :, tile * 128 : tile * 128 + 128] for ref in (za_ref, zb_ref))
         low_z_ref[:, tile] = pick(even_z, second, first)
         high_z_ref[:, tile] = pick(even_z, first, second)
-    low_y_ref[...] = pick(index_y == 0, 0.0, pick(even_y, yb_ref[:4], ya_ref[:4]))
-    high_y_ref[...] = pick(index_y == lax.axis_size("gy") - 1, 0.0, pick(even_y, ya_ref[:4], yb_ref[:4]))
+    low_y_ref[...] = pick(index_y == 0, 0.0, pick(even_y, yb_ref[0], ya_ref[0]))
+    high_y_ref[...] = pick(index_y == lax.axis_size("gy") - 1, 0.0, pick(even_y, ya_ref[0], yb_ref[0]))
     first = x_refs[0][...]
     second = x_refs[1][...] if len(x_refs) > 1 else 0.0
     low_x_ref[...] = pick(even_x, second, first)
@@ -238,10 +239,11 @@
         centre, up, down = [], [], []
         for comp in range(4):
             row = [q_ref[comp, x, :, tile * 128 : tile * 128 + 128] for tile in range(tiles)]
-            turn = (128 - x) % 128 if isinstance(x, int) else 128 - x
+            place = comp * count_x + x
+            turn = (128 - place) % 128 if isinstance(place, int) else 128 - place
             centre.append(row)
-            up.append([pltpu.roll(low_y_ref[comp], turn, 1)] + [pltpu.roll(c, 1, 1) for c in row])
-            down.append([pltpu.roll(c, 127, 1) for c in row] + [pltpu.roll(high_y_ref[comp], 127 - x, 1)])
+            up.append([pltpu.roll(low_y_ref[...], turn, 1)] + [pltpu.roll(c, 1, 1) for c in row])
+            down.append([pltpu.roll(c, 127, 1) for c in row] + [pltpu.roll(high_y_ref[...], 127 - place, 1)])
         for tile in range(tiles):
             here = slice(tile * 128, tile * 128 + 128)
             shifts = []
@@ -314,7 +316,7 @@
 def face_shapes(shape, extra=0):
     count_x, count_z, count_y = shape
     forms = [(4 + extra, count_x, count_y), (4, count_x, count_y)]
-    forms += [(4, count_z, 128)] * 2 + [(4, count_z, count_y)] * (1 if lax.axis_size("gx") == 2 else 2)
+    forms += [(1, count_z, 128)] * 2 + [(4, count_z, count_y)] * (1 if lax.axis_size("gx") == 2 else 2)
     return [jax.ShapeDtypeStruct(form, jnp.float32) for form in forms]
 
 
@@ -373,13 +375,14 @@
     table = jnp.concatenate([table[k] for k in range(size_z)], axis=1)
     rows = pl.cdiv(8 * steps, 2 * count_z) * 2 * count_z
     blocks = jnp.pad(table, ((0, rows - 8 * steps), (0, 0))).reshape(rows // count_z, count_z, points)
-    blocks, ya, yb, za = barrier((blocks, ya, yb, za))
+    blocks, ya = barrier((blocks, ya))
     ya = swap(jnp.concatenate([ya, blocks], axis=0), "gy", 0)
-    blocks = jnp.concatenate([blocks, ya[4:]], axis=0)
-    blocks, yb, zb, faces = barrier((blocks, yb, zb, list(faces)))
+    blocks = jnp.concatenate([blocks, ya[1:]], axis=0)
+    blocks, yb, za = barrier((blocks, yb, za))
     yb = from_distance(jnp.concatenate([yb, blocks], axis=0), "gy", 3)
     x_faces = [swap(face, "gx", first) for first, face in enumerate(faces[4:])]
-    blocks = jnp.concatenate([blocks, yb[4:]], axis=0)[None]
+    blocks = jnp.concatenate([blocks, yb[1:]], axis=0)[None]
+    blocks, zb = barrier((blocks, zb))
     table = gather_relative(blocks, "gx").reshape(size_x * size_y, rows, points)
     halos = [za, zb, ya, yb] + x_faces
 
@@ -408,7 +411,7 @@
             scratch_shapes=scratch
             + [pltpu.VMEM((3,) + shape, jnp.float32), pltpu.VMEM((8, lanes), jnp.float32)]
             + [pltpu.VMEM((4, count_y // 128, count_x, 128), jnp.float32)] * 2
-            + [pltpu.VMEM((4, count_z, 128), jnp.float32)] * 2
+            + [pltpu.VMEM((count_z, 128), jnp.float32)] * 2
             + [pltpu.VMEM((4, count_z, count_y), jnp.float32)] * 2,
             compiler_params=params,
             name="step",
@@ -432,10 +435,10 @@
         count = blocks.shape[0]
         ya_in = swap(jnp.concatenate([ya, blocks], axis=0), "gy", 0)
         x_faces = [swap(face, "gx", first) for first, face in enumerate(faces[4:])]
-        pieces = jnp.concatenate([blocks, ya_in[4:]], axis=0)
+        pieces = jnp.concatenate([blocks, ya_in[1:]], axis=0)
         pieces, yb, x_faces = barrier((pieces, yb, x_faces))
         yb_in = from_distance(jnp.concatenate([yb, pieces], axis=0), "gy", 3)
-        pieces = jnp.concatenate([pieces, yb_in[4:]], axis=0).reshape(size_y, count, count_z, 128)
+        pieces = jnp.concatenate([pieces, yb_in[1:]], axis=0).reshape(size_y, count, count_z, 128)
         halos = [za_in, zb_in, ya_in, yb_in] + x_faces
 
     distance = 2

time: 75.4 us -> 73.3 us (0.972)
  starting transfers between devices: 31.6 us -> 30.4 us
  waiting for transfers between devices: 21.8 us -> 20.7 us
    ppermute x13, waiting for transfers between devices: 12.7 us -> 10.4 us  [swap(): return lax.ppermute(value, axis, pairs)]
    ppermute x7, starting transfers between devices: 13.1 us -> 11.8 us  [from_distance(): return lax.ppermute(value, axis, [(i, i ^ distance) for i in range(count)])]
    ppermute x7, waiting for transfers between devices: 9.08 us -> 10.3 us  [from_distance(): return lax.ppermute(value, axis, [(i, i ^ distance) for i in range(count)])]
where the time goes in v3:
time: 73.3 us; the launch traced here: 73 us
  starting transfers between devices  30.4 us (41%)
  waiting for transfers between devices  20.7 us (28%)
  Pallas kernels  17.6 us (24%)
  local copies, waits for them, and re-layouts  3.06 us (4%)
  between operations  0.92 us (1%)
    ppermute x13, starting transfers between devices, swap(): return lax.ppermute(value, axis, pairs)  18.6 us
    pallas_call x3, Pallas kernels, shards(): pl.pallas_call(functools.partial(step_body, shape=shape, points=points, c...  16.9 us
    ppermute x7, starting transfers between devices, from_distance(): return lax.ppermute(value, axis, [(i, i ^ distance) for i in range(count)])  11.8 us
    ppermute x13, waiting for transfers between devices, swap(): return lax.ppermute(value, axis, pairs)  10.4 us
    ppermute x7, waiting for transfers between devices, from_distance(): return lax.ppermute(value, axis, [(i, i ^ distance) for i in range(count)])  10.3 us
    unnamed x10, local copies, waits for them, and re-layouts  2.33 us
  transfers between devices with their start and end apart: 20, of which 11 were waited for; matrix products, arithmetic and copies ran while one was open for 0% of the time, Pallas kernels for 8%

profile of v3, /device:TPU:0, one launch (start us, length us, event | category | flops | bytes accessed | tf_op | source)
XLA Modules:
  0.0 73.0 jit_solution(6116047732610236209)
XLA Ops:
  0.6 0.7 copy_bitcast_fusion
  1.4 3.1 %collective-permute-start = (f32[1,24,32]{2,1,0:T(8,128)S(1)}, f32[1,24,32]{2,1,0:T(8,128)S(1)}, u32[]{:S(2)}, u32[]{:S(2)}) collective-permute-start(f32[1,24,32]{2,1,0:T(8,128)S(1)} %fusion.6), channel_id=1, source_target_pairs={{0,1},{1,0},{2,3},{3,2},{4,5},{5,4},{6,7},{7,6},{8,9},{9,8},{10,11... | collective-permute-start | bytes 9224 | tf_op jit(solution)/shard_map/ppermute | solution.py:37
  4.5 1.6 %copy-done = f32[4,32,16,256]{3,2,1,0:T(8,128)S(1)} copy-done((f32[4,32,16,256]{3,2,1,0:T(8,128)S(1)}, f32[4,32,16,256]{3,2,1,0:T(8,128)}, u32[]{:S(2)}) %copy-start) | copy-done | bytes 2097176
  6.0 0.7 faces.1
  6.8 2.7 %collective-permute-start.1 = (f32[2,24,32]{2,1,0:T(8,128)S(1)}, f32[2,24,32]{2,1,0:T(8,128)S(1)}, u32[]{:S(2)}, u32[]{:S(2)}) collective-permute-start(f32[2,24,32]{2,1,0:T(8,128)S(1)} %pad_maximum_fusion.7), channel_id=1, source_target_pairs={{0,2},{1,3},{2,0},{3,1},{4,6},{5,7},{6,4},{7,5},{8,10},{9,11},{10,... | collective-permute-start | bytes 18440 | tf_op jit(solution)/shard_map/ppermute | solution.py:37
  9.5 2.1 %collective-permute-done.1 = f32[2,24,32]{2,1,0:T(8,128)S(1)} collective-permute-done((f32[2,24,32]{2,1,0:T(8,128)S(1)}, f32[2,24,32]{2,1,0:T(8,128)S(1)}, u32[]{:S(2)}, u32[]{:S(2)}) %collective-permute-start.1) | collective-permute-done | bytes 6176 | tf_op jit(solution)/shard_map/ppermute | solution.py:37
  11.8 1.5 %collective-permute-start.2 = (f32[3,16,128]{2,1,0:T(8,128)S(1)}, f32[3,16,128]{2,1,0:T(8,128)S(1)}, u32[]{:S(2)}, u32[]{:S(2)}) collective-permute-start(f32[3,16,128]{2,1,0:T(8,128)S(1)} %pad_maximum_fusion.8), channel_id=1, source_target_pairs={{0,4},{4,0},{8,12},{12,8},{1,5},{5,1},{9,13},{13,9},{2,6},{6,2},{1... | collective-permute-start | bytes 73736 | tf_op jit(solution)/shard_map/ppermute | solution.py:32
  13.3 1.3 %collective-permute-start.3 = (f32[4,32,256]{2,1,0:T(8,128)S(1)}, f32[4,32,256]{2,1,0:T(8,128)S(1)}, u32[]{:S(2)}, u32[]{:S(2)}) collective-permute-start(f32[4,32,256]{2,1,0:T(8,128)S(1)} %get-tuple-element.51), channel_id=1, source_target_pairs={{0,1},{1,0},{2,3},{3,2},{4,5},{5,4},{6,7},{7,6},{8,9},{9,8},{10,11... | collective-permute-start | bytes 393224 | tf_op jit(solution)/shard_map/ppermute | solution.py:32
  14.6 1.1 %collective-permute-done.2.refs_5_ = f32[3,16,128]{2,1,0:T(8,128)S(1)} collective-permute-done((f32[3,16,128]{2,1,0:T(8,128)S(1)}, f32[3,16,128]{2,1,0:T(8,128)S(1)}, u32[]{:S(2)}, u32[]{:S(2)}) %collective-permute-start.2) | collective-permute-done | bytes 24608 | tf_op jit(solution)/shard_map/ppermute | solution.py:32
  15.7 2.6 %collective-permute-done.3.refs_3_ = f32[4,32,256]{2,1,0:T(8,128)S(1)} collective-permute-done((f32[4,32,256]{2,1,0:T(8,128)S(1)}, f32[4,32,256]{2,1,0:T(8,128)S(1)}, u32[]{:S(2)}, u32[]{:S(2)}) %collective-permute-start.3) | collective-permute-done | bytes 131104 | tf_op jit(solution)/shard_map/ppermute | solution.py:32
  18.3 1.5 %collective-permute-start.4 = (f32[5,16,128]{2,1,0:T(8,128)S(1)}, f32[5,16,128]{2,1,0:T(8,128)S(1)}, u32[]{:S(2)}, u32[]{:S(2)}) collective-permute-start(f32[5,16,128]{2,1,0:T(8,128)S(1)} %pad_maximum_fusion.3), channel_id=1, source_target_pairs={{0,12},{4,8},{8,4},{12,0},{1,13},{5,9},{9,5},{13,1},{2,14},{6,10},... | collective-permute-start | bytes 122888 | tf_op jit(solution)/shard_map/ppermute | solution.py:37
  19.8 0.7 collective-permute-start.5
  20.4 2.7 %collective-permute-done.4.refs_6_ = f32[5,16,128]{2,1,0:T(8,128)S(1)} collective-permute-done((f32[5,16,128]{2,1,0:T(8,128)S(1)}, f32[5,16,128]{2,1,0:T(8,128)S(1)}, u32[]{:S(2)}, u32[]{:S(2)}) %collective-permute-start.4) | collective-permute-done | bytes 40992 | tf_op jit(solution)/shard_map/ppermute | solution.py:37
  23.8 0.7 %collective-permute-done.6 = f32[1,8,16,128]{3,2,1,0:T(8,128)S(1)} collective-permute-done((f32[1,8,16,128]{3,2,1,0:T(8,128)S(1)}, f32[1,8,16,128]{3,2,1,0:T(8,128)S(1)}, u32[]{:S(2)}, u32[]{:S(2)}) %collective-permute-start.6) | collective-permute-done | bytes 65568 | tf_op jit(solution)/shard_map/ppermute | solution.py:37
  24.7 6.2 %step.3 = (f32[4,32,16,256]{3,2,1,0:T(8,128)S(1)}, f32[4,32,256]{2,1,0:T(8,128)S(1)}, f32[4,32,256]{2,1,0:T(8,128)S(1)}, f32[1,16,128]{2,1,0:T(8,128)S(1)}, f32[...) custom-call(s32[2]{0:T(128)S(1)} %bitcast.68, f32[8,32,128]{2,1,0:T(8,128)S(1)} %bitcast.65, ...), custom_call_target="tpu_custom_call" | custom-call | tf_op jit(solution)/shard_map/step/pallas_call | solution.py:406
  30.9 4.7 %collective-permute-start.8 = (f32[4,32,256]{2,1,0:T(8,128)S(1)}, f32[4,32,256]{2,1,0:T(8,128)S(1)}, u32[]{:S(2)}, u32[]{:S(2)}) collective-permute-start(f32[4,32,256]{2,1,0:T(8,128)S(1)} %get-tuple-element.60), channel_id=1, source_target_pairs={{0,1},{1,0},{2,3},{3,2},{4,5},{5,4},{6,7},{7,6},{8,9},{9,8},{10,11... | collective-permute-start | bytes 393224 | tf_op jit(solution)/shard_map/ppermute | solution.py:32
  35.6 0.7 collective-permute-start.9
  36.4 1.5 %collective-permute-start.10 = (f32[1,16,128]{2,1,0:T(8,128)S(1)}, f32[1,16,128]{2,1,0:T(8,128)S(1)}, u32[]{:S(2)}, u32[]{:S(2)}) collective-permute-start(f32[1,16,128]{2,1,0:T(8,128)S(1)} %get-tuple-element.62), channel_id=1, source_target_pairs={{0,4},{4,0},{8,12},{12,8},{1,5},{5,1},{9,13},{13,9},{2,6},{6,2},{1... | collective-permute-start | bytes 24584 | tf_op jit(solution)/shard_map/ppermute | solution.py:32
  37.9 0.6 collective-permute-start.11
  38.6 1.5 %collective-permute-done.10.refs_5_ = f32[1,16,128]{2,1,0:T(8,128)S(1)} collective-permute-done((f32[1,16,128]{2,1,0:T(8,128)S(1)}, f32[1,16,128]{2,1,0:T(8,128)S(1)}, u32[]{:S(2)}, u32[]{:S(2)}) %collective-permute-start.10) | collective-permute-done | bytes 8224 | tf_op jit(solution)/shard_map/ppermute | solution.py:32
  40.1 5.7 %step.4 = (f32[4,32,16,256]{3,2,1,0:T(8,128)S(1)}, f32[5,32,256]{2,1,0:T(8,128)S(1)}, f32[4,32,256]{2,1,0:T(8,128)S(1)}, f32[1,16,128]{2,1,0:T(8,128)S(1)}, f32[...) custom-call(s32[2]{0:T(128)S(1)} %bitcast.69, f32[8,32,128]{2,1,0:T(8,128)S(1)} %bitcast.66, ...), custom_call_target="tpu_custom_call" | custom-call | tf_op jit(solution)/shard_map/step/pallas_call | solution.py:406
  45.8 3.2 %collective-permute-start.13 = (f32[5,32,256]{2,1,0:T(8,128)S(1)}, f32[5,32,256]{2,1,0:T(8,128)S(1)}, u32[]{:S(2)}, u32[]{:S(2)}) collective-permute-start(f32[5,32,256]{2,1,0:T(8,128)S(1)} %get-tuple-element.66), channel_id=1, source_target_pairs={{0,1},{1,0},{2,3},{3,2},{4,5},{5,4},{6,7},{7,6},{8,9},{9,8},{10,11... | collective-permute-start | bytes 491528 | tf_op jit(solution)/shard_map/ppermute | solution.py:32
  49.0 0.7 collective-permute-start.14
  49.7 3.2 %collective-permute-done.13.refs_3_ = f32[5,32,256]{2,1,0:T(8,128)S(1)} collective-permute-done((f32[5,32,256]{2,1,0:T(8,128)S(1)}, f32[5,32,256]{2,1,0:T(8,128)S(1)}, u32[]{:S(2)}, u32[]{:S(2)}) %collective-permute-start.13) | collective-permute-done | bytes 163872 | tf_op jit(solution)/shard_map/ppermute | solution.py:32
  53.0 3.1 %collective-permute-start.15 = (f32[3,16,128]{2,1,0:T(8,128)S(1)}, f32[3,16,128]{2,1,0:T(8,128)S(1)}, u32[]{:S(2)}, u32[]{:S(2)}) collective-permute-start(f32[3,16,128]{2,1,0:T(8,128)S(1)} %pad_maximum_fusion.9), channel_id=1, source_target_pairs={{0,4},{4,0},{8,12},{12,8},{1,5},{5,1},{9,13},{13,9},{2,6},{6,2},{1... | collective-permute-start | bytes 73736 | tf_op jit(solution)/shard_map/ppermute | solution.py:32
  56.1 1.8 %collective-permute-done.15.refs_5_ = f32[3,16,128]{2,1,0:T(8,128)S(1)} collective-permute-done((f32[3,16,128]{2,1,0:T(8,128)S(1)}, f32[3,16,128]{2,1,0:T(8,128)S(1)}, u32[]{:S(2)}, u32[]{:S(2)}) %collective-permute-start.15) | collective-permute-done | bytes 24608 | tf_op jit(solution)/shard_map/ppermute | solution.py:32
  57.9 1.5 %collective-permute-start.17 = (f32[5,16,128]{2,1,0:T(8,128)S(1)}, f32[5,16,128]{2,1,0:T(8,128)S(1)}, u32[]{:S(2)}, u32[]{:S(2)}) collective-permute-start(f32[5,16,128]{2,1,0:T(8,128)S(1)} %pad_maximum_fusion.4), channel_id=1, source_target_pairs={{0,12},{4,8},{8,4},{12,0},{1,13},{5,9},{9,5},{13,1},{2,14},{6,10},... | collective-permute-start | bytes 122888 | tf_op jit(solution)/shard_map/ppermute | solution.py:37
  59.4 3.5 %collective-permute-done.17.refs_6_ = f32[5,16,128]{2,1,0:T(8,128)S(1)} collective-permute-done((f32[5,16,128]{2,1,0:T(8,128)S(1)}, f32[5,16,128]{2,1,0:T(8,128)S(1)}, u32[]{:S(2)}, u32[]{:S(2)}) %collective-permute-start.17) | collective-permute-done | bytes 40992 | tf_op jit(solution)/shard_map/ppermute | solution.py:37
  62.9 3.0 %collective-permute-start.18 = (f32[4,2,16,128]{3,2,1,0:T(8,128)S(1)}, f32[4,2,16,128]{3,2,1,0:T(8,128)S(1)}, u32[]{:S(2)}, u32[]{:S(2)}) collective-permute-start(f32[4,2,16,128]{3,2,1,0:T(8,128)S(1)} %bitcast.76), channel_id=1, source_target_pairs={{0,2},{1,3},{2,0},{3,1},{4,6},{5,7},{6,4},{7,5},{8,10},{9,11},{10,... | collective-permute-start | bytes 196616 | tf_op jit(solution)/shard_map/ppermute | solution.py:37
  65.8 5.0 %step.5 = f32[4,32,16,256]{3,2,1,0:T(8,128)} custom-call(s32[2]{0:T(128)S(1)} %bitcast.70, f32[8,32,128]{2,1,0:T(8,128)S(1)} %bitcast.67, f32[4,32,16,256]{3,2,1,0:T(8,128)S(1)} %get-tuple-element.75.refs_2_, f32[5,32,256]{2,1,0:T(8,128)S(1)} %collective-permute-done.13.refs_3_, f32[4,32,256]{2,1,0:T(8,128)S(1)} %collective-permute-done.14.refs_4_, ...), custom_call_target="tpu_custom_call" | custom-call | tf_op jit(solution)/shard_map/step/pallas_call | solution.py:406
  71.0 1.2 %collective-permute-done.19 = f32[1,4,2,16,32]{4,3,2,1,0:T(8,128)S(1)} collective-permute-done((f32[1,4,2,16,32]{4,3,2,1,0:T(8,128)S(1)}, f32[1,4,2,16,32]{4,3,2,1,0:T(8,128)S(1)}, u32[]{:S(2)}, u32[]{:S(2)}) %collective-permute-start.19) | collective-permute-done | bytes 16416 | tf_op jit(solution)/shard_map/ppermute | solution.py:37
  72.4 0.6 add.42
  (56 shorter events, 1.3 us)
Async XLA Ops:
  0.6 24.1 %copy-start.2 = (s32[1,1,1,2]{3,2,1,0:T(1,128)S(1)}, s32[1,1,1,2]{3,2,1,0:T(1,128)}, u32[]{:S(2)}) copy-start(s32[1,1,1,2]{3,2,1,0:T(1,128)} %param.7) | copy-start | bytes 28
  1.4 5.4 %collective-permute-start = (f32[1,24,32]{2,1,0:T(8,128)S(1)}, f32[1,24,32]{2,1,0:T(8,128)S(1)}, u32[]{:S(2)}, u32[]{:S(2)}) collective-permute-start(f32[1,24,32]{2,1,0:T(8,128)S(1)} %fusion.6), channel_id=1, source_target_pairs={{0,1},{1,0},{2,3},{3,2},{4,5},{5,4},{6,7},{7,6},{8,9},{9,8},{10,11... | collective-permute-start | bytes 9224 | tf_op jit(solution)/shard_map/ppermute | solution.py:37
  4.5 1.6 %copy-start = (f32[4,32,16,256]{3,2,1,0:T(8,128)S(1)}, f32[4,32,16,256]{3,2,1,0:T(8,128)}, u32[]{:S(2)}) copy-start(f32[4,32,16,256]{3,2,1,0:T(8,128)} %refs_2_.1) | copy-start | bytes 6291460
  6.0 18.6 %copy-start.1 = (f32[4,32,16,256]{3,2,1,0:T(8,128)S(1)}, f32[4,32,16,256]{3,2,1,0:T(8,128)}, u32[]{:S(2)}) copy-start(f32[4,32,16,256]{3,2,1,0:T(8,128)} %refs_2_.1) | copy-start | bytes 6291460
  6.8 4.8 %collective-permute-start.1 = (f32[2,24,32]{2,1,0:T(8,128)S(1)}, f32[2,24,32]{2,1,0:T(8,128)S(1)}, u32[]{:S(2)}, u32[]{:S(2)}) collective-permute-start(f32[2,24,32]{2,1,0:T(8,128)S(1)} %pad_maximum_fusion.7), channel_id=1, source_target_pairs={{0,2},{1,3},{2,0},{3,1},{4,6},{5,7},{6,4},{7,5},{8,10},{9,11},{10,... | collective-permute-start | bytes 18440 | tf_op jit(solution)/shard_map/ppermute | solution.py:37
  11.8 3.9 %collective-permute-start.2 = (f32[3,16,128]{2,1,0:T(8,128)S(1)}, f32[3,16,128]{2,1,0:T(8,128)S(1)}, u32[]{:S(2)}, u32[]{:S(2)}) collective-permute-start(f32[3,16,128]{2,1,0:T(8,128)S(1)} %pad_maximum_fusion.8), channel_id=1, source_target_pairs={{0,4},{4,0},{8,12},{12,8},{1,5},{5,1},{9,13},{13,9},{2,6},{6,2},{1... | collective-permute-start | bytes 73736 | tf_op jit(solution)/shard_map/ppermute | solution.py:32
  13.3 5.0 %collective-permute-start.3 = (f32[4,32,256]{2,1,0:T(8,128)S(1)}, f32[4,32,256]{2,1,0:T(8,128)S(1)}, u32[]{:S(2)}, u32[]{:S(2)}) collective-permute-start(f32[4,32,256]{2,1,0:T(8,128)S(1)} %get-tuple-element.51), channel_id=1, source_target_pairs={{0,1},{1,0},{2,3},{3,2},{4,5},{5,4},{6,7},{7,6},{8,9},{9,8},{10,11... | collective-permute-start | bytes 393224 | tf_op jit(solution)/shard_map/ppermute | solution.py:32
  18.3 4.9 %collective-permute-start.4 = (f32[5,16,128]{2,1,0:T(8,128)S(1)}, f32[5,16,128]{2,1,0:T(8,128)S(1)}, u32[]{:S(2)}, u32[]{:S(2)}) collective-permute-start(f32[5,16,128]{2,1,0:T(8,128)S(1)} %pad_maximum_fusion.3), channel_id=1, source_target_pairs={{0,12},{4,8},{8,4},{12,0},{1,13},{5,9},{9,5},{13,1},{2,14},{6,10},... | collective-permute-start | bytes 122888 | tf_op jit(solution)/shard_map/ppermute | solution.py:37
  19.8 3.4 %collective-permute-start.5 = (f32[4,32,256]{2,1,0:T(8,128)S(1)}, f32[4,32,256]{2,1,0:T(8,128)S(1)}, u32[]{:S(2)}, u32[]{:S(2)}) collective-permute-start(f32[4,32,256]{2,1,0:T(8,128)S(1)} %get-tuple-element.54), channel_id=1, source_target_pairs={{1,2},{2,1},{5,6},{6,5},{9,10},{10,9},{13,14},{14,13},{17,18},{18,... | collective-permute-start | bytes 393224 | tf_op jit(solution)/shard_map/ppermute | solution.py:32
  23.2 1.3 %collective-permute-start.6 = (f32[1,8,16,128]{3,2,1,0:T(8,128)S(1)}, f32[1,8,16,128]{3,2,1,0:T(8,128)S(1)}, u32[]{:S(2)}, u32[]{:S(2)}) collective-permute-start(f32[1,8,16,128]{3,2,1,0:T(8,128)S(1)} %maximum_bitcast_fusion), channel_id=1, source_target_pairs={{0,16},{16,0},{1,17},{17,1},{2,18},{18,2},{3,19},{19,3},{4,20},{20... | collective-permute-start | bytes 196616 | tf_op jit(solution)/shard_map/ppermute | solution.py:37
  23.3 1.4 %collective-permute-start.7 = (f32[4,16,256]{2,1,0:T(8,128)S(1)}, f32[4,16,256]{2,1,0:T(8,128)S(1)}, u32[]{:S(2)}, u32[]{:S(2)}) collective-permute-start(f32[4,16,256]{2,1,0:T(8,128)S(1)} %get-tuple-element.58), channel_id=1, source_target_pairs={{0,16},{16,0},{1,17},{17,1},{2,18},{18,2},{3,19},{19,3},{4,20},{20... | collective-permute-start | bytes 196616 | tf_op jit(solution)/shard_map/ppermute | solution.py:32
  30.9 9.2 %collective-permute-start.8 = (f32[4,32,256]{2,1,0:T(8,128)S(1)}, f32[4,32,256]{2,1,0:T(8,128)S(1)}, u32[]{:S(2)}, u32[]{:S(2)}) collective-permute-start(f32[4,32,256]{2,1,0:T(8,128)S(1)} %get-tuple-element.60), channel_id=1, source_target_pairs={{0,1},{1,0},{2,3},{3,2},{4,5},{5,4},{6,7},{7,6},{8,9},{9,8},{10,11... | collective-permute-start | bytes 393224 | tf_op jit(solution)/shard_map/ppermute | solution.py:32
  35.6 4.5 %collective-permute-start.9 = (f32[4,32,256]{2,1,0:T(8,128)S(1)}, f32[4,32,256]{2,1,0:T(8,128)S(1)}, u32[]{:S(2)}, u32[]{:S(2)}) collective-permute-start(f32[4,32,256]{2,1,0:T(8,128)S(1)} %get-tuple-element.61), channel_id=1, source_target_pairs={{1,2},{2,1},{5,6},{6,5},{9,10},{10,9},{13,14},{14,13},{17,18},{18,... | collective-permute-start | bytes 393224 | tf_op jit(solution)/shard_map/ppermute | solution.py:32
  36.3 3.8 %collective-permute-start.12 = (f32[4,16,256]{2,1,0:T(8,128)S(1)}, f32[4,16,256]{2,1,0:T(8,128)S(1)}, u32[]{:S(2)}, u32[]{:S(2)}) collective-permute-start(f32[4,16,256]{2,1,0:T(8,128)S(1)} %get-tuple-element.64), channel_id=1, source_target_pairs={{0,16},{16,0},{1,17},{17,1},{2,18},{18,2},{3,19},{19,3},{4,20},{20... | collective-permute-start | bytes 196616 | tf_op jit(solution)/shard_map/ppermute | solution.py:32
  36.4 3.7 %collective-permute-start.10 = (f32[1,16,128]{2,1,0:T(8,128)S(1)}, f32[1,16,128]{2,1,0:T(8,128)S(1)}, u32[]{:S(2)}, u32[]{:S(2)}) collective-permute-start(f32[1,16,128]{2,1,0:T(8,128)S(1)} %get-tuple-element.62), channel_id=1, source_target_pairs={{0,4},{4,0},{8,12},{12,8},{1,5},{5,1},{9,13},{13,9},{2,6},{6,2},{1... | collective-permute-start | bytes 24584 | tf_op jit(solution)/shard_map/ppermute | solution.py:32
  37.9 2.2 %collective-permute-start.11 = (f32[1,16,128]{2,1,0:T(8,128)S(1)}, f32[1,16,128]{2,1,0:T(8,128)S(1)}, u32[]{:S(2)}, u32[]{:S(2)}) collective-permute-start(f32[1,16,128]{2,1,0:T(8,128)S(1)} %get-tuple-element.63), channel_id=1, source_target_pairs={{4,8},{8,4},{5,9},{9,5},{6,10},{10,6},{7,11},{11,7},{20,24},{24,20... | collective-permute-start | bytes 24584 | tf_op jit(solution)/shard_map/ppermute | solution.py:32
  45.8 7.1 %collective-permute-start.13 = (f32[5,32,256]{2,1,0:T(8,128)S(1)}, f32[5,32,256]{2,1,0:T(8,128)S(1)}, u32[]{:S(2)}, u32[]{:S(2)}) collective-permute-start(f32[5,32,256]{2,1,0:T(8,128)S(1)} %get-tuple-element.66), channel_id=1, source_target_pairs={{0,1},{1,0},{2,3},{3,2},{4,5},{5,4},{6,7},{7,6},{8,9},{9,8},{10,11... | collective-permute-start | bytes 491528 | tf_op jit(solution)/shard_map/ppermute | solution.py:32
  49.0 3.9 %collective-permute-start.14 = (f32[4,32,256]{2,1,0:T(8,128)S(1)}, f32[4,32,256]{2,1,0:T(8,128)S(1)}, u32[]{:S(2)}, u32[]{:S(2)}) collective-permute-start(f32[4,32,256]{2,1,0:T(8,128)S(1)} %get-tuple-element.68), channel_id=1, source_target_pairs={{1,2},{2,1},{5,6},{6,5},{9,10},{10,9},{13,14},{14,13},{17,18},{18,... | collective-permute-start | bytes 393224 | tf_op jit(solution)/shard_map/ppermute | solution.py:32
  53.0 4.9 %collective-permute-start.15 = (f32[3,16,128]{2,1,0:T(8,128)S(1)}, f32[3,16,128]{2,1,0:T(8,128)S(1)}, u32[]{:S(2)}, u32[]{:S(2)}) collective-permute-start(f32[3,16,128]{2,1,0:T(8,128)S(1)} %pad_maximum_fusion.9), channel_id=1, source_target_pairs={{0,4},{4,0},{8,12},{12,8},{1,5},{5,1},{9,13},{13,9},{2,6},{6,2},{1... | collective-permute-start | bytes 73736 | tf_op jit(solution)/shard_map/ppermute | solution.py:32
  56.1 1.8 %collective-permute-start.16 = (f32[4,16,256]{2,1,0:T(8,128)S(1)}, f32[4,16,256]{2,1,0:T(8,128)S(1)}, u32[]{:S(2)}, u32[]{:S(2)}) collective-permute-start(f32[4,16,256]{2,1,0:T(8,128)S(1)} %get-tuple-element.72), channel_id=1, source_target_pairs={{0,16},{16,0},{1,17},{17,1},{2,18},{18,2},{3,19},{19,3},{4,20},{20... | collective-permute-start | bytes 196616 | tf_op jit(solution)/shard_map/ppermute | solution.py:32
  57.9 5.0 %collective-permute-start.17 = (f32[5,16,128]{2,1,0:T(8,128)S(1)}, f32[5,16,128]{2,1,0:T(8,128)S(1)}, u32[]{:S(2)}, u32[]{:S(2)}) collective-permute-start(f32[5,16,128]{2,1,0:T(8,128)S(1)} %pad_maximum_fusion.4), channel_id=1, source_target_pairs={{0,12},{4,8},{8,4},{12,0},{1,13},{5,9},{9,5},{13,1},{2,14},{6,10},... | collective-permute-start | bytes 122888 | tf_op jit(solution)/shard_map/ppermute | solution.py:37
  62.9 8.0 %collective-permute-start.18 = (f32[4,2,16,128]{3,2,1,0:T(8,128)S(1)}, f32[4,2,16,128]{3,2,1,0:T(8,128)S(1)}, u32[]{:S(2)}, u32[]{:S(2)}) collective-permute-start(f32[4,2,16,128]{3,2,1,0:T(8,128)S(1)} %bitcast.76), channel_id=1, source_target_pairs={{0,2},{1,3},{2,0},{3,1},{4,6},{5,7},{6,4},{7,5},{8,10},{9,11},{10,... | collective-permute-start | bytes 196616 | tf_op jit(solution)/shard_map/ppermute | solution.py:37
  71.0 1.3 %collective-permute-start.19 = (f32[1,4,2,16,32]{4,3,2,1,0:T(8,128)S(1)}, f32[1,4,2,16,32]{4,3,2,1,0:T(8,128)S(1)}, u32[]{:S(2)}, u32[]{:S(2)}) collective-permute-start(f32[1,4,2,16,32]{4,3,2,1,0:T(8,128)S(1)} %dynamic-slice_bitcast_fusion), channel_id=1, source_target_pairs={{0,16},{16,0},{1,17},{17,1},{2,18},{18,2},{3,19},{19,3},{4,20},{20... | collective-permute-start | bytes 49160 | tf_op jit(solution)/shard_map/ppermute | solution.py:37

commit v4 on v3

--- a/solution.py
+++ b/solution.py
@@ -76,8 +76,8 @@
             last = q_ref[comp, x, :, count_y - 128 :]
             low = jnp.where(lane == place, pltpu.roll(first, place, 1), low)
             high = jnp.where(lane == place, pltpu.roll(last, (place + 1) % 128, 1), high)
-    ya_ref[0] = pick(even_y, high, low)
-    yb_ref[0] = pick(even_y, low, high)
+    ya_ref[...] = pick(even_y, high, low)
+    yb_ref[...] = pick(even_y, low, high)
 
 
 def faces_body(q_ref, *face_refs, shape):
@@ -181,54 +181,60 @@
     return sums
 
 
+def push_body(list_ref, table_ref, force_ref, rows_ref, *, shape, points, capacity, step):
+    slots = sorted_slots(list_ref, capacity)
+    listed = slots[0] < lax.axis_size("gx") * lax.axis_size("gy")
+
+    @pl.when(listed)
+    def _():
+        rows = turbine_rows(rows_ref, table_ref, slots, step, points)
+        push(force_ref, rows, *point_factors(rows, shape), shape)
+
+    @pl.when(jnp.logical_not(listed))
+    def _():
+        force_ref[...] = jnp.zeros(force_ref.shape, jnp.float32)
+
+
+def sample_body(list_ref, table_ref, q_ref, sample_ref, rows_ref, *, shape, points, capacity, step):
+    slots = sorted_slots(list_ref, capacity)
+    listed = slots[0] < lax.axis_size("gx") * lax.axis_size("gy")
+    sample_ref[...] = jnp.zeros(sample_ref.shape, jnp.float32)
+
+    @pl.when(listed)
+    def _():
+        rows = turbine_rows(rows_ref, table_ref, slots, step, points)
+        for comp, value in enumerate(sample(q_ref, *point_factors(rows, shape), shape)):
+            sample_ref[comp : comp + 1] = value
+
+
 def step_body(*refs, shape, points, capacity, step, steps):
     count_x, count_z, count_y = shape
     last, packs = step == steps - 1, step == steps - 2
     faces = len(face_shapes(shape))
     refs = list(refs)
-    list_ref, table_ref, q_ref = refs[:3]
-    za_ref, zb_ref, ya_ref, yb_ref = refs[3:7]
-    x_refs, refs = refs[7 : 3 + faces], refs[3 + faces :]
-    past_ref = None if step == 0 or last else refs.pop(0)
+    list_ref, table_ref, force_ref, q_ref = refs[:4]
+    za_ref, zb_ref, ya_ref, yb_ref = refs[4:8]
+    x_refs, refs = refs[8 : 4 + faces], refs[4 + faces :]
+    if packs:
+        past_refs, refs = refs[: steps - 1], refs[steps - 1 :]
     out_ref = refs.pop(0)
-    sample_ref = None
-    if not last:
+    if last:
+        far_ref, out_ref, sems = out_ref, refs.pop(0), refs.pop(0)
+    else:
         face_refs, refs = refs[:faces], refs[faces:]
-        sample_ref = refs.pop(0)
-    else:
-        far_ref, out_ref, sems = out_ref, refs.pop(0), refs.pop(0)
-    force_ref, rows_ref, low_z_ref, high_z_ref, low_y_ref, high_y_ref, low_x_ref, high_x_ref = refs
-    slots = sorted_slots(list_ref, capacity)
-    turbines = lax.axis_size("gx") * lax.axis_size("gy")
-    listed = slots[0] < turbines
-
-    if not last:
-        sample_ref[...] = jnp.zeros(sample_ref.shape, jnp.float32)
-        if past_ref is not None:
-            sample_ref[: 3 * step + 3] = past_ref[: 3 * step + 3]
-
-    @pl.when(listed)
-    def _():
-        rows = turbine_rows(rows_ref, table_ref, slots, step, points)
-        weights, factor_y = point_factors(rows, shape)
-        push(force_ref, rows, weights, factor_y, shape)
-        if step == 0:
-            for comp, value in enumerate(sample(q_ref, weights, factor_y, shape)):
-                sample_ref[comp : comp + 1] = value
-
-    @pl.when(jnp.logical_not(listed))
-    def _():
-        force_ref[...] = jnp.zeros(force_ref.shape, jnp.float32)
+    if packs:
+        pack_ref, rows_ref, sample_ref = refs.pop(0), refs.pop(0), refs.pop(0)
+    low_z_ref, high_z_ref, low_y_ref, high_y_ref, low_x_ref, high_x_ref = refs
 
     even_x, even_z, even_y = is_even("gx"), is_even("gz"), is_even("gy")
     index_y = lax.axis_index("gy")
     tiles = count_y // 128
     for tile in range(tiles):
-        first, second = (ref[:4, :, tile * 128 : tile * 128 + 128] for ref in (za_ref, zb_ref))
+        first, second = (ref[:, :, tile * 128 : tile * 128 + 128] for ref in (za_ref, zb_ref))
         low_z_ref[:, tile] = pick(even_z, second, first)
         high_z_ref[:, tile] = pick(even_z, first, second)
-    low_y_ref[...] = pick(index_y == 0, 0.0, pick(even_y, yb_ref[0], ya_ref[0]))
-    high_y_ref[...] = pick(index_y == lax.axis_size("gy") - 1, 0.0, pick(even_y, ya_ref[0], yb_ref[0]))
+    low_y_ref[...] = pick(index_y == 0, 0.0, pick(even_y, yb_ref[:count_z], ya_ref[:count_z]))
+    high_y_ref[...] = pick(index_y == lax.axis_size("gy") - 1, 0.0, pick(even_y, ya_ref[:count_z], yb_ref[:count_z]))
     first = x_refs[0][...]
     second = x_refs[1][...] if len(x_refs) > 1 else 0.0
     low_x_ref[...] = pick(even_x, second, first)
@@ -292,31 +298,28 @@
             edge.wait()
         return
 
-    za, others = face_refs[0], face_refs[1:]
-    write_faces(out_ref, [za.at[:4]] + list(others), shape)
-
-    @pl.when(listed)
-    def _():
-        rows = turbine_rows(rows_ref, table_ref, slots, step + 1, points)
-        weights, factor_y = point_factors(rows, shape)
-        for comp, value in enumerate(sample(out_ref, weights, factor_y, shape)):
-            sample_ref[3 * step + 3 + comp : 3 * step + 4 + comp] = value
-
-    if packs:
-        count = 3 * steps + 1
-        za[4] = jnp.zeros((count_x, count_y), jnp.float32)
-        for j, slot in enumerate(slots):
-            lane, row = (j % 2) * points, (j // 2) * count
-            values = sample_ref[: count - 1, j * points : (j + 1) * points]
-            za[4, row : row + count - 1, lane : lane + points] = values
-            name = jnp.where(listed, 0.5 * (slot + 1).astype(jnp.float32), 0.0)
-            za[4, row + count - 1 : row + count, lane : lane + points] = jnp.full((1, points), name)
-
-
-def face_shapes(shape, extra=0):
-    count_x, count_z, count_y = shape
-    forms = [(4 + extra, count_x, count_y), (4, count_x, count_y)]
-    forms += [(1, count_z, 128)] * 2 + [(4, count_z, count_y)] * (1 if lax.axis_size("gx") == 2 else 2)
+    write_faces(out_ref, face_refs, shape)
+    if not packs:
+        return
+
+    slots = sorted_slots(list_ref, capacity)
+    listed = slots[0] < lax.axis_size("gx") * lax.axis_size("gy")
+    sample_body(
+        list_ref, table_ref, out_ref, sample_ref, rows_ref, shape=shape, points=points, capacity=capacity, step=step + 1
+    )
+    pack_ref[...] = jnp.zeros(pack_ref.shape, jnp.float32)
+    for j, slot in enumerate(slots):
+        here, row = slice(j * points, (j + 1) * points), j * (3 * steps + 1)
+        for number, ref in enumerate(list(past_refs) + [sample_ref]):
+            pack_ref[row + 3 * number : row + 3 * number + 3] = ref[:3, here]
+        name = jnp.where(listed, 0.5 * (slot + 1).astype(jnp.float32), 0.0)
+        pack_ref[row + 3 * steps : row + 3 * steps + 1] = jnp.full((1, points), name)
+
+
+def face_shapes(shape):
+    count_x, count_z, count_y = shape
+    forms = [(4, count_x, count_y)] * 2
+    forms += [(count_z, 128)] * 2 + [(4, count_z, count_y)] * (1 if lax.axis_size("gx") == 2 else 2)
     return [jax.ShapeDtypeStruct(form, jnp.float32) for form in forms]
 
 
@@ -354,7 +357,8 @@
     forms = face_shapes(shape)
 
     own = jnp.concatenate([positions.reshape(steps, 3, part), loads.reshape(steps, 3, part)], axis=1)
-    table = jnp.pad(own, ((0, 0), (0, 2), (0, 0))).reshape(1, 8 * steps, part)
+    rows = 8 * steps
+    table = jnp.pad(own, ((0, 0), (0, 2), (0, 0))).reshape(1, rows, part)
     table = jnp.concatenate([table, from_distance(table, "gz", 1)], axis=0)
     faces = pl.pallas_call(
         functools.partial(faces_body, shape=shape),
@@ -366,96 +370,110 @@
     )(q)
     table, faces = barrier((table, list(faces)))
     za, zb, ya, yb = faces[:4]
+    za, zb = swap(za, "gz", 0), swap(zb, "gz", 1)
     distance = 2
     while distance < size_z:
         table = jnp.concatenate([table, from_distance(table, "gz", distance)], axis=0)
         distance *= 2
-    za, zb = swap(za, "gz", 0), swap(zb, "gz", 1)
     table = true_order(table, "gz")
     table = jnp.concatenate([table[k] for k in range(size_z)], axis=1)
-    rows = pl.cdiv(8 * steps, 2 * count_z) * 2 * count_z
-    blocks = jnp.pad(table, ((0, rows - 8 * steps), (0, 0))).reshape(rows // count_z, count_z, points)
-    blocks, ya = barrier((blocks, ya))
-    ya = swap(jnp.concatenate([ya, blocks], axis=0), "gy", 0)
-    blocks = jnp.concatenate([blocks, ya[1:]], axis=0)
-    blocks, yb, za = barrier((blocks, yb, za))
-    yb = from_distance(jnp.concatenate([yb, blocks], axis=0), "gy", 3)
+    table, ya, za, zb = barrier((table, ya, za, zb))
+    ya = swap(jnp.concatenate([ya, table], axis=0), "gy", 0)
     x_faces = [swap(face, "gx", first) for first, face in enumerate(faces[4:])]
-    blocks = jnp.concatenate([blocks, yb[1:]], axis=0)[None]
-    blocks, zb = barrier((blocks, zb))
-    table = gather_relative(blocks, "gx").reshape(size_x * size_y, rows, points)
+    table = jnp.concatenate([table, ya[count_z:]], axis=0)
+    table, yb, x_faces = barrier((table, yb, x_faces))
+    yb = from_distance(jnp.concatenate([yb, table], axis=0), "gy", 3)
+    table = jnp.concatenate([table, yb[count_z:]], axis=0)
+    table = gather_relative(table[None], "gx").reshape(size_x * size_y, rows, points)
     halos = [za, zb, ya, yb] + x_faces
 
-    samples = None
+    smem = pl.BlockSpec(memory_space=pltpu.SMEM)
+    row_scratch = pltpu.VMEM((8, lanes), jnp.float32)
+    count = 3 * steps + 1
+    pack_rows = pl.cdiv(capacity * count, 8) * 8
+    forces = [
+        pl.pallas_call(
+            functools.partial(push_body, shape=shape, points=points, capacity=capacity, step=step),
+            out_shape=jax.ShapeDtypeStruct((3,) + shape, jnp.float32),
+            in_specs=[smem] + vmem_specs(1),
+            out_specs=vmem_specs(1)[0],
+            scratch_shapes=[row_scratch],
+            compiler_params=params,
+            name="push",
+        )(turbines, table)
+        for step in range(steps)
+    ]
+    past = []
     for step in range(steps):
         last, packs = step == steps - 1, step == steps - 2
+        fixed = dict(shape=shape, points=points, capacity=capacity, step=step)
+        if not last:
+            past.append(
+                pl.pallas_call(
+                    functools.partial(sample_body, **fixed),
+                    out_shape=jax.ShapeDtypeStruct((8, lanes), jnp.float32),
+                    in_specs=[smem] + vmem_specs(2),
+                    out_specs=vmem_specs(1)[0],
+                    scratch_shapes=[row_scratch],
+                    compiler_params=params,
+                    name="sample",
+                )(turbines, table, q)
+            )
         shapes = [jax.ShapeDtypeStruct(q.shape, jnp.float32)]
-        out_specs = vmem_specs(1)
         scratch = []
         if last:
             out_specs = [pl.BlockSpec(memory_space=pl.ANY)]
             scratch = [pltpu.VMEM(q.shape, jnp.float32), pltpu.SemaphoreType.DMA((count_x,))]
         else:
-            shapes += face_shapes(shape, 1 if packs else 0)
+            shapes += forms
             if packs:
-                scratch = [pltpu.VMEM((16, lanes), jnp.float32)]
-            else:
-                shapes += [jax.ShapeDtypeStruct((16, lanes), jnp.float32)]
+                shapes += [jax.ShapeDtypeStruct((pack_rows, points), jnp.float32)]
+                scratch = [row_scratch, row_scratch]
             out_specs = vmem_specs(len(shapes))
-        past = [] if step == 0 or last else [samples]
+        inputs = [turbines, table, forces[step], q] + halos + (past if packs else [])
         results = pl.pallas_call(
-            functools.partial(step_body, shape=shape, points=points, capacity=capacity, step=step, steps=steps),
+            functools.partial(step_body, steps=steps, **fixed),
             out_shape=shapes,
-            in_specs=[pl.BlockSpec(memory_space=pltpu.SMEM)] + vmem_specs(2 + len(halos) + len(past)),
+            in_specs=[smem] + vmem_specs(len(inputs) - 1),
             out_specs=out_specs,
             scratch_shapes=scratch
-            + [pltpu.VMEM((3,) + shape, jnp.float32), pltpu.VMEM((8, lanes), jnp.float32)]
             + [pltpu.VMEM((4, count_y // 128, count_x, 128), jnp.float32)] * 2
             + [pltpu.VMEM((count_z, 128), jnp.float32)] * 2
             + [pltpu.VMEM((4, count_z, count_y), jnp.float32)] * 2,
             compiler_params=params,
             name="step",
-        )(turbines, table, q, *halos, *past)
+        )(*inputs)
         q = results[0]
         if last:
             break
         faces = results[1 : 1 + len(forms)]
         if not packs:
-            samples = results[-1]
             halos = swap_faces(faces)
             continue
         za, zb, ya, yb = faces[:4]
-        za_in, zb_in = swap(za, "gz", 0), swap(zb, "gz", 1)
-        sums = za[4] + za_in[4]
-        row_blocks = pl.cdiv((3 * steps + 1) * pl.cdiv(capacity, 2), count_z)
-        blocks = jnp.stack(
-            [sums[b * count_z : (b + 1) * count_z, h * 128 : h * 128 + 128] for b in range(row_blocks) for h in range(2)]
-        )
-        blocks, ya, zb_in = barrier((blocks, ya, zb_in))
-        count = blocks.shape[0]
-        ya_in = swap(jnp.concatenate([ya, blocks], axis=0), "gy", 0)
+        pieces = results[-1]
+        za, zb = swap(za, "gz", 0), swap(zb, "gz", 1)
+        ya = swap(jnp.concatenate([ya, pieces], axis=0), "gy", 0)
         x_faces = [swap(face, "gx", first) for first, face in enumerate(faces[4:])]
-        pieces = jnp.concatenate([blocks, ya_in[1:]], axis=0)
-        pieces, yb, x_faces = barrier((pieces, yb, x_faces))
-        yb_in = from_distance(jnp.concatenate([yb, pieces], axis=0), "gy", 3)
-        pieces = jnp.concatenate([pieces, yb_in[1:]], axis=0).reshape(size_y, count, count_z, 128)
-        halos = [za_in, zb_in, ya_in, yb_in] + x_faces
-
-    distance = 2
-    while distance < size_z:
-        pieces = pieces + from_distance(pieces, "gz", distance)
-        distance *= 2
+        pieces = jnp.concatenate([pieces, ya[count_z:]], axis=0)
+        pieces, yb, za, zb, x_faces = barrier((pieces, yb, za, zb, x_faces))
+        yb = from_distance(jnp.concatenate([yb, pieces], axis=0), "gy", 3)
+        pieces = jnp.concatenate([pieces, yb[count_z:]], axis=0)
+        halos = [za, zb, ya, yb] + x_faces
+        pieces, forces[-1] = barrier((pieces, forces[-1]))
+        distance = 1
+        while distance < size_z:
+            pieces = pieces + from_distance(pieces, "gz", distance)
+            distance *= 2
+
     pieces, q = barrier((pieces, q))
-    mine = lax.dynamic_slice_in_dim(pieces, lax.axis_index("gz") * part, part, axis=3)[None]
-    mine = gather_relative(mine, "gx")
-    mine = mine.reshape(size_x * size_y, row_blocks, 2, count_z, part).transpose(0, 2, 1, 3, 4)
-    mine = mine.reshape(size_x * size_y, 2, row_blocks * count_z, part)
+    mine = lax.dynamic_slice_in_dim(pieces, lax.axis_index("gz") * part, part, axis=1)[None]
+    mine = gather_relative(mine, "gx").reshape(size_x * size_y, pack_rows, part)
     holder = (lax.axis_index("gx") * size_y + lax.axis_index("gy") + 1).astype(jnp.float32)
     returned = 0.0
     for j in range(capacity):
-        row = (j // 2) * (3 * steps + 1)
-        values = mine[:, j % 2, row : row + 3 * steps]
-        match = mine[:, j % 2, row + 3 * steps :][:, :1] == holder
+        values = mine[:, j * count : j * count + 3 * steps]
+        match = mine[:, (j + 1) * count - 1 : (j + 1) * count, :1] == holder
         returned = returned + jnp.sum(jnp.where(match, values, 0.0), axis=0)
     return q, returned.reshape(positions.shape)
 

time: 73.3 us -> 80 us (1.091)
  Pallas kernels: 17.6 us -> 23.1 us
  local copies, waits for them, and re-layouts: 3.06 us -> 6.23 us
  waiting for transfers between devices: 20.7 us -> 18.3 us
    pallas_call x3 -> x8, Pallas kernels: 16.9 us -> 22.3 us  [the longest x3 15.3 us: shards(): pl.pallas_call(functools.partial(step_body, steps=steps, **fixed), out_sh...]
    unnamed x10 -> x14, local copies, waits for them, and re-layouts: 2.33 us -> 5.23 us
    ppermute x13, waiting for transfers between devices: 10.4 us -> 7.74 us  [swap(): return lax.ppermute(value, axis, pairs)]
    ppermute x7 -> x8, starting transfers between devices: 11.8 us -> 13.8 us  [from_distance(): return lax.ppermute(value, axis, [(i, i ^ distance) for i in range(count)])]
    ppermute x13, starting transfers between devices: 18.6 us -> 16.7 us  [swap(): return lax.ppermute(value, axis, pairs)]
    ppermute x7 -> x8, waiting for transfers between devices: 10.3 us -> 10.5 us  [from_distance(): return lax.ppermute(value, axis, [(i, i ^ distance) for i in range(count)])]
  transfers between devices with their start and end apart: 20 -> 21, of which waited for: 11 -> 10; matrix products, arithmetic and copies ran while one was open for 0% -> 0% of each run, Pallas kernels for 8% -> 13%
where the time goes in v4:
time: 80 us; the launch traced here: 79.6 us
  starting transfers between devices  30.5 us (38%)
  Pallas kernels  23.1 us (29%)
  waiting for transfers between devices  18.3 us (23%)
  local copies, waits for them, and re-layouts  6.23 us (8%)
  between operations  1.02 us (1%)
    ppermute x13, starting transfers between devices, swap(): return lax.ppermute(value, axis, pairs)  16.7 us
    pallas_call x3, Pallas kernels, shards(): pl.pallas_call(functools.partial(step_body, steps=steps, **fixed), out_sh...  15.3 us
    ppermute x8, starting transfers between devices, from_distance(): return lax.ppermute(value, axis, [(i, i ^ distance) for i in range(count)])  13.8 us
    ppermute x8, waiting for transfers between devices, from_distance(): return lax.ppermute(value, axis, [(i, i ^ distance) for i in range(count)])  10.5 us
    ppermute x13, waiting for transfers between devices, swap(): return lax.ppermute(value, axis, pairs)  7.74 us
    unnamed x14, local copies, waits for them, and re-layouts  5.23 us
    pallas_call x3, Pallas kernels, shards(): pl.pallas_call(functools.partial(push_body, shape=shape, points=points, c...  4.24 us
    pallas_call x2, Pallas kernels, shards(): pl.pallas_call(functools.partial(sample_body, **fixed), out_shape=jax.Sha...  2.8 us
  transfers between devices with their start and end apart: 21, of which 10 were waited for; matrix products, arithmetic and copies ran while one was open for 0% of the time, Pallas kernels for 13%

profile of v4, /device:TPU:0, one launch (start us, length us, event | category | flops | bytes accessed | tf_op | source)
XLA Modules:
  0.0 79.6 jit_solution(508793138833152263)
XLA Ops:
  1.4 3.1 %collective-permute-start = (f32[1,24,32]{2,1,0:T(8,128)S(1)}, f32[1,24,32]{2,1,0:T(8,128)S(1)}, u32[]{:S(2)}, u32[]{:S(2)}) collective-permute-start(f32[1,24,32]{2,1,0:T(8,128)S(1)} %fusion.3), channel_id=1, source_target_pairs={{0,1},{1,0},{2,3},{3,2},{4,5},{5,4},{6,7},{7,6},{8,9},{9,8},{10,11... | collective-permute-start | bytes 9224 | tf_op jit(solution)/shard_map/ppermute | solution.py:37
  4.5 1.6 %copy-done = f32[4,32,16,256]{3,2,1,0:T(8,128)S(1)} copy-done((f32[4,32,16,256]{3,2,1,0:T(8,128)S(1)}, f32[4,32,16,256]{3,2,1,0:T(8,128)}, u32[]{:S(2)}) %copy-start) | copy-done | bytes 2097176
  6.0 0.7 faces.1
  6.8 2.7 %collective-permute-start.1 = (f32[2,24,32]{2,1,0:T(8,128)S(1)}, f32[2,24,32]{2,1,0:T(8,128)S(1)}, u32[]{:S(2)}, u32[]{:S(2)}) collective-permute-start(f32[2,24,32]{2,1,0:T(8,128)S(1)} %pad_maximum_fusion.5), channel_id=1, source_target_pairs={{0,2},{1,3},{2,0},{3,1},{4,6},{5,7},{6,4},{7,5},{8,10},{9,11},{10,... | collective-permute-start | bytes 18440 | tf_op jit(solution)/shard_map/ppermute | solution.py:37
  9.5 1.3 %collective-permute-start.2 = (f32[4,32,256]{2,1,0:T(8,128)S(1)}, f32[4,32,256]{2,1,0:T(8,128)S(1)}, u32[]{:S(2)}, u32[]{:S(2)}) collective-permute-start(f32[4,32,256]{2,1,0:T(8,128)S(1)} %get-tuple-element.49), channel_id=1, source_target_pairs={{0,1},{1,0},{2,3},{3,2},{4,5},{5,4},{6,7},{7,6},{8,9},{9,8},{10,11... | collective-permute-start | bytes 393224 | tf_op jit(solution)/shard_map/ppermute | solution.py:32
  11.9 2.6 %collective-permute-done.2.refs_4_ = f32[4,32,256]{2,1,0:T(8,128)S(1)} collective-permute-done((f32[4,32,256]{2,1,0:T(8,128)S(1)}, f32[4,32,256]{2,1,0:T(8,128)S(1)}, u32[]{:S(2)}, u32[]{:S(2)}) %collective-permute-start.2) | collective-permute-done | bytes 131104 | tf_op jit(solution)/shard_map/ppermute | solution.py:32
  14.4 1.5 %collective-permute-start.4 = (f32[40,128]{1,0:T(8,128)S(1)}, f32[40,128]{1,0:T(8,128)S(1)}, u32[]{:S(2)}, u32[]{:S(2)}) collective-permute-start(f32[40,128]{1,0:T(8,128)S(1)} %pad_maximum_fusion.8), channel_id=1, source_target_pairs={{0,4},{4,0},{8,12},{12,8},{1,5},{5,1},{9,13},{13,9},{2,6},{6,2},{1... | collective-permute-start | bytes 61448 | tf_op jit(solution)/shard_map/ppermute | solution.py:32
  15.9 2.3 %collective-permute-done.4.refs_6_ = f32[40,128]{1,0:T(8,128)S(1)} collective-permute-done((f32[40,128]{1,0:T(8,128)S(1)}, f32[40,128]{1,0:T(8,128)S(1)}, u32[]{:S(2)}, u32[]{:S(2)}) %collective-permute-start.4) | collective-permute-done | bytes 20512 | tf_op jit(solution)/shard_map/ppermute | solution.py:32
  18.2 2.5 %collective-permute-start.6 = (f32[64,128]{1,0:T(8,128)S(1)}, f32[64,128]{1,0:T(8,128)S(1)}, u32[]{:S(2)}, u32[]{:S(2)}) collective-permute-start(f32[64,128]{1,0:T(8,128)S(1)} %pad_maximum_fusion.2), channel_id=1, source_target_pairs={{0,12},{4,8},{8,4},{12,0},{1,13},{5,9},{9,5},{13,1},{2,14},{6,10},... | collective-permute-start | bytes 98312 | tf_op jit(solution)/shard_map/ppermute | solution.py:37
  20.8 2.4 %collective-permute-done.6.refs_7_ = f32[64,128]{1,0:T(8,128)S(1)} collective-permute-done((f32[64,128]{1,0:T(8,128)S(1)}, f32[64,128]{1,0:T(8,128)S(1)}, u32[]{:S(2)}, u32[]{:S(2)}) %collective-permute-start.6) | collective-permute-done | bytes 32800 | tf_op jit(solution)/shard_map/ppermute | solution.py:37
  23.2 1.2 %collective-permute-done.7 = f32[1,96,128]{2,1,0:T(8,128)S(1)} collective-permute-done((f32[1,96,128]{2,1,0:T(8,128)S(1)}, f32[1,96,128]{2,1,0:T(8,128)S(1)}, u32[]{:S(2)}, u32[]{:S(2)}) %collective-permute-start.7) | collective-permute-done | bytes 49184 | tf_op jit(solution)/shard_map/ppermute | solution.py:37
  24.5 1.4 %push.4.refs_2_ = f32[3,32,16,256]{3,2,1,0:T(8,128)S(1)} custom-call(s32[2]{0:T(128)S(1)} %bitcast.39, f32[8,24,128]{2,1,0:T(8,128)S(1)} %bitcast.31), custom_call_target="tpu_custom_call" | custom-call | tf_op jit(solution)/shard_map/push/pallas_call | solution.py:395
  25.9 5.1 %step.3 = (f32[4,32,16,256]{3,2,1,0:T(8,128)S(1)}, f32[4,32,256]{2,1,0:T(8,128)S(1)}, f32[4,32,256]{2,1,0:T(8,128)S(1)}, f32[16,128]{1,0:T(8,128)S(1)}, f32[16,1...) custom-call(s32[2]{0:T(128)S(1)} %bitcast.40, f32[8,24,128]{2,1,0:T(8,128)S(1)} %bitcast.32, ...), custom_call_target="tpu_custom_call" | custom-call | tf_op jit(solution)/shard_map/step/pallas_call | solution.py:434
  31.0 4.0 %collective-permute-start.8 = (f32[4,32,256]{2,1,0:T(8,128)S(1)}, f32[4,32,256]{2,1,0:T(8,128)S(1)}, u32[]{:S(2)}, u32[]{:S(2)}) collective-permute-start(f32[4,32,256]{2,1,0:T(8,128)S(1)} %get-tuple-element.61), channel_id=1, source_target_pairs={{0,1},{1,0},{2,3},{3,2},{4,5},{5,4},{6,7},{7,6},{8,9},{9,8},{10,11... | collective-permute-start | bytes 393224 | tf_op jit(solution)/shard_map/ppermute | solution.py:32
  35.7 1.6 %collective-permute-start.10 = (f32[16,128]{1,0:T(8,128)S(1)}, f32[16,128]{1,0:T(8,128)S(1)}, u32[]{:S(2)}, u32[]{:S(2)}) collective-permute-start(f32[16,128]{1,0:T(8,128)S(1)} %get-tuple-element.63), channel_id=1, source_target_pairs={{0,4},{4,0},{8,12},{12,8},{1,5},{5,1},{9,13},{13,9},{2,6},{6,2},{1... | collective-permute-start | bytes 24584 | tf_op jit(solution)/shard_map/ppermute | solution.py:32
  37.9 1.4 %push.3.refs_2_ = f32[3,32,16,256]{3,2,1,0:T(8,128)S(1)} custom-call(s32[2]{0:T(128)S(1)} %bitcast.41, f32[8,24,128]{2,1,0:T(8,128)S(1)} %bitcast.33), custom_call_target="tpu_custom_call" | custom-call | tf_op jit(solution)/shard_map/push/pallas_call | solution.py:395
  39.4 1.4 %sample.2.refs_9_ = f32[8,256]{1,0:T(8,128)S(1)} custom-call(s32[2]{0:T(128)S(1)} %bitcast.42, f32[8,24,128]{2,1,0:T(8,128)S(1)} %bitcast.34, f32[4,32,16,256]{3,2,1,0:T(8,128)S(1)} %copy-done.1), custom_call_target="tpu_custom_call" | custom-call | tf_op jit(solution)/shard_map/sample/pallas_call | solution.py:412
  40.8 1.4 %sample.3.refs_10_ = f32[8,256]{1,0:T(8,128)S(1)} custom-call(s32[2]{0:T(128)S(1)} %bitcast.43, f32[8,24,128]{2,1,0:T(8,128)S(1)} %bitcast.35, f32[4,32,16,256]{3,2,1,0:T(8,128)S(1)} %get-tuple-element.60.q_ref.refs_3_), custom_call_target="tpu_custom_call" | custom-call | tf_op jit(solution)/shard_map/sample/pallas_call | solution.py:412
  42.2 5.9 %step.4 = (f32[4,32,16,256]{3,2,1,0:T(8,128)S(1)}, f32[4,32,256]{2,1,0:T(8,128)S(1)}, f32[4,32,256]{2,1,0:T(8,128)S(1)}, f32[16,128]{1,0:T(8,128)S(1)}, f32[16,1...) custom-call(s32[2]{0:T(128)S(1)} %bitcast.44, f32[8,24,128]{2,1,0:T(8,128)S(1)} %bitcast.36, ...), custom_call_target="tpu_custom_call" | custom-call | tf_op jit(solution)/shard_map/step/pallas_call | solution.py:434
  48.1 1.3 %copy-done.3 = f32[4,32,16,256]{3,2,1,0:T(8,128)} copy-done((f32[4,32,16,256]{3,2,1,0:T(8,128)}, f32[4,32,16,256]{3,2,1,0:T(8,128)S(1)}, u32[]{:S(2)}) %copy-start.3) | copy-done | bytes 2097176
  49.5 4.2 %collective-permute-start.13 = (f32[40,128]{1,0:T(8,128)S(1)}, f32[40,128]{1,0:T(8,128)S(1)}, u32[]{:S(2)}, u32[]{:S(2)}) collective-permute-start(f32[40,128]{1,0:T(8,128)S(1)} %pad_maximum_fusion.9), channel_id=1, source_target_pairs={{0,4},{4,0},{8,12},{12,8},{1,5},{5,1},{9,13},{13,9},{2,6},{6,2},{1... | collective-permute-start | bytes 61448 | tf_op jit(solution)/shard_map/ppermute | solution.py:32
  53.7 1.4 %collective-permute-start.14 = (f32[4,32,256]{2,1,0:T(8,128)S(1)}, f32[4,32,256]{2,1,0:T(8,128)S(1)}, u32[]{:S(2)}, u32[]{:S(2)}) collective-permute-start(f32[4,32,256]{2,1,0:T(8,128)S(1)} %get-tuple-element.69), channel_id=1, source_target_pairs={{0,1},{1,0},{2,3},{3,2},{4,5},{5,4},{6,7},{7,6},{8,9},{9,8},{10,11... | collective-permute-start | bytes 393224 | tf_op jit(solution)/shard_map/ppermute | solution.py:32
  55.8 1.2 %collective-permute-done.16.refs_8_ = f32[4,16,256]{2,1,0:T(8,128)S(1)} collective-permute-done((f32[4,16,256]{2,1,0:T(8,128)S(1)}, f32[4,16,256]{2,1,0:T(8,128)S(1)}, u32[]{:S(2)}, u32[]{:S(2)}) %collective-permute-start.16) | collective-permute-done | bytes 65568 | tf_op jit(solution)/shard_map/ppermute | solution.py:32
  57.0 1.7 %collective-permute-done.14.refs_4_ = f32[4,32,256]{2,1,0:T(8,128)S(1)} collective-permute-done((f32[4,32,256]{2,1,0:T(8,128)S(1)}, f32[4,32,256]{2,1,0:T(8,128)S(1)}, u32[]{:S(2)}, u32[]{:S(2)}) %collective-permute-start.14) | collective-permute-done | bytes 131104 | tf_op jit(solution)/shard_map/ppermute | solution.py:32
  59.2 1.4 %push.5.refs_2_ = f32[3,32,16,256]{3,2,1,0:T(8,128)S(1)} custom-call(s32[2]{0:T(128)S(1)} %bitcast.45, f32[8,24,128]{2,1,0:T(8,128)S(1)} %bitcast.37), custom_call_target="tpu_custom_call" | custom-call | tf_op jit(solution)/shard_map/push/pallas_call | solution.py:395
  60.6 2.9 %collective-permute-done.17.refs_7_ = f32[64,128]{1,0:T(8,128)S(1)} collective-permute-done((f32[64,128]{1,0:T(8,128)S(1)}, f32[64,128]{1,0:T(8,128)S(1)}, u32[]{:S(2)}, u32[]{:S(2)}) %collective-permute-start.17) | collective-permute-done | bytes 32800 | tf_op jit(solution)/shard_map/ppermute | solution.py:37
  63.5 3.9 %collective-permute-start.18 = (f32[96,128]{1,0:T(8,128)S(1)}, f32[96,128]{1,0:T(8,128)S(1)}, u32[]{:S(2)}, u32[]{:S(2)}) collective-permute-start(f32[96,128]{1,0:T(8,128)S(1)} %pad_maximum_fusion.1), channel_id=1, source_target_pairs={{0,1},{1,0},{2,3},{3,2},{4,5},{5,4},{6,7},{7,6},{8,9},{9,8},{10,11... | collective-permute-start | bytes 147464 | tf_op jit(solution)/shard_map/ppermute | solution.py:37
  67.5 2.6 %collective-permute-done.18 = f32[96,128]{1,0:T(8,128)S(1)} collective-permute-done((f32[96,128]{1,0:T(8,128)S(1)}, f32[96,128]{1,0:T(8,128)S(1)}, u32[]{:S(2)}, u32[]{:S(2)}) %collective-permute-start.18) | collective-permute-done | bytes 49184 | tf_op jit(solution)/shard_map/ppermute | solution.py:37
  70.1 1.0 %collective-permute-start.19 = (f32[96,128]{1,0:T(8,128)S(1)}, f32[96,128]{1,0:T(8,128)S(1)}, u32[]{:S(2)}, u32[]{:S(2)}) collective-permute-start(f32[96,128]{1,0:T(8,128)S(1)} %add.30), channel_id=1, source_target_pairs={{0,2},{1,3},{2,0},{3,1},{4,6},{5,7},{6,4},{7,5},{8,10},{9,11},{10,... | collective-permute-start | bytes 147464 | tf_op jit(solution)/shard_map/ppermute | solution.py:37
  71.1 1.6 %copy-done.4 = f32[4,32,16,256]{3,2,1,0:T(8,128)S(1)} copy-done((f32[4,32,16,256]{3,2,1,0:T(8,128)S(1)}, f32[4,32,16,256]{3,2,1,0:T(8,128)}, u32[]{:S(2)}) %copy-start.4) | copy-done | bytes 2097176
  72.7 4.3 %step.5 = f32[4,32,16,256]{3,2,1,0:T(8,128)} custom-call(s32[2]{0:T(128)S(1)} %bitcast.46, f32[8,24,128]{2,1,0:T(8,128)S(1)} %bitcast.38, f32[3,32,16,256]{3,2,1,0:T(8,128)S(1)} %push.5.refs_2_, f32[4,32,16,256]{3,2,1,0:T(8,128)S(1)} %copy-done.4, f32[4,32,256]{2,1,0:T(8,128)S(1)} %collective-permute-done.14.refs_4_, ...), custom_call_target="tpu_custom_call" | custom-call | tf_op jit(solution)/shard_map/step/pallas_call | solution.py:434
  77.2 1.2 %collective-permute-done.20 = f32[1,96,32]{1,2,0:T(8,128)S(1)} collective-permute-done((f32[1,96,32]{1,2,0:T(8,128)S(1)}, f32[1,96,32]{1,2,0:T(8,128)S(1)}, u32[]{:S(2)}, u32[]{:S(2)}) %collective-permute-start.20) | collective-permute-done | bytes 12320 | tf_op jit(solution)/shard_map/ppermute | solution.py:37
  (67 shorter events, 6.0 us)
Async XLA Ops:
  0.6 23.8 %copy-start.5 = (s32[1,1,1,2]{3,2,1,0:T(1,128)S(1)}, s32[1,1,1,2]{3,2,1,0:T(1,128)}, u32[]{:S(2)}) copy-start(s32[1,1,1,2]{3,2,1,0:T(1,128)} %param.7) | copy-start | bytes 28
  1.4 5.4 %collective-permute-start = (f32[1,24,32]{2,1,0:T(8,128)S(1)}, f32[1,24,32]{2,1,0:T(8,128)S(1)}, u32[]{:S(2)}, u32[]{:S(2)}) collective-permute-start(f32[1,24,32]{2,1,0:T(8,128)S(1)} %fusion.3), channel_id=1, source_target_pairs={{0,1},{1,0},{2,3},{3,2},{4,5},{5,4},{6,7},{7,6},{8,9},{9,8},{10,11... | collective-permute-start | bytes 9224 | tf_op jit(solution)/shard_map/ppermute | solution.py:37
  4.5 1.6 %copy-start = (f32[4,32,16,256]{3,2,1,0:T(8,128)S(1)}, f32[4,32,16,256]{3,2,1,0:T(8,128)}, u32[]{:S(2)}) copy-start(f32[4,32,16,256]{3,2,1,0:T(8,128)} %q_ref.3) | copy-start | bytes 6291460
  6.8 4.9 %collective-permute-start.1 = (f32[2,24,32]{2,1,0:T(8,128)S(1)}, f32[2,24,32]{2,1,0:T(8,128)S(1)}, u32[]{:S(2)}, u32[]{:S(2)}) collective-permute-start(f32[2,24,32]{2,1,0:T(8,128)S(1)} %pad_maximum_fusion.5), channel_id=1, source_target_pairs={{0,2},{1,3},{2,0},{3,1},{4,6},{5,7},{6,4},{7,5},{8,10},{9,11},{10,... | collective-permute-start | bytes 18440 | tf_op jit(solution)/shard_map/ppermute | solution.py:37
  9.5 5.0 %collective-permute-start.2 = (f32[4,32,256]{2,1,0:T(8,128)S(1)}, f32[4,32,256]{2,1,0:T(8,128)S(1)}, u32[]{:S(2)}, u32[]{:S(2)}) collective-permute-start(f32[4,32,256]{2,1,0:T(8,128)S(1)} %get-tuple-element.49), channel_id=1, source_target_pairs={{0,1},{1,0},{2,3},{3,2},{4,5},{5,4},{6,7},{7,6},{8,9},{9,8},{10,11... | collective-permute-start | bytes 393224 | tf_op jit(solution)/shard_map/ppermute | solution.py:32
  10.7 3.7 %collective-permute-start.3 = (f32[4,32,256]{2,1,0:T(8,128)S(1)}, f32[4,32,256]{2,1,0:T(8,128)S(1)}, u32[]{:S(2)}, u32[]{:S(2)}) collective-permute-start(f32[4,32,256]{2,1,0:T(8,128)S(1)} %get-tuple-element.50), channel_id=1, source_target_pairs={{1,2},{2,1},{5,6},{6,5},{9,10},{10,9},{13,14},{14,13},{17,18},{18,... | collective-permute-start | bytes 393224 | tf_op jit(solution)/shard_map/ppermute | solution.py:32
  14.4 3.8 %collective-permute-start.4 = (f32[40,128]{1,0:T(8,128)S(1)}, f32[40,128]{1,0:T(8,128)S(1)}, u32[]{:S(2)}, u32[]{:S(2)}) collective-permute-start(f32[40,128]{1,0:T(8,128)S(1)} %pad_maximum_fusion.8), channel_id=1, source_target_pairs={{0,4},{4,0},{8,12},{12,8},{1,5},{5,1},{9,13},{13,9},{2,6},{6,2},{1... | collective-permute-start | bytes 61448 | tf_op jit(solution)/shard_map/ppermute | solution.py:32
  15.9 2.3 %collective-permute-start.5 = (f32[4,16,256]{2,1,0:T(8,128)S(1)}, f32[4,16,256]{2,1,0:T(8,128)S(1)}, u32[]{:S(2)}, u32[]{:S(2)}) collective-permute-start(f32[4,16,256]{2,1,0:T(8,128)S(1)} %get-tuple-element.54), channel_id=1, source_target_pairs={{0,16},{16,0},{1,17},{17,1},{2,18},{18,2},{3,19},{19,3},{4,20},{20... | collective-permute-start | bytes 196616 | tf_op jit(solution)/shard_map/ppermute | solution.py:32
  18.2 4.9 %collective-permute-start.6 = (f32[64,128]{1,0:T(8,128)S(1)}, f32[64,128]{1,0:T(8,128)S(1)}, u32[]{:S(2)}, u32[]{:S(2)}) collective-permute-start(f32[64,128]{1,0:T(8,128)S(1)} %pad_maximum_fusion.2), channel_id=1, source_target_pairs={{0,12},{4,8},{8,4},{12,0},{1,13},{5,9},{9,5},{13,1},{2,14},{6,10},... | collective-permute-start | bytes 98312 | tf_op jit(solution)/shard_map/ppermute | solution.py:37
  23.1 1.3 %collective-permute-start.7 = (f32[1,96,128]{2,1,0:T(8,128)S(1)}, f32[1,96,128]{2,1,0:T(8,128)S(1)}, u32[]{:S(2)}, u32[]{:S(2)}) collective-permute-start(f32[1,96,128]{2,1,0:T(8,128)S(1)} %maximum_bitcast_fusion), channel_id=1, source_target_pairs={{0,16},{16,0},{1,17},{17,1},{2,18},{18,2},{3,19},{19,3},{4,20},{20... | collective-permute-start | bytes 147464 | tf_op jit(solution)/shard_map/ppermute | solution.py:37
  25.9 13.5 %copy-start.1 = (f32[4,32,16,256]{3,2,1,0:T(8,128)S(1)}, f32[4,32,16,256]{3,2,1,0:T(8,128)}, u32[]{:S(2)}) copy-start(f32[4,32,16,256]{3,2,1,0:T(8,128)} %q_ref.3) | copy-start | bytes 6291460
  31.0 11.2 %copy-start.2 = (f32[4,32,16,256]{3,2,1,0:T(8,128)}, f32[4,32,16,256]{3,2,1,0:T(8,128)S(1)}, u32[]{:S(2)}) copy-start(f32[4,32,16,256]{3,2,1,0:T(8,128)S(1)} %get-tuple-element.60.q_ref.refs_3_) | copy-start | bytes 6291460
  31.0 11.2 %collective-permute-start.8 = (f32[4,32,256]{2,1,0:T(8,128)S(1)}, f32[4,32,256]{2,1,0:T(8,128)S(1)}, u32[]{:S(2)}, u32[]{:S(2)}) collective-permute-start(f32[4,32,256]{2,1,0:T(8,128)S(1)} %get-tuple-element.61), channel_id=1, source_target_pairs={{0,1},{1,0},{2,3},{3,2},{4,5},{5,4},{6,7},{7,6},{8,9},{9,8},{10,11... | collective-permute-start | bytes 393224 | tf_op jit(solution)/shard_map/ppermute | solution.py:32
  35.0 7.3 %collective-permute-start.9 = (f32[4,32,256]{2,1,0:T(8,128)S(1)}, f32[4,32,256]{2,1,0:T(8,128)S(1)}, u32[]{:S(2)}, u32[]{:S(2)}) collective-permute-start(f32[4,32,256]{2,1,0:T(8,128)S(1)} %get-tuple-element.62), channel_id=1, source_target_pairs={{1,2},{2,1},{5,6},{6,5},{9,10},{10,9},{13,14},{14,13},{17,18},{18,... | collective-permute-start | bytes 393224 | tf_op jit(solution)/shard_map/ppermute | solution.py:32
  35.6 6.6 %collective-permute-start.12 = (f32[4,16,256]{2,1,0:T(8,128)S(1)}, f32[4,16,256]{2,1,0:T(8,128)S(1)}, u32[]{:S(2)}, u32[]{:S(2)}) collective-permute-start(f32[4,16,256]{2,1,0:T(8,128)S(1)} %get-tuple-element.65), channel_id=1, source_target_pairs={{0,16},{16,0},{1,17},{17,1},{2,18},{18,2},{3,19},{19,3},{4,20},{20... | collective-permute-start | bytes 196616 | tf_op jit(solution)/shard_map/ppermute | solution.py:32
  35.7 6.5 %collective-permute-start.10 = (f32[16,128]{1,0:T(8,128)S(1)}, f32[16,128]{1,0:T(8,128)S(1)}, u32[]{:S(2)}, u32[]{:S(2)}) collective-permute-start(f32[16,128]{1,0:T(8,128)S(1)} %get-tuple-element.63), channel_id=1, source_target_pairs={{0,4},{4,0},{8,12},{12,8},{1,5},{5,1},{9,13},{13,9},{2,6},{6,2},{1... | collective-permute-start | bytes 24584 | tf_op jit(solution)/shard_map/ppermute | solution.py:32
  37.3 4.9 %collective-permute-start.11 = (f32[16,128]{1,0:T(8,128)S(1)}, f32[16,128]{1,0:T(8,128)S(1)}, u32[]{:S(2)}, u32[]{:S(2)}) collective-permute-start(f32[16,128]{1,0:T(8,128)S(1)} %get-tuple-element.64), channel_id=1, source_target_pairs={{4,8},{8,4},{5,9},{9,5},{6,10},{10,6},{7,11},{11,7},{20,24},{24,20... | collective-permute-start | bytes 24584 | tf_op jit(solution)/shard_map/ppermute | solution.py:32
  48.1 1.3 %copy-start.3 = (f32[4,32,16,256]{3,2,1,0:T(8,128)}, f32[4,32,16,256]{3,2,1,0:T(8,128)S(1)}, u32[]{:S(2)}) copy-start(f32[4,32,16,256]{3,2,1,0:T(8,128)S(1)} %get-tuple-element.76.refs_3_) | copy-start | bytes 6291460
  49.5 6.3 %collective-permute-start.13 = (f32[40,128]{1,0:T(8,128)S(1)}, f32[40,128]{1,0:T(8,128)S(1)}, u32[]{:S(2)}, u32[]{:S(2)}) collective-permute-start(f32[40,128]{1,0:T(8,128)S(1)} %pad_maximum_fusion.9), channel_id=1, source_target_pairs={{0,4},{4,0},{8,12},{12,8},{1,5},{5,1},{9,13},{13,9},{2,6},{6,2},{1... | collective-permute-start | bytes 61448 | tf_op jit(solution)/shard_map/ppermute | solution.py:32
  53.7 5.0 %collective-permute-start.14 = (f32[4,32,256]{2,1,0:T(8,128)S(1)}, f32[4,32,256]{2,1,0:T(8,128)S(1)}, u32[]{:S(2)}, u32[]{:S(2)}) collective-permute-start(f32[4,32,256]{2,1,0:T(8,128)S(1)} %get-tuple-element.69), channel_id=1, source_target_pairs={{0,1},{1,0},{2,3},{3,2},{4,5},{5,4},{6,7},{7,6},{8,9},{9,8},{10,11... | collective-permute-start | bytes 393224 | tf_op jit(solution)/shard_map/ppermute | solution.py:32
  55.1 3.6 %collective-permute-start.15 = (f32[4,32,256]{2,1,0:T(8,128)S(1)}, f32[4,32,256]{2,1,0:T(8,128)S(1)}, u32[]{:S(2)}, u32[]{:S(2)}) collective-permute-start(f32[4,32,256]{2,1,0:T(8,128)S(1)} %get-tuple-element.70), channel_id=1, source_target_pairs={{1,2},{2,1},{5,6},{6,5},{9,10},{10,9},{13,14},{14,13},{17,18},{18,... | collective-permute-start | bytes 393224 | tf_op jit(solution)/shard_map/ppermute | solution.py:32
  55.7 1.3 %collective-permute-start.16 = (f32[4,16,256]{2,1,0:T(8,128)S(1)}, f32[4,16,256]{2,1,0:T(8,128)S(1)}, u32[]{:S(2)}, u32[]{:S(2)}) collective-permute-start(f32[4,16,256]{2,1,0:T(8,128)S(1)} %get-tuple-element.71), channel_id=1, source_target_pairs={{0,16},{16,0},{1,17},{17,1},{2,18},{18,2},{3,19},{19,3},{4,20},{20... | collective-permute-start | bytes 196616 | tf_op jit(solution)/shard_map/ppermute | solution.py:32
  58.7 4.8 %collective-permute-start.17 = (f32[64,128]{1,0:T(8,128)S(1)}, f32[64,128]{1,0:T(8,128)S(1)}, u32[]{:S(2)}, u32[]{:S(2)}) collective-permute-start(f32[64,128]{1,0:T(8,128)S(1)} %pad_maximum_fusion.3), channel_id=1, source_target_pairs={{0,12},{4,8},{8,4},{12,0},{1,13},{5,9},{9,5},{13,1},{2,14},{6,10},... | collective-permute-start | bytes 98312 | tf_op jit(solution)/shard_map/ppermute | solution.py:37
  63.5 6.5 %collective-permute-start.18 = (f32[96,128]{1,0:T(8,128)S(1)}, f32[96,128]{1,0:T(8,128)S(1)}, u32[]{:S(2)}, u32[]{:S(2)}) collective-permute-start(f32[96,128]{1,0:T(8,128)S(1)} %pad_maximum_fusion.1), channel_id=1, source_target_pairs={{0,1},{1,0},{2,3},{3,2},{4,5},{5,4},{6,7},{7,6},{8,9},{9,8},{10,11... | collective-permute-start | bytes 147464 | tf_op jit(solution)/shard_map/ppermute | solution.py:37
  70.1 7.0 %collective-permute-start.19 = (f32[96,128]{1,0:T(8,128)S(1)}, f32[96,128]{1,0:T(8,128)S(1)}, u32[]{:S(2)}, u32[]{:S(2)}) collective-permute-start(f32[96,128]{1,0:T(8,128)S(1)} %add.30), channel_id=1, source_target_pairs={{0,2},{1,3},{2,0},{3,1},{4,6},{5,7},{6,4},{7,5},{8,10},{9,11},{10,... | collective-permute-start | bytes 147464 | tf_op jit(solution)/shard_map/ppermute | solution.py:37
  71.1 1.6 %copy-start.4 = (f32[4,32,16,256]{3,2,1,0:T(8,128)S(1)}, f32[4,32,16,256]{3,2,1,0:T(8,128)}, u32[]{:S(2)}) copy-start(f32[4,32,16,256]{3,2,1,0:T(8,128)} %copy-done.3) | copy-start | bytes 6291460
  77.2 1.2 %collective-permute-start.20 = (f32[1,96,32]{1,2,0:T(8,128)S(1)}, f32[1,96,32]{1,2,0:T(8,128)S(1)}, u32[]{:S(2)}, u32[]{:S(2)}) collective-permute-start(f32[1,96,32]{1,2,0:T(8,128)S(1)} %bitcast.50), channel_id=1, source_target_pairs={{0,16},{16,0},{1,17},{17,1},{2,18},{18,2},{3,19},{19,3},{4,20},{20... | collective-permute-start | bytes 36872 | tf_op jit(solution)/shard_map/ppermute | solution.py:37

commit v5 on v3

--- a/solution.py
+++ b/solution.py
@@ -15,7 +15,7 @@
 viscosity = 0.02
 diffusivity = 0.02
 prandtl = 0.4
-vmem_limit = 48 << 20
+vmem_limit = 24 << 20
 
 
 def swap_pairs(count, first):
@@ -64,8 +64,8 @@
     for comp in range(4):
         low = q_ref[comp, :, 0, :]
         high = q_ref[comp, :, count_z - 1, :]
-        za_ref[comp] = pick(even_z, high, low)
-        zb_ref[comp] = pick(even_z, low, high)
+        za_ref[comp * count_x : (comp + 1) * count_x] = pick(even_z, high, low)
+        zb_ref[comp * count_x : (comp + 1) * count_x] = pick(even_z, low, high)
     lane = lax.broadcasted_iota(jnp.int32, (count_z, 128), 1)
     low = jnp.zeros((count_z, 128), jnp.float32)
     high = jnp.zeros((count_z, 128), jnp.float32)
@@ -76,8 +76,8 @@
             last = q_ref[comp, x, :, count_y - 128 :]
             low = jnp.where(lane == place, pltpu.roll(first, place, 1), low)
             high = jnp.where(lane == place, pltpu.roll(last, (place + 1) % 128, 1), high)
-    ya_ref[0] = pick(even_y, high, low)
-    yb_ref[0] = pick(even_y, low, high)
+    ya_ref[...] = pick(even_y, high, low)
+    yb_ref[...] = pick(even_y, low, high)
 
 
 def faces_body(q_ref, *face_refs, shape):
@@ -223,12 +223,14 @@
     even_x, even_z, even_y = is_even("gx"), is_even("gz"), is_even("gy")
     index_y = lax.axis_index("gy")
     tiles = count_y // 128
-    for tile in range(tiles):
-        first, second = (ref[:4, :, tile * 128 : tile * 128 + 128] for ref in (za_ref, zb_ref))
-        low_z_ref[:, tile] = pick(even_z, second, first)
-        high_z_ref[:, tile] = pick(even_z, first, second)
-    low_y_ref[...] = pick(index_y == 0, 0.0, pick(even_y, yb_ref[0], ya_ref[0]))
-    high_y_ref[...] = pick(index_y == lax.axis_size("gy") - 1, 0.0, pick(even_y, ya_ref[0], yb_ref[0]))
+    for comp in range(4):
+        for tile in range(tiles):
+            there = slice(comp * count_x, (comp + 1) * count_x), slice(tile * 128, tile * 128 + 128)
+            first, second = za_ref[there], zb_ref[there]
+            low_z_ref[comp, tile] = pick(even_z, second, first)
+            high_z_ref[comp, tile] = pick(even_z, first, second)
+    low_y_ref[...] = pick(index_y == 0, 0.0, pick(even_y, yb_ref[:count_z], ya_ref[:count_z]))
+    high_y_ref[...] = pick(index_y == lax.axis_size("gy") - 1, 0.0, pick(even_y, ya_ref[:count_z], yb_ref[:count_z]))
     first = x_refs[0][...]
     second = x_refs[1][...] if len(x_refs) > 1 else 0.0
     low_x_ref[...] = pick(even_x, second, first)
@@ -292,8 +294,7 @@
             edge.wait()
         return
 
-    za, others = face_refs[0], face_refs[1:]
-    write_faces(out_ref, [za.at[:4]] + list(others), shape)
+    write_faces(out_ref, face_refs, shape)
 
     @pl.when(listed)
     def _():
@@ -304,19 +305,21 @@
 
     if packs:
         count = 3 * steps + 1
-        za[4] = jnp.zeros((count_x, count_y), jnp.float32)
+        za_ref = face_refs[0]
+        start = 4 * count_x
+        za_ref[start:] = jnp.zeros((za_ref.shape[0] - start, count_y), jnp.float32)
         for j, slot in enumerate(slots):
-            lane, row = (j % 2) * points, (j // 2) * count
+            lane, row = (j % 2) * points, start + (j // 2) * count
             values = sample_ref[: count - 1, j * points : (j + 1) * points]
-            za[4, row : row + count - 1, lane : lane + points] = values
+            za_ref[row : row + count - 1, lane : lane + points] = values
             name = jnp.where(listed, 0.5 * (slot + 1).astype(jnp.float32), 0.0)
-            za[4, row + count - 1 : row + count, lane : lane + points] = jnp.full((1, points), name)
+            za_ref[row + count - 1 : row + count, lane : lane + points] = jnp.full((1, points), name)
 
 
 def face_shapes(shape, extra=0):
     count_x, count_z, count_y = shape
-    forms = [(4 + extra, count_x, count_y), (4, count_x, count_y)]
-    forms += [(1, count_z, 128)] * 2 + [(4, count_z, count_y)] * (1 if lax.axis_size("gx") == 2 else 2)
+    forms = [(4 * count_x + extra, count_y), (4 * count_x, count_y)]
+    forms += [(count_z, 128)] * 2 + [(4, count_z, count_y)] * (1 if lax.axis_size("gx") == 2 else 2)
     return [jax.ShapeDtypeStruct(form, jnp.float32) for form in forms]
 
 
@@ -327,6 +330,13 @@
 def swap_faces(faces):
     plan = [("gz", 0), ("gz", 1), ("gy", 0), ("gy", 1), ("gx", 0), ("gx", 1)]
     return [swap(face, axis, first) for face, (axis, first) in zip(faces, plan)]
+
+
+def masked(halo, axis, first):
+    index = lax.axis_index(axis)
+    partner = index + 1 - 2 * lax.rem(index + first, 2)
+    inside = jnp.logical_and(partner >= 0, partner < lax.axis_size(axis))
+    return jnp.where(inside, halo, 0.0)
 
 
 def true_order(pieces, axis):
@@ -352,6 +362,8 @@
     turbines = block_list.reshape(capacity)
     barrier = lax.optimization_barrier
     forms = face_shapes(shape)
+
+    extra = pl.cdiv((3 * steps + 1) * pl.cdiv(capacity, 2), 8) * 8
 
     own = jnp.concatenate([positions.reshape(steps, 3, part), loads.reshape(steps, 3, part)], axis=1)
     table = jnp.pad(own, ((0, 0), (0, 2), (0, 0))).reshape(1, 8 * steps, part)
@@ -366,24 +378,25 @@
     )(q)
     table, faces = barrier((table, list(faces)))
     za, zb, ya, yb = faces[:4]
+    za = masked(swap(za, "gz", 0), "gz", 0)
     distance = 2
     while distance < size_z:
-        table = jnp.concatenate([table, from_distance(table, "gz", distance)], axis=0)
+        received = from_distance(table, "gz", distance)
+        received, za = barrier((received, za))
+        table = jnp.concatenate([table, received], axis=0)
         distance *= 2
-    za, zb = swap(za, "gz", 0), swap(zb, "gz", 1)
     table = true_order(table, "gz")
     table = jnp.concatenate([table[k] for k in range(size_z)], axis=1)
-    rows = pl.cdiv(8 * steps, 2 * count_z) * 2 * count_z
-    blocks = jnp.pad(table, ((0, rows - 8 * steps), (0, 0))).reshape(rows // count_z, count_z, points)
-    blocks, ya = barrier((blocks, ya))
-    ya = swap(jnp.concatenate([ya, blocks], axis=0), "gy", 0)
-    blocks = jnp.concatenate([blocks, ya[1:]], axis=0)
-    blocks, yb, za = barrier((blocks, yb, za))
-    yb = from_distance(jnp.concatenate([yb, blocks], axis=0), "gy", 3)
+    rows = 8 * steps
+    zb, ya, table = barrier((zb, ya, table))
+    zb = masked(swap(zb, "gz", 1), "gz", 1)
+    ya = swap(jnp.concatenate([ya, table], axis=0), "gy", 0)
+    ya, zb = barrier((ya, zb))
+    table = jnp.concatenate([table, ya[count_z:]], axis=0)
+    yb = from_distance(jnp.concatenate([yb, table], axis=0), "gy", 3)
     x_faces = [swap(face, "gx", first) for first, face in enumerate(faces[4:])]
-    blocks = jnp.concatenate([blocks, yb[1:]], axis=0)[None]
-    blocks, zb = barrier((blocks, zb))
-    table = gather_relative(blocks, "gx").reshape(size_x * size_y, rows, points)
+    table = jnp.concatenate([table, yb[count_z:]], axis=0)
+    table = gather_relative(table[None], "gx").reshape(size_x * size_y, rows, points)
     halos = [za, zb, ya, yb] + x_faces
 
     samples = None
@@ -396,7 +409,7 @@
             out_specs = [pl.BlockSpec(memory_space=pl.ANY)]
             scratch = [pltpu.VMEM(q.shape, jnp.float32), pltpu.SemaphoreType.DMA((count_x,))]
         else:
-            shapes += face_shapes(shape, 1 if packs else 0)
+            shapes += face_shapes(shape, extra if packs else 0)
             if packs:
                 scratch = [pltpu.VMEM((16, lanes), jnp.float32)]
             else:
@@ -425,20 +438,18 @@
             halos = swap_faces(faces)
             continue
         za, zb, ya, yb = faces[:4]
-        za_in, zb_in = swap(za, "gz", 0), swap(zb, "gz", 1)
-        sums = za[4] + za_in[4]
-        row_blocks = pl.cdiv((3 * steps + 1) * pl.cdiv(capacity, 2), count_z)
-        blocks = jnp.stack(
-            [sums[b * count_z : (b + 1) * count_z, h * 128 : h * 128 + 128] for b in range(row_blocks) for h in range(2)]
-        )
-        blocks, ya, zb_in = barrier((blocks, ya, zb_in))
-        count = blocks.shape[0]
-        ya_in = swap(jnp.concatenate([ya, blocks], axis=0), "gy", 0)
-        x_faces = [swap(face, "gx", first) for first, face in enumerate(faces[4:])]
-        pieces = jnp.concatenate([blocks, ya_in[1:]], axis=0)
-        pieces, yb, x_faces = barrier((pieces, yb, x_faces))
+        za_in = swap(za, "gz", 0)
+        sums = za[4 * count_x :] + za_in[4 * count_x :]
+        pieces = jnp.concatenate([sums[:, h * 128 : h * 128 + 128] for h in range(2)], axis=0)
+        pieces, ya, zb = barrier((pieces, ya, zb))
+        zb_in = masked(swap(zb, "gz", 1), "gz", 1)
+        ya_in = swap(jnp.concatenate([ya, pieces], axis=0), "gy", 0)
+        ya_in, zb_in, x_faces = barrier((ya_in, zb_in, faces[4:]))
+        x_faces = [swap(face, "gx", first) for first, face in enumerate(x_faces)]
+        pieces = jnp.concatenate([pieces, ya_in[count_z:]], axis=0)
         yb_in = from_distance(jnp.concatenate([yb, pieces], axis=0), "gy", 3)
-        pieces = jnp.concatenate([pieces, yb_in[1:]], axis=0).reshape(size_y, count, count_z, 128)
+        pieces = jnp.concatenate([pieces, yb_in[count_z:]], axis=0)
+        pieces, x_faces = barrier((pieces, x_faces))
         halos = [za_in, zb_in, ya_in, yb_in] + x_faces
 
     distance = 2
@@ -446,10 +457,8 @@
         pieces = pieces + from_distance(pieces, "gz", distance)
         distance *= 2
     pieces, q = barrier((pieces, q))
-    mine = lax.dynamic_slice_in_dim(pieces, lax.axis_index("gz") * part, part, axis=3)[None]
-    mine = gather_relative(mine, "gx")
-    mine = mine.reshape(size_x * size_y, row_blocks, 2, count_z, part).transpose(0, 2, 1, 3, 4)
-    mine = mine.reshape(size_x * size_y, 2, row_blocks * count_z, part)
+    mine = lax.dynamic_slice_in_dim(pieces, lax.axis_index("gz") * part, part, axis=1)[None]
+    mine = gather_relative(mine, "gx").reshape(size_x * size_y, 2, extra, part)
     holder = (lax.axis_index("gx") * size_y + lax.axis_index("gy") + 1).astype(jnp.float32)
     returned = 0.0
     for j in range(capacity):

time: 73.3 us -> 74.6 us (1.018)
  starting transfers between devices: 30.4 us -> 33.9 us
  waiting for transfers between devices: 20.7 us -> 18 us
    ppermute x7, starting transfers between devices: 11.8 us -> 15.3 us  [from_distance(): return lax.ppermute(value, axis, [(i, i ^ distance) for i in range(count)])]
    ppermute x7, waiting for transfers between devices: 10.3 us -> 7.31 us  [from_distance(): return lax.ppermute(value, axis, [(i, i ^ distance) for i in range(count)])]
where the time goes in v5:
time: 74.6 us; the launch traced here: 73.9 us
  starting transfers between devices  33.9 us (45%)
  waiting for transfers between devices  18 us (24%)
  Pallas kernels  17.6 us (24%)
  local copies, waits for them, and re-layouts  3.22 us (4%)
  between operations  0.93 us (1%)
    ppermute x13, starting transfers between devices, swap(): return lax.ppermute(value, axis, pairs)  18.6 us
    pallas_call x3, Pallas kernels, shards(): pl.pallas_call(functools.partial(step_body, shape=shape, points=points, c...  16.9 us
    ppermute x7, starting transfers between devices, from_distance(): return lax.ppermute(value, axis, [(i, i ^ distance) for i in range(count)])  15.3 us
    ppermute x13, waiting for transfers between devices, swap(): return lax.ppermute(value, axis, pairs)  10.7 us
    ppermute x7, waiting for transfers between devices, from_distance(): return lax.ppermute(value, axis, [(i, i ^ distance) for i in range(count)])  7.31 us
    unnamed x10, local copies, waits for them, and re-layouts  2.33 us
  transfers between devices with their start and end apart: 20, of which 11 were waited for; matrix products, arithmetic and copies ran while one was open for 0% of the time, Pallas kernels for 8%

profile of v5, /device:TPU:0, one launch (start us, length us, event | category | flops | bytes accessed | tf_op | source)
XLA Modules:
  0.0 73.9 jit_solution(10004786445817985440)
XLA Ops:
  0.6 0.7 copy_bitcast_fusion
  1.4 3.1 %collective-permute-start = (f32[1,24,32]{2,1,0:T(8,128)S(1)}, f32[1,24,32]{2,1,0:T(8,128)S(1)}, u32[]{:S(2)}, u32[]{:S(2)}) collective-permute-start(f32[1,24,32]{2,1,0:T(8,128)S(1)} %fusion.5), channel_id=1, source_target_pairs={{0,1},{1,0},{2,3},{3,2},{4,5},{5,4},{6,7},{7,6},{8,9},{9,8},{10,11... | collective-permute-start | bytes 9224 | tf_op jit(solution)/shard_map/ppermute | solution.py:37
  4.5 1.6 %copy-done = f32[4,32,16,256]{3,2,1,0:T(8,128)S(1)} copy-done((f32[4,32,16,256]{3,2,1,0:T(8,128)S(1)}, f32[4,32,16,256]{3,2,1,0:T(8,128)}, u32[]{:S(2)}) %copy-start) | copy-done | bytes 2097176
  6.0 0.7 faces.1
  6.8 1.3 %collective-permute-start.2 = (f32[128,256]{1,0:T(8,128)S(1)}, f32[128,256]{1,0:T(8,128)S(1)}, u32[]{:S(2)}, u32[]{:S(2)}) collective-permute-start(f32[128,256]{1,0:T(8,128)S(1)} %get-tuple-element.51), channel_id=1, source_target_pairs={{0,1},{1,0},{2,3},{3,2},{4,5},{5,4},{6,7},{7,6},{8,9},{9,8},{10,11... | collective-permute-start | bytes 393224 | tf_op jit(solution)/shard_map/ppermute | solution.py:32
  8.2 2.6 %collective-permute-start.1 = (f32[2,24,32]{2,1,0:T(8,128)S(1)}, f32[2,24,32]{2,1,0:T(8,128)S(1)}, u32[]{:S(2)}, u32[]{:S(2)}) collective-permute-start(f32[2,24,32]{2,1,0:T(8,128)S(1)} %pad_maximum_fusion.5), channel_id=1, source_target_pairs={{0,2},{1,3},{2,0},{3,1},{4,6},{5,7},{6,4},{7,5},{8,10},{9,11},{10,... | collective-permute-start | bytes 18440 | tf_op jit(solution)/shard_map/ppermute | solution.py:37
  10.7 1.3 %collective-permute-done.2 = f32[128,256]{1,0:T(8,128)S(1)} collective-permute-done((f32[128,256]{1,0:T(8,128)S(1)}, f32[128,256]{1,0:T(8,128)S(1)}, u32[]{:S(2)}, u32[]{:S(2)}) %collective-permute-start.2) | collective-permute-done | bytes 131104 | tf_op jit(solution)/shard_map/ppermute | solution.py:32
  12.1 0.9 %collective-permute-done.1 = f32[2,24,32]{2,1,0:T(8,128)S(1)} collective-permute-done((f32[2,24,32]{2,1,0:T(8,128)S(1)}, f32[2,24,32]{2,1,0:T(8,128)S(1)}, u32[]{:S(2)}, u32[]{:S(2)}) %collective-permute-start.1) | collective-permute-done | bytes 6176 | tf_op jit(solution)/shard_map/ppermute | solution.py:37
  13.2 0.7 collective-permute-start.4
  13.9 1.6 %collective-permute-start.3 = (f32[40,128]{1,0:T(8,128)S(1)}, f32[40,128]{1,0:T(8,128)S(1)}, u32[]{:S(2)}, u32[]{:S(2)}) collective-permute-start(f32[40,128]{1,0:T(8,128)S(1)} %pad_maximum_fusion.7), channel_id=1, source_target_pairs={{0,4},{4,0},{8,12},{12,8},{1,5},{5,1},{9,13},{13,9},{2,6},{6,2},{1... | collective-permute-start | bytes 61448 | tf_op jit(solution)/shard_map/ppermute | solution.py:32
  15.5 2.3 %collective-permute-done.3.refs_5_ = f32[40,128]{1,0:T(8,128)S(1)} collective-permute-done((f32[40,128]{1,0:T(8,128)S(1)}, f32[40,128]{1,0:T(8,128)S(1)}, u32[]{:S(2)}, u32[]{:S(2)}) %collective-permute-start.3) | collective-permute-done | bytes 20512 | tf_op jit(solution)/shard_map/ppermute | solution.py:32
  17.7 2.4 %collective-permute-start.5 = (f32[64,128]{1,0:T(8,128)S(1)}, f32[64,128]{1,0:T(8,128)S(1)}, u32[]{:S(2)}, u32[]{:S(2)}) collective-permute-start(f32[64,128]{1,0:T(8,128)S(1)} %pad_maximum_fusion.3), channel_id=1, source_target_pairs={{0,12},{4,8},{8,4},{12,0},{1,13},{5,9},{9,5},{13,1},{2,14},{6,10},... | collective-permute-start | bytes 98312 | tf_op jit(solution)/shard_map/ppermute | solution.py:37
  20.2 2.4 %collective-permute-done.5.refs_6_ = f32[64,128]{1,0:T(8,128)S(1)} collective-permute-done((f32[64,128]{1,0:T(8,128)S(1)}, f32[64,128]{1,0:T(8,128)S(1)}, u32[]{:S(2)}, u32[]{:S(2)}) %collective-permute-start.5) | collective-permute-done | bytes 32800 | tf_op jit(solution)/shard_map/ppermute | solution.py:37
  23.1 0.7 collective-permute-done.6
  24.0 6.2 %step.3 = (f32[4,32,16,256]{3,2,1,0:T(8,128)S(1)}, f32[128,256]{1,0:T(8,128)S(1)}, f32[128,256]{1,0:T(8,128)S(1)}, f32[16,128]{1,0:T(8,128)S(1)}, f32[16,128]{1,...) custom-call(s32[2]{0:T(128)S(1)} %bitcast.59, f32[8,24,128]{2,1,0:T(8,128)S(1)} %bitcast.56, ...), custom_call_target="tpu_custom_call" | custom-call | tf_op jit(solution)/shard_map/step/pallas_call | solution.py:419
  30.2 4.4 %collective-permute-start.8 = (f32[128,256]{1,0:T(8,128)S(1)}, f32[128,256]{1,0:T(8,128)S(1)}, u32[]{:S(2)}, u32[]{:S(2)}) collective-permute-start(f32[128,256]{1,0:T(8,128)S(1)} %get-tuple-element.62), channel_id=1, source_target_pairs={{0,1},{1,0},{2,3},{3,2},{4,5},{5,4},{6,7},{7,6},{8,9},{9,8},{10,11... | collective-permute-start | bytes 393224 | tf_op jit(solution)/shard_map/ppermute | solution.py:32
  34.7 0.7 collective-permute-start.9
  35.5 1.5 %collective-permute-start.10 = (f32[16,128]{1,0:T(8,128)S(1)}, f32[16,128]{1,0:T(8,128)S(1)}, u32[]{:S(2)}, u32[]{:S(2)}) collective-permute-start(f32[16,128]{1,0:T(8,128)S(1)} %get-tuple-element.64), channel_id=1, source_target_pairs={{0,4},{4,0},{8,12},{12,8},{1,5},{5,1},{9,13},{13,9},{2,6},{6,2},{1... | collective-permute-start | bytes 24584 | tf_op jit(solution)/shard_map/ppermute | solution.py:32
  37.0 0.6 collective-permute-start.11
  37.6 1.5 %collective-permute-done.10.refs_5_ = f32[16,128]{1,0:T(8,128)S(1)} collective-permute-done((f32[16,128]{1,0:T(8,128)S(1)}, f32[16,128]{1,0:T(8,128)S(1)}, u32[]{:S(2)}, u32[]{:S(2)}) %collective-permute-start.10) | collective-permute-done | bytes 8224 | tf_op jit(solution)/shard_map/ppermute | solution.py:32
  39.1 5.7 %step.4 = (f32[4,32,16,256]{3,2,1,0:T(8,128)S(1)}, f32[144,256]{1,0:T(8,128)S(1)}, f32[128,256]{1,0:T(8,128)S(1)}, f32[16,128]{1,0:T(8,128)S(1)}, f32[16,128]{1,0:T(8,128)S(1)}, /*index=5*/f32[4,16,256]{2,1,0:T(8,128)S(1)}) custom-call(s32[2]{0:T(128)S(1)} %bitcast.60, f32[8,24,128]{2,1,0:T(8,128)S(1)} %bitcast.57, ...), custom_call_target="tpu_custom_call" | custom-call | tf_op jit(solution)/shard_map/step/pallas_call | solution.py:419
  44.8 3.2 %collective-permute-start.13 = (f32[144,256]{1,0:T(8,128)S(1)}, f32[144,256]{1,0:T(8,128)S(1)}, u32[]{:S(2)}, u32[]{:S(2)}) collective-permute-start(f32[144,256]{1,0:T(8,128)S(1)} %get-tuple-element.68), channel_id=1, source_target_pairs={{0,1},{1,0},{2,3},{3,2},{4,5},{5,4},{6,7},{7,6},{8,9},{9,8},{10,11... | collective-permute-start | bytes 442376 | tf_op jit(solution)/shard_map/ppermute | solution.py:32
  48.1 3.6 %collective-permute-done.13.refs_3_ = f32[144,256]{1,0:T(8,128)S(1)} collective-permute-done((f32[144,256]{1,0:T(8,128)S(1)}, f32[144,256]{1,0:T(8,128)S(1)}, u32[]{:S(2)}, u32[]{:S(2)}) %collective-permute-start.13) | collective-permute-done | bytes 147488 | tf_op jit(solution)/shard_map/ppermute | solution.py:32
  51.6 0.7 collective-permute-start.15
  52.3 3.3 %collective-permute-start.14 = (f32[48,128]{1,0:T(8,128)S(1)}, f32[48,128]{1,0:T(8,128)S(1)}, u32[]{:S(2)}, u32[]{:S(2)}) collective-permute-start(f32[48,128]{1,0:T(8,128)S(1)} %pad_maximum_fusion.6), channel_id=1, source_target_pairs={{0,4},{4,0},{8,12},{12,8},{1,5},{5,1},{9,13},{13,9},{2,6},{6,2},{1... | collective-permute-start | bytes 73736 | tf_op jit(solution)/shard_map/ppermute | solution.py:32
  55.6 1.8 %collective-permute-done.14.refs_5_ = f32[48,128]{1,0:T(8,128)S(1)} collective-permute-done((f32[48,128]{1,0:T(8,128)S(1)}, f32[48,128]{1,0:T(8,128)S(1)}, u32[]{:S(2)}, u32[]{:S(2)}) %collective-permute-start.14) | collective-permute-done | bytes 24608 | tf_op jit(solution)/shard_map/ppermute | solution.py:32
  57.4 2.8 %collective-permute-start.16 = (f32[80,128]{1,0:T(8,128)S(1)}, f32[80,128]{1,0:T(8,128)S(1)}, u32[]{:S(2)}, u32[]{:S(2)}) collective-permute-start(f32[80,128]{1,0:T(8,128)S(1)} %pad_maximum_fusion.2), channel_id=1, source_target_pairs={{0,12},{4,8},{8,4},{12,0},{1,13},{5,9},{9,5},{13,1},{2,14},{6,10},... | collective-permute-start | bytes 122888 | tf_op jit(solution)/shard_map/ppermute | solution.py:37
  60.2 2.1 %collective-permute-done.16.refs_6_ = f32[80,128]{1,0:T(8,128)S(1)} collective-permute-done((f32[80,128]{1,0:T(8,128)S(1)}, f32[80,128]{1,0:T(8,128)S(1)}, u32[]{:S(2)}, u32[]{:S(2)}) %collective-permute-start.16) | collective-permute-done | bytes 40992 | tf_op jit(solution)/shard_map/ppermute | solution.py:37
  62.3 4.3 %collective-permute-start.18 = (f32[128,128]{1,0:T(8,128)S(1)}, f32[128,128]{1,0:T(8,128)S(1)}, u32[]{:S(2)}, u32[]{:S(2)}) collective-permute-start(f32[128,128]{1,0:T(8,128)S(1)} %pad_maximum_fusion.1), channel_id=1, source_target_pairs={{0,2},{1,3},{2,0},{3,1},{4,6},{5,7},{6,4},{7,5},{8,10},{9,11},{10,... | collective-permute-start | bytes 196616 | tf_op jit(solution)/shard_map/ppermute | solution.py:37
  66.7 5.0 %step.5 = f32[4,32,16,256]{3,2,1,0:T(8,128)} custom-call(s32[2]{0:T(128)S(1)} %bitcast.61, f32[8,24,128]{2,1,0:T(8,128)S(1)} %bitcast.58, f32[4,32,16,256]{3,2,1,0:T(8,128)S(1)} %get-tuple-element.79.refs_2_, f32[144,256]{1,0:T(8,128)S(1)} %collective-permute-done.13.refs_3_, f32[128,256]{1,0:T(8,128)S(1)} %broadcast_select_fusion.refs_4_, ...), custom_call_target="tpu_custom_call" | custom-call | tf_op jit(solution)/shard_map/step/pallas_call | solution.py:419
  71.9 1.2 %collective-permute-done.19 = f32[1,128,32]{1,2,0:T(8,128)S(1)} collective-permute-done((f32[1,128,32]{1,2,0:T(8,128)S(1)}, f32[1,128,32]{1,2,0:T(8,128)S(1)}, u32[]{:S(2)}, u32[]{:S(2)}) %collective-permute-start.19) | collective-permute-done | bytes 16416 | tf_op jit(solution)/shard_map/ppermute | solution.py:37
  73.3 0.6 add.44
  (59 shorter events, 1.5 us)
Async XLA Ops:
  0.6 23.4 %copy-start.2 = (s32[1,1,1,2]{3,2,1,0:T(1,128)S(1)}, s32[1,1,1,2]{3,2,1,0:T(1,128)}, u32[]{:S(2)}) copy-start(s32[1,1,1,2]{3,2,1,0:T(1,128)} %param.7) | copy-start | bytes 28
  1.4 5.4 %collective-permute-start = (f32[1,24,32]{2,1,0:T(8,128)S(1)}, f32[1,24,32]{2,1,0:T(8,128)S(1)}, u32[]{:S(2)}, u32[]{:S(2)}) collective-permute-start(f32[1,24,32]{2,1,0:T(8,128)S(1)} %fusion.5), channel_id=1, source_target_pairs={{0,1},{1,0},{2,3},{3,2},{4,5},{5,4},{6,7},{7,6},{8,9},{9,8},{10,11... | collective-permute-start | bytes 9224 | tf_op jit(solution)/shard_map/ppermute | solution.py:37
  4.5 1.6 %copy-start = (f32[4,32,16,256]{3,2,1,0:T(8,128)S(1)}, f32[4,32,16,256]{3,2,1,0:T(8,128)}, u32[]{:S(2)}) copy-start(f32[4,32,16,256]{3,2,1,0:T(8,128)} %refs_2_.1) | copy-start | bytes 6291460
  6.0 18.0 %copy-start.1 = (f32[4,32,16,256]{3,2,1,0:T(8,128)S(1)}, f32[4,32,16,256]{3,2,1,0:T(8,128)}, u32[]{:S(2)}) copy-start(f32[4,32,16,256]{3,2,1,0:T(8,128)} %refs_2_.1) | copy-start | bytes 6291460
  6.8 5.3 %collective-permute-start.2 = (f32[128,256]{1,0:T(8,128)S(1)}, f32[128,256]{1,0:T(8,128)S(1)}, u32[]{:S(2)}, u32[]{:S(2)}) collective-permute-start(f32[128,256]{1,0:T(8,128)S(1)} %get-tuple-element.51), channel_id=1, source_target_pairs={{0,1},{1,0},{2,3},{3,2},{4,5},{5,4},{6,7},{7,6},{8,9},{9,8},{10,11... | collective-permute-start | bytes 393224 | tf_op jit(solution)/shard_map/ppermute | solution.py:32
  8.2 4.9 %collective-permute-start.1 = (f32[2,24,32]{2,1,0:T(8,128)S(1)}, f32[2,24,32]{2,1,0:T(8,128)S(1)}, u32[]{:S(2)}, u32[]{:S(2)}) collective-permute-start(f32[2,24,32]{2,1,0:T(8,128)S(1)} %pad_maximum_fusion.5), channel_id=1, source_target_pairs={{0,2},{1,3},{2,0},{3,1},{4,6},{5,7},{6,4},{7,5},{8,10},{9,11},{10,... | collective-permute-start | bytes 18440 | tf_op jit(solution)/shard_map/ppermute | solution.py:37
  13.2 2.3 %collective-permute-start.4 = (f32[128,256]{1,0:T(8,128)S(1)}, f32[128,256]{1,0:T(8,128)S(1)}, u32[]{:S(2)}, u32[]{:S(2)}) collective-permute-start(f32[128,256]{1,0:T(8,128)S(1)} %get-tuple-element.55), channel_id=1, source_target_pairs={{1,2},{2,1},{5,6},{6,5},{9,10},{10,9},{13,14},{14,13},{17,18},{18,... | collective-permute-start | bytes 393224 | tf_op jit(solution)/shard_map/ppermute | solution.py:32
  13.9 3.8 %collective-permute-start.3 = (f32[40,128]{1,0:T(8,128)S(1)}, f32[40,128]{1,0:T(8,128)S(1)}, u32[]{:S(2)}, u32[]{:S(2)}) collective-permute-start(f32[40,128]{1,0:T(8,128)S(1)} %pad_maximum_fusion.7), channel_id=1, source_target_pairs={{0,4},{4,0},{8,12},{12,8},{1,5},{5,1},{9,13},{13,9},{2,6},{6,2},{1... | collective-permute-start | bytes 61448 | tf_op jit(solution)/shard_map/ppermute | solution.py:32
  17.7 4.8 %collective-permute-start.5 = (f32[64,128]{1,0:T(8,128)S(1)}, f32[64,128]{1,0:T(8,128)S(1)}, u32[]{:S(2)}, u32[]{:S(2)}) collective-permute-start(f32[64,128]{1,0:T(8,128)S(1)} %pad_maximum_fusion.3), channel_id=1, source_target_pairs={{0,12},{4,8},{8,4},{12,0},{1,13},{5,9},{9,5},{13,1},{2,14},{6,10},... | collective-permute-start | bytes 98312 | tf_op jit(solution)/shard_map/ppermute | solution.py:37
  22.6 1.3 %collective-permute-start.6 = (f32[1,96,128]{2,1,0:T(8,128)S(1)}, f32[1,96,128]{2,1,0:T(8,128)S(1)}, u32[]{:S(2)}, u32[]{:S(2)}) collective-permute-start(f32[1,96,128]{2,1,0:T(8,128)S(1)} %maximum_bitcast_fusion), channel_id=1, source_target_pairs={{0,16},{16,0},{1,17},{17,1},{2,18},{18,2},{3,19},{19,3},{4,20},{20... | collective-permute-start | bytes 147464 | tf_op jit(solution)/shard_map/ppermute | solution.py:37
  22.6 1.4 %collective-permute-start.7 = (f32[4,16,256]{2,1,0:T(8,128)S(1)}, f32[4,16,256]{2,1,0:T(8,128)S(1)}, u32[]{:S(2)}, u32[]{:S(2)}) collective-permute-start(f32[4,16,256]{2,1,0:T(8,128)S(1)} %get-tuple-element.60), channel_id=1, source_target_pairs={{0,16},{16,0},{1,17},{17,1},{2,18},{18,2},{3,19},{19,3},{4,20},{20... | collective-permute-start | bytes 196616 | tf_op jit(solution)/shard_map/ppermute | solution.py:32
  30.2 8.9 %collective-permute-start.8 = (f32[128,256]{1,0:T(8,128)S(1)}, f32[128,256]{1,0:T(8,128)S(1)}, u32[]{:S(2)}, u32[]{:S(2)}) collective-permute-start(f32[128,256]{1,0:T(8,128)S(1)} %get-tuple-element.62), channel_id=1, source_target_pairs={{0,1},{1,0},{2,3},{3,2},{4,5},{5,4},{6,7},{7,6},{8,9},{9,8},{10,11... | collective-permute-start | bytes 393224 | tf_op jit(solution)/shard_map/ppermute | solution.py:32
  34.7 4.5 %collective-permute-start.9 = (f32[128,256]{1,0:T(8,128)S(1)}, f32[128,256]{1,0:T(8,128)S(1)}, u32[]{:S(2)}, u32[]{:S(2)}) collective-permute-start(f32[128,256]{1,0:T(8,128)S(1)} %get-tuple-element.63), channel_id=1, source_target_pairs={{1,2},{2,1},{5,6},{6,5},{9,10},{10,9},{13,14},{14,13},{17,18},{18,... | collective-permute-start | bytes 393224 | tf_op jit(solution)/shard_map/ppermute | solution.py:32
  35.3 3.8 %collective-permute-start.12 = (f32[4,16,256]{2,1,0:T(8,128)S(1)}, f32[4,16,256]{2,1,0:T(8,128)S(1)}, u32[]{:S(2)}, u32[]{:S(2)}) collective-permute-start(f32[4,16,256]{2,1,0:T(8,128)S(1)} %get-tuple-element.66), channel_id=1, source_target_pairs={{0,16},{16,0},{1,17},{17,1},{2,18},{18,2},{3,19},{19,3},{4,20},{20... | collective-permute-start | bytes 196616 | tf_op jit(solution)/shard_map/ppermute | solution.py:32
  35.5 3.7 %collective-permute-start.10 = (f32[16,128]{1,0:T(8,128)S(1)}, f32[16,128]{1,0:T(8,128)S(1)}, u32[]{:S(2)}, u32[]{:S(2)}) collective-permute-start(f32[16,128]{1,0:T(8,128)S(1)} %get-tuple-element.64), channel_id=1, source_target_pairs={{0,4},{4,0},{8,12},{12,8},{1,5},{5,1},{9,13},{13,9},{2,6},{6,2},{1... | collective-permute-start | bytes 24584 | tf_op jit(solution)/shard_map/ppermute | solution.py:32
  37.0 2.2 %collective-permute-start.11 = (f32[16,128]{1,0:T(8,128)S(1)}, f32[16,128]{1,0:T(8,128)S(1)}, u32[]{:S(2)}, u32[]{:S(2)}) collective-permute-start(f32[16,128]{1,0:T(8,128)S(1)} %get-tuple-element.65), channel_id=1, source_target_pairs={{4,8},{8,4},{5,9},{9,5},{6,10},{10,6},{7,11},{11,7},{20,24},{24,20... | collective-permute-start | bytes 24584 | tf_op jit(solution)/shard_map/ppermute | solution.py:32
  44.8 6.8 %collective-permute-start.13 = (f32[144,256]{1,0:T(8,128)S(1)}, f32[144,256]{1,0:T(8,128)S(1)}, u32[]{:S(2)}, u32[]{:S(2)}) collective-permute-start(f32[144,256]{1,0:T(8,128)S(1)} %get-tuple-element.68), channel_id=1, source_target_pairs={{0,1},{1,0},{2,3},{3,2},{4,5},{5,4},{6,7},{7,6},{8,9},{9,8},{10,11... | collective-permute-start | bytes 442376 | tf_op jit(solution)/shard_map/ppermute | solution.py:32
  51.6 4.0 %collective-permute-start.15 = (f32[128,256]{1,0:T(8,128)S(1)}, f32[128,256]{1,0:T(8,128)S(1)}, u32[]{:S(2)}, u32[]{:S(2)}) collective-permute-start(f32[128,256]{1,0:T(8,128)S(1)} %get-tuple-element.73), channel_id=1, source_target_pairs={{1,2},{2,1},{5,6},{6,5},{9,10},{10,9},{13,14},{14,13},{17,18},{18,... | collective-permute-start | bytes 393224 | tf_op jit(solution)/shard_map/ppermute | solution.py:32
  52.3 5.1 %collective-permute-start.14 = (f32[48,128]{1,0:T(8,128)S(1)}, f32[48,128]{1,0:T(8,128)S(1)}, u32[]{:S(2)}, u32[]{:S(2)}) collective-permute-start(f32[48,128]{1,0:T(8,128)S(1)} %pad_maximum_fusion.6), channel_id=1, source_target_pairs={{0,4},{4,0},{8,12},{12,8},{1,5},{5,1},{9,13},{13,9},{2,6},{6,2},{1... | collective-permute-start | bytes 73736 | tf_op jit(solution)/shard_map/ppermute | solution.py:32
  57.4 4.9 %collective-permute-start.16 = (f32[80,128]{1,0:T(8,128)S(1)}, f32[80,128]{1,0:T(8,128)S(1)}, u32[]{:S(2)}, u32[]{:S(2)}) collective-permute-start(f32[80,128]{1,0:T(8,128)S(1)} %pad_maximum_fusion.2), channel_id=1, source_target_pairs={{0,12},{4,8},{8,4},{12,0},{1,13},{5,9},{9,5},{13,1},{2,14},{6,10},... | collective-permute-start | bytes 122888 | tf_op jit(solution)/shard_map/ppermute | solution.py:37
  60.2 2.2 %collective-permute-start.17 = (f32[4,16,256]{2,1,0:T(8,128)S(1)}, f32[4,16,256]{2,1,0:T(8,128)S(1)}, u32[]{:S(2)}, u32[]{:S(2)}) collective-permute-start(f32[4,16,256]{2,1,0:T(8,128)S(1)} %get-tuple-element.77), channel_id=1, source_target_pairs={{0,16},{16,0},{1,17},{17,1},{2,18},{18,2},{3,19},{19,3},{4,20},{20... | collective-permute-start | bytes 196616 | tf_op jit(solution)/shard_map/ppermute | solution.py:32
  62.3 9.3 %collective-permute-start.18 = (f32[128,128]{1,0:T(8,128)S(1)}, f32[128,128]{1,0:T(8,128)S(1)}, u32[]{:S(2)}, u32[]{:S(2)}) collective-permute-start(f32[128,128]{1,0:T(8,128)S(1)} %pad_maximum_fusion.1), channel_id=1, source_target_pairs={{0,2},{1,3},{2,0},{3,1},{4,6},{5,7},{6,4},{7,5},{8,10},{9,11},{10,... | collective-permute-start | bytes 196616 | tf_op jit(solution)/shard_map/ppermute | solution.py:37
  71.8 1.2 %collective-permute-start.19 = (f32[1,128,32]{1,2,0:T(8,128)S(1)}, f32[1,128,32]{1,2,0:T(8,128)S(1)}, u32[]{:S(2)}, u32[]{:S(2)}) collective-permute-start(f32[1,128,32]{1,2,0:T(8,128)S(1)} %bitcast.67), channel_id=1, source_target_pairs={{0,16},{16,0},{1,17},{17,1},{2,18},{18,2},{3,19},{19,3},{4,20},{20... | collective-permute-start | bytes 49160 | tf_op jit(solution)/shard_map/ppermute | solution.py:37

commit v6 on v5

--- a/solution.py
+++ b/solution.py
@@ -328,8 +328,9 @@
 
 
 def swap_faces(faces):
-    plan = [("gz", 0), ("gz", 1), ("gy", 0), ("gy", 1), ("gx", 0), ("gx", 1)]
-    return [swap(face, axis, first) for face, (axis, first) in zip(faces, plan)]
+    za, zb, ya, yb = faces[:4]
+    halos = [swap(za, "gz", 0), swap(zb, "gz", 1), swap(ya, "gy", 0), from_distance(yb, "gy", 3)]
+    return halos + [swap(face, "gx", first) for first, face in enumerate(faces[4:])]
 
 
 def masked(halo, axis, first):
@@ -438,18 +439,16 @@
             halos = swap_faces(faces)
             continue
         za, zb, ya, yb = faces[:4]
-        za_in = swap(za, "gz", 0)
+        za_in, zb_in = swap(za, "gz", 0), swap(zb, "gz", 1)
         sums = za[4 * count_x :] + za_in[4 * count_x :]
         pieces = jnp.concatenate([sums[:, h * 128 : h * 128 + 128] for h in range(2)], axis=0)
-        pieces, ya, zb = barrier((pieces, ya, zb))
-        zb_in = masked(swap(zb, "gz", 1), "gz", 1)
+        pieces, ya, zb_in = barrier((pieces, ya, zb_in))
         ya_in = swap(jnp.concatenate([ya, pieces], axis=0), "gy", 0)
-        ya_in, zb_in, x_faces = barrier((ya_in, zb_in, faces[4:]))
-        x_faces = [swap(face, "gx", first) for first, face in enumerate(x_faces)]
+        x_faces = [swap(face, "gx", first) for first, face in enumerate(faces[4:])]
         pieces = jnp.concatenate([pieces, ya_in[count_z:]], axis=0)
+        pieces, yb, x_faces = barrier((pieces, yb, x_faces))
         yb_in = from_distance(jnp.concatenate([yb, pieces], axis=0), "gy", 3)
         pieces = jnp.concatenate([pieces, yb_in[count_z:]], axis=0)
-        pieces, x_faces = barrier((pieces, x_faces))
         halos = [za_in, zb_in, ya_in, yb_in] + x_faces
 
     distance = 2

time: 74.6 us -> 72 us (0.965)
  starting transfers between devices: 33.9 us -> 28.5 us
  waiting for transfers between devices: 18 us -> 21.2 us
    ppermute x13 -> x12, starting transfers between devices: 18.6 us -> 13.8 us  [swap(): return lax.ppermute(value, axis, pairs)]
    ppermute x7 -> x8, waiting for transfers between devices: 7.31 us -> 10.7 us  [from_distance(): return lax.ppermute(value, axis, [(i, i ^ distance) for i in range(count)])]
    ppermute x7 -> x8, starting transfers between devices: 15.3 us -> 14.7 us  [from_distance(): return lax.ppermute(value, axis, [(i, i ^ distance) for i in range(count)])]
    ppermute x13 -> x12, waiting for transfers between devices: 10.7 us -> 10.4 us  [swap(): return lax.ppermute(value, axis, pairs)]
  transfers between devices with their start and end apart: 20 -> 20, of which waited for: 11 -> 12; matrix products, arithmetic and copies ran while one was open for 0% -> 0% of each run, Pallas kernels for 8% -> 8%
where the time goes in v6:
time: 72 us; the launch traced here: 71.8 us
  starting transfers between devices  28.5 us (40%)
  waiting for transfers between devices  21.2 us (29%)
  Pallas kernels  17.6 us (24%)
  local copies, waits for them, and re-layouts  3.22 us (4%)
  between operations  0.92 us (1%)
    pallas_call x3, Pallas kernels, shards(): pl.pallas_call(functools.partial(step_body, shape=shape, points=points, c...  16.9 us
    ppermute x8, starting transfers between devices, from_distance(): return lax.ppermute(value, axis, [(i, i ^ distance) for i in range(count)])  14.7 us
    ppermute x12, starting transfers between devices, swap(): return lax.ppermute(value, axis, pairs)  13.8 us
    ppermute x8, waiting for transfers between devices, from_distance(): return lax.ppermute(value, axis, [(i, i ^ distance) for i in range(count)])  10.7 us
    ppermute x12, waiting for transfers between devices, swap(): return lax.ppermute(value, axis, pairs)  10.4 us
    unnamed x10, local copies, waits for them, and re-layouts  2.33 us
  transfers between devices with their start and end apart: 20, of which 12 were waited for; matrix products, arithmetic and copies ran while one was open for 0% of the time, Pallas kernels for 8%

profile of v6, /device:TPU:0, one launch (start us, length us, event | category | flops | bytes accessed | tf_op | source)
XLA Modules:
  0.0 71.8 jit_solution(17149901176543561608)
XLA Ops:
  0.6 0.7 copy_bitcast_fusion
  1.4 3.1 %collective-permute-start = (f32[1,24,32]{2,1,0:T(8,128)S(1)}, f32[1,24,32]{2,1,0:T(8,128)S(1)}, u32[]{:S(2)}, u32[]{:S(2)}) collective-permute-start(f32[1,24,32]{2,1,0:T(8,128)S(1)} %fusion.5), channel_id=1, source_target_pairs={{0,1},{1,0},{2,3},{3,2},{4,5},{5,4},{6,7},{7,6},{8,9},{9,8},{10,11... | collective-permute-start | bytes 9224 | tf_op jit(solution)/shard_map/ppermute | solution.py:37
  4.5 1.6 %copy-done = f32[4,32,16,256]{3,2,1,0:T(8,128)S(1)} copy-done((f32[4,32,16,256]{3,2,1,0:T(8,128)S(1)}, f32[4,32,16,256]{3,2,1,0:T(8,128)}, u32[]{:S(2)}) %copy-start) | copy-done | bytes 2097176
  6.0 0.7 %faces.1 = (f32[128,256]{1,0:T(8,128)S(1)}, f32[128,256]{1,0:T(8,128)S(1)}, f32[16,128]{1,0:T(8,128)S(1)}, f32[16,128]{1,0:T(8,128)S(1)}, f32[4,16,256]{2,1,0:T(8,128)S(1)}) custom-call(f32[4,32,16,256]{3,2,1,0:T(8,128)S(1)} %copy-done), custom_call_target="tpu_custom_call" | custom-call | tf_op jit(solution)/shard_map/faces/pallas_call | solution.py:372
  6.8 1.3 %collective-permute-start.2 = (f32[128,256]{1,0:T(8,128)S(1)}, f32[128,256]{1,0:T(8,128)S(1)}, u32[]{:S(2)}, u32[]{:S(2)}) collective-permute-start(f32[128,256]{1,0:T(8,128)S(1)} %get-tuple-element.49), channel_id=1, source_target_pairs={{0,1},{1,0},{2,3},{3,2},{4,5},{5,4},{6,7},{7,6},{8,9},{9,8},{10,11... | collective-permute-start | bytes 393224 | tf_op jit(solution)/shard_map/ppermute | solution.py:32
  8.2 2.6 %collective-permute-start.1 = (f32[2,24,32]{2,1,0:T(8,128)S(1)}, f32[2,24,32]{2,1,0:T(8,128)S(1)}, u32[]{:S(2)}, u32[]{:S(2)}) collective-permute-start(f32[2,24,32]{2,1,0:T(8,128)S(1)} %pad_maximum_fusion.6), channel_id=1, source_target_pairs={{0,2},{1,3},{2,0},{3,1},{4,6},{5,7},{6,4},{7,5},{8,10},{9,11},{10,... | collective-permute-start | bytes 18440 | tf_op jit(solution)/shard_map/ppermute | solution.py:37
  10.7 1.3 %collective-permute-done.2 = f32[128,256]{1,0:T(8,128)S(1)} collective-permute-done((f32[128,256]{1,0:T(8,128)S(1)}, f32[128,256]{1,0:T(8,128)S(1)}, u32[]{:S(2)}, u32[]{:S(2)}) %collective-permute-start.2) | collective-permute-done | bytes 131104 | tf_op jit(solution)/shard_map/ppermute | solution.py:32
  12.1 0.9 %collective-permute-done.1 = f32[2,24,32]{2,1,0:T(8,128)S(1)} collective-permute-done((f32[2,24,32]{2,1,0:T(8,128)S(1)}, f32[2,24,32]{2,1,0:T(8,128)S(1)}, u32[]{:S(2)}, u32[]{:S(2)}) %collective-permute-start.1) | collective-permute-done | bytes 6176 | tf_op jit(solution)/shard_map/ppermute | solution.py:37
  13.2 0.7 collective-permute-start.4
  13.9 1.6 %collective-permute-start.3 = (f32[40,128]{1,0:T(8,128)S(1)}, f32[40,128]{1,0:T(8,128)S(1)}, u32[]{:S(2)}, u32[]{:S(2)}) collective-permute-start(f32[40,128]{1,0:T(8,128)S(1)} %pad_maximum_fusion.8), channel_id=1, source_target_pairs={{0,4},{4,0},{8,12},{12,8},{1,5},{5,1},{9,13},{13,9},{2,6},{6,2},{1... | collective-permute-start | bytes 61448 | tf_op jit(solution)/shard_map/ppermute | solution.py:32
  15.5 2.3 %collective-permute-done.3.refs_5_ = f32[40,128]{1,0:T(8,128)S(1)} collective-permute-done((f32[40,128]{1,0:T(8,128)S(1)}, f32[40,128]{1,0:T(8,128)S(1)}, u32[]{:S(2)}, u32[]{:S(2)}) %collective-permute-start.3) | collective-permute-done | bytes 20512 | tf_op jit(solution)/shard_map/ppermute | solution.py:32
  17.7 2.4 %collective-permute-start.5 = (f32[64,128]{1,0:T(8,128)S(1)}, f32[64,128]{1,0:T(8,128)S(1)}, u32[]{:S(2)}, u32[]{:S(2)}) collective-permute-start(f32[64,128]{1,0:T(8,128)S(1)} %pad_maximum_fusion.3), channel_id=1, source_target_pairs={{0,12},{4,8},{8,4},{12,0},{1,13},{5,9},{9,5},{13,1},{2,14},{6,10},... | collective-permute-start | bytes 98312 | tf_op jit(solution)/shard_map/ppermute | solution.py:37
  20.2 2.4 %collective-permute-done.5.refs_6_ = f32[64,128]{1,0:T(8,128)S(1)} collective-permute-done((f32[64,128]{1,0:T(8,128)S(1)}, f32[64,128]{1,0:T(8,128)S(1)}, u32[]{:S(2)}, u32[]{:S(2)}) %collective-permute-start.5) | collective-permute-done | bytes 32800 | tf_op jit(solution)/shard_map/ppermute | solution.py:37
  23.1 0.7 %collective-permute-done.6 = f32[1,96,128]{2,1,0:T(8,128)S(1)} collective-permute-done((f32[1,96,128]{2,1,0:T(8,128)S(1)}, f32[1,96,128]{2,1,0:T(8,128)S(1)}, u32[]{:S(2)}, u32[]{:S(2)}) %collective-permute-start.6) | collective-permute-done | bytes 49184 | tf_op jit(solution)/shard_map/ppermute | solution.py:37
  24.0 6.2 %step.3 = (f32[4,32,16,256]{3,2,1,0:T(8,128)S(1)}, f32[128,256]{1,0:T(8,128)S(1)}, f32[128,256]{1,0:T(8,128)S(1)}, f32[16,128]{1,0:T(8,128)S(1)}, f32[16,128]{1,...) custom-call(s32[2]{0:T(128)S(1)} %bitcast.59, f32[8,24,128]{2,1,0:T(8,128)S(1)} %bitcast.56, ...), custom_call_target="tpu_custom_call" | custom-call | tf_op jit(solution)/shard_map/step/pallas_call | solution.py:420
  30.2 4.4 %collective-permute-start.8 = (f32[128,256]{1,0:T(8,128)S(1)}, f32[128,256]{1,0:T(8,128)S(1)}, u32[]{:S(2)}, u32[]{:S(2)}) collective-permute-start(f32[128,256]{1,0:T(8,128)S(1)} %get-tuple-element.60), channel_id=1, source_target_pairs={{0,1},{1,0},{2,3},{3,2},{4,5},{5,4},{6,7},{7,6},{8,9},{9,8},{10,11... | collective-permute-start | bytes 393224 | tf_op jit(solution)/shard_map/ppermute | solution.py:32
  34.7 0.7 collective-permute-start.9
  35.5 1.5 %collective-permute-start.10 = (f32[16,128]{1,0:T(8,128)S(1)}, f32[16,128]{1,0:T(8,128)S(1)}, u32[]{:S(2)}, u32[]{:S(2)}) collective-permute-start(f32[16,128]{1,0:T(8,128)S(1)} %get-tuple-element.62), channel_id=1, source_target_pairs={{0,4},{4,0},{8,12},{12,8},{1,5},{5,1},{9,13},{13,9},{2,6},{6,2},{1... | collective-permute-start | bytes 24584 | tf_op jit(solution)/shard_map/ppermute | solution.py:32
  36.9 1.6 %collective-permute-start.11 = (f32[16,128]{1,0:T(8,128)S(1)}, f32[16,128]{1,0:T(8,128)S(1)}, u32[]{:S(2)}, u32[]{:S(2)}) collective-permute-start(f32[16,128]{1,0:T(8,128)S(1)} %get-tuple-element.63), channel_id=1, source_target_pairs={{0,12},{4,8},{8,4},{12,0},{1,13},{5,9},{9,5},{13,1},{2,14},{6,10},... | collective-permute-start | bytes 24584 | tf_op jit(solution)/shard_map/ppermute | solution.py:37
  39.1 2.4 %collective-permute-done.11.refs_6_ = f32[16,128]{1,0:T(8,128)S(1)} collective-permute-done((f32[16,128]{1,0:T(8,128)S(1)}, f32[16,128]{1,0:T(8,128)S(1)}, u32[]{:S(2)}, u32[]{:S(2)}) %collective-permute-start.11) | collective-permute-done | bytes 8224 | tf_op jit(solution)/shard_map/ppermute | solution.py:37
  41.5 5.7 %step.4 = (f32[4,32,16,256]{3,2,1,0:T(8,128)S(1)}, f32[144,256]{1,0:T(8,128)S(1)}, f32[128,256]{1,0:T(8,128)S(1)}, f32[16,128]{1,0:T(8,128)S(1)}, f32[16,128]{1,0:T(8,128)S(1)}, /*index=5*/f32[4,16,256]{2,1,0:T(8,128)S(1)}) custom-call(s32[2]{0:T(128)S(1)} %bitcast.60, f32[8,24,128]{2,1,0:T(8,128)S(1)} %bitcast.57, ...), custom_call_target="tpu_custom_call" | custom-call | tf_op jit(solution)/shard_map/step/pallas_call | solution.py:420
  47.2 1.6 %collective-permute-start.13 = (f32[144,256]{1,0:T(8,128)S(1)}, f32[144,256]{1,0:T(8,128)S(1)}, u32[]{:S(2)}, u32[]{:S(2)}) collective-permute-start(f32[144,256]{1,0:T(8,128)S(1)} %get-tuple-element.66), channel_id=1, source_target_pairs={{0,1},{1,0},{2,3},{3,2},{4,5},{5,4},{6,7},{7,6},{8,9},{9,8},{10,11... | collective-permute-start | bytes 442376 | tf_op jit(solution)/shard_map/ppermute | solution.py:32
  48.8 0.7 collective-permute-start.14
  49.5 2.9 %collective-permute-done.13.refs_3_ = f32[144,256]{1,0:T(8,128)S(1)} collective-permute-done((f32[144,256]{1,0:T(8,128)S(1)}, f32[144,256]{1,0:T(8,128)S(1)}, u32[]{:S(2)}, u32[]{:S(2)}) %collective-permute-start.13) | collective-permute-done | bytes 147488 | tf_op jit(solution)/shard_map/ppermute | solution.py:32
  52.4 0.8 %collective-permute-start.15 = (f32[48,128]{1,0:T(8,128)S(1)}, f32[48,128]{1,0:T(8,128)S(1)}, u32[]{:S(2)}, u32[]{:S(2)}) collective-permute-start(f32[48,128]{1,0:T(8,128)S(1)} %pad_maximum_fusion.7), channel_id=1, source_target_pairs={{0,4},{4,0},{8,12},{12,8},{1,5},{5,1},{9,13},{13,9},{2,6},{6,2},{1... | collective-permute-start | bytes 73736 | tf_op jit(solution)/shard_map/ppermute | solution.py:32
  53.2 3.1 %collective-permute-done.15.refs_5_ = f32[48,128]{1,0:T(8,128)S(1)} collective-permute-done((f32[48,128]{1,0:T(8,128)S(1)}, f32[48,128]{1,0:T(8,128)S(1)}, u32[]{:S(2)}, u32[]{:S(2)}) %collective-permute-start.15) | collective-permute-done | bytes 24608 | tf_op jit(solution)/shard_map/ppermute | solution.py:32
  56.4 1.8 %collective-permute-start.17 = (f32[80,128]{1,0:T(8,128)S(1)}, f32[80,128]{1,0:T(8,128)S(1)}, u32[]{:S(2)}, u32[]{:S(2)}) collective-permute-start(f32[80,128]{1,0:T(8,128)S(1)} %pad_maximum_fusion.2), channel_id=1, source_target_pairs={{0,12},{4,8},{8,4},{12,0},{1,13},{5,9},{9,5},{13,1},{2,14},{6,10},... | collective-permute-start | bytes 122888 | tf_op jit(solution)/shard_map/ppermute | solution.py:37
  58.2 3.2 %collective-permute-done.17.refs_6_ = f32[80,128]{1,0:T(8,128)S(1)} collective-permute-done((f32[80,128]{1,0:T(8,128)S(1)}, f32[80,128]{1,0:T(8,128)S(1)}, u32[]{:S(2)}, u32[]{:S(2)}) %collective-permute-start.17) | collective-permute-done | bytes 40992 | tf_op jit(solution)/shard_map/ppermute | solution.py:37
  61.3 3.1 %collective-permute-start.18 = (f32[128,128]{1,0:T(8,128)S(1)}, f32[128,128]{1,0:T(8,128)S(1)}, u32[]{:S(2)}, u32[]{:S(2)}) collective-permute-start(f32[128,128]{1,0:T(8,128)S(1)} %pad_maximum_fusion.1), channel_id=1, source_target_pairs={{0,2},{1,3},{2,0},{3,1},{4,6},{5,7},{6,4},{7,5},{8,10},{9,11},{10,... | collective-permute-start | bytes 196616 | tf_op jit(solution)/shard_map/ppermute | solution.py:37
  64.5 5.0 %step.5 = f32[4,32,16,256]{3,2,1,0:T(8,128)} custom-call(s32[2]{0:T(128)S(1)} %bitcast.61, f32[8,24,128]{2,1,0:T(8,128)S(1)} %bitcast.58, f32[4,32,16,256]{3,2,1,0:T(8,128)S(1)} %get-tuple-element.75.refs_2_, f32[144,256]{1,0:T(8,128)S(1)} %collective-permute-done.13.refs_3_, f32[128,256]{1,0:T(8,128)S(1)} %collective-permute-done.14.refs_4_, ...), custom_call_target="tpu_custom_call" | custom-call | tf_op jit(solution)/shard_map/step/pallas_call | solution.py:420
  69.8 1.2 %collective-permute-done.19 = f32[1,128,32]{1,2,0:T(8,128)S(1)} collective-permute-done((f32[1,128,32]{1,2,0:T(8,128)S(1)}, f32[1,128,32]{1,2,0:T(8,128)S(1)}, u32[]{:S(2)}, u32[]{:S(2)}) %collective-permute-start.19) | collective-permute-done | bytes 16416 | tf_op jit(solution)/shard_map/ppermute | solution.py:37
  71.1 0.6 add.42
  (59 shorter events, 2.1 us)
Async XLA Ops:
  0.6 23.4 %copy-start.2 = (s32[1,1,1,2]{3,2,1,0:T(1,128)S(1)}, s32[1,1,1,2]{3,2,1,0:T(1,128)}, u32[]{:S(2)}) copy-start(s32[1,1,1,2]{3,2,1,0:T(1,128)} %param.7) | copy-start | bytes 28
  1.4 5.4 %collective-permute-start = (f32[1,24,32]{2,1,0:T(8,128)S(1)}, f32[1,24,32]{2,1,0:T(8,128)S(1)}, u32[]{:S(2)}, u32[]{:S(2)}) collective-permute-start(f32[1,24,32]{2,1,0:T(8,128)S(1)} %fusion.5), channel_id=1, source_target_pairs={{0,1},{1,0},{2,3},{3,2},{4,5},{5,4},{6,7},{7,6},{8,9},{9,8},{10,11... | collective-permute-start | bytes 9224 | tf_op jit(solution)/shard_map/ppermute | solution.py:37
  4.5 1.6 %copy-start = (f32[4,32,16,256]{3,2,1,0:T(8,128)S(1)}, f32[4,32,16,256]{3,2,1,0:T(8,128)}, u32[]{:S(2)}) copy-start(f32[4,32,16,256]{3,2,1,0:T(8,128)} %refs_2_.1) | copy-start | bytes 6291460
  6.0 18.0 %copy-start.1 = (f32[4,32,16,256]{3,2,1,0:T(8,128)S(1)}, f32[4,32,16,256]{3,2,1,0:T(8,128)}, u32[]{:S(2)}) copy-start(f32[4,32,16,256]{3,2,1,0:T(8,128)} %refs_2_.1) | copy-start | bytes 6291460
  6.8 5.3 %collective-permute-start.2 = (f32[128,256]{1,0:T(8,128)S(1)}, f32[128,256]{1,0:T(8,128)S(1)}, u32[]{:S(2)}, u32[]{:S(2)}) collective-permute-start(f32[128,256]{1,0:T(8,128)S(1)} %get-tuple-element.49), channel_id=1, source_target_pairs={{0,1},{1,0},{2,3},{3,2},{4,5},{5,4},{6,7},{7,6},{8,9},{9,8},{10,11... | collective-permute-start | bytes 393224 | tf_op jit(solution)/shard_map/ppermute | solution.py:32
  8.2 4.9 %collective-permute-start.1 = (f32[2,24,32]{2,1,0:T(8,128)S(1)}, f32[2,24,32]{2,1,0:T(8,128)S(1)}, u32[]{:S(2)}, u32[]{:S(2)}) collective-permute-start(f32[2,24,32]{2,1,0:T(8,128)S(1)} %pad_maximum_fusion.6), channel_id=1, source_target_pairs={{0,2},{1,3},{2,0},{3,1},{4,6},{5,7},{6,4},{7,5},{8,10},{9,11},{10,... | collective-permute-start | bytes 18440 | tf_op jit(solution)/shard_map/ppermute | solution.py:37
  13.2 2.3 %collective-permute-start.4 = (f32[128,256]{1,0:T(8,128)S(1)}, f32[128,256]{1,0:T(8,128)S(1)}, u32[]{:S(2)}, u32[]{:S(2)}) collective-permute-start(f32[128,256]{1,0:T(8,128)S(1)} %get-tuple-element.53), channel_id=1, source_target_pairs={{1,2},{2,1},{5,6},{6,5},{9,10},{10,9},{13,14},{14,13},{17,18},{18,... | collective-permute-start | bytes 393224 | tf_op jit(solution)/shard_map/ppermute | solution.py:32
  13.9 3.8 %collective-permute-start.3 = (f32[40,128]{1,0:T(8,128)S(1)}, f32[40,128]{1,0:T(8,128)S(1)}, u32[]{:S(2)}, u32[]{:S(2)}) collective-permute-start(f32[40,128]{1,0:T(8,128)S(1)} %pad_maximum_fusion.8), channel_id=1, source_target_pairs={{0,4},{4,0},{8,12},{12,8},{1,5},{5,1},{9,13},{13,9},{2,6},{6,2},{1... | collective-permute-start | bytes 61448 | tf_op jit(solution)/shard_map/ppermute | solution.py:32
  17.7 4.8 %collective-permute-start.5 = (f32[64,128]{1,0:T(8,128)S(1)}, f32[64,128]{1,0:T(8,128)S(1)}, u32[]{:S(2)}, u32[]{:S(2)}) collective-permute-start(f32[64,128]{1,0:T(8,128)S(1)} %pad_maximum_fusion.3), channel_id=1, source_target_pairs={{0,12},{4,8},{8,4},{12,0},{1,13},{5,9},{9,5},{13,1},{2,14},{6,10},... | collective-permute-start | bytes 98312 | tf_op jit(solution)/shard_map/ppermute | solution.py:37
  22.6 1.3 %collective-permute-start.6 = (f32[1,96,128]{2,1,0:T(8,128)S(1)}, f32[1,96,128]{2,1,0:T(8,128)S(1)}, u32[]{:S(2)}, u32[]{:S(2)}) collective-permute-start(f32[1,96,128]{2,1,0:T(8,128)S(1)} %maximum_bitcast_fusion), channel_id=1, source_target_pairs={{0,16},{16,0},{1,17},{17,1},{2,18},{18,2},{3,19},{19,3},{4,20},{20... | collective-permute-start | bytes 147464 | tf_op jit(solution)/shard_map/ppermute | solution.py:37
  22.6 1.4 %collective-permute-start.7 = (f32[4,16,256]{2,1,0:T(8,128)S(1)}, f32[4,16,256]{2,1,0:T(8,128)S(1)}, u32[]{:S(2)}, u32[]{:S(2)}) collective-permute-start(f32[4,16,256]{2,1,0:T(8,128)S(1)} %get-tuple-element.58), channel_id=1, source_target_pairs={{0,16},{16,0},{1,17},{17,1},{2,18},{18,2},{3,19},{19,3},{4,20},{20... | collective-permute-start | bytes 196616 | tf_op jit(solution)/shard_map/ppermute | solution.py:32
  30.2 11.3 %collective-permute-start.8 = (f32[128,256]{1,0:T(8,128)S(1)}, f32[128,256]{1,0:T(8,128)S(1)}, u32[]{:S(2)}, u32[]{:S(2)}) collective-permute-start(f32[128,256]{1,0:T(8,128)S(1)} %get-tuple-element.60), channel_id=1, source_target_pairs={{0,1},{1,0},{2,3},{3,2},{4,5},{5,4},{6,7},{7,6},{8,9},{9,8},{10,11... | collective-permute-start | bytes 393224 | tf_op jit(solution)/shard_map/ppermute | solution.py:32
  34.7 6.9 %collective-permute-start.9 = (f32[128,256]{1,0:T(8,128)S(1)}, f32[128,256]{1,0:T(8,128)S(1)}, u32[]{:S(2)}, u32[]{:S(2)}) collective-permute-start(f32[128,256]{1,0:T(8,128)S(1)} %get-tuple-element.61), channel_id=1, source_target_pairs={{1,2},{2,1},{5,6},{6,5},{9,10},{10,9},{13,14},{14,13},{17,18},{18,... | collective-permute-start | bytes 393224 | tf_op jit(solution)/shard_map/ppermute | solution.py:32
  35.3 6.2 %collective-permute-start.12 = (f32[4,16,256]{2,1,0:T(8,128)S(1)}, f32[4,16,256]{2,1,0:T(8,128)S(1)}, u32[]{:S(2)}, u32[]{:S(2)}) collective-permute-start(f32[4,16,256]{2,1,0:T(8,128)S(1)} %get-tuple-element.64), channel_id=1, source_target_pairs={{0,16},{16,0},{1,17},{17,1},{2,18},{18,2},{3,19},{19,3},{4,20},{20... | collective-permute-start | bytes 196616 | tf_op jit(solution)/shard_map/ppermute | solution.py:32
  35.5 3.7 %collective-permute-start.10 = (f32[16,128]{1,0:T(8,128)S(1)}, f32[16,128]{1,0:T(8,128)S(1)}, u32[]{:S(2)}, u32[]{:S(2)}) collective-permute-start(f32[16,128]{1,0:T(8,128)S(1)} %get-tuple-element.62), channel_id=1, source_target_pairs={{0,4},{4,0},{8,12},{12,8},{1,5},{5,1},{9,13},{13,9},{2,6},{6,2},{1... | collective-permute-start | bytes 24584 | tf_op jit(solution)/shard_map/ppermute | solution.py:32
  36.9 4.5 %collective-permute-start.11 = (f32[16,128]{1,0:T(8,128)S(1)}, f32[16,128]{1,0:T(8,128)S(1)}, u32[]{:S(2)}, u32[]{:S(2)}) collective-permute-start(f32[16,128]{1,0:T(8,128)S(1)} %get-tuple-element.63), channel_id=1, source_target_pairs={{0,12},{4,8},{8,4},{12,0},{1,13},{5,9},{9,5},{13,1},{2,14},{6,10},... | collective-permute-start | bytes 24584 | tf_op jit(solution)/shard_map/ppermute | solution.py:37
  47.2 5.2 %collective-permute-start.13 = (f32[144,256]{1,0:T(8,128)S(1)}, f32[144,256]{1,0:T(8,128)S(1)}, u32[]{:S(2)}, u32[]{:S(2)}) collective-permute-start(f32[144,256]{1,0:T(8,128)S(1)} %get-tuple-element.66), channel_id=1, source_target_pairs={{0,1},{1,0},{2,3},{3,2},{4,5},{5,4},{6,7},{7,6},{8,9},{9,8},{10,11... | collective-permute-start | bytes 442376 | tf_op jit(solution)/shard_map/ppermute | solution.py:32
  48.8 3.6 %collective-permute-start.14 = (f32[128,256]{1,0:T(8,128)S(1)}, f32[128,256]{1,0:T(8,128)S(1)}, u32[]{:S(2)}, u32[]{:S(2)}) collective-permute-start(f32[128,256]{1,0:T(8,128)S(1)} %get-tuple-element.68), channel_id=1, source_target_pairs={{1,2},{2,1},{5,6},{6,5},{9,10},{10,9},{13,14},{14,13},{17,18},{18,... | collective-permute-start | bytes 393224 | tf_op jit(solution)/shard_map/ppermute | solution.py:32
  52.4 3.9 %collective-permute-start.15 = (f32[48,128]{1,0:T(8,128)S(1)}, f32[48,128]{1,0:T(8,128)S(1)}, u32[]{:S(2)}, u32[]{:S(2)}) collective-permute-start(f32[48,128]{1,0:T(8,128)S(1)} %pad_maximum_fusion.7), channel_id=1, source_target_pairs={{0,4},{4,0},{8,12},{12,8},{1,5},{5,1},{9,13},{13,9},{2,6},{6,2},{1... | collective-permute-start | bytes 73736 | tf_op jit(solution)/shard_map/ppermute | solution.py:32
  53.2 3.1 %collective-permute-start.16 = (f32[4,16,256]{2,1,0:T(8,128)S(1)}, f32[4,16,256]{2,1,0:T(8,128)S(1)}, u32[]{:S(2)}, u32[]{:S(2)}) collective-permute-start(f32[4,16,256]{2,1,0:T(8,128)S(1)} %get-tuple-element.72), channel_id=1, source_target_pairs={{0,16},{16,0},{1,17},{17,1},{2,18},{18,2},{3,19},{19,3},{4,20},{20... | collective-permute-start | bytes 196616 | tf_op jit(solution)/shard_map/ppermute | solution.py:32
  56.4 5.0 %collective-permute-start.17 = (f32[80,128]{1,0:T(8,128)S(1)}, f32[80,128]{1,0:T(8,128)S(1)}, u32[]{:S(2)}, u32[]{:S(2)}) collective-permute-start(f32[80,128]{1,0:T(8,128)S(1)} %pad_maximum_fusion.2), channel_id=1, source_target_pairs={{0,12},{4,8},{8,4},{12,0},{1,13},{5,9},{9,5},{13,1},{2,14},{6,10},... | collective-permute-start | bytes 122888 | tf_op jit(solution)/shard_map/ppermute | solution.py:37
  61.3 8.2 %collective-permute-start.18 = (f32[128,128]{1,0:T(8,128)S(1)}, f32[128,128]{1,0:T(8,128)S(1)}, u32[]{:S(2)}, u32[]{:S(2)}) collective-permute-start(f32[128,128]{1,0:T(8,128)S(1)} %pad_maximum_fusion.1), channel_id=1, source_target_pairs={{0,2},{1,3},{2,0},{3,1},{4,6},{5,7},{6,4},{7,5},{8,10},{9,11},{10,... | collective-permute-start | bytes 196616 | tf_op jit(solution)/shard_map/ppermute | solution.py:37
  69.7 1.2 %collective-permute-start.19 = (f32[1,128,32]{1,2,0:T(8,128)S(1)}, f32[1,128,32]{1,2,0:T(8,128)S(1)}, u32[]{:S(2)}, u32[]{:S(2)}) collective-permute-start(f32[1,128,32]{1,2,0:T(8,128)S(1)} %bitcast.67), channel_id=1, source_target_pairs={{0,16},{16,0},{1,17},{17,1},{2,18},{18,2},{3,19},{19,3},{4,20},{20... | collective-permute-start | bytes 49160 | tf_op jit(solution)/shard_map/ppermute | solution.py:37

commit v7 on v6

--- a/solution.py
+++ b/solution.py
@@ -141,7 +141,7 @@
     return rows_ref[...]
 
 
-def point_factors(rows, shape):
+def point_factors(rows, listed, shape):
     lanes = rows.shape[1]
 
     def factor(row, axis, count):
@@ -153,32 +153,39 @@
     count_x, count_z, count_y = shape
     factor_x = factor(rows[0:1], "gx", count_x)
     factor_y = factor(rows[1:2], "gy", count_y)
-    factor_z = factor(rows[2:3], "gz", count_z) * kernel_norm
+    factor_z = factor(rows[2:3], "gz", count_z) * jnp.where(listed, kernel_norm, 0.0)
     weights = (factor_x[:, None, :] * factor_z[None, :, :]).reshape(count_x * count_z, lanes)
     return weights, split(factor_y)
 
 
-def push(force_ref, rows, weights, factor_y, shape):
-    high, low = factor_y
-    right = jnp.concatenate([high, high, low], axis=1)
+def store_factors(rows, listed, weight_ref, right_ref, shape, along_points):
+    weights, (high, low) = point_factors(rows, listed, shape)
+    weight_ref[...] = weights.reshape(weight_ref.shape)
+    right_ref[...] = jnp.concatenate([high, high, low], axis=1 if along_points else 0)
+
+
+def push(force_ref, rows, weight_ref, right_ref, start, planes, shape):
+    count_z = shape[1]
+    weights = weight_ref[start : start + planes].reshape(planes * count_z, -1)
+    left = []
     for comp in range(3):
         first, second = split(weights * (rows[3 + comp : 4 + comp] * time_step))
-        left = jnp.concatenate([first, second, first], axis=1)
-        pushed = lax.dot_general(left, right, (((1,), (1,)), ((), ())), preferred_element_type=jnp.float32)
-        force_ref[comp] = pushed.reshape(shape)
-
-
-def sample(q_ref, weights, factor_y, shape):
-    count_x, count_z, count_y = shape
-    high, low = factor_y
-    right = jnp.concatenate([high, high, low], axis=0)
-    sums = []
+        left.append(jnp.concatenate([first, second, first], axis=1))
+    left = jnp.concatenate(left, axis=0)
+    pushed = lax.dot_general(left, right_ref[...], (((1,), (1,)), ((), ())), preferred_element_type=jnp.float32)
+    force_ref[:, start : start + planes] = pushed.reshape((3, planes) + shape[1:])
+
+
+def sample(q_ref, weight_ref, right_ref, start, planes, shape):
+    count_z = shape[1]
+    left = []
     for comp in range(3):
-        first, second = split(q_ref[comp].reshape(count_x * count_z, count_y))
-        left = jnp.concatenate([first, second, first], axis=1)
-        along = jnp.dot(left, right, preferred_element_type=jnp.float32)
-        sums.append(jnp.sum(along * weights, axis=0, keepdims=True))
-    return sums
+        first, second = split(q_ref[comp, start : start + planes].reshape(planes * count_z, -1))
+        left.append(jnp.concatenate([first, second, first], axis=1))
+    along = jnp.dot(jnp.concatenate(left, axis=0), right_ref[...], preferred_element_type=jnp.float32)
+    weights = weight_ref[start : start + planes].reshape(planes * count_z, -1)
+    rows = planes * count_z
+    return [jnp.sum(along[k * rows : (k + 1) * rows] * weights, axis=0, keepdims=True) for k in range(3)]
 
 
 def step_body(*refs, shape, points, capacity, step, steps):
@@ -197,7 +204,12 @@
         sample_ref = refs.pop(0)
     else:
         far_ref, out_ref, sems = out_ref, refs.pop(0), refs.pop(0)
-    force_ref, rows_ref, low_z_ref, high_z_ref, low_y_ref, high_y_ref, low_x_ref, high_x_ref = refs
+    force_ref, rows_ref, low_z_ref, high_z_ref, low_y_ref, high_y_ref, low_x_ref, high_x_ref = refs[:8]
+    weight_ref, push_right_ref = refs[8:10]
+    if not last:
+        next_weight_ref, sample_right_ref = refs[10:12]
+    if step == 0:
+        first_right_ref = refs[12]
     slots = sorted_slots(list_ref, capacity)
     turbines = lax.axis_size("gx") * lax.axis_size("gy")
     listed = slots[0] < turbines
@@ -207,18 +219,15 @@
         if past_ref is not None:
             sample_ref[: 3 * step + 3] = past_ref[: 3 * step + 3]
 
-    @pl.when(listed)
-    def _():
-        rows = turbine_rows(rows_ref, table_ref, slots, step, points)
-        weights, factor_y = point_factors(rows, shape)
-        push(force_ref, rows, weights, factor_y, shape)
-        if step == 0:
-            for comp, value in enumerate(sample(q_ref, weights, factor_y, shape)):
-                sample_ref[comp : comp + 1] = value
-
-    @pl.when(jnp.logical_not(listed))
-    def _():
-        force_ref[...] = jnp.zeros(force_ref.shape, jnp.float32)
+    if not last:
+        rows = turbine_rows(rows_ref, table_ref, slots, step + 1, points)
+        store_factors(rows, listed, next_weight_ref, sample_right_ref, shape, False)
+    rows = turbine_rows(rows_ref, table_ref, slots, step, points)
+    store_factors(rows, listed, weight_ref, push_right_ref, shape, True)
+    if step == 0:
+        first_right_ref[...] = jnp.concatenate(
+            [part for part in (lambda high, low: (high, high, low))(*point_factors(rows, listed, shape)[1])], axis=0
+        )
 
     even_x, even_z, even_y = is_even("gx"), is_even("gz"), is_even("gy")
     index_y = lax.axis_index("gy")
@@ -269,39 +278,37 @@
         here = pl.ds(start, count)
         return pltpu.make_async_copy(out_ref.at[:, here], far_ref.at[:, here], sems.at[number])
 
-    inner = count_x - 2
-    group = max(g for g in range(1, 11) if inner % g == 0)
-
-    def middle(trip, carry):
-        for k in range(group):
-            x = 1 + trip * group + k
-            plane(x, of_plane(x - 1), of_plane(x + 1))
+    group = max(g for g in range(1, 9) if count_x % g == 0)
+    groups = count_x // group
+    sums = [0.0] * 3
+    first_sums = [0.0] * 3
+    push(force_ref, rows, weight_ref, push_right_ref, 0, group, shape)
+    for number in range(groups):
+        start = number * group
+        if number + 1 < groups:
+            push(force_ref, rows, weight_ref, push_right_ref, start + group, group, shape)
+        if step == 0:
+            more = sample(q_ref, weight_ref, first_right_ref, start, group, shape)
+            first_sums = [a + b for a, b in zip(first_sums, more)]
+        for x in range(start, start + group):
+            minus = of_plane(x - 1) if x else lambda comp, here: low_x_ref[comp, :, here]
+            plus = of_plane(x + 1) if x < count_x - 1 else lambda comp, here: high_x_ref[comp, :, here]
+            plane(x, minus, plus)
         if last:
-            copy_out(trip, 1 + trip * group, group).start()
-        return carry
-
-    lax.fori_loop(0, inner // group, middle, 0)
-    plane(0, lambda comp, here: low_x_ref[comp, :, here], of_plane(1))
-    plane(count_x - 1, of_plane(count_x - 2), lambda comp, here: high_x_ref[comp, :, here])
-
+            copy_out(number, start, group).start()
+        elif number:
+            more = sample(out_ref, next_weight_ref, sample_right_ref, start - group, group, shape)
+            sums = [a + b for a, b in zip(sums, more)]
     if last:
-        edges = [copy_out(inner // group, 0, 1), copy_out(inner // group + 1, count_x - 1, 1)]
-        for edge in edges:
-            edge.start()
-        for trip in range(inner // group):
-            copy_out(trip, 1 + trip * group, group).wait()
-        for edge in edges:
-            edge.wait()
+        for number in range(groups):
+            copy_out(number, number * group, group).wait()
         return
-
+    more = sample(out_ref, next_weight_ref, sample_right_ref, count_x - group, group, shape)
+    for comp in range(3):
+        sample_ref[3 * step + 3 + comp : 3 * step + 4 + comp] = sums[comp] + more[comp]
+        if step == 0:
+            sample_ref[comp : comp + 1] = first_sums[comp]
     write_faces(out_ref, face_refs, shape)
-
-    @pl.when(listed)
-    def _():
-        rows = turbine_rows(rows_ref, table_ref, slots, step + 1, points)
-        weights, factor_y = point_factors(rows, shape)
-        for comp, value in enumerate(sample(out_ref, weights, factor_y, shape)):
-            sample_ref[3 * step + 3 + comp : 3 * step + 4 + comp] = value
 
     if packs:
         count = 3 * steps + 1
@@ -426,7 +433,11 @@
             + [pltpu.VMEM((3,) + shape, jnp.float32), pltpu.VMEM((8, lanes), jnp.float32)]
             + [pltpu.VMEM((4, count_y // 128, count_x, 128), jnp.float32)] * 2
             + [pltpu.VMEM((count_z, 128), jnp.float32)] * 2
-            + [pltpu.VMEM((4, count_z, count_y), jnp.float32)] * 2,
+            + [pltpu.VMEM((4, count_z, count_y), jnp.float32)] * 2
+            + [pltpu.VMEM((count_x, count_z, lanes), jnp.float32), pltpu.VMEM((count_y, 3 * lanes), jnp.bfloat16)]
+            + ([] if last else [pltpu.VMEM((count_x, count_z, lanes), jnp.float32)])
+            + ([] if last else [pltpu.VMEM((3 * count_y, lanes), jnp.bfloat16)])
+            + ([pltpu.VMEM((3 * count_y, lanes), jnp.bfloat16)] if step == 0 else []),
             compiler_params=params,
             name="step",
         )(turbines, table, q, *halos, *past)

time: 72 us -> 71 us (0.986)
  Pallas kernels: 17.6 us -> 15.4 us
  starting transfers between devices: 28.5 us -> 30.1 us
    pallas_call x3, Pallas kernels: 16.9 us -> 14.7 us  [shards(): pl.pallas_call(functools.partial(step_body, shape=shape, points=points, c...]
    ppermute x12, starting transfers between devices: 13.8 us -> 14.6 us  [swap(): return lax.ppermute(value, axis, pairs)]
where the time goes in v7:
time: 71 us; the launch traced here: 70.8 us
  starting transfers between devices  30.1 us (42%)
  waiting for transfers between devices  20.9 us (29%)
  Pallas kernels  15.4 us (22%)
  local copies, waits for them, and re-layouts  3.22 us (5%)
  between operations  0.92 us (1%)
    ppermute x8, starting transfers between devices, from_distance(): return lax.ppermute(value, axis, [(i, i ^ distance) for i in range(count)])  15.4 us
    pallas_call x3, Pallas kernels, shards(): pl.pallas_call(functools.partial(step_body, shape=shape, points=points, c...  14.7 us
    ppermute x12, starting transfers between devices, swap(): return lax.ppermute(value, axis, pairs)  14.6 us
    ppermute x8, waiting for transfers between devices, from_distance(): return lax.ppermute(value, axis, [(i, i ^ distance) for i in range(count)])  11 us
    ppermute x12, waiting for transfers between devices, swap(): return lax.ppermute(value, axis, pairs)  9.95 us
    unnamed x10, local copies, waits for them, and re-layouts  2.33 us
  transfers between devices with their start and end apart: 20, of which 12 were waited for; matrix products, arithmetic and copies ran while one was open for 0% of the time, Pallas kernels for 8%

profile of v7, /device:TPU:0, one launch (start us, length us, event | category | flops | bytes accessed | tf_op | source)
XLA Modules:
  0.0 70.8 jit_solution(4522690720028211040)
XLA Ops:
  0.6 0.7 %copy_bitcast_fusion = (f32[3,3,32]{2,1,0:T(4,128)S(1)}, f32[3,3,32]{2,1,0:T(4,128)S(1)}) fusion(f32[3,3,1,32]{3,2,1,0:T(1,128)} %param.6, f32[3,3,1,32]{3,2,1,0:T(1,128)} %param.5), kind=kLoop, calls=%fused_computation.35 | loop fusion | bytes 4608
  1.4 3.1 %collective-permute-start = (f32[1,24,32]{2,1,0:T(8,128)S(1)}, f32[1,24,32]{2,1,0:T(8,128)S(1)}, u32[]{:S(2)}, u32[]{:S(2)}) collective-permute-start(f32[1,24,32]{2,1,0:T(8,128)S(1)} %fusion.5), channel_id=1, source_target_pairs={{0,1},{1,0},{2,3},{3,2},{4,5},{5,4},{6,7},{7,6},{8,9},{9,8},{10,11... | collective-permute-start | bytes 9224 | tf_op jit(solution)/shard_map/ppermute | solution.py:37
  4.5 1.6 %copy-done = f32[4,32,16,256]{3,2,1,0:T(8,128)S(1)} copy-done((f32[4,32,16,256]{3,2,1,0:T(8,128)S(1)}, f32[4,32,16,256]{3,2,1,0:T(8,128)}, u32[]{:S(2)}) %copy-start) | copy-done | bytes 2097176
  6.0 0.7 %faces.1 = (f32[128,256]{1,0:T(8,128)S(1)}, f32[128,256]{1,0:T(8,128)S(1)}, f32[16,128]{1,0:T(8,128)S(1)}, f32[16,128]{1,0:T(8,128)S(1)}, f32[4,16,256]{2,1,0:T(8,128)S(1)}) custom-call(f32[4,32,16,256]{3,2,1,0:T(8,128)S(1)} %copy-done), custom_call_target="tpu_custom_call" | custom-call | tf_op jit(solution)/shard_map/faces/pallas_call | solution.py:379
  6.8 1.3 %collective-permute-start.2 = (f32[128,256]{1,0:T(8,128)S(1)}, f32[128,256]{1,0:T(8,128)S(1)}, u32[]{:S(2)}, u32[]{:S(2)}) collective-permute-start(f32[128,256]{1,0:T(8,128)S(1)} %get-tuple-element.49), channel_id=1, source_target_pairs={{0,1},{1,0},{2,3},{3,2},{4,5},{5,4},{6,7},{7,6},{8,9},{9,8},{10,11... | collective-permute-start | bytes 393224 | tf_op jit(solution)/shard_map/ppermute | solution.py:32
  8.2 2.6 %collective-permute-start.1 = (f32[2,24,32]{2,1,0:T(8,128)S(1)}, f32[2,24,32]{2,1,0:T(8,128)S(1)}, u32[]{:S(2)}, u32[]{:S(2)}) collective-permute-start(f32[2,24,32]{2,1,0:T(8,128)S(1)} %pad_maximum_fusion.6), channel_id=1, source_target_pairs={{0,2},{1,3},{2,0},{3,1},{4,6},{5,7},{6,4},{7,5},{8,10},{9,11},{10,... | collective-permute-start | bytes 18440 | tf_op jit(solution)/shard_map/ppermute | solution.py:37
  10.7 1.3 %collective-permute-done.2 = f32[128,256]{1,0:T(8,128)S(1)} collective-permute-done((f32[128,256]{1,0:T(8,128)S(1)}, f32[128,256]{1,0:T(8,128)S(1)}, u32[]{:S(2)}, u32[]{:S(2)}) %collective-permute-start.2) | collective-permute-done | bytes 131104 | tf_op jit(solution)/shard_map/ppermute | solution.py:32
  12.1 0.9 %collective-permute-done.1 = f32[2,24,32]{2,1,0:T(8,128)S(1)} collective-permute-done((f32[2,24,32]{2,1,0:T(8,128)S(1)}, f32[2,24,32]{2,1,0:T(8,128)S(1)}, u32[]{:S(2)}, u32[]{:S(2)}) %collective-permute-start.1) | collective-permute-done | bytes 6176 | tf_op jit(solution)/shard_map/ppermute | solution.py:37
  13.2 0.7 collective-permute-start.4
  13.9 1.6 %collective-permute-start.3 = (f32[40,128]{1,0:T(8,128)S(1)}, f32[40,128]{1,0:T(8,128)S(1)}, u32[]{:S(2)}, u32[]{:S(2)}) collective-permute-start(f32[40,128]{1,0:T(8,128)S(1)} %pad_maximum_fusion.8), channel_id=1, source_target_pairs={{0,4},{4,0},{8,12},{12,8},{1,5},{5,1},{9,13},{13,9},{2,6},{6,2},{1... | collective-permute-start | bytes 61448 | tf_op jit(solution)/shard_map/ppermute | solution.py:32
  15.5 2.3 %collective-permute-done.3.refs_5_ = f32[40,128]{1,0:T(8,128)S(1)} collective-permute-done((f32[40,128]{1,0:T(8,128)S(1)}, f32[40,128]{1,0:T(8,128)S(1)}, u32[]{:S(2)}, u32[]{:S(2)}) %collective-permute-start.3) | collective-permute-done | bytes 20512 | tf_op jit(solution)/shard_map/ppermute | solution.py:32
  17.7 2.4 %collective-permute-start.5 = (f32[64,128]{1,0:T(8,128)S(1)}, f32[64,128]{1,0:T(8,128)S(1)}, u32[]{:S(2)}, u32[]{:S(2)}) collective-permute-start(f32[64,128]{1,0:T(8,128)S(1)} %pad_maximum_fusion.3), channel_id=1, source_target_pairs={{0,12},{4,8},{8,4},{12,0},{1,13},{5,9},{9,5},{13,1},{2,14},{6,10},... | collective-permute-start | bytes 98312 | tf_op jit(solution)/shard_map/ppermute | solution.py:37
  20.2 2.4 %collective-permute-done.5.refs_6_ = f32[64,128]{1,0:T(8,128)S(1)} collective-permute-done((f32[64,128]{1,0:T(8,128)S(1)}, f32[64,128]{1,0:T(8,128)S(1)}, u32[]{:S(2)}, u32[]{:S(2)}) %collective-permute-start.5) | collective-permute-done | bytes 32800 | tf_op jit(solution)/shard_map/ppermute | solution.py:37
  23.1 0.7 %collective-permute-done.6 = f32[1,96,128]{2,1,0:T(8,128)S(1)} collective-permute-done((f32[1,96,128]{2,1,0:T(8,128)S(1)}, f32[1,96,128]{2,1,0:T(8,128)S(1)}, u32[]{:S(2)}, u32[]{:S(2)}) %collective-permute-start.6) | collective-permute-done | bytes 49184 | tf_op jit(solution)/shard_map/ppermute | solution.py:37
  24.0 5.2 %step.3 = (f32[4,32,16,256]{3,2,1,0:T(8,128)S(1)}, f32[128,256]{1,0:T(8,128)S(1)}, f32[128,256]{1,0:T(8,128)S(1)}, f32[16,128]{1,0:T(8,128)S(1)}, f32[16,128]{1,...) custom-call(s32[2]{0:T(128)S(1)} %bitcast.59, f32[8,24,128]{2,1,0:T(8,128)S(1)} %bitcast.56, ...), custom_call_target="tpu_custom_call" | custom-call | tf_op jit(solution)/shard_map/step/pallas_call | solution.py:427
  29.2 4.4 %collective-permute-start.8 = (f32[128,256]{1,0:T(8,128)S(1)}, f32[128,256]{1,0:T(8,128)S(1)}, u32[]{:S(2)}, u32[]{:S(2)}) collective-permute-start(f32[128,256]{1,0:T(8,128)S(1)} %get-tuple-element.60), channel_id=1, source_target_pairs={{0,1},{1,0},{2,3},{3,2},{4,5},{5,4},{6,7},{7,6},{8,9},{9,8},{10,11... | collective-permute-start | bytes 393224 | tf_op jit(solution)/shard_map/ppermute | solution.py:32
  33.6 0.7 collective-permute-start.9
  34.4 1.5 %collective-permute-start.10 = (f32[16,128]{1,0:T(8,128)S(1)}, f32[16,128]{1,0:T(8,128)S(1)}, u32[]{:S(2)}, u32[]{:S(2)}) collective-permute-start(f32[16,128]{1,0:T(8,128)S(1)} %get-tuple-element.62), channel_id=1, source_target_pairs={{0,4},{4,0},{8,12},{12,8},{1,5},{5,1},{9,13},{13,9},{2,6},{6,2},{1... | collective-permute-start | bytes 24584 | tf_op jit(solution)/shard_map/ppermute | solution.py:32
  35.9 1.6 %collective-permute-start.11 = (f32[16,128]{1,0:T(8,128)S(1)}, f32[16,128]{1,0:T(8,128)S(1)}, u32[]{:S(2)}, u32[]{:S(2)}) collective-permute-start(f32[16,128]{1,0:T(8,128)S(1)} %get-tuple-element.63), channel_id=1, source_target_pairs={{0,12},{4,8},{8,4},{12,0},{1,13},{5,9},{9,5},{13,1},{2,14},{6,10},... | collective-permute-start | bytes 24584 | tf_op jit(solution)/shard_map/ppermute | solution.py:37
  38.1 2.4 %collective-permute-done.11.refs_6_ = f32[16,128]{1,0:T(8,128)S(1)} collective-permute-done((f32[16,128]{1,0:T(8,128)S(1)}, f32[16,128]{1,0:T(8,128)S(1)}, u32[]{:S(2)}, u32[]{:S(2)}) %collective-permute-start.11) | collective-permute-done | bytes 8224 | tf_op jit(solution)/shard_map/ppermute | solution.py:37
  40.5 4.9 %step.4 = (f32[4,32,16,256]{3,2,1,0:T(8,128)S(1)}, f32[144,256]{1,0:T(8,128)S(1)}, f32[128,256]{1,0:T(8,128)S(1)}, f32[16,128]{1,0:T(8,128)S(1)}, f32[16,128]{1,0:T(8,128)S(1)}, /*index=5*/f32[4,16,256]{2,1,0:T(8,128)S(1)}) custom-call(s32[2]{0:T(128)S(1)} %bitcast.60, f32[8,24,128]{2,1,0:T(8,128)S(1)} %bitcast.57, ...), custom_call_target="tpu_custom_call" | custom-call | tf_op jit(solution)/shard_map/step/pallas_call | solution.py:427
  45.4 2.4 %collective-permute-start.13 = (f32[144,256]{1,0:T(8,128)S(1)}, f32[144,256]{1,0:T(8,128)S(1)}, u32[]{:S(2)}, u32[]{:S(2)}) collective-permute-start(f32[144,256]{1,0:T(8,128)S(1)} %get-tuple-element.66), channel_id=1, source_target_pairs={{0,1},{1,0},{2,3},{3,2},{4,5},{5,4},{6,7},{7,6},{8,9},{9,8},{10,11... | collective-permute-start | bytes 442376 | tf_op jit(solution)/shard_map/ppermute | solution.py:32
  47.8 0.8 %collective-permute-start.14 = (f32[128,256]{1,0:T(8,128)S(1)}, f32[128,256]{1,0:T(8,128)S(1)}, u32[]{:S(2)}, u32[]{:S(2)}) collective-permute-start(f32[128,256]{1,0:T(8,128)S(1)} %get-tuple-element.68), channel_id=1, source_target_pairs={{1,2},{2,1},{5,6},{6,5},{9,10},{10,9},{13,14},{14,13},{17,18},{18,... | collective-permute-start | bytes 393224 | tf_op jit(solution)/shard_map/ppermute | solution.py:32
  48.6 2.3 %collective-permute-done.13.refs_3_ = f32[144,256]{1,0:T(8,128)S(1)} collective-permute-done((f32[144,256]{1,0:T(8,128)S(1)}, f32[144,256]{1,0:T(8,128)S(1)}, u32[]{:S(2)}, u32[]{:S(2)}) %collective-permute-start.13) | collective-permute-done | bytes 147488 | tf_op jit(solution)/shard_map/ppermute | solution.py:32
  51.0 0.6 collective-permute-start.15
  51.6 3.3 %collective-permute-done.15.refs_5_ = f32[48,128]{1,0:T(8,128)S(1)} collective-permute-done((f32[48,128]{1,0:T(8,128)S(1)}, f32[48,128]{1,0:T(8,128)S(1)}, u32[]{:S(2)}, u32[]{:S(2)}) %collective-permute-start.15) | collective-permute-done | bytes 24608 | tf_op jit(solution)/shard_map/ppermute | solution.py:32
  54.9 1.6 %collective-permute-start.17 = (f32[80,128]{1,0:T(8,128)S(1)}, f32[80,128]{1,0:T(8,128)S(1)}, u32[]{:S(2)}, u32[]{:S(2)}) collective-permute-start(f32[80,128]{1,0:T(8,128)S(1)} %pad_maximum_fusion.2), channel_id=1, source_target_pairs={{0,12},{4,8},{8,4},{12,0},{1,13},{5,9},{9,5},{13,1},{2,14},{6,10},... | collective-permute-start | bytes 122888 | tf_op jit(solution)/shard_map/ppermute | solution.py:37
  56.4 3.4 %collective-permute-done.17.refs_6_ = f32[80,128]{1,0:T(8,128)S(1)} collective-permute-done((f32[80,128]{1,0:T(8,128)S(1)}, f32[80,128]{1,0:T(8,128)S(1)}, u32[]{:S(2)}, u32[]{:S(2)}) %collective-permute-start.17) | collective-permute-done | bytes 40992 | tf_op jit(solution)/shard_map/ppermute | solution.py:37
  59.9 4.1 %collective-permute-start.18 = (f32[128,128]{1,0:T(8,128)S(1)}, f32[128,128]{1,0:T(8,128)S(1)}, u32[]{:S(2)}, u32[]{:S(2)}) collective-permute-start(f32[128,128]{1,0:T(8,128)S(1)} %pad_maximum_fusion.1), channel_id=1, source_target_pairs={{0,2},{1,3},{2,0},{3,1},{4,6},{5,7},{6,4},{7,5},{8,10},{9,11},{10,... | collective-permute-start | bytes 196616 | tf_op jit(solution)/shard_map/ppermute | solution.py:37
  63.9 4.6 %step.5 = f32[4,32,16,256]{3,2,1,0:T(8,128)} custom-call(s32[2]{0:T(128)S(1)} %bitcast.61, f32[8,24,128]{2,1,0:T(8,128)S(1)} %bitcast.58, f32[4,32,16,256]{3,2,1,0:T(8,128)S(1)} %get-tuple-element.75.refs_2_, f32[144,256]{1,0:T(8,128)S(1)} %collective-permute-done.13.refs_3_, f32[128,256]{1,0:T(8,128)S(1)} %collective-permute-done.14.refs_4_, ...), custom_call_target="tpu_custom_call" | custom-call | tf_op jit(solution)/shard_map/step/pallas_call | solution.py:427
  68.8 1.2 %collective-permute-done.19 = f32[1,128,32]{1,2,0:T(8,128)S(1)} collective-permute-done((f32[1,128,32]{1,2,0:T(8,128)S(1)}, f32[1,128,32]{1,2,0:T(8,128)S(1)}, u32[]{:S(2)}, u32[]{:S(2)}) %collective-permute-start.19) | collective-permute-done | bytes 16416 | tf_op jit(solution)/shard_map/ppermute | solution.py:37
  70.2 0.6 add.42
  (59 shorter events, 2.1 us)
Async XLA Ops:
  0.6 23.4 %copy-start.2 = (s32[1,1,1,2]{3,2,1,0:T(1,128)S(1)}, s32[1,1,1,2]{3,2,1,0:T(1,128)}, u32[]{:S(2)}) copy-start(s32[1,1,1,2]{3,2,1,0:T(1,128)} %param.7) | copy-start | bytes 28
  1.4 5.4 %collective-permute-start = (f32[1,24,32]{2,1,0:T(8,128)S(1)}, f32[1,24,32]{2,1,0:T(8,128)S(1)}, u32[]{:S(2)}, u32[]{:S(2)}) collective-permute-start(f32[1,24,32]{2,1,0:T(8,128)S(1)} %fusion.5), channel_id=1, source_target_pairs={{0,1},{1,0},{2,3},{3,2},{4,5},{5,4},{6,7},{7,6},{8,9},{9,8},{10,11... | collective-permute-start | bytes 9224 | tf_op jit(solution)/shard_map/ppermute | solution.py:37
  4.5 1.6 %copy-start = (f32[4,32,16,256]{3,2,1,0:T(8,128)S(1)}, f32[4,32,16,256]{3,2,1,0:T(8,128)}, u32[]{:S(2)}) copy-start(f32[4,32,16,256]{3,2,1,0:T(8,128)} %refs_2_.1) | copy-start | bytes 6291460
  6.0 18.0 %copy-start.1 = (f32[4,32,16,256]{3,2,1,0:T(8,128)S(1)}, f32[4,32,16,256]{3,2,1,0:T(8,128)}, u32[]{:S(2)}) copy-start(f32[4,32,16,256]{3,2,1,0:T(8,128)} %refs_2_.1) | copy-start | bytes 6291460
  6.8 5.3 %collective-permute-start.2 = (f32[128,256]{1,0:T(8,128)S(1)}, f32[128,256]{1,0:T(8,128)S(1)}, u32[]{:S(2)}, u32[]{:S(2)}) collective-permute-start(f32[128,256]{1,0:T(8,128)S(1)} %get-tuple-element.49), channel_id=1, source_target_pairs={{0,1},{1,0},{2,3},{3,2},{4,5},{5,4},{6,7},{7,6},{8,9},{9,8},{10,11... | collective-permute-start | bytes 393224 | tf_op jit(solution)/shard_map/ppermute | solution.py:32
  8.2 4.9 %collective-permute-start.1 = (f32[2,24,32]{2,1,0:T(8,128)S(1)}, f32[2,24,32]{2,1,0:T(8,128)S(1)}, u32[]{:S(2)}, u32[]{:S(2)}) collective-permute-start(f32[2,24,32]{2,1,0:T(8,128)S(1)} %pad_maximum_fusion.6), channel_id=1, source_target_pairs={{0,2},{1,3},{2,0},{3,1},{4,6},{5,7},{6,4},{7,5},{8,10},{9,11},{10,... | collective-permute-start | bytes 18440 | tf_op jit(solution)/shard_map/ppermute | solution.py:37
  13.2 2.3 %collective-permute-start.4 = (f32[128,256]{1,0:T(8,128)S(1)}, f32[128,256]{1,0:T(8,128)S(1)}, u32[]{:S(2)}, u32[]{:S(2)}) collective-permute-start(f32[128,256]{1,0:T(8,128)S(1)} %get-tuple-element.53), channel_id=1, source_target_pairs={{1,2},{2,1},{5,6},{6,5},{9,10},{10,9},{13,14},{14,13},{17,18},{18,... | collective-permute-start | bytes 393224 | tf_op jit(solution)/shard_map/ppermute | solution.py:32
  13.9 3.8 %collective-permute-start.3 = (f32[40,128]{1,0:T(8,128)S(1)}, f32[40,128]{1,0:T(8,128)S(1)}, u32[]{:S(2)}, u32[]{:S(2)}) collective-permute-start(f32[40,128]{1,0:T(8,128)S(1)} %pad_maximum_fusion.8), channel_id=1, source_target_pairs={{0,4},{4,0},{8,12},{12,8},{1,5},{5,1},{9,13},{13,9},{2,6},{6,2},{1... | collective-permute-start | bytes 61448 | tf_op jit(solution)/shard_map/ppermute | solution.py:32
  17.7 4.8 %collective-permute-start.5 = (f32[64,128]{1,0:T(8,128)S(1)}, f32[64,128]{1,0:T(8,128)S(1)}, u32[]{:S(2)}, u32[]{:S(2)}) collective-permute-start(f32[64,128]{1,0:T(8,128)S(1)} %pad_maximum_fusion.3), channel_id=1, source_target_pairs={{0,12},{4,8},{8,4},{12,0},{1,13},{5,9},{9,5},{13,1},{2,14},{6,10},... | collective-permute-start | bytes 98312 | tf_op jit(solution)/shard_map/ppermute | solution.py:37
  22.6 1.3 %collective-permute-start.6 = (f32[1,96,128]{2,1,0:T(8,128)S(1)}, f32[1,96,128]{2,1,0:T(8,128)S(1)}, u32[]{:S(2)}, u32[]{:S(2)}) collective-permute-start(f32[1,96,128]{2,1,0:T(8,128)S(1)} %maximum_bitcast_fusion), channel_id=1, source_target_pairs={{0,16},{16,0},{1,17},{17,1},{2,18},{18,2},{3,19},{19,3},{4,20},{20... | collective-permute-start | bytes 147464 | tf_op jit(solution)/shard_map/ppermute | solution.py:37
  22.6 1.4 %collective-permute-start.7 = (f32[4,16,256]{2,1,0:T(8,128)S(1)}, f32[4,16,256]{2,1,0:T(8,128)S(1)}, u32[]{:S(2)}, u32[]{:S(2)}) collective-permute-start(f32[4,16,256]{2,1,0:T(8,128)S(1)} %get-tuple-element.58), channel_id=1, source_target_pairs={{0,16},{16,0},{1,17},{17,1},{2,18},{18,2},{3,19},{19,3},{4,20},{20... | collective-permute-start | bytes 196616 | tf_op jit(solution)/shard_map/ppermute | solution.py:32
  29.2 11.3 %collective-permute-start.8 = (f32[128,256]{1,0:T(8,128)S(1)}, f32[128,256]{1,0:T(8,128)S(1)}, u32[]{:S(2)}, u32[]{:S(2)}) collective-permute-start(f32[128,256]{1,0:T(8,128)S(1)} %get-tuple-element.60), channel_id=1, source_target_pairs={{0,1},{1,0},{2,3},{3,2},{4,5},{5,4},{6,7},{7,6},{8,9},{9,8},{10,11... | collective-permute-start | bytes 393224 | tf_op jit(solution)/shard_map/ppermute | solution.py:32
  33.6 6.9 %collective-permute-start.9 = (f32[128,256]{1,0:T(8,128)S(1)}, f32[128,256]{1,0:T(8,128)S(1)}, u32[]{:S(2)}, u32[]{:S(2)}) collective-permute-start(f32[128,256]{1,0:T(8,128)S(1)} %get-tuple-element.61), channel_id=1, source_target_pairs={{1,2},{2,1},{5,6},{6,5},{9,10},{10,9},{13,14},{14,13},{17,18},{18,... | collective-permute-start | bytes 393224 | tf_op jit(solution)/shard_map/ppermute | solution.py:32
  34.3 6.2 %collective-permute-start.12 = (f32[4,16,256]{2,1,0:T(8,128)S(1)}, f32[4,16,256]{2,1,0:T(8,128)S(1)}, u32[]{:S(2)}, u32[]{:S(2)}) collective-permute-start(f32[4,16,256]{2,1,0:T(8,128)S(1)} %get-tuple-element.64), channel_id=1, source_target_pairs={{0,16},{16,0},{1,17},{17,1},{2,18},{18,2},{3,19},{19,3},{4,20},{20... | collective-permute-start | bytes 196616 | tf_op jit(solution)/shard_map/ppermute | solution.py:32
  34.4 3.7 %collective-permute-start.10 = (f32[16,128]{1,0:T(8,128)S(1)}, f32[16,128]{1,0:T(8,128)S(1)}, u32[]{:S(2)}, u32[]{:S(2)}) collective-permute-start(f32[16,128]{1,0:T(8,128)S(1)} %get-tuple-element.62), channel_id=1, source_target_pairs={{0,4},{4,0},{8,12},{12,8},{1,5},{5,1},{9,13},{13,9},{2,6},{6,2},{1... | collective-permute-start | bytes 24584 | tf_op jit(solution)/shard_map/ppermute | solution.py:32
  35.9 4.5 %collective-permute-start.11 = (f32[16,128]{1,0:T(8,128)S(1)}, f32[16,128]{1,0:T(8,128)S(1)}, u32[]{:S(2)}, u32[]{:S(2)}) collective-permute-start(f32[16,128]{1,0:T(8,128)S(1)} %get-tuple-element.63), channel_id=1, source_target_pairs={{0,12},{4,8},{8,4},{12,0},{1,13},{5,9},{9,5},{13,1},{2,14},{6,10},... | collective-permute-start | bytes 24584 | tf_op jit(solution)/shard_map/ppermute | solution.py:37
  45.4 5.5 %collective-permute-start.13 = (f32[144,256]{1,0:T(8,128)S(1)}, f32[144,256]{1,0:T(8,128)S(1)}, u32[]{:S(2)}, u32[]{:S(2)}) collective-permute-start(f32[144,256]{1,0:T(8,128)S(1)} %get-tuple-element.66), channel_id=1, source_target_pairs={{0,1},{1,0},{2,3},{3,2},{4,5},{5,4},{6,7},{7,6},{8,9},{9,8},{10,11... | collective-permute-start | bytes 442376 | tf_op jit(solution)/shard_map/ppermute | solution.py:32
  47.8 3.1 %collective-permute-start.14 = (f32[128,256]{1,0:T(8,128)S(1)}, f32[128,256]{1,0:T(8,128)S(1)}, u32[]{:S(2)}, u32[]{:S(2)}) collective-permute-start(f32[128,256]{1,0:T(8,128)S(1)} %get-tuple-element.68), channel_id=1, source_target_pairs={{1,2},{2,1},{5,6},{6,5},{9,10},{10,9},{13,14},{14,13},{17,18},{18,... | collective-permute-start | bytes 393224 | tf_op jit(solution)/shard_map/ppermute | solution.py:32
  51.0 3.9 %collective-permute-start.15 = (f32[48,128]{1,0:T(8,128)S(1)}, f32[48,128]{1,0:T(8,128)S(1)}, u32[]{:S(2)}, u32[]{:S(2)}) collective-permute-start(f32[48,128]{1,0:T(8,128)S(1)} %pad_maximum_fusion.7), channel_id=1, source_target_pairs={{0,4},{4,0},{8,12},{12,8},{1,5},{5,1},{9,13},{13,9},{2,6},{6,2},{1... | collective-permute-start | bytes 73736 | tf_op jit(solution)/shard_map/ppermute | solution.py:32
  51.6 3.3 %collective-permute-start.16 = (f32[4,16,256]{2,1,0:T(8,128)S(1)}, f32[4,16,256]{2,1,0:T(8,128)S(1)}, u32[]{:S(2)}, u32[]{:S(2)}) collective-permute-start(f32[4,16,256]{2,1,0:T(8,128)S(1)} %get-tuple-element.72), channel_id=1, source_target_pairs={{0,16},{16,0},{1,17},{17,1},{2,18},{18,2},{3,19},{19,3},{4,20},{20... | collective-permute-start | bytes 196616 | tf_op jit(solution)/shard_map/ppermute | solution.py:32
  54.9 5.0 %collective-permute-start.17 = (f32[80,128]{1,0:T(8,128)S(1)}, f32[80,128]{1,0:T(8,128)S(1)}, u32[]{:S(2)}, u32[]{:S(2)}) collective-permute-start(f32[80,128]{1,0:T(8,128)S(1)} %pad_maximum_fusion.2), channel_id=1, source_target_pairs={{0,12},{4,8},{8,4},{12,0},{1,13},{5,9},{9,5},{13,1},{2,14},{6,10},... | collective-permute-start | bytes 122888 | tf_op jit(solution)/shard_map/ppermute | solution.py:37
  59.9 8.7 %collective-permute-start.18 = (f32[128,128]{1,0:T(8,128)S(1)}, f32[128,128]{1,0:T(8,128)S(1)}, u32[]{:S(2)}, u32[]{:S(2)}) collective-permute-start(f32[128,128]{1,0:T(8,128)S(1)} %pad_maximum_fusion.1), channel_id=1, source_target_pairs={{0,2},{1,3},{2,0},{3,1},{4,6},{5,7},{6,4},{7,5},{8,10},{9,11},{10,... | collective-permute-start | bytes 196616 | tf_op jit(solution)/shard_map/ppermute | solution.py:37
  68.7 1.2 %collective-permute-start.19 = (f32[1,128,32]{1,2,0:T(8,128)S(1)}, f32[1,128,32]{1,2,0:T(8,128)S(1)}, u32[]{:S(2)}, u32[]{:S(2)}) collective-permute-start(f32[1,128,32]{1,2,0:T(8,128)S(1)} %bitcast.67), channel_id=1, source_target_pairs={{0,16},{16,0},{1,17},{17,1},{2,18},{18,2},{3,19},{19,3},{4,20},{20... | collective-permute-start | bytes 49160 | tf_op jit(solution)/shard_map/ppermute | solution.py:37

commit v8 on v7

--- a/solution.py
+++ b/solution.py
@@ -30,6 +30,16 @@
     if not pairs:
         return jnp.zeros_like(value)
     return lax.ppermute(value, axis, pairs)
+
+
+def swap_inner(value, axis):
+    size, chips = lax.axis_size(axis), lax.axis_size("gx")
+    target = {low: high for low, high in swap_pairs(size, 1)}
+    pairs = []
+    for x in range(chips):
+        for k in range(size):
+            pairs.append((x * size + k, x * size + target[k] if k in target else (x ^ 1) * size + k))
+    return lax.ppermute(value, ("gx", axis), pairs)
 
 
 def from_distance(value, axis, distance):
@@ -225,19 +235,18 @@
     rows = turbine_rows(rows_ref, table_ref, slots, step, points)
     store_factors(rows, listed, weight_ref, push_right_ref, shape, True)
     if step == 0:
-        first_right_ref[...] = jnp.concatenate(
-            [part for part in (lambda high, low: (high, high, low))(*point_factors(rows, listed, shape)[1])], axis=0
-        )
+        high, low = point_factors(rows, listed, shape)[1]
+        first_right_ref[...] = jnp.concatenate([high, high, low], axis=0)
 
     even_x, even_z, even_y = is_even("gx"), is_even("gz"), is_even("gy")
-    index_y = lax.axis_index("gy")
+    index_y, index_z = lax.axis_index("gy"), lax.axis_index("gz")
     tiles = count_y // 128
     for comp in range(4):
         for tile in range(tiles):
             there = slice(comp * count_x, (comp + 1) * count_x), slice(tile * 128, tile * 128 + 128)
             first, second = za_ref[there], zb_ref[there]
-            low_z_ref[comp, tile] = pick(even_z, second, first)
-            high_z_ref[comp, tile] = pick(even_z, first, second)
+            low_z_ref[comp, tile] = pick(index_z == 0, 0.0, pick(even_z, second, first))
+            high_z_ref[comp, tile] = pick(index_z == lax.axis_size("gz") - 1, 0.0, pick(even_z, first, second))
     low_y_ref[...] = pick(index_y == 0, 0.0, pick(even_y, yb_ref[:count_z], ya_ref[:count_z]))
     high_y_ref[...] = pick(index_y == lax.axis_size("gy") - 1, 0.0, pick(even_y, ya_ref[:count_z], yb_ref[:count_z]))
     first = x_refs[0][...]
@@ -336,7 +345,9 @@
 
 def swap_faces(faces):
     za, zb, ya, yb = faces[:4]
-    halos = [swap(za, "gz", 0), swap(zb, "gz", 1), swap(ya, "gy", 0), from_distance(yb, "gy", 3)]
+    zb, za = swap_inner(zb, "gz"), swap(za, "gz", 0)
+    yb, ya = swap_inner(yb, "gy"), swap(ya, "gy", 0)
+    halos = [za, zb, ya, yb]
     return halos + [swap(face, "gx", first) for first, face in enumerate(faces[4:])]
 
 
@@ -397,7 +408,7 @@
     table = jnp.concatenate([table[k] for k in range(size_z)], axis=1)
     rows = 8 * steps
     zb, ya, table = barrier((zb, ya, table))
-    zb = masked(swap(zb, "gz", 1), "gz", 1)
+    zb = masked(swap_inner(zb, "gz"), "gz", 1)
     ya = swap(jnp.concatenate([ya, table], axis=0), "gy", 0)
     ya, zb = barrier((ya, zb))
     table = jnp.concatenate([table, ya[count_z:]], axis=0)
@@ -450,7 +461,7 @@
             halos = swap_faces(faces)
             continue
         za, zb, ya, yb = faces[:4]
-        za_in, zb_in = swap(za, "gz", 0), swap(zb, "gz", 1)
+        za_in, zb_in = swap(za, "gz", 0), swap_inner(zb, "gz")
         sums = za[4 * count_x :] + za_in[4 * count_x :]
         pieces = jnp.concatenate([sums[:, h * 128 : h * 128 + 128] for h in range(2)], axis=0)
         pieces, ya, zb_in = barrier((pieces, ya, zb_in))

time: 71 us -> 65.6 us (0.924)
  starting transfers between devices: 30.1 us -> 26.1 us
  waiting for transfers between devices: 20.9 us -> 19.1 us
    ppermute x8 -> x7, waiting for transfers between devices: 11 us -> 7.64 us  [from_distance(): return lax.ppermute(value, axis, [(i, i ^ distance) for i in range(count)])]
    ppermute x8 -> x7, starting transfers between devices: 15.4 us -> 13.1 us  [from_distance(): return lax.ppermute(value, axis, [(i, i ^ distance) for i in range(count)])]
    ppermute x12 -> x9, starting transfers between devices: 14.6 us -> 13 us  [swap(): return lax.ppermute(value, axis, pairs)]
    ppermute x12 -> x9, waiting for transfers between devices: 9.95 us -> 11.5 us  [swap(): return lax.ppermute(value, axis, pairs)]
  transfers between devices with their start and end apart: 20 -> 20, of which waited for: 12 -> 11; matrix products, arithmetic and copies ran while one was open for 0% -> 0% of each run, Pallas kernels for 8% -> 8%
where the time goes in v8:
time: 65.6 us; the launch traced here: 65.1 us
  starting transfers between devices  26.1 us (40%)
  waiting for transfers between devices  19.1 us (29%)
  Pallas kernels  15.4 us (23%)
  local copies, waits for them, and re-layouts  3.22 us (5%)
  between operations  0.91 us (1%)
    pallas_call x3, Pallas kernels, shards(): pl.pallas_call(functools.partial(step_body, shape=shape, points=points, c...  14.7 us
    ppermute x7, starting transfers between devices, from_distance(): return lax.ppermute(value, axis, [(i, i ^ distance) for i in range(count)])  13.1 us
    ppermute x9, starting transfers between devices, swap(): return lax.ppermute(value, axis, pairs)  13 us
    ppermute x9, waiting for transfers between devices, swap(): return lax.ppermute(value, axis, pairs)  11.5 us
    ppermute x7, waiting for transfers between devices, from_distance(): return lax.ppermute(value, axis, [(i, i ^ distance) for i in range(count)])  7.64 us
    unnamed x10, local copies, waits for them, and re-layouts  2.33 us
  transfers between devices with their start and end apart: 20, of which 11 were waited for; matrix products, arithmetic and copies ran while one was open for 0% of the time, Pallas kernels for 8%

profile of v8, /device:TPU:0, one launch (start us, length us, event | category | flops | bytes accessed | tf_op | source)
XLA Modules:
  0.0 65.1 jit_solution(18438255888596872900)
XLA Ops:
  0.6 0.7 %copy_bitcast_fusion = (f32[3,3,32]{2,1,0:T(4,128)S(1)}, f32[3,3,32]{2,1,0:T(4,128)S(1)}) fusion(f32[3,3,1,32]{3,2,1,0:T(1,128)} %param.6, f32[3,3,1,32]{3,2,1,0:T(1,128)} %param.5), kind=kLoop, calls=%fused_computation.35 | loop fusion | bytes 4608
  1.4 3.1 %collective-permute-start = (f32[1,24,32]{2,1,0:T(8,128)S(1)}, f32[1,24,32]{2,1,0:T(8,128)S(1)}, u32[]{:S(2)}, u32[]{:S(2)}) collective-permute-start(f32[1,24,32]{2,1,0:T(8,128)S(1)} %fusion.5), channel_id=1, source_target_pairs={{0,1},{1,0},{2,3},{3,2},{4,5},{5,4},{6,7},{7,6},{8,9},{9,8},{10,11... | collective-permute-start | bytes 9224 | tf_op jit(solution)/shard_map/ppermute | solution.py:47
  4.5 1.6 %copy-done = f32[4,32,16,256]{3,2,1,0:T(8,128)S(1)} copy-done((f32[4,32,16,256]{3,2,1,0:T(8,128)S(1)}, f32[4,32,16,256]{3,2,1,0:T(8,128)}, u32[]{:S(2)}) %copy-start) | copy-done | bytes 2097176
  6.0 0.7 %faces.1 = (f32[128,256]{1,0:T(8,128)S(1)}, f32[128,256]{1,0:T(8,128)S(1)}, f32[16,128]{1,0:T(8,128)S(1)}, f32[16,128]{1,0:T(8,128)S(1)}, f32[4,16,256]{2,1,0:T(8,128)S(1)}) custom-call(f32[4,32,16,256]{3,2,1,0:T(8,128)S(1)} %copy-done), custom_call_target="tpu_custom_call" | custom-call | tf_op jit(solution)/shard_map/faces/pallas_call | solution.py:390
  6.8 1.3 %collective-permute-start.2 = (f32[128,256]{1,0:T(8,128)S(1)}, f32[128,256]{1,0:T(8,128)S(1)}, u32[]{:S(2)}, u32[]{:S(2)}) collective-permute-start(f32[128,256]{1,0:T(8,128)S(1)} %get-tuple-element.49), channel_id=1, source_target_pairs={{0,1},{1,0},{2,3},{3,2},{4,5},{5,4},{6,7},{7,6},{8,9},{9,8},{10,11... | collective-permute-start | bytes 393224 | tf_op jit(solution)/shard_map/ppermute | solution.py:32
  8.2 2.6 %collective-permute-start.1 = (f32[2,24,32]{2,1,0:T(8,128)S(1)}, f32[2,24,32]{2,1,0:T(8,128)S(1)}, u32[]{:S(2)}, u32[]{:S(2)}) collective-permute-start(f32[2,24,32]{2,1,0:T(8,128)S(1)} %pad_maximum_fusion.6), channel_id=1, source_target_pairs={{0,2},{1,3},{2,0},{3,1},{4,6},{5,7},{6,4},{7,5},{8,10},{9,11},{10,... | collective-permute-start | bytes 18440 | tf_op jit(solution)/shard_map/ppermute | solution.py:47
  10.7 1.3 %collective-permute-done.2 = f32[128,256]{1,0:T(8,128)S(1)} collective-permute-done((f32[128,256]{1,0:T(8,128)S(1)}, f32[128,256]{1,0:T(8,128)S(1)}, u32[]{:S(2)}, u32[]{:S(2)}) %collective-permute-start.2) | collective-permute-done | bytes 131104 | tf_op jit(solution)/shard_map/ppermute | solution.py:32
  12.1 0.9 %collective-permute-done.1 = f32[2,24,32]{2,1,0:T(8,128)S(1)} collective-permute-done((f32[2,24,32]{2,1,0:T(8,128)S(1)}, f32[2,24,32]{2,1,0:T(8,128)S(1)}, u32[]{:S(2)}, u32[]{:S(2)}) %collective-permute-start.1) | collective-permute-done | bytes 6176 | tf_op jit(solution)/shard_map/ppermute | solution.py:47
  13.2 1.6 %collective-permute-start.3 = (f32[40,128]{1,0:T(8,128)S(1)}, f32[40,128]{1,0:T(8,128)S(1)}, u32[]{:S(2)}, u32[]{:S(2)}) collective-permute-start(f32[40,128]{1,0:T(8,128)S(1)} %pad_maximum_fusion.8), channel_id=1, source_target_pairs={{0,4},{4,0},{8,12},{12,8},{1,5},{5,1},{9,13},{13,9},{2,6},{6,2},{1... | collective-permute-start | bytes 61448 | tf_op jit(solution)/shard_map/ppermute | solution.py:32
  14.8 2.3 %collective-permute-done.3.refs_5_ = f32[40,128]{1,0:T(8,128)S(1)} collective-permute-done((f32[40,128]{1,0:T(8,128)S(1)}, f32[40,128]{1,0:T(8,128)S(1)}, u32[]{:S(2)}, u32[]{:S(2)}) %collective-permute-start.3) | collective-permute-done | bytes 20512 | tf_op jit(solution)/shard_map/ppermute | solution.py:32
  17.1 2.4 %collective-permute-start.5 = (f32[64,128]{1,0:T(8,128)S(1)}, f32[64,128]{1,0:T(8,128)S(1)}, u32[]{:S(2)}, u32[]{:S(2)}) collective-permute-start(f32[64,128]{1,0:T(8,128)S(1)} %pad_maximum_fusion.3), channel_id=1, source_target_pairs={{0,12},{4,8},{8,4},{12,0},{1,13},{5,9},{9,5},{13,1},{2,14},{6,10},... | collective-permute-start | bytes 98312 | tf_op jit(solution)/shard_map/ppermute | solution.py:47
  19.5 2.4 %collective-permute-done.5.refs_6_ = f32[64,128]{1,0:T(8,128)S(1)} collective-permute-done((f32[64,128]{1,0:T(8,128)S(1)}, f32[64,128]{1,0:T(8,128)S(1)}, u32[]{:S(2)}, u32[]{:S(2)}) %collective-permute-start.5) | collective-permute-done | bytes 32800 | tf_op jit(solution)/shard_map/ppermute | solution.py:47
  22.0 0.5 collective-permute-start.7
  22.5 0.7 %collective-permute-done.6 = f32[1,96,128]{2,1,0:T(8,128)S(1)} collective-permute-done((f32[1,96,128]{2,1,0:T(8,128)S(1)}, f32[1,96,128]{2,1,0:T(8,128)S(1)}, u32[]{:S(2)}, u32[]{:S(2)}) %collective-permute-start.6) | collective-permute-done | bytes 49184 | tf_op jit(solution)/shard_map/ppermute | solution.py:47
  23.2 0.2 collective-permute-done.7.refs_7_
  23.4 5.2 %step.3 = (f32[4,32,16,256]{3,2,1,0:T(8,128)S(1)}, f32[128,256]{1,0:T(8,128)S(1)}, f32[128,256]{1,0:T(8,128)S(1)}, f32[16,128]{1,0:T(8,128)S(1)}, f32[16,128]{1,...) custom-call(s32[2]{0:T(128)S(1)} %bitcast.59, f32[8,24,128]{2,1,0:T(8,128)S(1)} %bitcast.56, ...), custom_call_target="tpu_custom_call" | custom-call | tf_op jit(solution)/shard_map/step/pallas_call | solution.py:438
  28.6 3.2 %collective-permute-start.8 = (f32[128,256]{1,0:T(8,128)S(1)}, f32[128,256]{1,0:T(8,128)S(1)}, u32[]{:S(2)}, u32[]{:S(2)}) collective-permute-start(f32[128,256]{1,0:T(8,128)S(1)} %get-tuple-element.60), channel_id=1, source_target_pairs={{0,1},{1,0},{2,3},{3,2},{4,5},{5,4},{6,7},{7,6},{8,9},{9,8},{10,11... | collective-permute-start | bytes 393224 | tf_op jit(solution)/shard_map/ppermute | solution.py:32
  31.8 0.4 collective-permute-start.12
  32.3 1.5 %collective-permute-start.10 = (f32[16,128]{1,0:T(8,128)S(1)}, f32[16,128]{1,0:T(8,128)S(1)}, u32[]{:S(2)}, u32[]{:S(2)}) collective-permute-start(f32[16,128]{1,0:T(8,128)S(1)} %get-tuple-element.62), channel_id=1, source_target_pairs={{0,4},{4,0},{8,12},{12,8},{1,5},{5,1},{9,13},{13,9},{2,6},{6,2},{1... | collective-permute-start | bytes 24584 | tf_op jit(solution)/shard_map/ppermute | solution.py:32
  33.8 2.2 %collective-permute-done.10.refs_5_ = f32[16,128]{1,0:T(8,128)S(1)} collective-permute-done((f32[16,128]{1,0:T(8,128)S(1)}, f32[16,128]{1,0:T(8,128)S(1)}, u32[]{:S(2)}, u32[]{:S(2)}) %collective-permute-start.10) | collective-permute-done | bytes 8224 | tf_op jit(solution)/shard_map/ppermute | solution.py:32
  35.9 4.9 %step.4 = (f32[4,32,16,256]{3,2,1,0:T(8,128)S(1)}, f32[144,256]{1,0:T(8,128)S(1)}, f32[128,256]{1,0:T(8,128)S(1)}, f32[16,128]{1,0:T(8,128)S(1)}, f32[16,128]{1,0:T(8,128)S(1)}, /*index=5*/f32[4,16,256]{2,1,0:T(8,128)S(1)}) custom-call(s32[2]{0:T(128)S(1)} %bitcast.60, f32[8,24,128]{2,1,0:T(8,128)S(1)} %bitcast.57, ...), custom_call_target="tpu_custom_call" | custom-call | tf_op jit(solution)/shard_map/step/pallas_call | solution.py:438
  40.8 1.7 %collective-permute-start.13 = (f32[144,256]{1,0:T(8,128)S(1)}, f32[144,256]{1,0:T(8,128)S(1)}, u32[]{:S(2)}, u32[]{:S(2)}) collective-permute-start(f32[144,256]{1,0:T(8,128)S(1)} %get-tuple-element.66), channel_id=1, source_target_pairs={{0,1},{1,0},{2,3},{3,2},{4,5},{5,4},{6,7},{7,6},{8,9},{9,8},{10,11... | collective-permute-start | bytes 442376 | tf_op jit(solution)/shard_map/ppermute | solution.py:32
  42.5 3.7 %collective-permute-done.13.refs_3_ = f32[144,256]{1,0:T(8,128)S(1)} collective-permute-done((f32[144,256]{1,0:T(8,128)S(1)}, f32[144,256]{1,0:T(8,128)S(1)}, u32[]{:S(2)}, u32[]{:S(2)}) %collective-permute-start.13) | collective-permute-done | bytes 147488 | tf_op jit(solution)/shard_map/ppermute | solution.py:32
  46.3 2.8 %collective-permute-start.15 = (f32[48,128]{1,0:T(8,128)S(1)}, f32[48,128]{1,0:T(8,128)S(1)}, u32[]{:S(2)}, u32[]{:S(2)}) collective-permute-start(f32[48,128]{1,0:T(8,128)S(1)} %pad_maximum_fusion.7), channel_id=1, source_target_pairs={{0,4},{4,0},{8,12},{12,8},{1,5},{5,1},{9,13},{13,9},{2,6},{6,2},{1... | collective-permute-start | bytes 73736 | tf_op jit(solution)/shard_map/ppermute | solution.py:32
  49.1 1.8 %collective-permute-done.15.refs_5_ = f32[48,128]{1,0:T(8,128)S(1)} collective-permute-done((f32[48,128]{1,0:T(8,128)S(1)}, f32[48,128]{1,0:T(8,128)S(1)}, u32[]{:S(2)}, u32[]{:S(2)}) %collective-permute-start.15) | collective-permute-done | bytes 24608 | tf_op jit(solution)/shard_map/ppermute | solution.py:32
  50.9 2.5 %collective-permute-start.17 = (f32[80,128]{1,0:T(8,128)S(1)}, f32[80,128]{1,0:T(8,128)S(1)}, u32[]{:S(2)}, u32[]{:S(2)}) collective-permute-start(f32[80,128]{1,0:T(8,128)S(1)} %pad_maximum_fusion.2), channel_id=1, source_target_pairs={{0,12},{4,8},{8,4},{12,0},{1,13},{5,9},{9,5},{13,1},{2,14},{6,10},... | collective-permute-start | bytes 122888 | tf_op jit(solution)/shard_map/ppermute | solution.py:47
  53.4 2.5 %collective-permute-done.17.refs_6_ = f32[80,128]{1,0:T(8,128)S(1)} collective-permute-done((f32[80,128]{1,0:T(8,128)S(1)}, f32[80,128]{1,0:T(8,128)S(1)}, u32[]{:S(2)}, u32[]{:S(2)}) %collective-permute-start.17) | collective-permute-done | bytes 40992 | tf_op jit(solution)/shard_map/ppermute | solution.py:47
  55.9 2.3 %collective-permute-start.18 = (f32[128,128]{1,0:T(8,128)S(1)}, f32[128,128]{1,0:T(8,128)S(1)}, u32[]{:S(2)}, u32[]{:S(2)}) collective-permute-start(f32[128,128]{1,0:T(8,128)S(1)} %pad_maximum_fusion.1), channel_id=1, source_target_pairs={{0,2},{1,3},{2,0},{3,1},{4,6},{5,7},{6,4},{7,5},{8,10},{9,11},{10,... | collective-permute-start | bytes 196616 | tf_op jit(solution)/shard_map/ppermute | solution.py:47
  58.2 4.6 %step.5 = f32[4,32,16,256]{3,2,1,0:T(8,128)} custom-call(s32[2]{0:T(128)S(1)} %bitcast.61, f32[8,24,128]{2,1,0:T(8,128)S(1)} %bitcast.58, f32[4,32,16,256]{3,2,1,0:T(8,128)S(1)} %get-tuple-element.75.refs_2_, f32[144,256]{1,0:T(8,128)S(1)} %collective-permute-done.13.refs_3_, f32[128,256]{1,0:T(8,128)S(1)} %collective-permute-done.14.refs_4_, ...), custom_call_target="tpu_custom_call" | custom-call | tf_op jit(solution)/shard_map/step/pallas_call | solution.py:438
  63.1 1.2 %collective-permute-done.19 = f32[1,128,32]{1,2,0:T(8,128)S(1)} collective-permute-done((f32[1,128,32]{1,2,0:T(8,128)S(1)}, f32[1,128,32]{1,2,0:T(8,128)S(1)}, u32[]{:S(2)}, u32[]{:S(2)}) %collective-permute-start.19) | collective-permute-done | bytes 16416 | tf_op jit(solution)/shard_map/ppermute | solution.py:47
  64.3 0.1 copy.14
  64.5 0.6 add.42
  (59 shorter events, 0.7 us)
Async XLA Ops:
  0.6 22.8 %copy-start.2 = (s32[1,1,1,2]{3,2,1,0:T(1,128)S(1)}, s32[1,1,1,2]{3,2,1,0:T(1,128)}, u32[]{:S(2)}) copy-start(s32[1,1,1,2]{3,2,1,0:T(1,128)} %param.7) | copy-start | bytes 28
  1.4 5.4 %collective-permute-start = (f32[1,24,32]{2,1,0:T(8,128)S(1)}, f32[1,24,32]{2,1,0:T(8,128)S(1)}, u32[]{:S(2)}, u32[]{:S(2)}) collective-permute-start(f32[1,24,32]{2,1,0:T(8,128)S(1)} %fusion.5), channel_id=1, source_target_pairs={{0,1},{1,0},{2,3},{3,2},{4,5},{5,4},{6,7},{7,6},{8,9},{9,8},{10,11... | collective-permute-start | bytes 9224 | tf_op jit(solution)/shard_map/ppermute | solution.py:47
  4.5 1.6 %copy-start = (f32[4,32,16,256]{3,2,1,0:T(8,128)S(1)}, f32[4,32,16,256]{3,2,1,0:T(8,128)}, u32[]{:S(2)}) copy-start(f32[4,32,16,256]{3,2,1,0:T(8,128)} %refs_2_.1) | copy-start | bytes 6291460
  6.0 17.4 %copy-start.1 = (f32[4,32,16,256]{3,2,1,0:T(8,128)S(1)}, f32[4,32,16,256]{3,2,1,0:T(8,128)}, u32[]{:S(2)}) copy-start(f32[4,32,16,256]{3,2,1,0:T(8,128)} %refs_2_.1) | copy-start | bytes 6291460
  6.8 5.3 %collective-permute-start.2 = (f32[128,256]{1,0:T(8,128)S(1)}, f32[128,256]{1,0:T(8,128)S(1)}, u32[]{:S(2)}, u32[]{:S(2)}) collective-permute-start(f32[128,256]{1,0:T(8,128)S(1)} %get-tuple-element.49), channel_id=1, source_target_pairs={{0,1},{1,0},{2,3},{3,2},{4,5},{5,4},{6,7},{7,6},{8,9},{9,8},{10,11... | collective-permute-start | bytes 393224 | tf_op jit(solution)/shard_map/ppermute | solution.py:32
  8.2 4.9 %collective-permute-start.1 = (f32[2,24,32]{2,1,0:T(8,128)S(1)}, f32[2,24,32]{2,1,0:T(8,128)S(1)}, u32[]{:S(2)}, u32[]{:S(2)}) collective-permute-start(f32[2,24,32]{2,1,0:T(8,128)S(1)} %pad_maximum_fusion.6), channel_id=1, source_target_pairs={{0,2},{1,3},{2,0},{3,1},{4,6},{5,7},{6,4},{7,5},{8,10},{9,11},{10,... | collective-permute-start | bytes 18440 | tf_op jit(solution)/shard_map/ppermute | solution.py:47
  13.2 1.6 %collective-permute-start.4 = (f32[128,256]{1,0:T(8,128)S(1)}, f32[128,256]{1,0:T(8,128)S(1)}, u32[]{:S(2)}, u32[]{:S(2)}) collective-permute-start(f32[128,256]{1,0:T(8,128)S(1)} %get-tuple-element.53), channel_id=1, source_target_pairs={{0,16},{1,2},{2,1},{3,19},{16,0},{17,18},{18,17},{19,3},{4,20},{5,... | collective-permute-start | bytes 393224 | tf_op jit(solution)/shard_map/ppermute | solution.py:42
  13.2 3.8 %collective-permute-start.3 = (f32[40,128]{1,0:T(8,128)S(1)}, f32[40,128]{1,0:T(8,128)S(1)}, u32[]{:S(2)}, u32[]{:S(2)}) collective-permute-start(f32[40,128]{1,0:T(8,128)S(1)} %pad_maximum_fusion.8), channel_id=1, source_target_pairs={{0,4},{4,0},{8,12},{12,8},{1,5},{5,1},{9,13},{13,9},{2,6},{6,2},{1... | collective-permute-start | bytes 61448 | tf_op jit(solution)/shard_map/ppermute | solution.py:32
  17.1 4.8 %collective-permute-start.5 = (f32[64,128]{1,0:T(8,128)S(1)}, f32[64,128]{1,0:T(8,128)S(1)}, u32[]{:S(2)}, u32[]{:S(2)}) collective-permute-start(f32[64,128]{1,0:T(8,128)S(1)} %pad_maximum_fusion.3), channel_id=1, source_target_pairs={{0,12},{4,8},{8,4},{12,0},{1,13},{5,9},{9,5},{13,1},{2,14},{6,10},... | collective-permute-start | bytes 98312 | tf_op jit(solution)/shard_map/ppermute | solution.py:47
  21.9 1.3 %collective-permute-start.6 = (f32[1,96,128]{2,1,0:T(8,128)S(1)}, f32[1,96,128]{2,1,0:T(8,128)S(1)}, u32[]{:S(2)}, u32[]{:S(2)}) collective-permute-start(f32[1,96,128]{2,1,0:T(8,128)S(1)} %maximum_bitcast_fusion), channel_id=1, source_target_pairs={{0,16},{16,0},{1,17},{17,1},{2,18},{18,2},{3,19},{19,3},{4,20},{20... | collective-permute-start | bytes 147464 | tf_op jit(solution)/shard_map/ppermute | solution.py:47
  22.0 1.4 %collective-permute-start.7 = (f32[4,16,256]{2,1,0:T(8,128)S(1)}, f32[4,16,256]{2,1,0:T(8,128)S(1)}, u32[]{:S(2)}, u32[]{:S(2)}) collective-permute-start(f32[4,16,256]{2,1,0:T(8,128)S(1)} %get-tuple-element.58), channel_id=1, source_target_pairs={{0,16},{16,0},{1,17},{17,1},{2,18},{18,2},{3,19},{19,3},{4,20},{20... | collective-permute-start | bytes 196616 | tf_op jit(solution)/shard_map/ppermute | solution.py:32
  28.6 7.4 %collective-permute-start.8 = (f32[128,256]{1,0:T(8,128)S(1)}, f32[128,256]{1,0:T(8,128)S(1)}, u32[]{:S(2)}, u32[]{:S(2)}) collective-permute-start(f32[128,256]{1,0:T(8,128)S(1)} %get-tuple-element.60), channel_id=1, source_target_pairs={{0,1},{1,0},{2,3},{3,2},{4,5},{5,4},{6,7},{7,6},{8,9},{9,8},{10,11... | collective-permute-start | bytes 393224 | tf_op jit(solution)/shard_map/ppermute | solution.py:32
  31.8 4.2 %collective-permute-start.9 = (f32[128,256]{1,0:T(8,128)S(1)}, f32[128,256]{1,0:T(8,128)S(1)}, u32[]{:S(2)}, u32[]{:S(2)}) collective-permute-start(f32[128,256]{1,0:T(8,128)S(1)} %get-tuple-element.61), channel_id=1, source_target_pairs={{0,16},{1,2},{2,1},{3,19},{16,0},{17,18},{18,17},{19,3},{4,20},{5,... | collective-permute-start | bytes 393224 | tf_op jit(solution)/shard_map/ppermute | solution.py:42
  31.8 4.1 %collective-permute-start.12 = (f32[4,16,256]{2,1,0:T(8,128)S(1)}, f32[4,16,256]{2,1,0:T(8,128)S(1)}, u32[]{:S(2)}, u32[]{:S(2)}) collective-permute-start(f32[4,16,256]{2,1,0:T(8,128)S(1)} %get-tuple-element.64), channel_id=1, source_target_pairs={{0,16},{16,0},{1,17},{17,1},{2,18},{18,2},{3,19},{19,3},{4,20},{20... | collective-permute-start | bytes 196616 | tf_op jit(solution)/shard_map/ppermute | solution.py:32
  32.3 3.7 %collective-permute-start.10 = (f32[16,128]{1,0:T(8,128)S(1)}, f32[16,128]{1,0:T(8,128)S(1)}, u32[]{:S(2)}, u32[]{:S(2)}) collective-permute-start(f32[16,128]{1,0:T(8,128)S(1)} %get-tuple-element.62), channel_id=1, source_target_pairs={{0,4},{4,0},{8,12},{12,8},{1,5},{5,1},{9,13},{13,9},{2,6},{6,2},{1... | collective-permute-start | bytes 24584 | tf_op jit(solution)/shard_map/ppermute | solution.py:32
  33.8 2.2 %collective-permute-start.11 = (f32[16,128]{1,0:T(8,128)S(1)}, f32[16,128]{1,0:T(8,128)S(1)}, u32[]{:S(2)}, u32[]{:S(2)}) collective-permute-start(f32[16,128]{1,0:T(8,128)S(1)} %get-tuple-element.63), channel_id=1, source_target_pairs={{0,16},{4,8},{8,4},{12,28},{16,0},{20,24},{24,20},{28,12},{1,17},{... | collective-permute-start | bytes 24584 | tf_op jit(solution)/shard_map/ppermute | solution.py:42
  40.8 5.4 %collective-permute-start.13 = (f32[144,256]{1,0:T(8,128)S(1)}, f32[144,256]{1,0:T(8,128)S(1)}, u32[]{:S(2)}, u32[]{:S(2)}) collective-permute-start(f32[144,256]{1,0:T(8,128)S(1)} %get-tuple-element.66), channel_id=1, source_target_pairs={{0,1},{1,0},{2,3},{3,2},{4,5},{5,4},{6,7},{7,6},{8,9},{9,8},{10,11... | collective-permute-start | bytes 442376 | tf_op jit(solution)/shard_map/ppermute | solution.py:32
  42.5 3.7 %collective-permute-start.14 = (f32[128,256]{1,0:T(8,128)S(1)}, f32[128,256]{1,0:T(8,128)S(1)}, u32[]{:S(2)}, u32[]{:S(2)}) collective-permute-start(f32[128,256]{1,0:T(8,128)S(1)} %get-tuple-element.68), channel_id=1, source_target_pairs={{0,16},{1,2},{2,1},{3,19},{16,0},{17,18},{18,17},{19,3},{4,20},{5,... | collective-permute-start | bytes 393224 | tf_op jit(solution)/shard_map/ppermute | solution.py:42
  46.3 4.6 %collective-permute-start.15 = (f32[48,128]{1,0:T(8,128)S(1)}, f32[48,128]{1,0:T(8,128)S(1)}, u32[]{:S(2)}, u32[]{:S(2)}) collective-permute-start(f32[48,128]{1,0:T(8,128)S(1)} %pad_maximum_fusion.7), channel_id=1, source_target_pairs={{0,4},{4,0},{8,12},{12,8},{1,5},{5,1},{9,13},{13,9},{2,6},{6,2},{1... | collective-permute-start | bytes 73736 | tf_op jit(solution)/shard_map/ppermute | solution.py:32
  49.1 1.8 %collective-permute-start.16 = (f32[4,16,256]{2,1,0:T(8,128)S(1)}, f32[4,16,256]{2,1,0:T(8,128)S(1)}, u32[]{:S(2)}, u32[]{:S(2)}) collective-permute-start(f32[4,16,256]{2,1,0:T(8,128)S(1)} %get-tuple-element.72), channel_id=1, source_target_pairs={{0,16},{16,0},{1,17},{17,1},{2,18},{18,2},{3,19},{19,3},{4,20},{20... | collective-permute-start | bytes 196616 | tf_op jit(solution)/shard_map/ppermute | solution.py:32
  50.9 5.0 %collective-permute-start.17 = (f32[80,128]{1,0:T(8,128)S(1)}, f32[80,128]{1,0:T(8,128)S(1)}, u32[]{:S(2)}, u32[]{:S(2)}) collective-permute-start(f32[80,128]{1,0:T(8,128)S(1)} %pad_maximum_fusion.2), channel_id=1, source_target_pairs={{0,12},{4,8},{8,4},{12,0},{1,13},{5,9},{9,5},{13,1},{2,14},{6,10},... | collective-permute-start | bytes 122888 | tf_op jit(solution)/shard_map/ppermute | solution.py:47
  55.9 7.0 %collective-permute-start.18 = (f32[128,128]{1,0:T(8,128)S(1)}, f32[128,128]{1,0:T(8,128)S(1)}, u32[]{:S(2)}, u32[]{:S(2)}) collective-permute-start(f32[128,128]{1,0:T(8,128)S(1)} %pad_maximum_fusion.1), channel_id=1, source_target_pairs={{0,2},{1,3},{2,0},{3,1},{4,6},{5,7},{6,4},{7,5},{8,10},{9,11},{10,... | collective-permute-start | bytes 196616 | tf_op jit(solution)/shard_map/ppermute | solution.py:47
  63.0 1.2 %collective-permute-start.19 = (f32[1,128,32]{1,2,0:T(8,128)S(1)}, f32[1,128,32]{1,2,0:T(8,128)S(1)}, u32[]{:S(2)}, u32[]{:S(2)}) collective-permute-start(f32[1,128,32]{1,2,0:T(8,128)S(1)} %bitcast.67), channel_id=1, source_target_pairs={{0,16},{16,0},{1,17},{17,1},{2,18},{18,2},{3,19},{19,3},{4,20},{20... | collective-permute-start | bytes 49160 | tf_op jit(solution)/shard_map/ppermute | solution.py:47

commit v9 on v8

--- a/solution.py
+++ b/solution.py
@@ -47,8 +47,7 @@
     return lax.ppermute(value, axis, [(i, i ^ distance) for i in range(count)])
 
 
-def gather_relative(value, axis):
-    distance = 1
+def gather_relative(value, axis, distance=1):
     while distance < lax.axis_size(axis):
         value = jnp.concatenate([value, from_distance(value, axis, distance)], axis=0)
         distance *= 2
@@ -146,7 +145,7 @@
         t = jnp.minimum(slot, size_x * size_y - 1)
         place_x = lax.bitwise_xor(lax.div(t, size_y), lax.axis_index("gx"))
         place_y = lax.bitwise_xor(lax.rem(t, size_y), lax.axis_index("gy"))
-        entry = place_x * size_y + lax.bitwise_xor(place_y, lax.div(place_y, 2))
+        entry = place_x * size_y + place_y
         rows_ref[:, j * points : (j + 1) * points] = table_ref[entry, 8 * step : 8 * step + 8, :]
     return rows_ref[...]
 
@@ -407,14 +406,14 @@
     table = true_order(table, "gz")
     table = jnp.concatenate([table[k] for k in range(size_z)], axis=1)
     rows = 8 * steps
-    zb, ya, table = barrier((zb, ya, table))
+    zb, yb, ya, table = barrier((zb, yb, ya, table))
     zb = masked(swap_inner(zb, "gz"), "gz", 1)
+    yb = swap_inner(yb, "gy")
     ya = swap(jnp.concatenate([ya, table], axis=0), "gy", 0)
-    ya, zb = barrier((ya, zb))
-    table = jnp.concatenate([table, ya[count_z:]], axis=0)
-    yb = from_distance(jnp.concatenate([yb, table], axis=0), "gy", 3)
+    ya, zb, yb = barrier((ya, zb, yb))
+    table = jnp.concatenate([table, ya[count_z:]], axis=0).reshape(2, rows, points)
+    table = gather_relative(table, "gy", 2)
     x_faces = [swap(face, "gx", first) for first, face in enumerate(faces[4:])]
-    table = jnp.concatenate([table, yb[count_z:]], axis=0)
     table = gather_relative(table[None], "gx").reshape(size_x * size_y, rows, points)
     halos = [za, zb, ya, yb] + x_faces
 
@@ -461,16 +460,15 @@
             halos = swap_faces(faces)
             continue
         za, zb, ya, yb = faces[:4]
-        za_in, zb_in = swap(za, "gz", 0), swap_inner(zb, "gz")
+        za_in, zb_in, yb_in = swap(za, "gz", 0), swap_inner(zb, "gz"), swap_inner(yb, "gy")
         sums = za[4 * count_x :] + za_in[4 * count_x :]
         pieces = jnp.concatenate([sums[:, h * 128 : h * 128 + 128] for h in range(2)], axis=0)
-        pieces, ya, zb_in = barrier((pieces, ya, zb_in))
+        pieces, ya, zb_in, yb_in = barrier((pieces, ya, zb_in, yb_in))
         ya_in = swap(jnp.concatenate([ya, pieces], axis=0), "gy", 0)
         x_faces = [swap(face, "gx", first) for first, face in enumerate(faces[4:])]
-        pieces = jnp.concatenate([pieces, ya_in[count_z:]], axis=0)
-        pieces, yb, x_faces = barrier((pieces, yb, x_faces))
-        yb_in = from_distance(jnp.concatenate([yb, pieces], axis=0), "gy", 3)
-        pieces = jnp.concatenate([pieces, yb_in[count_z:]], axis=0)
+        pieces = jnp.concatenate([pieces, ya_in[count_z:]], axis=0).reshape(2, -1, points)
+        pieces, x_faces = barrier((pieces, x_faces))
+        pieces = gather_relative(pieces, "gy", 2).reshape(-1, points)
         halos = [za_in, zb_in, ya_in, yb_in] + x_faces
 
     distance = 2

time: 65.6 us -> 66.2 us (level)
  starting transfers between devices: 26.1 us -> 29 us
  waiting for transfers between devices: 19.1 us -> 16.7 us
    ppermute x9, waiting for transfers between devices: 11.5 us -> 10.1 us  [swap(): return lax.ppermute(value, axis, pairs)]
    ppermute x9, starting transfers between devices: 13 us -> 14.2 us  [swap(): return lax.ppermute(value, axis, pairs)]
    ppermute x7, waiting for transfers between devices: 7.64 us -> 6.62 us  [from_distance(): return lax.ppermute(value, axis, [(i, i ^ distance) for i in range(count)])]
    ppermute x4 -> x6, starting transfers between devices: 0.08 us -> 1.09 us  [swap_inner(): return lax.ppermute(value, ('gx', axis), pairs)]
  transfers between devices with their start and end apart: 20 -> 22, of which waited for: 11 -> 11; matrix products, arithmetic and copies ran while one was open for 0% -> 0% of each run, Pallas kernels for 8% -> 8%
where the time goes in v9:
time: 66.2 us; the launch traced here: 66 us
  starting transfers between devices  29 us (44%)
  waiting for transfers between devices  16.7 us (25%)
  Pallas kernels  16 us (24%)
  local copies, waits for them, and re-layouts  3.17 us (5%)
  between operations  0.92 us (1%)
    pallas_call x3, Pallas kernels, shards(): pl.pallas_call(functools.partial(step_body, shape=shape, points=points, c...  15.3 us
    ppermute x9, starting transfers between devices, swap(): return lax.ppermute(value, axis, pairs)  14.2 us
    ppermute x7, starting transfers between devices, from_distance(): return lax.ppermute(value, axis, [(i, i ^ distance) for i in range(count)])  13.7 us
    ppermute x9, waiting for transfers between devices, swap(): return lax.ppermute(value, axis, pairs)  10.1 us
    ppermute x7, waiting for transfers between devices, from_distance(): return lax.ppermute(value, axis, [(i, i ^ distance) for i in range(count)])  6.62 us
    unnamed x10, local copies, waits for them, and re-layouts  2.33 us
  transfers between devices with their start and end apart: 22, of which 11 were waited for; matrix products, arithmetic and copies ran while one was open for 0% of the time, Pallas kernels for 8%

profile of v9, /device:TPU:0, one launch (start us, length us, event | category | flops | bytes accessed | tf_op | source)
XLA Modules:
  0.0 66.0 jit_solution(11943168708056601659)
XLA Ops:
  0.6 0.7 %copy_bitcast_fusion = (f32[3,3,32]{2,1,0:T(4,128)S(1)}, f32[3,3,32]{2,1,0:T(4,128)S(1)}) fusion(f32[3,3,1,32]{3,2,1,0:T(1,128)} %param.6, f32[3,3,1,32]{3,2,1,0:T(1,128)} %param.5), kind=kLoop, calls=%fused_computation.35 | loop fusion | bytes 4608
  1.4 3.1 %collective-permute-start = (f32[1,24,32]{2,1,0:T(8,128)S(1)}, f32[1,24,32]{2,1,0:T(8,128)S(1)}, u32[]{:S(2)}, u32[]{:S(2)}) collective-permute-start(f32[1,24,32]{2,1,0:T(8,128)S(1)} %fusion.5), channel_id=1, source_target_pairs={{0,1},{1,0},{2,3},{3,2},{4,5},{5,4},{6,7},{7,6},{8,9},{9,8},{10,11... | collective-permute-start | bytes 9224 | tf_op jit(solution)/shard_map/ppermute | solution.py:47
  4.5 1.6 %copy-done = f32[4,32,16,256]{3,2,1,0:T(8,128)S(1)} copy-done((f32[4,32,16,256]{3,2,1,0:T(8,128)S(1)}, f32[4,32,16,256]{3,2,1,0:T(8,128)}, u32[]{:S(2)}) %copy-start) | copy-done | bytes 2097176
  6.0 0.7 %faces.1 = (f32[128,256]{1,0:T(8,128)S(1)}, f32[128,256]{1,0:T(8,128)S(1)}, f32[16,128]{1,0:T(8,128)S(1)}, f32[16,128]{1,0:T(8,128)S(1)}, f32[4,16,256]{2,1,0:T(8,128)S(1)}) custom-call(f32[4,32,16,256]{3,2,1,0:T(8,128)S(1)} %copy-done), custom_call_target="tpu_custom_call" | custom-call | tf_op jit(solution)/shard_map/faces/pallas_call | solution.py:389
  6.8 1.3 %collective-permute-start.2 = (f32[128,256]{1,0:T(8,128)S(1)}, f32[128,256]{1,0:T(8,128)S(1)}, u32[]{:S(2)}, u32[]{:S(2)}) collective-permute-start(f32[128,256]{1,0:T(8,128)S(1)} %get-tuple-element.52), channel_id=1, source_target_pairs={{0,1},{1,0},{2,3},{3,2},{4,5},{5,4},{6,7},{7,6},{8,9},{9,8},{10,11... | collective-permute-start | bytes 393224 | tf_op jit(solution)/shard_map/ppermute | solution.py:32
  8.2 2.6 %collective-permute-start.1 = (f32[2,24,32]{2,1,0:T(8,128)S(1)}, f32[2,24,32]{2,1,0:T(8,128)S(1)}, u32[]{:S(2)}, u32[]{:S(2)}) collective-permute-start(f32[2,24,32]{2,1,0:T(8,128)S(1)} %pad_maximum_fusion.4), channel_id=1, source_target_pairs={{0,2},{1,3},{2,0},{3,1},{4,6},{5,7},{6,4},{7,5},{8,10},{9,11},{10,... | collective-permute-start | bytes 18440 | tf_op jit(solution)/shard_map/ppermute | solution.py:47
  10.7 1.3 %collective-permute-done.2 = f32[128,256]{1,0:T(8,128)S(1)} collective-permute-done((f32[128,256]{1,0:T(8,128)S(1)}, f32[128,256]{1,0:T(8,128)S(1)}, u32[]{:S(2)}, u32[]{:S(2)}) %collective-permute-start.2) | collective-permute-done | bytes 131104 | tf_op jit(solution)/shard_map/ppermute | solution.py:32
  12.1 0.9 %collective-permute-done.1 = f32[2,24,32]{2,1,0:T(8,128)S(1)} collective-permute-done((f32[2,24,32]{2,1,0:T(8,128)S(1)}, f32[2,24,32]{2,1,0:T(8,128)S(1)}, u32[]{:S(2)}, u32[]{:S(2)}) %collective-permute-start.1) | collective-permute-done | bytes 6176 | tf_op jit(solution)/shard_map/ppermute | solution.py:47
  13.2 0.5 collective-permute-start.5
  13.7 2.6 %collective-permute-start.3 = (f32[40,128]{1,0:T(8,128)S(1)}, f32[40,128]{1,0:T(8,128)S(1)}, u32[]{:S(2)}, u32[]{:S(2)}) collective-permute-start(f32[40,128]{1,0:T(8,128)S(1)} %pad_maximum_fusion.7), channel_id=1, source_target_pairs={{0,4},{4,0},{8,12},{12,8},{1,5},{5,1},{9,13},{13,9},{2,6},{6,2},{1... | collective-permute-start | bytes 61448 | tf_op jit(solution)/shard_map/ppermute | solution.py:32
  16.3 1.8 %collective-permute-done.3.refs_5_ = f32[40,128]{1,0:T(8,128)S(1)} collective-permute-done((f32[40,128]{1,0:T(8,128)S(1)}, f32[40,128]{1,0:T(8,128)S(1)}, u32[]{:S(2)}, u32[]{:S(2)}) %collective-permute-start.3) | collective-permute-done | bytes 20512 | tf_op jit(solution)/shard_map/ppermute | solution.py:32
  18.1 1.9 %collective-permute-start.6 = (f32[2,24,128]{2,1,0:T(8,128)S(1)}, f32[2,24,128]{2,1,0:T(8,128)S(1)}, u32[]{:S(2)}, u32[]{:S(2)}) collective-permute-start(f32[2,24,128]{2,1,0:T(8,128)S(1)} %bitcast.74), channel_id=1, source_target_pairs={{0,8},{4,12},{8,0},{12,4},{1,9},{5,13},{9,1},{13,5},{2,10},{6,14},... | collective-permute-start | bytes 73736 | tf_op jit(solution)/shard_map/ppermute | solution.py:47
  20.0 1.9 %collective-permute-done.6 = f32[2,24,128]{2,1,0:T(8,128)S(1)} collective-permute-done((f32[2,24,128]{2,1,0:T(8,128)S(1)}, f32[2,24,128]{2,1,0:T(8,128)S(1)}, u32[]{:S(2)}, u32[]{:S(2)}) %collective-permute-start.6) | collective-permute-done | bytes 24608 | tf_op jit(solution)/shard_map/ppermute | solution.py:47
  22.0 0.5 collective-permute-start.8
  22.5 0.7 %collective-permute-done.7 = f32[1,4,24,128]{3,2,1,0:T(8,128)S(1)} collective-permute-done((f32[1,4,24,128]{3,2,1,0:T(8,128)S(1)}, f32[1,4,24,128]{3,2,1,0:T(8,128)S(1)}, u32[]{:S(2)}, u32[]{:S(2)}) %collective-permute-start.7) | collective-permute-done | bytes 49184 | tf_op jit(solution)/shard_map/ppermute | solution.py:47
  23.4 5.7 %step.3 = (f32[4,32,16,256]{3,2,1,0:T(8,128)S(1)}, f32[128,256]{1,0:T(8,128)S(1)}, f32[128,256]{1,0:T(8,128)S(1)}, f32[16,128]{1,0:T(8,128)S(1)}, f32[16,128]{1,...) custom-call(s32[2]{0:T(128)S(1)} %bitcast.63, f32[8,24,128]{2,1,0:T(8,128)S(1)} %bitcast.60, ...), custom_call_target="tpu_custom_call" | custom-call | tf_op jit(solution)/shard_map/step/pallas_call | solution.py:437
  29.1 3.0 %collective-permute-start.9 = (f32[128,256]{1,0:T(8,128)S(1)}, f32[128,256]{1,0:T(8,128)S(1)}, u32[]{:S(2)}, u32[]{:S(2)}) collective-permute-start(f32[128,256]{1,0:T(8,128)S(1)} %get-tuple-element.64), channel_id=1, source_target_pairs={{0,1},{1,0},{2,3},{3,2},{4,5},{5,4},{6,7},{7,6},{8,9},{9,8},{10,11... | collective-permute-start | bytes 393224 | tf_op jit(solution)/shard_map/ppermute | solution.py:32
  32.1 0.4 collective-permute-start.13
  32.6 1.9 %collective-permute-start.11 = (f32[16,128]{1,0:T(8,128)S(1)}, f32[16,128]{1,0:T(8,128)S(1)}, u32[]{:S(2)}, u32[]{:S(2)}) collective-permute-start(f32[16,128]{1,0:T(8,128)S(1)} %get-tuple-element.66), channel_id=1, source_target_pairs={{0,4},{4,0},{8,12},{12,8},{1,5},{5,1},{9,13},{13,9},{2,6},{6,2},{1... | collective-permute-start | bytes 24584 | tf_op jit(solution)/shard_map/ppermute | solution.py:32
  34.5 1.7 %collective-permute-done.11.refs_5_ = f32[16,128]{1,0:T(8,128)S(1)} collective-permute-done((f32[16,128]{1,0:T(8,128)S(1)}, f32[16,128]{1,0:T(8,128)S(1)}, u32[]{:S(2)}, u32[]{:S(2)}) %collective-permute-start.11) | collective-permute-done | bytes 8224 | tf_op jit(solution)/shard_map/ppermute | solution.py:32
  36.2 4.9 %step.4 = (f32[4,32,16,256]{3,2,1,0:T(8,128)S(1)}, f32[144,256]{1,0:T(8,128)S(1)}, f32[128,256]{1,0:T(8,128)S(1)}, f32[16,128]{1,0:T(8,128)S(1)}, f32[16,128]{1,0:T(8,128)S(1)}, /*index=5*/f32[4,16,256]{2,1,0:T(8,128)S(1)}) custom-call(s32[2]{0:T(128)S(1)} %bitcast.64, f32[8,24,128]{2,1,0:T(8,128)S(1)} %bitcast.61, ...), custom_call_target="tpu_custom_call" | custom-call | tf_op jit(solution)/shard_map/step/pallas_call | solution.py:437
  41.2 1.7 %collective-permute-start.14 = (f32[144,256]{1,0:T(8,128)S(1)}, f32[144,256]{1,0:T(8,128)S(1)}, u32[]{:S(2)}, u32[]{:S(2)}) collective-permute-start(f32[144,256]{1,0:T(8,128)S(1)} %get-tuple-element.70), channel_id=1, source_target_pairs={{0,1},{1,0},{2,3},{3,2},{4,5},{5,4},{6,7},{7,6},{8,9},{9,8},{10,11... | collective-permute-start | bytes 442376 | tf_op jit(solution)/shard_map/ppermute | solution.py:32
  42.9 0.5 collective-permute-start.15
  43.4 3.2 %collective-permute-done.14.refs_3_ = f32[144,256]{1,0:T(8,128)S(1)} collective-permute-done((f32[144,256]{1,0:T(8,128)S(1)}, f32[144,256]{1,0:T(8,128)S(1)}, u32[]{:S(2)}, u32[]{:S(2)}) %collective-permute-start.14) | collective-permute-done | bytes 147488 | tf_op jit(solution)/shard_map/ppermute | solution.py:32
  46.7 2.8 %collective-permute-start.17 = (f32[48,128]{1,0:T(8,128)S(1)}, f32[48,128]{1,0:T(8,128)S(1)}, u32[]{:S(2)}, u32[]{:S(2)}) collective-permute-start(f32[48,128]{1,0:T(8,128)S(1)} %pad_maximum_fusion.6), channel_id=1, source_target_pairs={{0,4},{4,0},{8,12},{12,8},{1,5},{5,1},{9,13},{13,9},{2,6},{6,2},{1... | collective-permute-start | bytes 73736 | tf_op jit(solution)/shard_map/ppermute | solution.py:32
  49.4 1.8 %collective-permute-done.17.refs_5_ = f32[48,128]{1,0:T(8,128)S(1)} collective-permute-done((f32[48,128]{1,0:T(8,128)S(1)}, f32[48,128]{1,0:T(8,128)S(1)}, u32[]{:S(2)}, u32[]{:S(2)}) %collective-permute-start.17) | collective-permute-done | bytes 24608 | tf_op jit(solution)/shard_map/ppermute | solution.py:32
  51.2 2.3 %collective-permute-start.19 = (f32[2,32,128]{2,1,0:T(8,128)S(1)}, f32[2,32,128]{2,1,0:T(8,128)S(1)}, u32[]{:S(2)}, u32[]{:S(2)}) collective-permute-start(f32[2,32,128]{2,1,0:T(8,128)S(1)} %bitcast.72), channel_id=1, source_target_pairs={{0,8},{4,12},{8,0},{12,4},{1,9},{5,13},{9,1},{13,5},{2,10},{6,14},... | collective-permute-start | bytes 98312 | tf_op jit(solution)/shard_map/ppermute | solution.py:47
  53.5 1.9 %collective-permute-done.19 = f32[2,32,128]{2,1,0:T(8,128)S(1)} collective-permute-done((f32[2,32,128]{2,1,0:T(8,128)S(1)}, f32[2,32,128]{2,1,0:T(8,128)S(1)}, u32[]{:S(2)}, u32[]{:S(2)}) %collective-permute-start.19) | collective-permute-done | bytes 32800 | tf_op jit(solution)/shard_map/ppermute | solution.py:47
  55.5 3.8 %collective-permute-start.20 = (f32[128,128]{0,1:T(8,128)S(1)}, f32[128,128]{0,1:T(8,128)S(1)}, u32[]{:S(2)}, u32[]{:S(2)}) collective-permute-start(f32[128,128]{0,1:T(8,128)S(1)} %copy.11), channel_id=1, source_target_pairs={{0,2},{1,3},{2,0},{3,1},{4,6},{5,7},{6,4},{7,5},{8,10},{9,11},{10,... | collective-permute-start | bytes 196616 | tf_op jit(solution)/shard_map/ppermute | solution.py:47
  59.3 4.6 %step.5 = f32[4,32,16,256]{3,2,1,0:T(8,128)} custom-call(s32[2]{0:T(128)S(1)} %bitcast.65, f32[8,24,128]{2,1,0:T(8,128)S(1)} %bitcast.62, f32[4,32,16,256]{3,2,1,0:T(8,128)S(1)} %get-tuple-element.78.refs_2_, f32[144,256]{1,0:T(8,128)S(1)} %collective-permute-done.14.refs_3_, f32[128,256]{1,0:T(8,128)S(1)} %collective-permute-done.15.refs_4_, ...), custom_call_target="tpu_custom_call" | custom-call | tf_op jit(solution)/shard_map/step/pallas_call | solution.py:437
  64.0 1.2 %collective-permute-done.21 = f32[1,128,32]{1,2,0:T(8,128)S(1)} collective-permute-done((f32[1,128,32]{1,2,0:T(8,128)S(1)}, f32[1,128,32]{1,2,0:T(8,128)S(1)}, u32[]{:S(2)}, u32[]{:S(2)}) %collective-permute-start.21) | collective-permute-done | bytes 16416 | tf_op jit(solution)/shard_map/ppermute | solution.py:47
  65.4 0.6 add.42
  (60 shorter events, 0.9 us)
Async XLA Ops:
  0.6 22.7 %copy-start.2 = (s32[1,1,1,2]{3,2,1,0:T(1,128)S(1)}, s32[1,1,1,2]{3,2,1,0:T(1,128)}, u32[]{:S(2)}) copy-start(s32[1,1,1,2]{3,2,1,0:T(1,128)} %param.7) | copy-start | bytes 28
  1.4 5.4 %collective-permute-start = (f32[1,24,32]{2,1,0:T(8,128)S(1)}, f32[1,24,32]{2,1,0:T(8,128)S(1)}, u32[]{:S(2)}, u32[]{:S(2)}) collective-permute-start(f32[1,24,32]{2,1,0:T(8,128)S(1)} %fusion.5), channel_id=1, source_target_pairs={{0,1},{1,0},{2,3},{3,2},{4,5},{5,4},{6,7},{7,6},{8,9},{9,8},{10,11... | collective-permute-start | bytes 9224 | tf_op jit(solution)/shard_map/ppermute | solution.py:47
  4.5 1.6 %copy-start = (f32[4,32,16,256]{3,2,1,0:T(8,128)S(1)}, f32[4,32,16,256]{3,2,1,0:T(8,128)}, u32[]{:S(2)}) copy-start(f32[4,32,16,256]{3,2,1,0:T(8,128)} %refs_2_.1) | copy-start | bytes 6291460
  6.0 17.3 %copy-start.1 = (f32[4,32,16,256]{3,2,1,0:T(8,128)S(1)}, f32[4,32,16,256]{3,2,1,0:T(8,128)}, u32[]{:S(2)}) copy-start(f32[4,32,16,256]{3,2,1,0:T(8,128)} %refs_2_.1) | copy-start | bytes 6291460
  6.8 5.3 %collective-permute-start.2 = (f32[128,256]{1,0:T(8,128)S(1)}, f32[128,256]{1,0:T(8,128)S(1)}, u32[]{:S(2)}, u32[]{:S(2)}) collective-permute-start(f32[128,256]{1,0:T(8,128)S(1)} %get-tuple-element.52), channel_id=1, source_target_pairs={{0,1},{1,0},{2,3},{3,2},{4,5},{5,4},{6,7},{7,6},{8,9},{9,8},{10,11... | collective-permute-start | bytes 393224 | tf_op jit(solution)/shard_map/ppermute | solution.py:32
  8.2 4.9 %collective-permute-start.1 = (f32[2,24,32]{2,1,0:T(8,128)S(1)}, f32[2,24,32]{2,1,0:T(8,128)S(1)}, u32[]{:S(2)}, u32[]{:S(2)}) collective-permute-start(f32[2,24,32]{2,1,0:T(8,128)S(1)} %pad_maximum_fusion.4), channel_id=1, source_target_pairs={{0,2},{1,3},{2,0},{3,1},{4,6},{5,7},{6,4},{7,5},{8,10},{9,11},{10,... | collective-permute-start | bytes 18440 | tf_op jit(solution)/shard_map/ppermute | solution.py:47
  13.2 3.1 %collective-permute-start.4 = (f32[128,256]{1,0:T(8,128)S(1)}, f32[128,256]{1,0:T(8,128)S(1)}, u32[]{:S(2)}, u32[]{:S(2)}) collective-permute-start(f32[128,256]{1,0:T(8,128)S(1)} %get-tuple-element.56), channel_id=1, source_target_pairs={{0,16},{1,2},{2,1},{3,19},{16,0},{17,18},{18,17},{19,3},{4,20},{5,... | collective-permute-start | bytes 393224 | tf_op jit(solution)/shard_map/ppermute | solution.py:42
  13.2 3.1 %collective-permute-start.5 = (f32[16,128]{1,0:T(8,128)S(1)}, f32[16,128]{1,0:T(8,128)S(1)}, u32[]{:S(2)}, u32[]{:S(2)}) collective-permute-start(f32[16,128]{1,0:T(8,128)S(1)} %get-tuple-element.57), channel_id=1, source_target_pairs={{0,16},{4,8},{8,4},{12,28},{16,0},{20,24},{24,20},{28,12},{1,17},{... | collective-permute-start | bytes 24584 | tf_op jit(solution)/shard_map/ppermute | solution.py:42
  13.7 4.4 %collective-permute-start.3 = (f32[40,128]{1,0:T(8,128)S(1)}, f32[40,128]{1,0:T(8,128)S(1)}, u32[]{:S(2)}, u32[]{:S(2)}) collective-permute-start(f32[40,128]{1,0:T(8,128)S(1)} %pad_maximum_fusion.7), channel_id=1, source_target_pairs={{0,4},{4,0},{8,12},{12,8},{1,5},{5,1},{9,13},{13,9},{2,6},{6,2},{1... | collective-permute-start | bytes 61448 | tf_op jit(solution)/shard_map/ppermute | solution.py:32
  18.1 3.8 %collective-permute-start.6 = (f32[2,24,128]{2,1,0:T(8,128)S(1)}, f32[2,24,128]{2,1,0:T(8,128)S(1)}, u32[]{:S(2)}, u32[]{:S(2)}) collective-permute-start(f32[2,24,128]{2,1,0:T(8,128)S(1)} %bitcast.74), channel_id=1, source_target_pairs={{0,8},{4,12},{8,0},{12,4},{1,9},{5,13},{9,1},{13,5},{2,10},{6,14},... | collective-permute-start | bytes 73736 | tf_op jit(solution)/shard_map/ppermute | solution.py:47
  22.0 1.2 %collective-permute-start.7 = (f32[1,4,24,128]{3,2,1,0:T(8,128)S(1)}, f32[1,4,24,128]{3,2,1,0:T(8,128)S(1)}, u32[]{:S(2)}, u32[]{:S(2)}) collective-permute-start(f32[1,4,24,128]{3,2,1,0:T(8,128)S(1)} %maximum_bitcast_fusion), channel_id=1, source_target_pairs={{0,16},{16,0},{1,17},{17,1},{2,18},{18,2},{3,19},{19,3},{4,20},{20... | collective-permute-start | bytes 147464 | tf_op jit(solution)/shard_map/ppermute | solution.py:47
  22.0 1.4 %collective-permute-start.8 = (f32[4,16,256]{2,1,0:T(8,128)S(1)}, f32[4,16,256]{2,1,0:T(8,128)S(1)}, u32[]{:S(2)}, u32[]{:S(2)}) collective-permute-start(f32[4,16,256]{2,1,0:T(8,128)S(1)} %get-tuple-element.62), channel_id=1, source_target_pairs={{0,16},{16,0},{1,17},{17,1},{2,18},{18,2},{3,19},{19,3},{4,20},{20... | collective-permute-start | bytes 196616 | tf_op jit(solution)/shard_map/ppermute | solution.py:32
  29.1 7.2 %collective-permute-start.9 = (f32[128,256]{1,0:T(8,128)S(1)}, f32[128,256]{1,0:T(8,128)S(1)}, u32[]{:S(2)}, u32[]{:S(2)}) collective-permute-start(f32[128,256]{1,0:T(8,128)S(1)} %get-tuple-element.64), channel_id=1, source_target_pairs={{0,1},{1,0},{2,3},{3,2},{4,5},{5,4},{6,7},{7,6},{8,9},{9,8},{10,11... | collective-permute-start | bytes 393224 | tf_op jit(solution)/shard_map/ppermute | solution.py:32
  32.0 4.2 %collective-permute-start.10 = (f32[128,256]{1,0:T(8,128)S(1)}, f32[128,256]{1,0:T(8,128)S(1)}, u32[]{:S(2)}, u32[]{:S(2)}) collective-permute-start(f32[128,256]{1,0:T(8,128)S(1)} %get-tuple-element.65), channel_id=1, source_target_pairs={{0,16},{1,2},{2,1},{3,19},{16,0},{17,18},{18,17},{19,3},{4,20},{5,... | collective-permute-start | bytes 393224 | tf_op jit(solution)/shard_map/ppermute | solution.py:42
  32.1 4.1 %collective-permute-start.13 = (f32[4,16,256]{2,1,0:T(8,128)S(1)}, f32[4,16,256]{2,1,0:T(8,128)S(1)}, u32[]{:S(2)}, u32[]{:S(2)}) collective-permute-start(f32[4,16,256]{2,1,0:T(8,128)S(1)} %get-tuple-element.68), channel_id=1, source_target_pairs={{0,16},{16,0},{1,17},{17,1},{2,18},{18,2},{3,19},{19,3},{4,20},{20... | collective-permute-start | bytes 196616 | tf_op jit(solution)/shard_map/ppermute | solution.py:32
  32.6 3.7 %collective-permute-start.11 = (f32[16,128]{1,0:T(8,128)S(1)}, f32[16,128]{1,0:T(8,128)S(1)}, u32[]{:S(2)}, u32[]{:S(2)}) collective-permute-start(f32[16,128]{1,0:T(8,128)S(1)} %get-tuple-element.66), channel_id=1, source_target_pairs={{0,4},{4,0},{8,12},{12,8},{1,5},{5,1},{9,13},{13,9},{2,6},{6,2},{1... | collective-permute-start | bytes 24584 | tf_op jit(solution)/shard_map/ppermute | solution.py:32
  34.5 1.7 %collective-permute-start.12 = (f32[16,128]{1,0:T(8,128)S(1)}, f32[16,128]{1,0:T(8,128)S(1)}, u32[]{:S(2)}, u32[]{:S(2)}) collective-permute-start(f32[16,128]{1,0:T(8,128)S(1)} %get-tuple-element.67), channel_id=1, source_target_pairs={{0,16},{4,8},{8,4},{12,28},{16,0},{20,24},{24,20},{28,12},{1,17},{... | collective-permute-start | bytes 24584 | tf_op jit(solution)/shard_map/ppermute | solution.py:42
  41.2 5.4 %collective-permute-start.14 = (f32[144,256]{1,0:T(8,128)S(1)}, f32[144,256]{1,0:T(8,128)S(1)}, u32[]{:S(2)}, u32[]{:S(2)}) collective-permute-start(f32[144,256]{1,0:T(8,128)S(1)} %get-tuple-element.70), channel_id=1, source_target_pairs={{0,1},{1,0},{2,3},{3,2},{4,5},{5,4},{6,7},{7,6},{8,9},{9,8},{10,11... | collective-permute-start | bytes 442376 | tf_op jit(solution)/shard_map/ppermute | solution.py:32
  42.9 3.8 %collective-permute-start.16 = (f32[16,128]{1,0:T(8,128)S(1)}, f32[16,128]{1,0:T(8,128)S(1)}, u32[]{:S(2)}, u32[]{:S(2)}) collective-permute-start(f32[16,128]{1,0:T(8,128)S(1)} %get-tuple-element.73), channel_id=1, source_target_pairs={{0,16},{4,8},{8,4},{12,28},{16,0},{20,24},{24,20},{28,12},{1,17},{... | collective-permute-start | bytes 24584 | tf_op jit(solution)/shard_map/ppermute | solution.py:42
  42.9 3.8 %collective-permute-start.15 = (f32[128,256]{1,0:T(8,128)S(1)}, f32[128,256]{1,0:T(8,128)S(1)}, u32[]{:S(2)}, u32[]{:S(2)}) collective-permute-start(f32[128,256]{1,0:T(8,128)S(1)} %get-tuple-element.72), channel_id=1, source_target_pairs={{0,16},{1,2},{2,1},{3,19},{16,0},{17,18},{18,17},{19,3},{4,20},{5,... | collective-permute-start | bytes 393224 | tf_op jit(solution)/shard_map/ppermute | solution.py:42
  46.7 4.6 %collective-permute-start.17 = (f32[48,128]{1,0:T(8,128)S(1)}, f32[48,128]{1,0:T(8,128)S(1)}, u32[]{:S(2)}, u32[]{:S(2)}) collective-permute-start(f32[48,128]{1,0:T(8,128)S(1)} %pad_maximum_fusion.6), channel_id=1, source_target_pairs={{0,4},{4,0},{8,12},{12,8},{1,5},{5,1},{9,13},{13,9},{2,6},{6,2},{1... | collective-permute-start | bytes 73736 | tf_op jit(solution)/shard_map/ppermute | solution.py:32
  49.4 1.8 %collective-permute-start.18 = (f32[4,16,256]{2,1,0:T(8,128)S(1)}, f32[4,16,256]{2,1,0:T(8,128)S(1)}, u32[]{:S(2)}, u32[]{:S(2)}) collective-permute-start(f32[4,16,256]{2,1,0:T(8,128)S(1)} %get-tuple-element.76), channel_id=1, source_target_pairs={{0,16},{16,0},{1,17},{17,1},{2,18},{18,2},{3,19},{19,3},{4,20},{20... | collective-permute-start | bytes 196616 | tf_op jit(solution)/shard_map/ppermute | solution.py:32
  51.2 4.2 %collective-permute-start.19 = (f32[2,32,128]{2,1,0:T(8,128)S(1)}, f32[2,32,128]{2,1,0:T(8,128)S(1)}, u32[]{:S(2)}, u32[]{:S(2)}) collective-permute-start(f32[2,32,128]{2,1,0:T(8,128)S(1)} %bitcast.72), channel_id=1, source_target_pairs={{0,8},{4,12},{8,0},{12,4},{1,9},{5,13},{9,1},{13,5},{2,10},{6,14},... | collective-permute-start | bytes 98312 | tf_op jit(solution)/shard_map/ppermute | solution.py:47
  55.5 8.4 %collective-permute-start.20 = (f32[128,128]{0,1:T(8,128)S(1)}, f32[128,128]{0,1:T(8,128)S(1)}, u32[]{:S(2)}, u32[]{:S(2)}) collective-permute-start(f32[128,128]{0,1:T(8,128)S(1)} %copy.11), channel_id=1, source_target_pairs={{0,2},{1,3},{2,0},{3,1},{4,6},{5,7},{6,4},{7,5},{8,10},{9,11},{10,... | collective-permute-start | bytes 196616 | tf_op jit(solution)/shard_map/ppermute | solution.py:47
  64.0 1.2 %collective-permute-start.21 = (f32[1,128,32]{1,2,0:T(8,128)S(1)}, f32[1,128,32]{1,2,0:T(8,128)S(1)}, u32[]{:S(2)}, u32[]{:S(2)}) collective-permute-start(f32[1,128,32]{1,2,0:T(8,128)S(1)} %dynamic-slice_bitcast_fusion), channel_id=1, source_target_pairs={{0,16},{16,0},{1,17},{17,1},{2,18},{18,2},{3,19},{19,3},{4,20},{20... | collective-permute-start | bytes 49160 | tf_op jit(solution)/shard_map/ppermute | solution.py:47

commit v10 on v9

--- a/solution.py
+++ b/solution.py
@@ -406,13 +406,14 @@
     table = true_order(table, "gz")
     table = jnp.concatenate([table[k] for k in range(size_z)], axis=1)
     rows = 8 * steps
-    zb, yb, ya, table = barrier((zb, yb, ya, table))
+    zb, ya, table = barrier((zb, ya, table))
     zb = masked(swap_inner(zb, "gz"), "gz", 1)
-    yb = swap_inner(yb, "gy")
     ya = swap(jnp.concatenate([ya, table], axis=0), "gy", 0)
     ya, zb, yb = barrier((ya, zb, yb))
     table = jnp.concatenate([table, ya[count_z:]], axis=0).reshape(2, rows, points)
     table = gather_relative(table, "gy", 2)
+    yb = swap_inner(yb, "gy")
+    table, yb = barrier((table, yb))
     x_faces = [swap(face, "gx", first) for first, face in enumerate(faces[4:])]
     table = gather_relative(table[None], "gx").reshape(size_x * size_y, rows, points)
     halos = [za, zb, ya, yb] + x_faces
@@ -460,15 +461,17 @@
             halos = swap_faces(faces)
             continue
         za, zb, ya, yb = faces[:4]
-        za_in, zb_in, yb_in = swap(za, "gz", 0), swap_inner(zb, "gz"), swap_inner(yb, "gy")
+        za_in, zb_in = swap(za, "gz", 0), swap_inner(zb, "gz")
         sums = za[4 * count_x :] + za_in[4 * count_x :]
         pieces = jnp.concatenate([sums[:, h * 128 : h * 128 + 128] for h in range(2)], axis=0)
-        pieces, ya, zb_in, yb_in = barrier((pieces, ya, zb_in, yb_in))
+        pieces, ya, zb_in = barrier((pieces, ya, zb_in))
         ya_in = swap(jnp.concatenate([ya, pieces], axis=0), "gy", 0)
         x_faces = [swap(face, "gx", first) for first, face in enumerate(faces[4:])]
         pieces = jnp.concatenate([pieces, ya_in[count_z:]], axis=0).reshape(2, -1, points)
-        pieces, x_faces = barrier((pieces, x_faces))
+        pieces, yb, x_faces = barrier((pieces, yb, x_faces))
         pieces = gather_relative(pieces, "gy", 2).reshape(-1, points)
+        yb_in = swap_inner(yb, "gy")
+        pieces, yb_in = barrier((pieces, yb_in))
         halos = [za_in, zb_in, ya_in, yb_in] + x_faces
 
     distance = 2

time: 66.2 us -> 65.6 us (level)
  starting transfers between devices: 29 us -> 25.4 us
  waiting for transfers between devices: 16.7 us -> 19.5 us
    ppermute x7, starting transfers between devices: 13.7 us -> 11.1 us  [from_distance(): return lax.ppermute(value, axis, [(i, i ^ distance) for i in range(count)])]
    ppermute x9, waiting for transfers between devices: 10.1 us -> 11.9 us  [swap(): return lax.ppermute(value, axis, pairs)]
    ppermute x7, waiting for transfers between devices: 6.62 us -> 7.65 us  [from_distance(): return lax.ppermute(value, axis, [(i, i ^ distance) for i in range(count)])]
    ppermute x6, starting transfers between devices: 1.09 us -> 0.09 us  [swap_inner(): return lax.ppermute(value, ('gx', axis), pairs)]
where the time goes in v10:
time: 65.6 us; the launch traced here: 65.3 us
  starting transfers between devices  25.4 us (39%)
  waiting for transfers between devices  19.5 us (30%)
  Pallas kernels  16 us (24%)
  local copies, waits for them, and re-layouts  3.17 us (5%)
  between operations  0.92 us (1%)
    pallas_call x3, Pallas kernels, shards(): pl.pallas_call(functools.partial(step_body, shape=shape, points=points, c...  15.3 us
    ppermute x9, starting transfers between devices, swap(): return lax.ppermute(value, axis, pairs)  14.2 us
    ppermute x9, waiting for transfers between devices, swap(): return lax.ppermute(value, axis, pairs)  11.9 us
    ppermute x7, starting transfers between devices, from_distance(): return lax.ppermute(value, axis, [(i, i ^ distance) for i in range(count)])  11.1 us
    ppermute x7, waiting for transfers between devices, from_distance(): return lax.ppermute(value, axis, [(i, i ^ distance) for i in range(count)])  7.65 us
    unnamed x10, local copies, waits for them, and re-layouts  2.33 us
  transfers between devices with their start and end apart: 22, of which 11 were waited for; matrix products, arithmetic and copies ran while one was open for 0% of the time, Pallas kernels for 8%

profile of v10, /device:TPU:0, one launch (start us, length us, event | category | flops | bytes accessed | tf_op | source)
XLA Modules:
  0.0 65.3 jit_solution(4718587700254901330)
XLA Ops:
  0.6 0.7 %copy_bitcast_fusion = (f32[3,3,32]{2,1,0:T(4,128)S(1)}, f32[3,3,32]{2,1,0:T(4,128)S(1)}) fusion(f32[3,3,1,32]{3,2,1,0:T(1,128)} %param.6, f32[3,3,1,32]{3,2,1,0:T(1,128)} %param.5), kind=kLoop, calls=%fused_computation.35 | loop fusion | bytes 4608
  1.4 3.1 %collective-permute-start = (f32[1,24,32]{2,1,0:T(8,128)S(1)}, f32[1,24,32]{2,1,0:T(8,128)S(1)}, u32[]{:S(2)}, u32[]{:S(2)}) collective-permute-start(f32[1,24,32]{2,1,0:T(8,128)S(1)} %fusion.5), channel_id=1, source_target_pairs={{0,1},{1,0},{2,3},{3,2},{4,5},{5,4},{6,7},{7,6},{8,9},{9,8},{10,11... | collective-permute-start | bytes 9224 | tf_op jit(solution)/shard_map/ppermute | solution.py:47
  4.5 1.6 %copy-done = f32[4,32,16,256]{3,2,1,0:T(8,128)S(1)} copy-done((f32[4,32,16,256]{3,2,1,0:T(8,128)S(1)}, f32[4,32,16,256]{3,2,1,0:T(8,128)}, u32[]{:S(2)}) %copy-start) | copy-done | bytes 2097176
  6.0 0.7 %faces.1 = (f32[128,256]{1,0:T(8,128)S(1)}, f32[128,256]{1,0:T(8,128)S(1)}, f32[16,128]{1,0:T(8,128)S(1)}, f32[16,128]{1,0:T(8,128)S(1)}, f32[4,16,256]{2,1,0:T(8,128)S(1)}) custom-call(f32[4,32,16,256]{3,2,1,0:T(8,128)S(1)} %copy-done), custom_call_target="tpu_custom_call" | custom-call | tf_op jit(solution)/shard_map/faces/pallas_call | solution.py:389
  6.8 1.3 %collective-permute-start.2 = (f32[128,256]{1,0:T(8,128)S(1)}, f32[128,256]{1,0:T(8,128)S(1)}, u32[]{:S(2)}, u32[]{:S(2)}) collective-permute-start(f32[128,256]{1,0:T(8,128)S(1)} %get-tuple-element.54), channel_id=1, source_target_pairs={{0,1},{1,0},{2,3},{3,2},{4,5},{5,4},{6,7},{7,6},{8,9},{9,8},{10,11... | collective-permute-start | bytes 393224 | tf_op jit(solution)/shard_map/ppermute | solution.py:32
  8.2 2.6 %collective-permute-start.1 = (f32[2,24,32]{2,1,0:T(8,128)S(1)}, f32[2,24,32]{2,1,0:T(8,128)S(1)}, u32[]{:S(2)}, u32[]{:S(2)}) collective-permute-start(f32[2,24,32]{2,1,0:T(8,128)S(1)} %pad_maximum_fusion.5), channel_id=1, source_target_pairs={{0,2},{1,3},{2,0},{3,1},{4,6},{5,7},{6,4},{7,5},{8,10},{9,11},{10,... | collective-permute-start | bytes 18440 | tf_op jit(solution)/shard_map/ppermute | solution.py:47
  10.7 1.3 %collective-permute-done.2 = f32[128,256]{1,0:T(8,128)S(1)} collective-permute-done((f32[128,256]{1,0:T(8,128)S(1)}, f32[128,256]{1,0:T(8,128)S(1)}, u32[]{:S(2)}, u32[]{:S(2)}) %collective-permute-start.2) | collective-permute-done | bytes 131104 | tf_op jit(solution)/shard_map/ppermute | solution.py:32
  12.1 0.9 %collective-permute-done.1 = f32[2,24,32]{2,1,0:T(8,128)S(1)} collective-permute-done((f32[2,24,32]{2,1,0:T(8,128)S(1)}, f32[2,24,32]{2,1,0:T(8,128)S(1)}, u32[]{:S(2)}, u32[]{:S(2)}) %collective-permute-start.1) | collective-permute-done | bytes 6176 | tf_op jit(solution)/shard_map/ppermute | solution.py:47
  13.2 1.6 %collective-permute-start.3 = (f32[40,128]{1,0:T(8,128)S(1)}, f32[40,128]{1,0:T(8,128)S(1)}, u32[]{:S(2)}, u32[]{:S(2)}) collective-permute-start(f32[40,128]{1,0:T(8,128)S(1)} %pad_maximum_fusion.8), channel_id=1, source_target_pairs={{0,4},{4,0},{8,12},{12,8},{1,5},{5,1},{9,13},{13,9},{2,6},{6,2},{1... | collective-permute-start | bytes 61448 | tf_op jit(solution)/shard_map/ppermute | solution.py:32
  14.8 2.3 %collective-permute-done.3.refs_5_ = f32[40,128]{1,0:T(8,128)S(1)} collective-permute-done((f32[40,128]{1,0:T(8,128)S(1)}, f32[40,128]{1,0:T(8,128)S(1)}, u32[]{:S(2)}, u32[]{:S(2)}) %collective-permute-start.3) | collective-permute-done | bytes 20512 | tf_op jit(solution)/shard_map/ppermute | solution.py:32
  17.1 1.5 %collective-permute-start.5 = (f32[2,24,128]{2,1,0:T(8,128)S(1)}, f32[2,24,128]{2,1,0:T(8,128)S(1)}, u32[]{:S(2)}, u32[]{:S(2)}) collective-permute-start(f32[2,24,128]{2,1,0:T(8,128)S(1)} %bitcast.75), channel_id=1, source_target_pairs={{0,8},{4,12},{8,0},{12,4},{1,9},{5,13},{9,1},{13,5},{2,10},{6,14},... | collective-permute-start | bytes 73736 | tf_op jit(solution)/shard_map/ppermute | solution.py:47
  18.6 2.3 %collective-permute-done.5 = f32[2,24,128]{2,1,0:T(8,128)S(1)} collective-permute-done((f32[2,24,128]{2,1,0:T(8,128)S(1)}, f32[2,24,128]{2,1,0:T(8,128)S(1)}, u32[]{:S(2)}, u32[]{:S(2)}) %collective-permute-start.5) | collective-permute-done | bytes 24608 | tf_op jit(solution)/shard_map/ppermute | solution.py:47
  21.0 0.5 collective-permute-start.8
  21.5 0.7 %collective-permute-done.7 = f32[1,4,24,128]{3,2,1,0:T(8,128)S(1)} collective-permute-done((f32[1,4,24,128]{3,2,1,0:T(8,128)S(1)}, f32[1,4,24,128]{3,2,1,0:T(8,128)S(1)}, u32[]{:S(2)}, u32[]{:S(2)}) %collective-permute-start.7) | collective-permute-done | bytes 49184 | tf_op jit(solution)/shard_map/ppermute | solution.py:47
  22.2 0.2 collective-permute-done.8.refs_7_
  22.4 5.7 %step.3 = (f32[4,32,16,256]{3,2,1,0:T(8,128)S(1)}, f32[128,256]{1,0:T(8,128)S(1)}, f32[128,256]{1,0:T(8,128)S(1)}, f32[16,128]{1,0:T(8,128)S(1)}, f32[16,128]{1,...) custom-call(s32[2]{0:T(128)S(1)} %bitcast.62, f32[8,24,128]{2,1,0:T(8,128)S(1)} %bitcast.59, ...), custom_call_target="tpu_custom_call" | custom-call | tf_op jit(solution)/shard_map/step/pallas_call | solution.py:438
  28.1 3.2 %collective-permute-start.9 = (f32[128,256]{1,0:T(8,128)S(1)}, f32[128,256]{1,0:T(8,128)S(1)}, u32[]{:S(2)}, u32[]{:S(2)}) collective-permute-start(f32[128,256]{1,0:T(8,128)S(1)} %get-tuple-element.68), channel_id=1, source_target_pairs={{0,1},{1,0},{2,3},{3,2},{4,5},{5,4},{6,7},{7,6},{8,9},{9,8},{10,11... | collective-permute-start | bytes 393224 | tf_op jit(solution)/shard_map/ppermute | solution.py:32
  31.3 0.4 collective-permute-start.13
  31.8 3.7 %collective-permute-start.11 = (f32[16,128]{1,0:T(8,128)S(1)}, f32[16,128]{1,0:T(8,128)S(1)}, u32[]{:S(2)}, u32[]{:S(2)}) collective-permute-start(f32[16,128]{1,0:T(8,128)S(1)} %get-tuple-element.70), channel_id=1, source_target_pairs={{0,4},{4,0},{8,12},{12,8},{1,5},{5,1},{9,13},{13,9},{2,6},{6,2},{1... | collective-permute-start | bytes 24584 | tf_op jit(solution)/shard_map/ppermute | solution.py:32
  35.5 1.6 %collective-permute-done.11.refs_5_ = f32[16,128]{1,0:T(8,128)S(1)} collective-permute-done((f32[16,128]{1,0:T(8,128)S(1)}, f32[16,128]{1,0:T(8,128)S(1)}, u32[]{:S(2)}, u32[]{:S(2)}) %collective-permute-start.11) | collective-permute-done | bytes 8224 | tf_op jit(solution)/shard_map/ppermute | solution.py:32
  37.1 4.9 %step.4 = (f32[4,32,16,256]{3,2,1,0:T(8,128)S(1)}, f32[144,256]{1,0:T(8,128)S(1)}, f32[128,256]{1,0:T(8,128)S(1)}, f32[16,128]{1,0:T(8,128)S(1)}, f32[16,128]{1,0:T(8,128)S(1)}, /*index=5*/f32[4,16,256]{2,1,0:T(8,128)S(1)}) custom-call(s32[2]{0:T(128)S(1)} %bitcast.63, f32[8,24,128]{2,1,0:T(8,128)S(1)} %bitcast.60, ...), custom_call_target="tpu_custom_call" | custom-call | tf_op jit(solution)/shard_map/step/pallas_call | solution.py:438
  42.1 0.9 %collective-permute-start.14 = (f32[144,256]{1,0:T(8,128)S(1)}, f32[144,256]{1,0:T(8,128)S(1)}, u32[]{:S(2)}, u32[]{:S(2)}) collective-permute-start(f32[144,256]{1,0:T(8,128)S(1)} %get-tuple-element.74), channel_id=1, source_target_pairs={{0,1},{1,0},{2,3},{3,2},{4,5},{5,4},{6,7},{7,6},{8,9},{9,8},{10,11... | collective-permute-start | bytes 442376 | tf_op jit(solution)/shard_map/ppermute | solution.py:32
  42.9 4.6 %collective-permute-done.14.refs_3_ = f32[144,256]{1,0:T(8,128)S(1)} collective-permute-done((f32[144,256]{1,0:T(8,128)S(1)}, f32[144,256]{1,0:T(8,128)S(1)}, u32[]{:S(2)}, u32[]{:S(2)}) %collective-permute-start.14) | collective-permute-done | bytes 147488 | tf_op jit(solution)/shard_map/ppermute | solution.py:32
  47.6 2.7 %collective-permute-start.16 = (f32[48,128]{1,0:T(8,128)S(1)}, f32[48,128]{1,0:T(8,128)S(1)}, u32[]{:S(2)}, u32[]{:S(2)}) collective-permute-start(f32[48,128]{1,0:T(8,128)S(1)} %pad_maximum_fusion.7), channel_id=1, source_target_pairs={{0,4},{4,0},{8,12},{12,8},{1,5},{5,1},{9,13},{13,9},{2,6},{6,2},{1... | collective-permute-start | bytes 73736 | tf_op jit(solution)/shard_map/ppermute | solution.py:32
  50.3 1.8 %collective-permute-done.16.refs_5_ = f32[48,128]{1,0:T(8,128)S(1)} collective-permute-done((f32[48,128]{1,0:T(8,128)S(1)}, f32[48,128]{1,0:T(8,128)S(1)}, u32[]{:S(2)}, u32[]{:S(2)}) %collective-permute-start.16) | collective-permute-done | bytes 24608 | tf_op jit(solution)/shard_map/ppermute | solution.py:32
  52.1 1.4 %collective-permute-start.18 = (f32[2,32,128]{2,1,0:T(8,128)S(1)}, f32[2,32,128]{2,1,0:T(8,128)S(1)}, u32[]{:S(2)}, u32[]{:S(2)}) collective-permute-start(f32[2,32,128]{2,1,0:T(8,128)S(1)} %bitcast.73), channel_id=1, source_target_pairs={{0,8},{4,12},{8,0},{12,4},{1,9},{5,13},{9,1},{13,5},{2,10},{6,14},... | collective-permute-start | bytes 98312 | tf_op jit(solution)/shard_map/ppermute | solution.py:47
  53.5 2.5 %collective-permute-done.18 = f32[2,32,128]{2,1,0:T(8,128)S(1)} collective-permute-done((f32[2,32,128]{2,1,0:T(8,128)S(1)}, f32[2,32,128]{2,1,0:T(8,128)S(1)}, u32[]{:S(2)}, u32[]{:S(2)}) %collective-permute-start.18) | collective-permute-done | bytes 32800 | tf_op jit(solution)/shard_map/ppermute | solution.py:47
  56.2 2.4 %collective-permute-start.20 = (f32[128,128]{0,1:T(8,128)S(1)}, f32[128,128]{0,1:T(8,128)S(1)}, u32[]{:S(2)}, u32[]{:S(2)}) collective-permute-start(f32[128,128]{0,1:T(8,128)S(1)} %copy.11), channel_id=1, source_target_pairs={{0,2},{1,3},{2,0},{3,1},{4,6},{5,7},{6,4},{7,5},{8,10},{9,11},{10,... | collective-permute-start | bytes 196616 | tf_op jit(solution)/shard_map/ppermute | solution.py:47
  58.5 4.6 %step.5 = f32[4,32,16,256]{3,2,1,0:T(8,128)} custom-call(s32[2]{0:T(128)S(1)} %bitcast.64, f32[8,24,128]{2,1,0:T(8,128)S(1)} %bitcast.61, f32[4,32,16,256]{3,2,1,0:T(8,128)S(1)} %get-tuple-element.84.refs_2_, f32[144,256]{1,0:T(8,128)S(1)} %collective-permute-done.14.refs_3_, f32[128,256]{1,0:T(8,128)S(1)} %collective-permute-done.15.refs_4_, ...), custom_call_target="tpu_custom_call" | custom-call | tf_op jit(solution)/shard_map/step/pallas_call | solution.py:438
  63.3 1.2 %collective-permute-done.21 = f32[1,128,32]{1,2,0:T(8,128)S(1)} collective-permute-done((f32[1,128,32]{1,2,0:T(8,128)S(1)}, f32[1,128,32]{1,2,0:T(8,128)S(1)}, u32[]{:S(2)}, u32[]{:S(2)}) %collective-permute-start.21) | collective-permute-done | bytes 16416 | tf_op jit(solution)/shard_map/ppermute | solution.py:47
  64.5 0.1 copy.12
  64.7 0.6 add.42
  (60 shorter events, 0.7 us)
Async XLA Ops:
  0.6 21.8 %copy-start.2 = (s32[1,1,1,2]{3,2,1,0:T(1,128)S(1)}, s32[1,1,1,2]{3,2,1,0:T(1,128)}, u32[]{:S(2)}) copy-start(s32[1,1,1,2]{3,2,1,0:T(1,128)} %param.7) | copy-start | bytes 28
  1.4 5.4 %collective-permute-start = (f32[1,24,32]{2,1,0:T(8,128)S(1)}, f32[1,24,32]{2,1,0:T(8,128)S(1)}, u32[]{:S(2)}, u32[]{:S(2)}) collective-permute-start(f32[1,24,32]{2,1,0:T(8,128)S(1)} %fusion.5), channel_id=1, source_target_pairs={{0,1},{1,0},{2,3},{3,2},{4,5},{5,4},{6,7},{7,6},{8,9},{9,8},{10,11... | collective-permute-start | bytes 9224 | tf_op jit(solution)/shard_map/ppermute | solution.py:47
  4.5 1.6 %copy-start = (f32[4,32,16,256]{3,2,1,0:T(8,128)S(1)}, f32[4,32,16,256]{3,2,1,0:T(8,128)}, u32[]{:S(2)}) copy-start(f32[4,32,16,256]{3,2,1,0:T(8,128)} %refs_2_.1) | copy-start | bytes 6291460
  6.0 16.4 %copy-start.1 = (f32[4,32,16,256]{3,2,1,0:T(8,128)S(1)}, f32[4,32,16,256]{3,2,1,0:T(8,128)}, u32[]{:S(2)}) copy-start(f32[4,32,16,256]{3,2,1,0:T(8,128)} %refs_2_.1) | copy-start | bytes 6291460
  6.8 5.3 %collective-permute-start.2 = (f32[128,256]{1,0:T(8,128)S(1)}, f32[128,256]{1,0:T(8,128)S(1)}, u32[]{:S(2)}, u32[]{:S(2)}) collective-permute-start(f32[128,256]{1,0:T(8,128)S(1)} %get-tuple-element.54), channel_id=1, source_target_pairs={{0,1},{1,0},{2,3},{3,2},{4,5},{5,4},{6,7},{7,6},{8,9},{9,8},{10,11... | collective-permute-start | bytes 393224 | tf_op jit(solution)/shard_map/ppermute | solution.py:32
  8.2 4.9 %collective-permute-start.1 = (f32[2,24,32]{2,1,0:T(8,128)S(1)}, f32[2,24,32]{2,1,0:T(8,128)S(1)}, u32[]{:S(2)}, u32[]{:S(2)}) collective-permute-start(f32[2,24,32]{2,1,0:T(8,128)S(1)} %pad_maximum_fusion.5), channel_id=1, source_target_pairs={{0,2},{1,3},{2,0},{3,1},{4,6},{5,7},{6,4},{7,5},{8,10},{9,11},{10,... | collective-permute-start | bytes 18440 | tf_op jit(solution)/shard_map/ppermute | solution.py:47
  13.2 1.6 %collective-permute-start.4 = (f32[128,256]{1,0:T(8,128)S(1)}, f32[128,256]{1,0:T(8,128)S(1)}, u32[]{:S(2)}, u32[]{:S(2)}) collective-permute-start(f32[128,256]{1,0:T(8,128)S(1)} %get-tuple-element.58), channel_id=1, source_target_pairs={{0,16},{1,2},{2,1},{3,19},{16,0},{17,18},{18,17},{19,3},{4,20},{5,... | collective-permute-start | bytes 393224 | tf_op jit(solution)/shard_map/ppermute | solution.py:42
  13.2 3.8 %collective-permute-start.3 = (f32[40,128]{1,0:T(8,128)S(1)}, f32[40,128]{1,0:T(8,128)S(1)}, u32[]{:S(2)}, u32[]{:S(2)}) collective-permute-start(f32[40,128]{1,0:T(8,128)S(1)} %pad_maximum_fusion.8), channel_id=1, source_target_pairs={{0,4},{4,0},{8,12},{12,8},{1,5},{5,1},{9,13},{13,9},{2,6},{6,2},{1... | collective-permute-start | bytes 61448 | tf_op jit(solution)/shard_map/ppermute | solution.py:32
  17.1 3.8 %collective-permute-start.5 = (f32[2,24,128]{2,1,0:T(8,128)S(1)}, f32[2,24,128]{2,1,0:T(8,128)S(1)}, u32[]{:S(2)}, u32[]{:S(2)}) collective-permute-start(f32[2,24,128]{2,1,0:T(8,128)S(1)} %bitcast.75), channel_id=1, source_target_pairs={{0,8},{4,12},{8,0},{12,4},{1,9},{5,13},{9,1},{13,5},{2,10},{6,14},... | collective-permute-start | bytes 73736 | tf_op jit(solution)/shard_map/ppermute | solution.py:47
  18.6 2.3 %collective-permute-start.6 = (f32[16,128]{1,0:T(8,128)S(1)}, f32[16,128]{1,0:T(8,128)S(1)}, u32[]{:S(2)}, u32[]{:S(2)}) collective-permute-start(f32[16,128]{1,0:T(8,128)S(1)} %get-tuple-element.61), channel_id=1, source_target_pairs={{0,16},{4,8},{8,4},{12,28},{16,0},{20,24},{24,20},{28,12},{1,17},{... | collective-permute-start | bytes 24584 | tf_op jit(solution)/shard_map/ppermute | solution.py:42
  20.9 1.3 %collective-permute-start.7 = (f32[1,4,24,128]{3,2,1,0:T(8,128)S(1)}, f32[1,4,24,128]{3,2,1,0:T(8,128)S(1)}, u32[]{:S(2)}, u32[]{:S(2)}) collective-permute-start(f32[1,4,24,128]{3,2,1,0:T(8,128)S(1)} %bitcast.71), channel_id=1, source_target_pairs={{0,16},{16,0},{1,17},{17,1},{2,18},{18,2},{3,19},{19,3},{4,20},{20... | collective-permute-start | bytes 147464 | tf_op jit(solution)/shard_map/ppermute | solution.py:47
  21.0 1.4 %collective-permute-start.8 = (f32[4,16,256]{2,1,0:T(8,128)S(1)}, f32[4,16,256]{2,1,0:T(8,128)S(1)}, u32[]{:S(2)}, u32[]{:S(2)}) collective-permute-start(f32[4,16,256]{2,1,0:T(8,128)S(1)} %get-tuple-element.66), channel_id=1, source_target_pairs={{0,16},{16,0},{1,17},{17,1},{2,18},{18,2},{3,19},{19,3},{4,20},{20... | collective-permute-start | bytes 196616 | tf_op jit(solution)/shard_map/ppermute | solution.py:32
  28.1 9.0 %collective-permute-start.9 = (f32[128,256]{1,0:T(8,128)S(1)}, f32[128,256]{1,0:T(8,128)S(1)}, u32[]{:S(2)}, u32[]{:S(2)}) collective-permute-start(f32[128,256]{1,0:T(8,128)S(1)} %get-tuple-element.68), channel_id=1, source_target_pairs={{0,1},{1,0},{2,3},{3,2},{4,5},{5,4},{6,7},{7,6},{8,9},{9,8},{10,11... | collective-permute-start | bytes 393224 | tf_op jit(solution)/shard_map/ppermute | solution.py:32
  31.3 5.8 %collective-permute-start.10 = (f32[128,256]{1,0:T(8,128)S(1)}, f32[128,256]{1,0:T(8,128)S(1)}, u32[]{:S(2)}, u32[]{:S(2)}) collective-permute-start(f32[128,256]{1,0:T(8,128)S(1)} %get-tuple-element.69), channel_id=1, source_target_pairs={{0,16},{1,2},{2,1},{3,19},{16,0},{17,18},{18,17},{19,3},{4,20},{5,... | collective-permute-start | bytes 393224 | tf_op jit(solution)/shard_map/ppermute | solution.py:42
  31.3 5.8 %collective-permute-start.13 = (f32[4,16,256]{2,1,0:T(8,128)S(1)}, f32[4,16,256]{2,1,0:T(8,128)S(1)}, u32[]{:S(2)}, u32[]{:S(2)}) collective-permute-start(f32[4,16,256]{2,1,0:T(8,128)S(1)} %get-tuple-element.72), channel_id=1, source_target_pairs={{0,16},{16,0},{1,17},{17,1},{2,18},{18,2},{3,19},{19,3},{4,20},{20... | collective-permute-start | bytes 196616 | tf_op jit(solution)/shard_map/ppermute | solution.py:32
  31.8 5.3 %collective-permute-start.11 = (f32[16,128]{1,0:T(8,128)S(1)}, f32[16,128]{1,0:T(8,128)S(1)}, u32[]{:S(2)}, u32[]{:S(2)}) collective-permute-start(f32[16,128]{1,0:T(8,128)S(1)} %get-tuple-element.70), channel_id=1, source_target_pairs={{0,4},{4,0},{8,12},{12,8},{1,5},{5,1},{9,13},{13,9},{2,6},{6,2},{1... | collective-permute-start | bytes 24584 | tf_op jit(solution)/shard_map/ppermute | solution.py:32
  35.5 1.6 %collective-permute-start.12 = (f32[16,128]{1,0:T(8,128)S(1)}, f32[16,128]{1,0:T(8,128)S(1)}, u32[]{:S(2)}, u32[]{:S(2)}) collective-permute-start(f32[16,128]{1,0:T(8,128)S(1)} %get-tuple-element.71), channel_id=1, source_target_pairs={{0,16},{4,8},{8,4},{12,28},{16,0},{20,24},{24,20},{28,12},{1,17},{... | collective-permute-start | bytes 24584 | tf_op jit(solution)/shard_map/ppermute | solution.py:42
  42.1 5.5 %collective-permute-start.14 = (f32[144,256]{1,0:T(8,128)S(1)}, f32[144,256]{1,0:T(8,128)S(1)}, u32[]{:S(2)}, u32[]{:S(2)}) collective-permute-start(f32[144,256]{1,0:T(8,128)S(1)} %get-tuple-element.74), channel_id=1, source_target_pairs={{0,1},{1,0},{2,3},{3,2},{4,5},{5,4},{6,7},{7,6},{8,9},{9,8},{10,11... | collective-permute-start | bytes 442376 | tf_op jit(solution)/shard_map/ppermute | solution.py:32
  42.9 4.7 %collective-permute-start.15 = (f32[128,256]{1,0:T(8,128)S(1)}, f32[128,256]{1,0:T(8,128)S(1)}, u32[]{:S(2)}, u32[]{:S(2)}) collective-permute-start(f32[128,256]{1,0:T(8,128)S(1)} %get-tuple-element.76), channel_id=1, source_target_pairs={{0,16},{1,2},{2,1},{3,19},{16,0},{17,18},{18,17},{19,3},{4,20},{5,... | collective-permute-start | bytes 393224 | tf_op jit(solution)/shard_map/ppermute | solution.py:42
  47.6 4.5 %collective-permute-start.16 = (f32[48,128]{1,0:T(8,128)S(1)}, f32[48,128]{1,0:T(8,128)S(1)}, u32[]{:S(2)}, u32[]{:S(2)}) collective-permute-start(f32[48,128]{1,0:T(8,128)S(1)} %pad_maximum_fusion.7), channel_id=1, source_target_pairs={{0,4},{4,0},{8,12},{12,8},{1,5},{5,1},{9,13},{13,9},{2,6},{6,2},{1... | collective-permute-start | bytes 73736 | tf_op jit(solution)/shard_map/ppermute | solution.py:32
  50.3 1.8 %collective-permute-start.17 = (f32[4,16,256]{2,1,0:T(8,128)S(1)}, f32[4,16,256]{2,1,0:T(8,128)S(1)}, u32[]{:S(2)}, u32[]{:S(2)}) collective-permute-start(f32[4,16,256]{2,1,0:T(8,128)S(1)} %get-tuple-element.80), channel_id=1, source_target_pairs={{0,16},{16,0},{1,17},{17,1},{2,18},{18,2},{3,19},{19,3},{4,20},{20... | collective-permute-start | bytes 196616 | tf_op jit(solution)/shard_map/ppermute | solution.py:32
  52.1 4.0 %collective-permute-start.18 = (f32[2,32,128]{2,1,0:T(8,128)S(1)}, f32[2,32,128]{2,1,0:T(8,128)S(1)}, u32[]{:S(2)}, u32[]{:S(2)}) collective-permute-start(f32[2,32,128]{2,1,0:T(8,128)S(1)} %bitcast.73), channel_id=1, source_target_pairs={{0,8},{4,12},{8,0},{12,4},{1,9},{5,13},{9,1},{13,5},{2,10},{6,14},... | collective-permute-start | bytes 98312 | tf_op jit(solution)/shard_map/ppermute | solution.py:47
  53.5 2.5 %collective-permute-start.19 = (f32[16,128]{1,0:T(8,128)S(1)}, f32[16,128]{1,0:T(8,128)S(1)}, u32[]{:S(2)}, u32[]{:S(2)}) collective-permute-start(f32[16,128]{1,0:T(8,128)S(1)} %get-tuple-element.82), channel_id=1, source_target_pairs={{0,16},{4,8},{8,4},{12,28},{16,0},{20,24},{24,20},{28,12},{1,17},{... | collective-permute-start | bytes 24584 | tf_op jit(solution)/shard_map/ppermute | solution.py:42
  56.2 7.0 %collective-permute-start.20 = (f32[128,128]{0,1:T(8,128)S(1)}, f32[128,128]{0,1:T(8,128)S(1)}, u32[]{:S(2)}, u32[]{:S(2)}) collective-permute-start(f32[128,128]{0,1:T(8,128)S(1)} %copy.11), channel_id=1, source_target_pairs={{0,2},{1,3},{2,0},{3,1},{4,6},{5,7},{6,4},{7,5},{8,10},{9,11},{10,... | collective-permute-start | bytes 196616 | tf_op jit(solution)/shard_map/ppermute | solution.py:47
  63.2 1.2 %collective-permute-start.21 = (f32[1,128,32]{1,2,0:T(8,128)S(1)}, f32[1,128,32]{1,2,0:T(8,128)S(1)}, u32[]{:S(2)}, u32[]{:S(2)}) collective-permute-start(f32[1,128,32]{1,2,0:T(8,128)S(1)} %dynamic-slice_bitcast_fusion), channel_id=1, source_target_pairs={{0,16},{16,0},{1,17},{17,1},{2,18},{18,2},{3,19},{19,3},{4,20},{20... | collective-permute-start | bytes 49160 | tf_op jit(solution)/shard_map/ppermute | solution.py:47

commit v11 on v8

--- a/solution.py
+++ b/solution.py
@@ -47,8 +47,7 @@
     return lax.ppermute(value, axis, [(i, i ^ distance) for i in range(count)])
 
 
-def gather_relative(value, axis):
-    distance = 1
+def gather_relative(value, axis, distance=1):
     while distance < lax.axis_size(axis):
         value = jnp.concatenate([value, from_distance(value, axis, distance)], axis=0)
         distance *= 2
@@ -467,10 +466,11 @@
         pieces, ya, zb_in = barrier((pieces, ya, zb_in))
         ya_in = swap(jnp.concatenate([ya, pieces], axis=0), "gy", 0)
         x_faces = [swap(face, "gx", first) for first, face in enumerate(faces[4:])]
-        pieces = jnp.concatenate([pieces, ya_in[count_z:]], axis=0)
+        pieces = jnp.concatenate([pieces, ya_in[count_z:]], axis=0).reshape(2, -1, points)
         pieces, yb, x_faces = barrier((pieces, yb, x_faces))
-        yb_in = from_distance(jnp.concatenate([yb, pieces], axis=0), "gy", 3)
-        pieces = jnp.concatenate([pieces, yb_in[count_z:]], axis=0)
+        pieces = gather_relative(pieces, "gy", 2).reshape(-1, points)
+        yb_in = swap_inner(yb, "gy")
+        pieces, yb_in = barrier((pieces, yb_in))
         halos = [za_in, zb_in, ya_in, yb_in] + x_faces
 
     distance = 2

time: 65.6 us -> 65.3 us (level)
  starting transfers between devices: 26.1 us -> 26.8 us
  transfers between devices with their start and end apart: 20 -> 21, of which waited for: 11 -> 11; matrix products, arithmetic and copies ran while one was open for 0% -> 0% of each run, Pallas kernels for 8% -> 8%
where the time goes in v11:
time: 65.3 us; the launch traced here: 65.1 us
  starting transfers between devices  26.8 us (41%)
  waiting for transfers between devices  18.5 us (28%)
  Pallas kernels  15.4 us (24%)
  local copies, waits for them, and re-layouts  3.17 us (5%)
  between operations  0.92 us (1%)
    pallas_call x3, Pallas kernels, shards(): pl.pallas_call(functools.partial(step_body, shape=shape, points=points, c...  14.7 us
    ppermute x7, starting transfers between devices, from_distance(): return lax.ppermute(value, axis, [(i, i ^ distance) for i in range(count)])  13.7 us
    ppermute x9, starting transfers between devices, swap(): return lax.ppermute(value, axis, pairs)  13 us
    ppermute x9, waiting for transfers between devices, swap(): return lax.ppermute(value, axis, pairs)  11.5 us
    ppermute x7, waiting for transfers between devices, from_distance(): return lax.ppermute(value, axis, [(i, i ^ distance) for i in range(count)])  7.07 us
    unnamed x10, local copies, waits for them, and re-layouts  2.33 us
  transfers between devices with their start and end apart: 21, of which 11 were waited for; matrix products, arithmetic and copies ran while one was open for 0% of the time, Pallas kernels for 8%

profile of v11, /device:TPU:0, one launch (start us, length us, event | category | flops | bytes accessed | tf_op | source)
XLA Modules:
  0.0 65.1 jit_solution(11720862206372083577)
XLA Ops:
  0.6 0.7 %copy_bitcast_fusion = (f32[3,3,32]{2,1,0:T(4,128)S(1)}, f32[3,3,32]{2,1,0:T(4,128)S(1)}) fusion(f32[3,3,1,32]{3,2,1,0:T(1,128)} %param.6, f32[3,3,1,32]{3,2,1,0:T(1,128)} %param.5), kind=kLoop, calls=%fused_computation.35 | loop fusion | bytes 4608
  1.4 3.1 %collective-permute-start = (f32[1,24,32]{2,1,0:T(8,128)S(1)}, f32[1,24,32]{2,1,0:T(8,128)S(1)}, u32[]{:S(2)}, u32[]{:S(2)}) collective-permute-start(f32[1,24,32]{2,1,0:T(8,128)S(1)} %fusion.5), channel_id=1, source_target_pairs={{0,1},{1,0},{2,3},{3,2},{4,5},{5,4},{6,7},{7,6},{8,9},{9,8},{10,11... | collective-permute-start | bytes 9224 | tf_op jit(solution)/shard_map/ppermute | solution.py:47
  4.5 1.6 %copy-done = f32[4,32,16,256]{3,2,1,0:T(8,128)S(1)} copy-done((f32[4,32,16,256]{3,2,1,0:T(8,128)S(1)}, f32[4,32,16,256]{3,2,1,0:T(8,128)}, u32[]{:S(2)}) %copy-start) | copy-done | bytes 2097176
  6.0 0.7 %faces.1 = (f32[128,256]{1,0:T(8,128)S(1)}, f32[128,256]{1,0:T(8,128)S(1)}, f32[16,128]{1,0:T(8,128)S(1)}, f32[16,128]{1,0:T(8,128)S(1)}, f32[4,16,256]{2,1,0:T(8,128)S(1)}) custom-call(f32[4,32,16,256]{3,2,1,0:T(8,128)S(1)} %copy-done), custom_call_target="tpu_custom_call" | custom-call | tf_op jit(solution)/shard_map/faces/pallas_call | solution.py:389
  6.8 1.3 %collective-permute-start.2 = (f32[128,256]{1,0:T(8,128)S(1)}, f32[128,256]{1,0:T(8,128)S(1)}, u32[]{:S(2)}, u32[]{:S(2)}) collective-permute-start(f32[128,256]{1,0:T(8,128)S(1)} %get-tuple-element.51), channel_id=1, source_target_pairs={{0,1},{1,0},{2,3},{3,2},{4,5},{5,4},{6,7},{7,6},{8,9},{9,8},{10,11... | collective-permute-start | bytes 393224 | tf_op jit(solution)/shard_map/ppermute | solution.py:32
  8.2 2.6 %collective-permute-start.1 = (f32[2,24,32]{2,1,0:T(8,128)S(1)}, f32[2,24,32]{2,1,0:T(8,128)S(1)}, u32[]{:S(2)}, u32[]{:S(2)}) collective-permute-start(f32[2,24,32]{2,1,0:T(8,128)S(1)} %pad_maximum_fusion.5), channel_id=1, source_target_pairs={{0,2},{1,3},{2,0},{3,1},{4,6},{5,7},{6,4},{7,5},{8,10},{9,11},{10,... | collective-permute-start | bytes 18440 | tf_op jit(solution)/shard_map/ppermute | solution.py:47
  10.7 1.3 %collective-permute-done.2 = f32[128,256]{1,0:T(8,128)S(1)} collective-permute-done((f32[128,256]{1,0:T(8,128)S(1)}, f32[128,256]{1,0:T(8,128)S(1)}, u32[]{:S(2)}, u32[]{:S(2)}) %collective-permute-start.2) | collective-permute-done | bytes 131104 | tf_op jit(solution)/shard_map/ppermute | solution.py:32
  12.1 0.9 %collective-permute-done.1 = f32[2,24,32]{2,1,0:T(8,128)S(1)} collective-permute-done((f32[2,24,32]{2,1,0:T(8,128)S(1)}, f32[2,24,32]{2,1,0:T(8,128)S(1)}, u32[]{:S(2)}, u32[]{:S(2)}) %collective-permute-start.1) | collective-permute-done | bytes 6176 | tf_op jit(solution)/shard_map/ppermute | solution.py:47
  13.2 1.6 %collective-permute-start.3 = (f32[40,128]{1,0:T(8,128)S(1)}, f32[40,128]{1,0:T(8,128)S(1)}, u32[]{:S(2)}, u32[]{:S(2)}) collective-permute-start(f32[40,128]{1,0:T(8,128)S(1)} %pad_maximum_fusion.7), channel_id=1, source_target_pairs={{0,4},{4,0},{8,12},{12,8},{1,5},{5,1},{9,13},{13,9},{2,6},{6,2},{1... | collective-permute-start | bytes 61448 | tf_op jit(solution)/shard_map/ppermute | solution.py:32
  14.8 2.3 %collective-permute-done.3.refs_5_ = f32[40,128]{1,0:T(8,128)S(1)} collective-permute-done((f32[40,128]{1,0:T(8,128)S(1)}, f32[40,128]{1,0:T(8,128)S(1)}, u32[]{:S(2)}, u32[]{:S(2)}) %collective-permute-start.3) | collective-permute-done | bytes 20512 | tf_op jit(solution)/shard_map/ppermute | solution.py:32
  17.1 2.4 %collective-permute-start.5 = (f32[64,128]{1,0:T(8,128)S(1)}, f32[64,128]{1,0:T(8,128)S(1)}, u32[]{:S(2)}, u32[]{:S(2)}) collective-permute-start(f32[64,128]{1,0:T(8,128)S(1)} %pad_maximum_fusion.2), channel_id=1, source_target_pairs={{0,12},{4,8},{8,4},{12,0},{1,13},{5,9},{9,5},{13,1},{2,14},{6,10},... | collective-permute-start | bytes 98312 | tf_op jit(solution)/shard_map/ppermute | solution.py:47
  19.5 2.4 %collective-permute-done.5.refs_6_ = f32[64,128]{1,0:T(8,128)S(1)} collective-permute-done((f32[64,128]{1,0:T(8,128)S(1)}, f32[64,128]{1,0:T(8,128)S(1)}, u32[]{:S(2)}, u32[]{:S(2)}) %collective-permute-start.5) | collective-permute-done | bytes 32800 | tf_op jit(solution)/shard_map/ppermute | solution.py:47
  22.0 0.5 collective-permute-start.7
  22.5 0.7 %collective-permute-done.6 = f32[1,96,128]{2,1,0:T(8,128)S(1)} collective-permute-done((f32[1,96,128]{2,1,0:T(8,128)S(1)}, f32[1,96,128]{2,1,0:T(8,128)S(1)}, u32[]{:S(2)}, u32[]{:S(2)}) %collective-permute-start.6) | collective-permute-done | bytes 49184 | tf_op jit(solution)/shard_map/ppermute | solution.py:47
  23.2 0.2 collective-permute-done.7.refs_7_
  23.4 5.2 %step.3 = (f32[4,32,16,256]{3,2,1,0:T(8,128)S(1)}, f32[128,256]{1,0:T(8,128)S(1)}, f32[128,256]{1,0:T(8,128)S(1)}, f32[16,128]{1,0:T(8,128)S(1)}, f32[16,128]{1,...) custom-call(s32[2]{0:T(128)S(1)} %bitcast.62, f32[8,24,128]{2,1,0:T(8,128)S(1)} %bitcast.59, ...), custom_call_target="tpu_custom_call" | custom-call | tf_op jit(solution)/shard_map/step/pallas_call | solution.py:437
  28.6 3.2 %collective-permute-start.8 = (f32[128,256]{1,0:T(8,128)S(1)}, f32[128,256]{1,0:T(8,128)S(1)}, u32[]{:S(2)}, u32[]{:S(2)}) collective-permute-start(f32[128,256]{1,0:T(8,128)S(1)} %get-tuple-element.62), channel_id=1, source_target_pairs={{0,1},{1,0},{2,3},{3,2},{4,5},{5,4},{6,7},{7,6},{8,9},{9,8},{10,11... | collective-permute-start | bytes 393224 | tf_op jit(solution)/shard_map/ppermute | solution.py:32
  31.8 0.4 collective-permute-start.12
  32.3 1.5 %collective-permute-start.10 = (f32[16,128]{1,0:T(8,128)S(1)}, f32[16,128]{1,0:T(8,128)S(1)}, u32[]{:S(2)}, u32[]{:S(2)}) collective-permute-start(f32[16,128]{1,0:T(8,128)S(1)} %get-tuple-element.64), channel_id=1, source_target_pairs={{0,4},{4,0},{8,12},{12,8},{1,5},{5,1},{9,13},{13,9},{2,6},{6,2},{1... | collective-permute-start | bytes 24584 | tf_op jit(solution)/shard_map/ppermute | solution.py:32
  33.8 2.2 %collective-permute-done.10.refs_5_ = f32[16,128]{1,0:T(8,128)S(1)} collective-permute-done((f32[16,128]{1,0:T(8,128)S(1)}, f32[16,128]{1,0:T(8,128)S(1)}, u32[]{:S(2)}, u32[]{:S(2)}) %collective-permute-start.10) | collective-permute-done | bytes 8224 | tf_op jit(solution)/shard_map/ppermute | solution.py:32
  35.9 4.9 %step.4 = (f32[4,32,16,256]{3,2,1,0:T(8,128)S(1)}, f32[144,256]{1,0:T(8,128)S(1)}, f32[128,256]{1,0:T(8,128)S(1)}, f32[16,128]{1,0:T(8,128)S(1)}, f32[16,128]{1,0:T(8,128)S(1)}, /*index=5*/f32[4,16,256]{2,1,0:T(8,128)S(1)}) custom-call(s32[2]{0:T(128)S(1)} %bitcast.63, f32[8,24,128]{2,1,0:T(8,128)S(1)} %bitcast.60, ...), custom_call_target="tpu_custom_call" | custom-call | tf_op jit(solution)/shard_map/step/pallas_call | solution.py:437
  40.8 1.7 %collective-permute-start.13 = (f32[144,256]{1,0:T(8,128)S(1)}, f32[144,256]{1,0:T(8,128)S(1)}, u32[]{:S(2)}, u32[]{:S(2)}) collective-permute-start(f32[144,256]{1,0:T(8,128)S(1)} %get-tuple-element.68), channel_id=1, source_target_pairs={{0,1},{1,0},{2,3},{3,2},{4,5},{5,4},{6,7},{7,6},{8,9},{9,8},{10,11... | collective-permute-start | bytes 442376 | tf_op jit(solution)/shard_map/ppermute | solution.py:32
  42.5 3.7 %collective-permute-done.13.refs_3_ = f32[144,256]{1,0:T(8,128)S(1)} collective-permute-done((f32[144,256]{1,0:T(8,128)S(1)}, f32[144,256]{1,0:T(8,128)S(1)}, u32[]{:S(2)}, u32[]{:S(2)}) %collective-permute-start.13) | collective-permute-done | bytes 147488 | tf_op jit(solution)/shard_map/ppermute | solution.py:32
  46.3 2.8 %collective-permute-start.15 = (f32[48,128]{1,0:T(8,128)S(1)}, f32[48,128]{1,0:T(8,128)S(1)}, u32[]{:S(2)}, u32[]{:S(2)}) collective-permute-start(f32[48,128]{1,0:T(8,128)S(1)} %pad_maximum_fusion.6), channel_id=1, source_target_pairs={{0,4},{4,0},{8,12},{12,8},{1,5},{5,1},{9,13},{13,9},{2,6},{6,2},{1... | collective-permute-start | bytes 73736 | tf_op jit(solution)/shard_map/ppermute | solution.py:32
  49.1 1.8 %collective-permute-done.15.refs_5_ = f32[48,128]{1,0:T(8,128)S(1)} collective-permute-done((f32[48,128]{1,0:T(8,128)S(1)}, f32[48,128]{1,0:T(8,128)S(1)}, u32[]{:S(2)}, u32[]{:S(2)}) %collective-permute-start.15) | collective-permute-done | bytes 24608 | tf_op jit(solution)/shard_map/ppermute | solution.py:32
  50.9 3.1 %collective-permute-start.17 = (f32[2,32,128]{2,1,0:T(8,128)S(1)}, f32[2,32,128]{2,1,0:T(8,128)S(1)}, u32[]{:S(2)}, u32[]{:S(2)}) collective-permute-start(f32[2,32,128]{2,1,0:T(8,128)S(1)} %bitcast.71), channel_id=1, source_target_pairs={{0,8},{4,12},{8,0},{12,4},{1,9},{5,13},{9,1},{13,5},{2,10},{6,14},... | collective-permute-start | bytes 98312 | tf_op jit(solution)/shard_map/ppermute | solution.py:47
  53.9 1.9 %collective-permute-done.17 = f32[2,32,128]{2,1,0:T(8,128)S(1)} collective-permute-done((f32[2,32,128]{2,1,0:T(8,128)S(1)}, f32[2,32,128]{2,1,0:T(8,128)S(1)}, u32[]{:S(2)}, u32[]{:S(2)}) %collective-permute-start.17) | collective-permute-done | bytes 32800 | tf_op jit(solution)/shard_map/ppermute | solution.py:47
  55.9 2.3 %collective-permute-start.19 = (f32[128,128]{0,1:T(8,128)S(1)}, f32[128,128]{0,1:T(8,128)S(1)}, u32[]{:S(2)}, u32[]{:S(2)}) collective-permute-start(f32[128,128]{0,1:T(8,128)S(1)} %copy.11), channel_id=1, source_target_pairs={{0,2},{1,3},{2,0},{3,1},{4,6},{5,7},{6,4},{7,5},{8,10},{9,11},{10,... | collective-permute-start | bytes 196616 | tf_op jit(solution)/shard_map/ppermute | solution.py:47
  58.3 4.6 %step.5 = f32[4,32,16,256]{3,2,1,0:T(8,128)} custom-call(s32[2]{0:T(128)S(1)} %bitcast.64, f32[8,24,128]{2,1,0:T(8,128)S(1)} %bitcast.61, f32[4,32,16,256]{3,2,1,0:T(8,128)S(1)} %get-tuple-element.78.refs_2_, f32[144,256]{1,0:T(8,128)S(1)} %collective-permute-done.13.refs_3_, f32[128,256]{1,0:T(8,128)S(1)} %collective-permute-done.14.refs_4_, ...), custom_call_target="tpu_custom_call" | custom-call | tf_op jit(solution)/shard_map/step/pallas_call | solution.py:437
  63.1 1.2 %collective-permute-done.20 = f32[1,128,32]{1,2,0:T(8,128)S(1)} collective-permute-done((f32[1,128,32]{1,2,0:T(8,128)S(1)}, f32[1,128,32]{1,2,0:T(8,128)S(1)}, u32[]{:S(2)}, u32[]{:S(2)}) %collective-permute-start.20) | collective-permute-done | bytes 16416 | tf_op jit(solution)/shard_map/ppermute | solution.py:47
  64.2 0.1 copy.12
  64.5 0.6 add.42
  (59 shorter events, 0.7 us)
Async XLA Ops:
  0.6 22.8 %copy-start.2 = (s32[1,1,1,2]{3,2,1,0:T(1,128)S(1)}, s32[1,1,1,2]{3,2,1,0:T(1,128)}, u32[]{:S(2)}) copy-start(s32[1,1,1,2]{3,2,1,0:T(1,128)} %param.7) | copy-start | bytes 28
  1.4 5.4 %collective-permute-start = (f32[1,24,32]{2,1,0:T(8,128)S(1)}, f32[1,24,32]{2,1,0:T(8,128)S(1)}, u32[]{:S(2)}, u32[]{:S(2)}) collective-permute-start(f32[1,24,32]{2,1,0:T(8,128)S(1)} %fusion.5), channel_id=1, source_target_pairs={{0,1},{1,0},{2,3},{3,2},{4,5},{5,4},{6,7},{7,6},{8,9},{9,8},{10,11... | collective-permute-start | bytes 9224 | tf_op jit(solution)/shard_map/ppermute | solution.py:47
  4.5 1.6 %copy-start = (f32[4,32,16,256]{3,2,1,0:T(8,128)S(1)}, f32[4,32,16,256]{3,2,1,0:T(8,128)}, u32[]{:S(2)}) copy-start(f32[4,32,16,256]{3,2,1,0:T(8,128)} %refs_2_.1) | copy-start | bytes 6291460
  6.0 17.4 %copy-start.1 = (f32[4,32,16,256]{3,2,1,0:T(8,128)S(1)}, f32[4,32,16,256]{3,2,1,0:T(8,128)}, u32[]{:S(2)}) copy-start(f32[4,32,16,256]{3,2,1,0:T(8,128)} %refs_2_.1) | copy-start | bytes 6291460
  6.8 5.3 %collective-permute-start.2 = (f32[128,256]{1,0:T(8,128)S(1)}, f32[128,256]{1,0:T(8,128)S(1)}, u32[]{:S(2)}, u32[]{:S(2)}) collective-permute-start(f32[128,256]{1,0:T(8,128)S(1)} %get-tuple-element.51), channel_id=1, source_target_pairs={{0,1},{1,0},{2,3},{3,2},{4,5},{5,4},{6,7},{7,6},{8,9},{9,8},{10,11... | collective-permute-start | bytes 393224 | tf_op jit(solution)/shard_map/ppermute | solution.py:32
  8.2 4.9 %collective-permute-start.1 = (f32[2,24,32]{2,1,0:T(8,128)S(1)}, f32[2,24,32]{2,1,0:T(8,128)S(1)}, u32[]{:S(2)}, u32[]{:S(2)}) collective-permute-start(f32[2,24,32]{2,1,0:T(8,128)S(1)} %pad_maximum_fusion.5), channel_id=1, source_target_pairs={{0,2},{1,3},{2,0},{3,1},{4,6},{5,7},{6,4},{7,5},{8,10},{9,11},{10,... | collective-permute-start | bytes 18440 | tf_op jit(solution)/shard_map/ppermute | solution.py:47
  13.2 1.6 %collective-permute-start.4 = (f32[128,256]{1,0:T(8,128)S(1)}, f32[128,256]{1,0:T(8,128)S(1)}, u32[]{:S(2)}, u32[]{:S(2)}) collective-permute-start(f32[128,256]{1,0:T(8,128)S(1)} %get-tuple-element.55), channel_id=1, source_target_pairs={{0,16},{1,2},{2,1},{3,19},{16,0},{17,18},{18,17},{19,3},{4,20},{5,... | collective-permute-start | bytes 393224 | tf_op jit(solution)/shard_map/ppermute | solution.py:42
  13.2 3.8 %collective-permute-start.3 = (f32[40,128]{1,0:T(8,128)S(1)}, f32[40,128]{1,0:T(8,128)S(1)}, u32[]{:S(2)}, u32[]{:S(2)}) collective-permute-start(f32[40,128]{1,0:T(8,128)S(1)} %pad_maximum_fusion.7), channel_id=1, source_target_pairs={{0,4},{4,0},{8,12},{12,8},{1,5},{5,1},{9,13},{13,9},{2,6},{6,2},{1... | collective-permute-start | bytes 61448 | tf_op jit(solution)/shard_map/ppermute | solution.py:32
  17.1 4.8 %collective-permute-start.5 = (f32[64,128]{1,0:T(8,128)S(1)}, f32[64,128]{1,0:T(8,128)S(1)}, u32[]{:S(2)}, u32[]{:S(2)}) collective-permute-start(f32[64,128]{1,0:T(8,128)S(1)} %pad_maximum_fusion.2), channel_id=1, source_target_pairs={{0,12},{4,8},{8,4},{12,0},{1,13},{5,9},{9,5},{13,1},{2,14},{6,10},... | collective-permute-start | bytes 98312 | tf_op jit(solution)/shard_map/ppermute | solution.py:47
  21.9 1.3 %collective-permute-start.6 = (f32[1,96,128]{2,1,0:T(8,128)S(1)}, f32[1,96,128]{2,1,0:T(8,128)S(1)}, u32[]{:S(2)}, u32[]{:S(2)}) collective-permute-start(f32[1,96,128]{2,1,0:T(8,128)S(1)} %maximum_bitcast_fusion), channel_id=1, source_target_pairs={{0,16},{16,0},{1,17},{17,1},{2,18},{18,2},{3,19},{19,3},{4,20},{20... | collective-permute-start | bytes 147464 | tf_op jit(solution)/shard_map/ppermute | solution.py:47
  22.0 1.4 %collective-permute-start.7 = (f32[4,16,256]{2,1,0:T(8,128)S(1)}, f32[4,16,256]{2,1,0:T(8,128)S(1)}, u32[]{:S(2)}, u32[]{:S(2)}) collective-permute-start(f32[4,16,256]{2,1,0:T(8,128)S(1)} %get-tuple-element.60), channel_id=1, source_target_pairs={{0,16},{16,0},{1,17},{17,1},{2,18},{18,2},{3,19},{19,3},{4,20},{20... | collective-permute-start | bytes 196616 | tf_op jit(solution)/shard_map/ppermute | solution.py:32
  28.6 7.3 %collective-permute-start.8 = (f32[128,256]{1,0:T(8,128)S(1)}, f32[128,256]{1,0:T(8,128)S(1)}, u32[]{:S(2)}, u32[]{:S(2)}) collective-permute-start(f32[128,256]{1,0:T(8,128)S(1)} %get-tuple-element.62), channel_id=1, source_target_pairs={{0,1},{1,0},{2,3},{3,2},{4,5},{5,4},{6,7},{7,6},{8,9},{9,8},{10,11... | collective-permute-start | bytes 393224 | tf_op jit(solution)/shard_map/ppermute | solution.py:32
  31.7 4.2 %collective-permute-start.9 = (f32[128,256]{1,0:T(8,128)S(1)}, f32[128,256]{1,0:T(8,128)S(1)}, u32[]{:S(2)}, u32[]{:S(2)}) collective-permute-start(f32[128,256]{1,0:T(8,128)S(1)} %get-tuple-element.63), channel_id=1, source_target_pairs={{0,16},{1,2},{2,1},{3,19},{16,0},{17,18},{18,17},{19,3},{4,20},{5,... | collective-permute-start | bytes 393224 | tf_op jit(solution)/shard_map/ppermute | solution.py:42
  31.8 4.1 %collective-permute-start.12 = (f32[4,16,256]{2,1,0:T(8,128)S(1)}, f32[4,16,256]{2,1,0:T(8,128)S(1)}, u32[]{:S(2)}, u32[]{:S(2)}) collective-permute-start(f32[4,16,256]{2,1,0:T(8,128)S(1)} %get-tuple-element.66), channel_id=1, source_target_pairs={{0,16},{16,0},{1,17},{17,1},{2,18},{18,2},{3,19},{19,3},{4,20},{20... | collective-permute-start | bytes 196616 | tf_op jit(solution)/shard_map/ppermute | solution.py:32
  32.3 3.7 %collective-permute-start.10 = (f32[16,128]{1,0:T(8,128)S(1)}, f32[16,128]{1,0:T(8,128)S(1)}, u32[]{:S(2)}, u32[]{:S(2)}) collective-permute-start(f32[16,128]{1,0:T(8,128)S(1)} %get-tuple-element.64), channel_id=1, source_target_pairs={{0,4},{4,0},{8,12},{12,8},{1,5},{5,1},{9,13},{13,9},{2,6},{6,2},{1... | collective-permute-start | bytes 24584 | tf_op jit(solution)/shard_map/ppermute | solution.py:32
  33.8 2.2 %collective-permute-start.11 = (f32[16,128]{1,0:T(8,128)S(1)}, f32[16,128]{1,0:T(8,128)S(1)}, u32[]{:S(2)}, u32[]{:S(2)}) collective-permute-start(f32[16,128]{1,0:T(8,128)S(1)} %get-tuple-element.65), channel_id=1, source_target_pairs={{0,16},{4,8},{8,4},{12,28},{16,0},{20,24},{24,20},{28,12},{1,17},{... | collective-permute-start | bytes 24584 | tf_op jit(solution)/shard_map/ppermute | solution.py:42
  40.8 5.4 %collective-permute-start.13 = (f32[144,256]{1,0:T(8,128)S(1)}, f32[144,256]{1,0:T(8,128)S(1)}, u32[]{:S(2)}, u32[]{:S(2)}) collective-permute-start(f32[144,256]{1,0:T(8,128)S(1)} %get-tuple-element.68), channel_id=1, source_target_pairs={{0,1},{1,0},{2,3},{3,2},{4,5},{5,4},{6,7},{7,6},{8,9},{9,8},{10,11... | collective-permute-start | bytes 442376 | tf_op jit(solution)/shard_map/ppermute | solution.py:32
  42.5 3.7 %collective-permute-start.14 = (f32[128,256]{1,0:T(8,128)S(1)}, f32[128,256]{1,0:T(8,128)S(1)}, u32[]{:S(2)}, u32[]{:S(2)}) collective-permute-start(f32[128,256]{1,0:T(8,128)S(1)} %get-tuple-element.70), channel_id=1, source_target_pairs={{0,16},{1,2},{2,1},{3,19},{16,0},{17,18},{18,17},{19,3},{4,20},{5,... | collective-permute-start | bytes 393224 | tf_op jit(solution)/shard_map/ppermute | solution.py:42
  46.3 4.6 %collective-permute-start.15 = (f32[48,128]{1,0:T(8,128)S(1)}, f32[48,128]{1,0:T(8,128)S(1)}, u32[]{:S(2)}, u32[]{:S(2)}) collective-permute-start(f32[48,128]{1,0:T(8,128)S(1)} %pad_maximum_fusion.6), channel_id=1, source_target_pairs={{0,4},{4,0},{8,12},{12,8},{1,5},{5,1},{9,13},{13,9},{2,6},{6,2},{1... | collective-permute-start | bytes 73736 | tf_op jit(solution)/shard_map/ppermute | solution.py:32
  49.0 1.8 %collective-permute-start.16 = (f32[4,16,256]{2,1,0:T(8,128)S(1)}, f32[4,16,256]{2,1,0:T(8,128)S(1)}, u32[]{:S(2)}, u32[]{:S(2)}) collective-permute-start(f32[4,16,256]{2,1,0:T(8,128)S(1)} %get-tuple-element.74), channel_id=1, source_target_pairs={{0,16},{16,0},{1,17},{17,1},{2,18},{18,2},{3,19},{19,3},{4,20},{20... | collective-permute-start | bytes 196616 | tf_op jit(solution)/shard_map/ppermute | solution.py:32
  50.9 5.0 %collective-permute-start.17 = (f32[2,32,128]{2,1,0:T(8,128)S(1)}, f32[2,32,128]{2,1,0:T(8,128)S(1)}, u32[]{:S(2)}, u32[]{:S(2)}) collective-permute-start(f32[2,32,128]{2,1,0:T(8,128)S(1)} %bitcast.71), channel_id=1, source_target_pairs={{0,8},{4,12},{8,0},{12,4},{1,9},{5,13},{9,1},{13,5},{2,10},{6,14},... | collective-permute-start | bytes 98312 | tf_op jit(solution)/shard_map/ppermute | solution.py:47
  53.9 1.9 %collective-permute-start.18 = (f32[16,128]{1,0:T(8,128)S(1)}, f32[16,128]{1,0:T(8,128)S(1)}, u32[]{:S(2)}, u32[]{:S(2)}) collective-permute-start(f32[16,128]{1,0:T(8,128)S(1)} %get-tuple-element.76), channel_id=1, source_target_pairs={{0,16},{4,8},{8,4},{12,28},{16,0},{20,24},{24,20},{28,12},{1,17},{... | collective-permute-start | bytes 24584 | tf_op jit(solution)/shard_map/ppermute | solution.py:42
  55.9 7.0 %collective-permute-start.19 = (f32[128,128]{0,1:T(8,128)S(1)}, f32[128,128]{0,1:T(8,128)S(1)}, u32[]{:S(2)}, u32[]{:S(2)}) collective-permute-start(f32[128,128]{0,1:T(8,128)S(1)} %copy.11), channel_id=1, source_target_pairs={{0,2},{1,3},{2,0},{3,1},{4,6},{5,7},{6,4},{7,5},{8,10},{9,11},{10,... | collective-permute-start | bytes 196616 | tf_op jit(solution)/shard_map/ppermute | solution.py:47
  63.0 1.2 %collective-permute-start.20 = (f32[1,128,32]{1,2,0:T(8,128)S(1)}, f32[1,128,32]{1,2,0:T(8,128)S(1)}, u32[]{:S(2)}, u32[]{:S(2)}) collective-permute-start(f32[1,128,32]{1,2,0:T(8,128)S(1)} %dynamic-slice_bitcast_fusion), channel_id=1, source_target_pairs={{0,16},{16,0},{1,17},{17,1},{2,18},{18,2},{3,19},{19,3},{4,20},{20... | collective-permute-start | bytes 49160 | tf_op jit(solution)/shard_map/ppermute | solution.py:47

commit v12 on v11

--- a/solution.py
+++ b/solution.py
@@ -167,10 +167,11 @@
     return weights, split(factor_y)
 
 
-def store_factors(rows, listed, weight_ref, right_ref, shape, along_points):
+def store_factors(rows, listed, weight_ref, right_refs, shape):
     weights, (high, low) = point_factors(rows, listed, shape)
     weight_ref[...] = weights.reshape(weight_ref.shape)
-    right_ref[...] = jnp.concatenate([high, high, low], axis=1 if along_points else 0)
+    for axis, right_ref in right_refs.items():
+        right_ref[...] = jnp.concatenate([high, high, low], axis=axis)
 
 
 def push(force_ref, rows, weight_ref, right_ref, start, planes, shape):
@@ -228,14 +229,8 @@
         if past_ref is not None:
             sample_ref[: 3 * step + 3] = past_ref[: 3 * step + 3]
 
-    if not last:
-        rows = turbine_rows(rows_ref, table_ref, slots, step + 1, points)
-        store_factors(rows, listed, next_weight_ref, sample_right_ref, shape, False)
     rows = turbine_rows(rows_ref, table_ref, slots, step, points)
-    store_factors(rows, listed, weight_ref, push_right_ref, shape, True)
-    if step == 0:
-        high, low = point_factors(rows, listed, shape)[1]
-        first_right_ref[...] = jnp.concatenate([high, high, low], axis=0)
+    store_factors(rows, listed, weight_ref, {1: push_right_ref, 0: first_right_ref} if step == 0 else {1: push_right_ref}, shape)
 
     even_x, even_z, even_y = is_even("gx"), is_even("gz"), is_even("gy")
     index_y, index_z = lax.axis_index("gy"), lax.axis_index("gz")
@@ -302,6 +297,9 @@
             minus = of_plane(x - 1) if x else lambda comp, here: low_x_ref[comp, :, here]
             plus = of_plane(x + 1) if x < count_x - 1 else lambda comp, here: high_x_ref[comp, :, here]
             plane(x, minus, plus)
+        if not last and not number:
+            next_rows = turbine_rows(rows_ref, table_ref, slots, step + 1, points)
+            store_factors(next_rows, listed, next_weight_ref, {0: sample_right_ref}, shape)
         if last:
             copy_out(number, start, group).start()
         elif number:
@@ -311,12 +309,12 @@
         for number in range(groups):
             copy_out(number, number * group, group).wait()
         return
+    write_faces(out_ref, face_refs, shape)
     more = sample(out_ref, next_weight_ref, sample_right_ref, count_x - group, group, shape)
     for comp in range(3):
         sample_ref[3 * step + 3 + comp : 3 * step + 4 + comp] = sums[comp] + more[comp]
         if step == 0:
             sample_ref[comp : comp + 1] = first_sums[comp]
-    write_faces(out_ref, face_refs, shape)
 
     if packs:
         count = 3 * steps + 1

time: 65.3 us -> 65.3 us (level)
  no operation moved by 1% of the time
where the time goes in v12:
time: 65.3 us; the launch traced here: 65.1 us
  starting transfers between devices  26.7 us (41%)
  waiting for transfers between devices  18.6 us (28%)
  Pallas kernels  15.4 us (24%)
  local copies, waits for them, and re-layouts  3.17 us (5%)
  between operations  0.92 us (1%)
    pallas_call x3, Pallas kernels, shards(): pl.pallas_call(functools.partial(step_body, shape=shape, points=points, c...  14.7 us
    ppermute x7, starting transfers between devices, from_distance(): return lax.ppermute(value, axis, [(i, i ^ distance) for i in range(count)])  13.7 us
    ppermute x9, starting transfers between devices, swap(): return lax.ppermute(value, axis, pairs)  13 us
    ppermute x9, waiting for transfers between devices, swap(): return lax.ppermute(value, axis, pairs)  11.5 us
    ppermute x7, waiting for transfers between devices, from_distance(): return lax.ppermute(value, axis, [(i, i ^ distance) for i in range(count)])  7.07 us
    unnamed x10, local copies, waits for them, and re-layouts  2.33 us
  transfers between devices with their start and end apart: 21, of which 11 were waited for; matrix products, arithmetic and copies ran while one was open for 0% of the time, Pallas kernels for 8%

profile of v12, /device:TPU:0, one launch (start us, length us, event | category | flops | bytes accessed | tf_op | source)
XLA Modules:
  0.0 65.1 jit_solution(7280697289199253470)
XLA Ops:
  0.6 0.7 %copy_bitcast_fusion = (f32[3,3,32]{2,1,0:T(4,128)S(1)}, f32[3,3,32]{2,1,0:T(4,128)S(1)}) fusion(f32[3,3,1,32]{3,2,1,0:T(1,128)} %param.6, f32[3,3,1,32]{3,2,1,0:T(1,128)} %param.5), kind=kLoop, calls=%fused_computation.35 | loop fusion | bytes 4608
  1.4 3.1 %collective-permute-start = (f32[1,24,32]{2,1,0:T(8,128)S(1)}, f32[1,24,32]{2,1,0:T(8,128)S(1)}, u32[]{:S(2)}, u32[]{:S(2)}) collective-permute-start(f32[1,24,32]{2,1,0:T(8,128)S(1)} %fusion.5), channel_id=1, source_target_pairs={{0,1},{1,0},{2,3},{3,2},{4,5},{5,4},{6,7},{7,6},{8,9},{9,8},{10,11... | collective-permute-start | bytes 9224 | tf_op jit(solution)/shard_map/ppermute | solution.py:47
  4.5 1.6 %copy-done = f32[4,32,16,256]{3,2,1,0:T(8,128)S(1)} copy-done((f32[4,32,16,256]{3,2,1,0:T(8,128)S(1)}, f32[4,32,16,256]{3,2,1,0:T(8,128)}, u32[]{:S(2)}) %copy-start) | copy-done | bytes 2097176
  6.0 0.7 %faces.1 = (f32[128,256]{1,0:T(8,128)S(1)}, f32[128,256]{1,0:T(8,128)S(1)}, f32[16,128]{1,0:T(8,128)S(1)}, f32[16,128]{1,0:T(8,128)S(1)}, f32[4,16,256]{2,1,0:T(8,128)S(1)}) custom-call(f32[4,32,16,256]{3,2,1,0:T(8,128)S(1)} %copy-done), custom_call_target="tpu_custom_call" | custom-call | tf_op jit(solution)/shard_map/faces/pallas_call | solution.py:387
  6.8 1.3 %collective-permute-start.2 = (f32[128,256]{1,0:T(8,128)S(1)}, f32[128,256]{1,0:T(8,128)S(1)}, u32[]{:S(2)}, u32[]{:S(2)}) collective-permute-start(f32[128,256]{1,0:T(8,128)S(1)} %get-tuple-element.51), channel_id=1, source_target_pairs={{0,1},{1,0},{2,3},{3,2},{4,5},{5,4},{6,7},{7,6},{8,9},{9,8},{10,11... | collective-permute-start | bytes 393224 | tf_op jit(solution)/shard_map/ppermute | solution.py:32
  8.2 2.6 %collective-permute-start.1 = (f32[2,24,32]{2,1,0:T(8,128)S(1)}, f32[2,24,32]{2,1,0:T(8,128)S(1)}, u32[]{:S(2)}, u32[]{:S(2)}) collective-permute-start(f32[2,24,32]{2,1,0:T(8,128)S(1)} %pad_maximum_fusion.5), channel_id=1, source_target_pairs={{0,2},{1,3},{2,0},{3,1},{4,6},{5,7},{6,4},{7,5},{8,10},{9,11},{10,... | collective-permute-start | bytes 18440 | tf_op jit(solution)/shard_map/ppermute | solution.py:47
  10.7 1.3 %collective-permute-done.2 = f32[128,256]{1,0:T(8,128)S(1)} collective-permute-done((f32[128,256]{1,0:T(8,128)S(1)}, f32[128,256]{1,0:T(8,128)S(1)}, u32[]{:S(2)}, u32[]{:S(2)}) %collective-permute-start.2) | collective-permute-done | bytes 131104 | tf_op jit(solution)/shard_map/ppermute | solution.py:32
  12.1 0.9 %collective-permute-done.1 = f32[2,24,32]{2,1,0:T(8,128)S(1)} collective-permute-done((f32[2,24,32]{2,1,0:T(8,128)S(1)}, f32[2,24,32]{2,1,0:T(8,128)S(1)}, u32[]{:S(2)}, u32[]{:S(2)}) %collective-permute-start.1) | collective-permute-done | bytes 6176 | tf_op jit(solution)/shard_map/ppermute | solution.py:47
  13.2 1.6 %collective-permute-start.3 = (f32[40,128]{1,0:T(8,128)S(1)}, f32[40,128]{1,0:T(8,128)S(1)}, u32[]{:S(2)}, u32[]{:S(2)}) collective-permute-start(f32[40,128]{1,0:T(8,128)S(1)} %pad_maximum_fusion.7), channel_id=1, source_target_pairs={{0,4},{4,0},{8,12},{12,8},{1,5},{5,1},{9,13},{13,9},{2,6},{6,2},{1... | collective-permute-start | bytes 61448 | tf_op jit(solution)/shard_map/ppermute | solution.py:32
  14.8 2.3 %collective-permute-done.3.refs_5_ = f32[40,128]{1,0:T(8,128)S(1)} collective-permute-done((f32[40,128]{1,0:T(8,128)S(1)}, f32[40,128]{1,0:T(8,128)S(1)}, u32[]{:S(2)}, u32[]{:S(2)}) %collective-permute-start.3) | collective-permute-done | bytes 20512 | tf_op jit(solution)/shard_map/ppermute | solution.py:32
  17.1 2.4 %collective-permute-start.5 = (f32[64,128]{1,0:T(8,128)S(1)}, f32[64,128]{1,0:T(8,128)S(1)}, u32[]{:S(2)}, u32[]{:S(2)}) collective-permute-start(f32[64,128]{1,0:T(8,128)S(1)} %pad_maximum_fusion.2), channel_id=1, source_target_pairs={{0,12},{4,8},{8,4},{12,0},{1,13},{5,9},{9,5},{13,1},{2,14},{6,10},... | collective-permute-start | bytes 98312 | tf_op jit(solution)/shard_map/ppermute | solution.py:47
  19.5 2.4 %collective-permute-done.5.refs_6_ = f32[64,128]{1,0:T(8,128)S(1)} collective-permute-done((f32[64,128]{1,0:T(8,128)S(1)}, f32[64,128]{1,0:T(8,128)S(1)}, u32[]{:S(2)}, u32[]{:S(2)}) %collective-permute-start.5) | collective-permute-done | bytes 32800 | tf_op jit(solution)/shard_map/ppermute | solution.py:47
  22.0 0.5 collective-permute-start.7
  22.5 0.7 %collective-permute-done.6 = f32[1,96,128]{2,1,0:T(8,128)S(1)} collective-permute-done((f32[1,96,128]{2,1,0:T(8,128)S(1)}, f32[1,96,128]{2,1,0:T(8,128)S(1)}, u32[]{:S(2)}, u32[]{:S(2)}) %collective-permute-start.6) | collective-permute-done | bytes 49184 | tf_op jit(solution)/shard_map/ppermute | solution.py:47
  23.2 0.2 collective-permute-done.7.refs_7_
  23.4 5.2 %step.3 = (f32[4,32,16,256]{3,2,1,0:T(8,128)S(1)}, f32[128,256]{1,0:T(8,128)S(1)}, f32[128,256]{1,0:T(8,128)S(1)}, f32[16,128]{1,0:T(8,128)S(1)}, f32[16,128]{1,...) custom-call(s32[2]{0:T(128)S(1)} %bitcast.62, f32[8,24,128]{2,1,0:T(8,128)S(1)} %bitcast.59, ...), custom_call_target="tpu_custom_call" | custom-call | tf_op jit(solution)/shard_map/step/pallas_call | solution.py:435
  28.6 3.2 %collective-permute-start.8 = (f32[128,256]{1,0:T(8,128)S(1)}, f32[128,256]{1,0:T(8,128)S(1)}, u32[]{:S(2)}, u32[]{:S(2)}) collective-permute-start(f32[128,256]{1,0:T(8,128)S(1)} %get-tuple-element.62), channel_id=1, source_target_pairs={{0,1},{1,0},{2,3},{3,2},{4,5},{5,4},{6,7},{7,6},{8,9},{9,8},{10,11... | collective-permute-start | bytes 393224 | tf_op jit(solution)/shard_map/ppermute | solution.py:32
  31.8 0.4 collective-permute-start.12
  32.3 1.5 %collective-permute-start.10 = (f32[16,128]{1,0:T(8,128)S(1)}, f32[16,128]{1,0:T(8,128)S(1)}, u32[]{:S(2)}, u32[]{:S(2)}) collective-permute-start(f32[16,128]{1,0:T(8,128)S(1)} %get-tuple-element.64), channel_id=1, source_target_pairs={{0,4},{4,0},{8,12},{12,8},{1,5},{5,1},{9,13},{13,9},{2,6},{6,2},{1... | collective-permute-start | bytes 24584 | tf_op jit(solution)/shard_map/ppermute | solution.py:32
  33.8 2.2 %collective-permute-done.10.refs_5_ = f32[16,128]{1,0:T(8,128)S(1)} collective-permute-done((f32[16,128]{1,0:T(8,128)S(1)}, f32[16,128]{1,0:T(8,128)S(1)}, u32[]{:S(2)}, u32[]{:S(2)}) %collective-permute-start.10) | collective-permute-done | bytes 8224 | tf_op jit(solution)/shard_map/ppermute | solution.py:32
  36.0 4.9 %step.4 = (f32[4,32,16,256]{3,2,1,0:T(8,128)S(1)}, f32[144,256]{1,0:T(8,128)S(1)}, f32[128,256]{1,0:T(8,128)S(1)}, f32[16,128]{1,0:T(8,128)S(1)}, f32[16,128]{1,0:T(8,128)S(1)}, /*index=5*/f32[4,16,256]{2,1,0:T(8,128)S(1)}) custom-call(s32[2]{0:T(128)S(1)} %bitcast.63, f32[8,24,128]{2,1,0:T(8,128)S(1)} %bitcast.60, ...), custom_call_target="tpu_custom_call" | custom-call | tf_op jit(solution)/shard_map/step/pallas_call | solution.py:435
  40.8 1.7 %collective-permute-start.13 = (f32[144,256]{1,0:T(8,128)S(1)}, f32[144,256]{1,0:T(8,128)S(1)}, u32[]{:S(2)}, u32[]{:S(2)}) collective-permute-start(f32[144,256]{1,0:T(8,128)S(1)} %get-tuple-element.68), channel_id=1, source_target_pairs={{0,1},{1,0},{2,3},{3,2},{4,5},{5,4},{6,7},{7,6},{8,9},{9,8},{10,11... | collective-permute-start | bytes 442376 | tf_op jit(solution)/shard_map/ppermute | solution.py:32
  42.5 3.7 %collective-permute-done.13.refs_3_ = f32[144,256]{1,0:T(8,128)S(1)} collective-permute-done((f32[144,256]{1,0:T(8,128)S(1)}, f32[144,256]{1,0:T(8,128)S(1)}, u32[]{:S(2)}, u32[]{:S(2)}) %collective-permute-start.13) | collective-permute-done | bytes 147488 | tf_op jit(solution)/shard_map/ppermute | solution.py:32
  46.3 2.8 %collective-permute-start.15 = (f32[48,128]{1,0:T(8,128)S(1)}, f32[48,128]{1,0:T(8,128)S(1)}, u32[]{:S(2)}, u32[]{:S(2)}) collective-permute-start(f32[48,128]{1,0:T(8,128)S(1)} %pad_maximum_fusion.6), channel_id=1, source_target_pairs={{0,4},{4,0},{8,12},{12,8},{1,5},{5,1},{9,13},{13,9},{2,6},{6,2},{1... | collective-permute-start | bytes 73736 | tf_op jit(solution)/shard_map/ppermute | solution.py:32
  49.1 1.8 %collective-permute-done.15.refs_5_ = f32[48,128]{1,0:T(8,128)S(1)} collective-permute-done((f32[48,128]{1,0:T(8,128)S(1)}, f32[48,128]{1,0:T(8,128)S(1)}, u32[]{:S(2)}, u32[]{:S(2)}) %collective-permute-start.15) | collective-permute-done | bytes 24608 | tf_op jit(solution)/shard_map/ppermute | solution.py:32
  50.9 3.1 %collective-permute-start.17 = (f32[2,32,128]{2,1,0:T(8,128)S(1)}, f32[2,32,128]{2,1,0:T(8,128)S(1)}, u32[]{:S(2)}, u32[]{:S(2)}) collective-permute-start(f32[2,32,128]{2,1,0:T(8,128)S(1)} %bitcast.71), channel_id=1, source_target_pairs={{0,8},{4,12},{8,0},{12,4},{1,9},{5,13},{9,1},{13,5},{2,10},{6,14},... | collective-permute-start | bytes 98312 | tf_op jit(solution)/shard_map/ppermute | solution.py:47
  53.9 1.9 %collective-permute-done.17 = f32[2,32,128]{2,1,0:T(8,128)S(1)} collective-permute-done((f32[2,32,128]{2,1,0:T(8,128)S(1)}, f32[2,32,128]{2,1,0:T(8,128)S(1)}, u32[]{:S(2)}, u32[]{:S(2)}) %collective-permute-start.17) | collective-permute-done | bytes 32800 | tf_op jit(solution)/shard_map/ppermute | solution.py:47
  55.9 2.3 %collective-permute-start.19 = (f32[128,128]{0,1:T(8,128)S(1)}, f32[128,128]{0,1:T(8,128)S(1)}, u32[]{:S(2)}, u32[]{:S(2)}) collective-permute-start(f32[128,128]{0,1:T(8,128)S(1)} %copy.11), channel_id=1, source_target_pairs={{0,2},{1,3},{2,0},{3,1},{4,6},{5,7},{6,4},{7,5},{8,10},{9,11},{10,... | collective-permute-start | bytes 196616 | tf_op jit(solution)/shard_map/ppermute | solution.py:47
  58.3 4.6 %step.5 = f32[4,32,16,256]{3,2,1,0:T(8,128)} custom-call(s32[2]{0:T(128)S(1)} %bitcast.64, f32[8,24,128]{2,1,0:T(8,128)S(1)} %bitcast.61, f32[4,32,16,256]{3,2,1,0:T(8,128)S(1)} %get-tuple-element.78.refs_2_, f32[144,256]{1,0:T(8,128)S(1)} %collective-permute-done.13.refs_3_, f32[128,256]{1,0:T(8,128)S(1)} %collective-permute-done.14.refs_4_, ...), custom_call_target="tpu_custom_call" | custom-call | tf_op jit(solution)/shard_map/step/pallas_call | solution.py:435
  63.1 1.2 %collective-permute-done.20 = f32[1,128,32]{1,2,0:T(8,128)S(1)} collective-permute-done((f32[1,128,32]{1,2,0:T(8,128)S(1)}, f32[1,128,32]{1,2,0:T(8,128)S(1)}, u32[]{:S(2)}, u32[]{:S(2)}) %collective-permute-start.20) | collective-permute-done | bytes 16416 | tf_op jit(solution)/shard_map/ppermute | solution.py:47
  64.2 0.1 copy.12
  64.5 0.6 add.42
  (59 shorter events, 0.7 us)
Async XLA Ops:
  0.6 22.8 %copy-start.2 = (s32[1,1,1,2]{3,2,1,0:T(1,128)S(1)}, s32[1,1,1,2]{3,2,1,0:T(1,128)}, u32[]{:S(2)}) copy-start(s32[1,1,1,2]{3,2,1,0:T(1,128)} %param.7) | copy-start | bytes 28
  1.4 5.4 %collective-permute-start = (f32[1,24,32]{2,1,0:T(8,128)S(1)}, f32[1,24,32]{2,1,0:T(8,128)S(1)}, u32[]{:S(2)}, u32[]{:S(2)}) collective-permute-start(f32[1,24,32]{2,1,0:T(8,128)S(1)} %fusion.5), channel_id=1, source_target_pairs={{0,1},{1,0},{2,3},{3,2},{4,5},{5,4},{6,7},{7,6},{8,9},{9,8},{10,11... | collective-permute-start | bytes 9224 | tf_op jit(solution)/shard_map/ppermute | solution.py:47
  4.5 1.6 %copy-start = (f32[4,32,16,256]{3,2,1,0:T(8,128)S(1)}, f32[4,32,16,256]{3,2,1,0:T(8,128)}, u32[]{:S(2)}) copy-start(f32[4,32,16,256]{3,2,1,0:T(8,128)} %refs_2_.1) | copy-start | bytes 6291460
  6.0 17.4 %copy-start.1 = (f32[4,32,16,256]{3,2,1,0:T(8,128)S(1)}, f32[4,32,16,256]{3,2,1,0:T(8,128)}, u32[]{:S(2)}) copy-start(f32[4,32,16,256]{3,2,1,0:T(8,128)} %refs_2_.1) | copy-start | bytes 6291460
  6.8 5.3 %collective-permute-start.2 = (f32[128,256]{1,0:T(8,128)S(1)}, f32[128,256]{1,0:T(8,128)S(1)}, u32[]{:S(2)}, u32[]{:S(2)}) collective-permute-start(f32[128,256]{1,0:T(8,128)S(1)} %get-tuple-element.51), channel_id=1, source_target_pairs={{0,1},{1,0},{2,3},{3,2},{4,5},{5,4},{6,7},{7,6},{8,9},{9,8},{10,11... | collective-permute-start | bytes 393224 | tf_op jit(solution)/shard_map/ppermute | solution.py:32
  8.2 4.9 %collective-permute-start.1 = (f32[2,24,32]{2,1,0:T(8,128)S(1)}, f32[2,24,32]{2,1,0:T(8,128)S(1)}, u32[]{:S(2)}, u32[]{:S(2)}) collective-permute-start(f32[2,24,32]{2,1,0:T(8,128)S(1)} %pad_maximum_fusion.5), channel_id=1, source_target_pairs={{0,2},{1,3},{2,0},{3,1},{4,6},{5,7},{6,4},{7,5},{8,10},{9,11},{10,... | collective-permute-start | bytes 18440 | tf_op jit(solution)/shard_map/ppermute | solution.py:47
  13.2 1.6 %collective-permute-start.4 = (f32[128,256]{1,0:T(8,128)S(1)}, f32[128,256]{1,0:T(8,128)S(1)}, u32[]{:S(2)}, u32[]{:S(2)}) collective-permute-start(f32[128,256]{1,0:T(8,128)S(1)} %get-tuple-element.55), channel_id=1, source_target_pairs={{0,16},{1,2},{2,1},{3,19},{16,0},{17,18},{18,17},{19,3},{4,20},{5,... | collective-permute-start | bytes 393224 | tf_op jit(solution)/shard_map/ppermute | solution.py:42
  13.2 3.8 %collective-permute-start.3 = (f32[40,128]{1,0:T(8,128)S(1)}, f32[40,128]{1,0:T(8,128)S(1)}, u32[]{:S(2)}, u32[]{:S(2)}) collective-permute-start(f32[40,128]{1,0:T(8,128)S(1)} %pad_maximum_fusion.7), channel_id=1, source_target_pairs={{0,4},{4,0},{8,12},{12,8},{1,5},{5,1},{9,13},{13,9},{2,6},{6,2},{1... | collective-permute-start | bytes 61448 | tf_op jit(solution)/shard_map/ppermute | solution.py:32
  17.1 4.8 %collective-permute-start.5 = (f32[64,128]{1,0:T(8,128)S(1)}, f32[64,128]{1,0:T(8,128)S(1)}, u32[]{:S(2)}, u32[]{:S(2)}) collective-permute-start(f32[64,128]{1,0:T(8,128)S(1)} %pad_maximum_fusion.2), channel_id=1, source_target_pairs={{0,12},{4,8},{8,4},{12,0},{1,13},{5,9},{9,5},{13,1},{2,14},{6,10},... | collective-permute-start | bytes 98312 | tf_op jit(solution)/shard_map/ppermute | solution.py:47
  21.9 1.3 %collective-permute-start.6 = (f32[1,96,128]{2,1,0:T(8,128)S(1)}, f32[1,96,128]{2,1,0:T(8,128)S(1)}, u32[]{:S(2)}, u32[]{:S(2)}) collective-permute-start(f32[1,96,128]{2,1,0:T(8,128)S(1)} %maximum_bitcast_fusion), channel_id=1, source_target_pairs={{0,16},{16,0},{1,17},{17,1},{2,18},{18,2},{3,19},{19,3},{4,20},{20... | collective-permute-start | bytes 147464 | tf_op jit(solution)/shard_map/ppermute | solution.py:47
  22.0 1.4 %collective-permute-start.7 = (f32[4,16,256]{2,1,0:T(8,128)S(1)}, f32[4,16,256]{2,1,0:T(8,128)S(1)}, u32[]{:S(2)}, u32[]{:S(2)}) collective-permute-start(f32[4,16,256]{2,1,0:T(8,128)S(1)} %get-tuple-element.60), channel_id=1, source_target_pairs={{0,16},{16,0},{1,17},{17,1},{2,18},{18,2},{3,19},{19,3},{4,20},{20... | collective-permute-start | bytes 196616 | tf_op jit(solution)/shard_map/ppermute | solution.py:32
  28.6 7.4 %collective-permute-start.8 = (f32[128,256]{1,0:T(8,128)S(1)}, f32[128,256]{1,0:T(8,128)S(1)}, u32[]{:S(2)}, u32[]{:S(2)}) collective-permute-start(f32[128,256]{1,0:T(8,128)S(1)} %get-tuple-element.62), channel_id=1, source_target_pairs={{0,1},{1,0},{2,3},{3,2},{4,5},{5,4},{6,7},{7,6},{8,9},{9,8},{10,11... | collective-permute-start | bytes 393224 | tf_op jit(solution)/shard_map/ppermute | solution.py:32
  31.8 4.2 %collective-permute-start.9 = (f32[128,256]{1,0:T(8,128)S(1)}, f32[128,256]{1,0:T(8,128)S(1)}, u32[]{:S(2)}, u32[]{:S(2)}) collective-permute-start(f32[128,256]{1,0:T(8,128)S(1)} %get-tuple-element.63), channel_id=1, source_target_pairs={{0,16},{1,2},{2,1},{3,19},{16,0},{17,18},{18,17},{19,3},{4,20},{5,... | collective-permute-start | bytes 393224 | tf_op jit(solution)/shard_map/ppermute | solution.py:42
  31.8 4.1 %collective-permute-start.12 = (f32[4,16,256]{2,1,0:T(8,128)S(1)}, f32[4,16,256]{2,1,0:T(8,128)S(1)}, u32[]{:S(2)}, u32[]{:S(2)}) collective-permute-start(f32[4,16,256]{2,1,0:T(8,128)S(1)} %get-tuple-element.66), channel_id=1, source_target_pairs={{0,16},{16,0},{1,17},{17,1},{2,18},{18,2},{3,19},{19,3},{4,20},{20... | collective-permute-start | bytes 196616 | tf_op jit(solution)/shard_map/ppermute | solution.py:32
  32.3 3.7 %collective-permute-start.10 = (f32[16,128]{1,0:T(8,128)S(1)}, f32[16,128]{1,0:T(8,128)S(1)}, u32[]{:S(2)}, u32[]{:S(2)}) collective-permute-start(f32[16,128]{1,0:T(8,128)S(1)} %get-tuple-element.64), channel_id=1, source_target_pairs={{0,4},{4,0},{8,12},{12,8},{1,5},{5,1},{9,13},{13,9},{2,6},{6,2},{1... | collective-permute-start | bytes 24584 | tf_op jit(solution)/shard_map/ppermute | solution.py:32
  33.8 2.2 %collective-permute-start.11 = (f32[16,128]{1,0:T(8,128)S(1)}, f32[16,128]{1,0:T(8,128)S(1)}, u32[]{:S(2)}, u32[]{:S(2)}) collective-permute-start(f32[16,128]{1,0:T(8,128)S(1)} %get-tuple-element.65), channel_id=1, source_target_pairs={{0,16},{4,8},{8,4},{12,28},{16,0},{20,24},{24,20},{28,12},{1,17},{... | collective-permute-start | bytes 24584 | tf_op jit(solution)/shard_map/ppermute | solution.py:42
  40.8 5.4 %collective-permute-start.13 = (f32[144,256]{1,0:T(8,128)S(1)}, f32[144,256]{1,0:T(8,128)S(1)}, u32[]{:S(2)}, u32[]{:S(2)}) collective-permute-start(f32[144,256]{1,0:T(8,128)S(1)} %get-tuple-element.68), channel_id=1, source_target_pairs={{0,1},{1,0},{2,3},{3,2},{4,5},{5,4},{6,7},{7,6},{8,9},{9,8},{10,11... | collective-permute-start | bytes 442376 | tf_op jit(solution)/shard_map/ppermute | solution.py:32
  42.5 3.7 %collective-permute-start.14 = (f32[128,256]{1,0:T(8,128)S(1)}, f32[128,256]{1,0:T(8,128)S(1)}, u32[]{:S(2)}, u32[]{:S(2)}) collective-permute-start(f32[128,256]{1,0:T(8,128)S(1)} %get-tuple-element.70), channel_id=1, source_target_pairs={{0,16},{1,2},{2,1},{3,19},{16,0},{17,18},{18,17},{19,3},{4,20},{5,... | collective-permute-start | bytes 393224 | tf_op jit(solution)/shard_map/ppermute | solution.py:42
  46.3 4.6 %collective-permute-start.15 = (f32[48,128]{1,0:T(8,128)S(1)}, f32[48,128]{1,0:T(8,128)S(1)}, u32[]{:S(2)}, u32[]{:S(2)}) collective-permute-start(f32[48,128]{1,0:T(8,128)S(1)} %pad_maximum_fusion.6), channel_id=1, source_target_pairs={{0,4},{4,0},{8,12},{12,8},{1,5},{5,1},{9,13},{13,9},{2,6},{6,2},{1... | collective-permute-start | bytes 73736 | tf_op jit(solution)/shard_map/ppermute | solution.py:32
  49.1 1.8 %collective-permute-start.16 = (f32[4,16,256]{2,1,0:T(8,128)S(1)}, f32[4,16,256]{2,1,0:T(8,128)S(1)}, u32[]{:S(2)}, u32[]{:S(2)}) collective-permute-start(f32[4,16,256]{2,1,0:T(8,128)S(1)} %get-tuple-element.74), channel_id=1, source_target_pairs={{0,16},{16,0},{1,17},{17,1},{2,18},{18,2},{3,19},{19,3},{4,20},{20... | collective-permute-start | bytes 196616 | tf_op jit(solution)/shard_map/ppermute | solution.py:32
  50.9 5.0 %collective-permute-start.17 = (f32[2,32,128]{2,1,0:T(8,128)S(1)}, f32[2,32,128]{2,1,0:T(8,128)S(1)}, u32[]{:S(2)}, u32[]{:S(2)}) collective-permute-start(f32[2,32,128]{2,1,0:T(8,128)S(1)} %bitcast.71), channel_id=1, source_target_pairs={{0,8},{4,12},{8,0},{12,4},{1,9},{5,13},{9,1},{13,5},{2,10},{6,14},... | collective-permute-start | bytes 98312 | tf_op jit(solution)/shard_map/ppermute | solution.py:47
  53.9 1.9 %collective-permute-start.18 = (f32[16,128]{1,0:T(8,128)S(1)}, f32[16,128]{1,0:T(8,128)S(1)}, u32[]{:S(2)}, u32[]{:S(2)}) collective-permute-start(f32[16,128]{1,0:T(8,128)S(1)} %get-tuple-element.76), channel_id=1, source_target_pairs={{0,16},{4,8},{8,4},{12,28},{16,0},{20,24},{24,20},{28,12},{1,17},{... | collective-permute-start | bytes 24584 | tf_op jit(solution)/shard_map/ppermute | solution.py:42
  55.9 7.0 %collective-permute-start.19 = (f32[128,128]{0,1:T(8,128)S(1)}, f32[128,128]{0,1:T(8,128)S(1)}, u32[]{:S(2)}, u32[]{:S(2)}) collective-permute-start(f32[128,128]{0,1:T(8,128)S(1)} %copy.11), channel_id=1, source_target_pairs={{0,2},{1,3},{2,0},{3,1},{4,6},{5,7},{6,4},{7,5},{8,10},{9,11},{10,... | collective-permute-start | bytes 196616 | tf_op jit(solution)/shard_map/ppermute | solution.py:47
  63.0 1.2 %collective-permute-start.20 = (f32[1,128,32]{1,2,0:T(8,128)S(1)}, f32[1,128,32]{1,2,0:T(8,128)S(1)}, u32[]{:S(2)}, u32[]{:S(2)}) collective-permute-start(f32[1,128,32]{1,2,0:T(8,128)S(1)} %dynamic-slice_bitcast_fusion), channel_id=1, source_target_pairs={{0,16},{16,0},{1,17},{17,1},{2,18},{18,2},{3,19},{19,3},{4,20},{20... | collective-permute-start | bytes 49160 | tf_op jit(solution)/shard_map/ppermute | solution.py:47

commit v13 on v12

--- a/solution.py
+++ b/solution.py
@@ -62,35 +62,40 @@
     return lax.rem(lax.axis_index(axis), 2) == 0
 
 
-def write_faces(q_ref, face_refs, shape):
+def write_faces(q_ref, face_refs, shape, await_component=None):
     count_x, count_z, count_y = shape
     za_ref, zb_ref, ya_ref, yb_ref, xa_ref = face_refs[:5]
     even_x, even_z, even_y = is_even("gx"), is_even("gz"), is_even("gy")
-    low, high = q_ref[:, 0], q_ref[:, count_x - 1]
-    xa_ref[...] = pick(even_x, high, low)
-    for xb_ref in face_refs[5:]:
-        xb_ref[...] = pick(even_x, low, high)
+    lane = lax.broadcasted_iota(jnp.int32, (count_z, 128), 1)
+    low_y = jnp.zeros((count_z, 128), jnp.float32)
+    high_y = jnp.zeros((count_z, 128), jnp.float32)
     for comp in range(4):
+        if await_component is not None:
+            await_component(comp)
+        low, high = q_ref[comp, 0], q_ref[comp, count_x - 1]
+        xa_ref[comp] = pick(even_x, high, low)
+        for xb_ref in face_refs[5:]:
+            xb_ref[comp] = pick(even_x, low, high)
         low = q_ref[comp, :, 0, :]
         high = q_ref[comp, :, count_z - 1, :]
         za_ref[comp * count_x : (comp + 1) * count_x] = pick(even_z, high, low)
         zb_ref[comp * count_x : (comp + 1) * count_x] = pick(even_z, low, high)
-    lane = lax.broadcasted_iota(jnp.int32, (count_z, 128), 1)
-    low = jnp.zeros((count_z, 128), jnp.float32)
-    high = jnp.zeros((count_z, 128), jnp.float32)
-    for comp in range(4):
         for x in range(count_x):
             place = comp * count_x + x
             first = q_ref[comp, x, :, :128]
             last = q_ref[comp, x, :, count_y - 128 :]
-            low = jnp.where(lane == place, pltpu.roll(first, place, 1), low)
-            high = jnp.where(lane == place, pltpu.roll(last, (place + 1) % 128, 1), high)
-    ya_ref[...] = pick(even_y, high, low)
-    yb_ref[...] = pick(even_y, low, high)
-
-
-def faces_body(q_ref, *face_refs, shape):
-    write_faces(q_ref, face_refs, shape)
+            low_y = jnp.where(lane == place, pltpu.roll(first, place, 1), low_y)
+            high_y = jnp.where(lane == place, pltpu.roll(last, (place + 1) % 128, 1), high_y)
+    ya_ref[...] = pick(even_y, high_y, low_y)
+    yb_ref[...] = pick(even_y, low_y, high_y)
+
+
+def faces_body(far_ref, *refs, shape):
+    face_refs, q_ref, sems = refs[:-2], refs[-2], refs[-1]
+    copies = [pltpu.make_async_copy(far_ref.at[comp], q_ref.at[comp], sems.at[comp]) for comp in range(4)]
+    for copy in copies:
+        copy.start()
+    write_faces(q_ref, face_refs, shape, lambda comp: copies[comp].wait())
 
 
 def sorted_slots(list_ref, capacity):
@@ -387,8 +392,9 @@
     faces = pl.pallas_call(
         functools.partial(faces_body, shape=shape),
         out_shape=forms,
-        in_specs=vmem_specs(1),
+        in_specs=[pl.BlockSpec(memory_space=pl.ANY)],
         out_specs=vmem_specs(len(forms)),
+        scratch_shapes=[pltpu.VMEM(q.shape, jnp.float32), pltpu.SemaphoreType.DMA((4,))],
         compiler_params=params,
         name="faces",
     )(q)

time: 65.3 us -> 65.4 us (level)
  transfers between devices with their start and end apart: 21 -> 21, of which waited for: 11 -> 11; matrix products, arithmetic and copies ran while one was open for 0% -> 0% of each run, Pallas kernels for 8% -> 9%
where the time goes in v13:
time: 65.4 us; the launch traced here: 65.1 us
  starting transfers between devices  26.6 us (41%)
  waiting for transfers between devices  18.4 us (28%)
  Pallas kernels  15.8 us (24%)
  local copies, waits for them, and re-layouts  3.17 us (5%)
  between operations  0.92 us (1%)
    pallas_call x3, Pallas kernels, shards(): pl.pallas_call(functools.partial(step_body, shape=shape, points=points, c...  14.7 us
    ppermute x7, starting transfers between devices, from_distance(): return lax.ppermute(value, axis, [(i, i ^ distance) for i in range(count)])  13.4 us
    ppermute x9, starting transfers between devices, swap(): return lax.ppermute(value, axis, pairs)  13.1 us
    ppermute x9, waiting for transfers between devices, swap(): return lax.ppermute(value, axis, pairs)  11.8 us
    ppermute x7, waiting for transfers between devices, from_distance(): return lax.ppermute(value, axis, [(i, i ^ distance) for i in range(count)])  6.56 us
    unnamed x10, local copies, waits for them, and re-layouts  2.33 us
  transfers between devices with their start and end apart: 21, of which 11 were waited for; matrix products, arithmetic and copies ran while one was open for 0% of the time, Pallas kernels for 9%

profile of v13, /device:TPU:0, one launch (start us, length us, event | category | flops | bytes accessed | tf_op | source)
XLA Modules:
  0.0 65.1 jit_solution(11260431599780678982)
XLA Ops:
  0.6 0.7 %copy_bitcast_fusion = (f32[3,3,32]{2,1,0:T(4,128)S(1)}, f32[3,3,32]{2,1,0:T(4,128)S(1)}) fusion(f32[3,3,1,32]{3,2,1,0:T(1,128)} %param.6, f32[3,3,1,32]{3,2,1,0:T(1,128)} %param.5), kind=kLoop, calls=%fused_computation.35 | loop fusion | bytes 4608
  1.4 3.1 %collective-permute-start = (f32[1,24,32]{2,1,0:T(8,128)S(1)}, f32[1,24,32]{2,1,0:T(8,128)S(1)}, u32[]{:S(2)}, u32[]{:S(2)}) collective-permute-start(f32[1,24,32]{2,1,0:T(8,128)S(1)} %fusion.5), channel_id=1, source_target_pairs={{0,1},{1,0},{2,3},{3,2},{4,5},{5,4},{6,7},{7,6},{8,9},{9,8},{10,11... | collective-permute-start | bytes 9224 | tf_op jit(solution)/shard_map/ppermute | solution.py:47
  4.5 1.6 %copy-done = f32[4,32,16,256]{3,2,1,0:T(8,128)S(1)} copy-done((f32[4,32,16,256]{3,2,1,0:T(8,128)S(1)}, f32[4,32,16,256]{3,2,1,0:T(8,128)}, u32[]{:S(2)}) %copy-start) | copy-done | bytes 2097176
  6.0 1.1 %faces.1 = (f32[128,256]{1,0:T(8,128)S(1)}, f32[128,256]{1,0:T(8,128)S(1)}, f32[16,128]{1,0:T(8,128)S(1)}, f32[16,128]{1,0:T(8,128)S(1)}, f32[4,16,256]{2,1,0:T(8,128)S(1)}) custom-call(f32[4,32,16,256]{3,2,1,0:T(8,128)S(1)} %copy-done), custom_call_target="tpu_custom_call" | custom-call | tf_op jit(solution)/shard_map/faces/pallas_call | solution.py:392
  7.2 1.0 %collective-permute-start.2 = (f32[128,256]{1,0:T(8,128)S(1)}, f32[128,256]{1,0:T(8,128)S(1)}, u32[]{:S(2)}, u32[]{:S(2)}) collective-permute-start(f32[128,256]{1,0:T(8,128)S(1)} %get-tuple-element.51), channel_id=1, source_target_pairs={{0,1},{1,0},{2,3},{3,2},{4,5},{5,4},{6,7},{7,6},{8,9},{9,8},{10,11... | collective-permute-start | bytes 393224 | tf_op jit(solution)/shard_map/ppermute | solution.py:32
  8.2 2.6 %collective-permute-start.1 = (f32[2,24,32]{2,1,0:T(8,128)S(1)}, f32[2,24,32]{2,1,0:T(8,128)S(1)}, u32[]{:S(2)}, u32[]{:S(2)}) collective-permute-start(f32[2,24,32]{2,1,0:T(8,128)S(1)} %pad_maximum_fusion.5), channel_id=1, source_target_pairs={{0,2},{1,3},{2,0},{3,1},{4,6},{5,7},{6,4},{7,5},{8,10},{9,11},{10,... | collective-permute-start | bytes 18440 | tf_op jit(solution)/shard_map/ppermute | solution.py:47
  10.7 1.7 %collective-permute-done.2 = f32[128,256]{1,0:T(8,128)S(1)} collective-permute-done((f32[128,256]{1,0:T(8,128)S(1)}, f32[128,256]{1,0:T(8,128)S(1)}, u32[]{:S(2)}, u32[]{:S(2)}) %collective-permute-start.2) | collective-permute-done | bytes 131104 | tf_op jit(solution)/shard_map/ppermute | solution.py:32
  12.5 0.4 collective-permute-done.1
  13.1 1.6 %collective-permute-start.3 = (f32[40,128]{1,0:T(8,128)S(1)}, f32[40,128]{1,0:T(8,128)S(1)}, u32[]{:S(2)}, u32[]{:S(2)}) collective-permute-start(f32[40,128]{1,0:T(8,128)S(1)} %pad_maximum_fusion.7), channel_id=1, source_target_pairs={{0,4},{4,0},{8,12},{12,8},{1,5},{5,1},{9,13},{13,9},{2,6},{6,2},{1... | collective-permute-start | bytes 61448 | tf_op jit(solution)/shard_map/ppermute | solution.py:32
  14.7 2.3 %collective-permute-done.3.refs_5_ = f32[40,128]{1,0:T(8,128)S(1)} collective-permute-done((f32[40,128]{1,0:T(8,128)S(1)}, f32[40,128]{1,0:T(8,128)S(1)}, u32[]{:S(2)}, u32[]{:S(2)}) %collective-permute-start.3) | collective-permute-done | bytes 20512 | tf_op jit(solution)/shard_map/ppermute | solution.py:32
  17.0 2.4 %collective-permute-start.5 = (f32[64,128]{1,0:T(8,128)S(1)}, f32[64,128]{1,0:T(8,128)S(1)}, u32[]{:S(2)}, u32[]{:S(2)}) collective-permute-start(f32[64,128]{1,0:T(8,128)S(1)} %pad_maximum_fusion.2), channel_id=1, source_target_pairs={{0,12},{4,8},{8,4},{12,0},{1,13},{5,9},{9,5},{13,1},{2,14},{6,10},... | collective-permute-start | bytes 98312 | tf_op jit(solution)/shard_map/ppermute | solution.py:47
  19.4 2.4 %collective-permute-done.5.refs_6_ = f32[64,128]{1,0:T(8,128)S(1)} collective-permute-done((f32[64,128]{1,0:T(8,128)S(1)}, f32[64,128]{1,0:T(8,128)S(1)}, u32[]{:S(2)}, u32[]{:S(2)}) %collective-permute-start.5) | collective-permute-done | bytes 32800 | tf_op jit(solution)/shard_map/ppermute | solution.py:47
  21.9 0.5 collective-permute-start.7
  22.4 0.7 %collective-permute-done.6 = f32[1,96,128]{2,1,0:T(8,128)S(1)} collective-permute-done((f32[1,96,128]{2,1,0:T(8,128)S(1)}, f32[1,96,128]{2,1,0:T(8,128)S(1)}, u32[]{:S(2)}, u32[]{:S(2)}) %collective-permute-start.6) | collective-permute-done | bytes 49184 | tf_op jit(solution)/shard_map/ppermute | solution.py:47
  23.1 0.2 collective-permute-done.7.refs_7_
  23.3 5.2 %step.3 = (f32[4,32,16,256]{3,2,1,0:T(8,128)S(1)}, f32[128,256]{1,0:T(8,128)S(1)}, f32[128,256]{1,0:T(8,128)S(1)}, f32[16,128]{1,0:T(8,128)S(1)}, f32[16,128]{1,...) custom-call(s32[2]{0:T(128)S(1)} %bitcast.62, f32[8,24,128]{2,1,0:T(8,128)S(1)} %bitcast.59, ...), custom_call_target="tpu_custom_call" | custom-call | tf_op jit(solution)/shard_map/step/pallas_call | solution.py:441
  28.5 3.7 %collective-permute-start.8 = (f32[128,256]{1,0:T(8,128)S(1)}, f32[128,256]{1,0:T(8,128)S(1)}, u32[]{:S(2)}, u32[]{:S(2)}) collective-permute-start(f32[128,256]{1,0:T(8,128)S(1)} %get-tuple-element.62), channel_id=1, source_target_pairs={{0,1},{1,0},{2,3},{3,2},{4,5},{5,4},{6,7},{7,6},{8,9},{9,8},{10,11... | collective-permute-start | bytes 393224 | tf_op jit(solution)/shard_map/ppermute | solution.py:32
  32.2 0.4 collective-permute-start.12
  32.6 1.5 %collective-permute-start.10 = (f32[16,128]{1,0:T(8,128)S(1)}, f32[16,128]{1,0:T(8,128)S(1)}, u32[]{:S(2)}, u32[]{:S(2)}) collective-permute-start(f32[16,128]{1,0:T(8,128)S(1)} %get-tuple-element.64), channel_id=1, source_target_pairs={{0,4},{4,0},{8,12},{12,8},{1,5},{5,1},{9,13},{13,9},{2,6},{6,2},{1... | collective-permute-start | bytes 24584 | tf_op jit(solution)/shard_map/ppermute | solution.py:32
  34.1 2.2 %collective-permute-done.10.refs_5_ = f32[16,128]{1,0:T(8,128)S(1)} collective-permute-done((f32[16,128]{1,0:T(8,128)S(1)}, f32[16,128]{1,0:T(8,128)S(1)}, u32[]{:S(2)}, u32[]{:S(2)}) %collective-permute-start.10) | collective-permute-done | bytes 8224 | tf_op jit(solution)/shard_map/ppermute | solution.py:32
  36.3 4.9 %step.4 = (f32[4,32,16,256]{3,2,1,0:T(8,128)S(1)}, f32[144,256]{1,0:T(8,128)S(1)}, f32[128,256]{1,0:T(8,128)S(1)}, f32[16,128]{1,0:T(8,128)S(1)}, f32[16,128]{1,0:T(8,128)S(1)}, /*index=5*/f32[4,16,256]{2,1,0:T(8,128)S(1)}) custom-call(s32[2]{0:T(128)S(1)} %bitcast.63, f32[8,24,128]{2,1,0:T(8,128)S(1)} %bitcast.60, ...), custom_call_target="tpu_custom_call" | custom-call | tf_op jit(solution)/shard_map/step/pallas_call | solution.py:441
  41.2 1.7 %collective-permute-start.13 = (f32[144,256]{1,0:T(8,128)S(1)}, f32[144,256]{1,0:T(8,128)S(1)}, u32[]{:S(2)}, u32[]{:S(2)}) collective-permute-start(f32[144,256]{1,0:T(8,128)S(1)} %get-tuple-element.68), channel_id=1, source_target_pairs={{0,1},{1,0},{2,3},{3,2},{4,5},{5,4},{6,7},{7,6},{8,9},{9,8},{10,11... | collective-permute-start | bytes 442376 | tf_op jit(solution)/shard_map/ppermute | solution.py:32
  42.9 3.7 %collective-permute-done.13.refs_3_ = f32[144,256]{1,0:T(8,128)S(1)} collective-permute-done((f32[144,256]{1,0:T(8,128)S(1)}, f32[144,256]{1,0:T(8,128)S(1)}, u32[]{:S(2)}, u32[]{:S(2)}) %collective-permute-start.13) | collective-permute-done | bytes 147488 | tf_op jit(solution)/shard_map/ppermute | solution.py:32
  46.6 2.8 %collective-permute-start.15 = (f32[48,128]{1,0:T(8,128)S(1)}, f32[48,128]{1,0:T(8,128)S(1)}, u32[]{:S(2)}, u32[]{:S(2)}) collective-permute-start(f32[48,128]{1,0:T(8,128)S(1)} %pad_maximum_fusion.6), channel_id=1, source_target_pairs={{0,4},{4,0},{8,12},{12,8},{1,5},{5,1},{9,13},{13,9},{2,6},{6,2},{1... | collective-permute-start | bytes 73736 | tf_op jit(solution)/shard_map/ppermute | solution.py:32
  49.4 1.8 %collective-permute-done.15.refs_5_ = f32[48,128]{1,0:T(8,128)S(1)} collective-permute-done((f32[48,128]{1,0:T(8,128)S(1)}, f32[48,128]{1,0:T(8,128)S(1)}, u32[]{:S(2)}, u32[]{:S(2)}) %collective-permute-start.15) | collective-permute-done | bytes 24608 | tf_op jit(solution)/shard_map/ppermute | solution.py:32
  51.2 3.1 %collective-permute-start.17 = (f32[2,32,128]{2,1,0:T(8,128)S(1)}, f32[2,32,128]{2,1,0:T(8,128)S(1)}, u32[]{:S(2)}, u32[]{:S(2)}) collective-permute-start(f32[2,32,128]{2,1,0:T(8,128)S(1)} %bitcast.71), channel_id=1, source_target_pairs={{0,8},{4,12},{8,0},{12,4},{1,9},{5,13},{9,1},{13,5},{2,10},{6,14},... | collective-permute-start | bytes 98312 | tf_op jit(solution)/shard_map/ppermute | solution.py:47
  54.3 1.9 %collective-permute-done.17 = f32[2,32,128]{2,1,0:T(8,128)S(1)} collective-permute-done((f32[2,32,128]{2,1,0:T(8,128)S(1)}, f32[2,32,128]{2,1,0:T(8,128)S(1)}, u32[]{:S(2)}, u32[]{:S(2)}) %collective-permute-start.17) | collective-permute-done | bytes 32800 | tf_op jit(solution)/shard_map/ppermute | solution.py:47
  56.3 2.0 %collective-permute-start.19 = (f32[128,128]{0,1:T(8,128)S(1)}, f32[128,128]{0,1:T(8,128)S(1)}, u32[]{:S(2)}, u32[]{:S(2)}) collective-permute-start(f32[128,128]{0,1:T(8,128)S(1)} %copy.11), channel_id=1, source_target_pairs={{0,2},{1,3},{2,0},{3,1},{4,6},{5,7},{6,4},{7,5},{8,10},{9,11},{10,... | collective-permute-start | bytes 196616 | tf_op jit(solution)/shard_map/ppermute | solution.py:47
  58.3 4.6 %step.5 = f32[4,32,16,256]{3,2,1,0:T(8,128)} custom-call(s32[2]{0:T(128)S(1)} %bitcast.64, f32[8,24,128]{2,1,0:T(8,128)S(1)} %bitcast.61, f32[4,32,16,256]{3,2,1,0:T(8,128)S(1)} %get-tuple-element.78.refs_2_, f32[144,256]{1,0:T(8,128)S(1)} %collective-permute-done.13.refs_3_, f32[128,256]{1,0:T(8,128)S(1)} %collective-permute-done.14.refs_4_, ...), custom_call_target="tpu_custom_call" | custom-call | tf_op jit(solution)/shard_map/step/pallas_call | solution.py:441
  63.1 1.2 %collective-permute-done.20 = f32[1,128,32]{1,2,0:T(8,128)S(1)} collective-permute-done((f32[1,128,32]{1,2,0:T(8,128)S(1)}, f32[1,128,32]{1,2,0:T(8,128)S(1)}, u32[]{:S(2)}, u32[]{:S(2)}) %collective-permute-start.20) | collective-permute-done | bytes 16416 | tf_op jit(solution)/shard_map/ppermute | solution.py:47
  64.3 0.1 copy.12
  64.5 0.6 add.42
  (59 shorter events, 0.7 us)
Async XLA Ops:
  0.6 22.6 %copy-start.2 = (s32[1,1,1,2]{3,2,1,0:T(1,128)S(1)}, s32[1,1,1,2]{3,2,1,0:T(1,128)}, u32[]{:S(2)}) copy-start(s32[1,1,1,2]{3,2,1,0:T(1,128)} %param.7) | copy-start | bytes 28
  1.4 5.8 %collective-permute-start = (f32[1,24,32]{2,1,0:T(8,128)S(1)}, f32[1,24,32]{2,1,0:T(8,128)S(1)}, u32[]{:S(2)}, u32[]{:S(2)}) collective-permute-start(f32[1,24,32]{2,1,0:T(8,128)S(1)} %fusion.5), channel_id=1, source_target_pairs={{0,1},{1,0},{2,3},{3,2},{4,5},{5,4},{6,7},{7,6},{8,9},{9,8},{10,11... | collective-permute-start | bytes 9224 | tf_op jit(solution)/shard_map/ppermute | solution.py:47
  4.5 1.6 %copy-start = (f32[4,32,16,256]{3,2,1,0:T(8,128)S(1)}, f32[4,32,16,256]{3,2,1,0:T(8,128)}, u32[]{:S(2)}) copy-start(f32[4,32,16,256]{3,2,1,0:T(8,128)} %refs_2_.1) | copy-start | bytes 6291460
  6.0 17.2 %copy-start.1 = (f32[4,32,16,256]{3,2,1,0:T(8,128)S(1)}, f32[4,32,16,256]{3,2,1,0:T(8,128)}, u32[]{:S(2)}) copy-start(f32[4,32,16,256]{3,2,1,0:T(8,128)} %refs_2_.1) | copy-start | bytes 6291460
  7.2 5.3 %collective-permute-start.2 = (f32[128,256]{1,0:T(8,128)S(1)}, f32[128,256]{1,0:T(8,128)S(1)}, u32[]{:S(2)}, u32[]{:S(2)}) collective-permute-start(f32[128,256]{1,0:T(8,128)S(1)} %get-tuple-element.51), channel_id=1, source_target_pairs={{0,1},{1,0},{2,3},{3,2},{4,5},{5,4},{6,7},{7,6},{8,9},{9,8},{10,11... | collective-permute-start | bytes 393224 | tf_op jit(solution)/shard_map/ppermute | solution.py:32
  8.2 4.7 %collective-permute-start.1 = (f32[2,24,32]{2,1,0:T(8,128)S(1)}, f32[2,24,32]{2,1,0:T(8,128)S(1)}, u32[]{:S(2)}, u32[]{:S(2)}) collective-permute-start(f32[2,24,32]{2,1,0:T(8,128)S(1)} %pad_maximum_fusion.5), channel_id=1, source_target_pairs={{0,2},{1,3},{2,0},{3,1},{4,6},{5,7},{6,4},{7,5},{8,10},{9,11},{10,... | collective-permute-start | bytes 18440 | tf_op jit(solution)/shard_map/ppermute | solution.py:47
  13.0 1.6 %collective-permute-start.4 = (f32[128,256]{1,0:T(8,128)S(1)}, f32[128,256]{1,0:T(8,128)S(1)}, u32[]{:S(2)}, u32[]{:S(2)}) collective-permute-start(f32[128,256]{1,0:T(8,128)S(1)} %get-tuple-element.55), channel_id=1, source_target_pairs={{0,16},{1,2},{2,1},{3,19},{16,0},{17,18},{18,17},{19,3},{4,20},{5,... | collective-permute-start | bytes 393224 | tf_op jit(solution)/shard_map/ppermute | solution.py:42
  13.1 3.8 %collective-permute-start.3 = (f32[40,128]{1,0:T(8,128)S(1)}, f32[40,128]{1,0:T(8,128)S(1)}, u32[]{:S(2)}, u32[]{:S(2)}) collective-permute-start(f32[40,128]{1,0:T(8,128)S(1)} %pad_maximum_fusion.7), channel_id=1, source_target_pairs={{0,4},{4,0},{8,12},{12,8},{1,5},{5,1},{9,13},{13,9},{2,6},{6,2},{1... | collective-permute-start | bytes 61448 | tf_op jit(solution)/shard_map/ppermute | solution.py:32
  17.0 4.8 %collective-permute-start.5 = (f32[64,128]{1,0:T(8,128)S(1)}, f32[64,128]{1,0:T(8,128)S(1)}, u32[]{:S(2)}, u32[]{:S(2)}) collective-permute-start(f32[64,128]{1,0:T(8,128)S(1)} %pad_maximum_fusion.2), channel_id=1, source_target_pairs={{0,12},{4,8},{8,4},{12,0},{1,13},{5,9},{9,5},{13,1},{2,14},{6,10},... | collective-permute-start | bytes 98312 | tf_op jit(solution)/shard_map/ppermute | solution.py:47
  21.8 1.3 %collective-permute-start.6 = (f32[1,96,128]{2,1,0:T(8,128)S(1)}, f32[1,96,128]{2,1,0:T(8,128)S(1)}, u32[]{:S(2)}, u32[]{:S(2)}) collective-permute-start(f32[1,96,128]{2,1,0:T(8,128)S(1)} %maximum_bitcast_fusion), channel_id=1, source_target_pairs={{0,16},{16,0},{1,17},{17,1},{2,18},{18,2},{3,19},{19,3},{4,20},{20... | collective-permute-start | bytes 147464 | tf_op jit(solution)/shard_map/ppermute | solution.py:47
  21.9 1.4 %collective-permute-start.7 = (f32[4,16,256]{2,1,0:T(8,128)S(1)}, f32[4,16,256]{2,1,0:T(8,128)S(1)}, u32[]{:S(2)}, u32[]{:S(2)}) collective-permute-start(f32[4,16,256]{2,1,0:T(8,128)S(1)} %get-tuple-element.60), channel_id=1, source_target_pairs={{0,16},{16,0},{1,17},{17,1},{2,18},{18,2},{3,19},{19,3},{4,20},{20... | collective-permute-start | bytes 196616 | tf_op jit(solution)/shard_map/ppermute | solution.py:32
  28.5 7.8 %collective-permute-start.8 = (f32[128,256]{1,0:T(8,128)S(1)}, f32[128,256]{1,0:T(8,128)S(1)}, u32[]{:S(2)}, u32[]{:S(2)}) collective-permute-start(f32[128,256]{1,0:T(8,128)S(1)} %get-tuple-element.62), channel_id=1, source_target_pairs={{0,1},{1,0},{2,3},{3,2},{4,5},{5,4},{6,7},{7,6},{8,9},{9,8},{10,11... | collective-permute-start | bytes 393224 | tf_op jit(solution)/shard_map/ppermute | solution.py:32
  32.1 4.2 %collective-permute-start.9 = (f32[128,256]{1,0:T(8,128)S(1)}, f32[128,256]{1,0:T(8,128)S(1)}, u32[]{:S(2)}, u32[]{:S(2)}) collective-permute-start(f32[128,256]{1,0:T(8,128)S(1)} %get-tuple-element.63), channel_id=1, source_target_pairs={{0,16},{1,2},{2,1},{3,19},{16,0},{17,18},{18,17},{19,3},{4,20},{5,... | collective-permute-start | bytes 393224 | tf_op jit(solution)/shard_map/ppermute | solution.py:42
  32.2 4.1 %collective-permute-start.12 = (f32[4,16,256]{2,1,0:T(8,128)S(1)}, f32[4,16,256]{2,1,0:T(8,128)S(1)}, u32[]{:S(2)}, u32[]{:S(2)}) collective-permute-start(f32[4,16,256]{2,1,0:T(8,128)S(1)} %get-tuple-element.66), channel_id=1, source_target_pairs={{0,16},{16,0},{1,17},{17,1},{2,18},{18,2},{3,19},{19,3},{4,20},{20... | collective-permute-start | bytes 196616 | tf_op jit(solution)/shard_map/ppermute | solution.py:32
  32.6 3.7 %collective-permute-start.10 = (f32[16,128]{1,0:T(8,128)S(1)}, f32[16,128]{1,0:T(8,128)S(1)}, u32[]{:S(2)}, u32[]{:S(2)}) collective-permute-start(f32[16,128]{1,0:T(8,128)S(1)} %get-tuple-element.64), channel_id=1, source_target_pairs={{0,4},{4,0},{8,12},{12,8},{1,5},{5,1},{9,13},{13,9},{2,6},{6,2},{1... | collective-permute-start | bytes 24584 | tf_op jit(solution)/shard_map/ppermute | solution.py:32
  34.1 2.2 %collective-permute-start.11 = (f32[16,128]{1,0:T(8,128)S(1)}, f32[16,128]{1,0:T(8,128)S(1)}, u32[]{:S(2)}, u32[]{:S(2)}) collective-permute-start(f32[16,128]{1,0:T(8,128)S(1)} %get-tuple-element.65), channel_id=1, source_target_pairs={{0,16},{4,8},{8,4},{12,28},{16,0},{20,24},{24,20},{28,12},{1,17},{... | collective-permute-start | bytes 24584 | tf_op jit(solution)/shard_map/ppermute | solution.py:42
  41.2 5.4 %collective-permute-start.13 = (f32[144,256]{1,0:T(8,128)S(1)}, f32[144,256]{1,0:T(8,128)S(1)}, u32[]{:S(2)}, u32[]{:S(2)}) collective-permute-start(f32[144,256]{1,0:T(8,128)S(1)} %get-tuple-element.68), channel_id=1, source_target_pairs={{0,1},{1,0},{2,3},{3,2},{4,5},{5,4},{6,7},{7,6},{8,9},{9,8},{10,11... | collective-permute-start | bytes 442376 | tf_op jit(solution)/shard_map/ppermute | solution.py:32
  42.9 3.7 %collective-permute-start.14 = (f32[128,256]{1,0:T(8,128)S(1)}, f32[128,256]{1,0:T(8,128)S(1)}, u32[]{:S(2)}, u32[]{:S(2)}) collective-permute-start(f32[128,256]{1,0:T(8,128)S(1)} %get-tuple-element.70), channel_id=1, source_target_pairs={{0,16},{1,2},{2,1},{3,19},{16,0},{17,18},{18,17},{19,3},{4,20},{5,... | collective-permute-start | bytes 393224 | tf_op jit(solution)/shard_map/ppermute | solution.py:42
  46.6 4.6 %collective-permute-start.15 = (f32[48,128]{1,0:T(8,128)S(1)}, f32[48,128]{1,0:T(8,128)S(1)}, u32[]{:S(2)}, u32[]{:S(2)}) collective-permute-start(f32[48,128]{1,0:T(8,128)S(1)} %pad_maximum_fusion.6), channel_id=1, source_target_pairs={{0,4},{4,0},{8,12},{12,8},{1,5},{5,1},{9,13},{13,9},{2,6},{6,2},{1... | collective-permute-start | bytes 73736 | tf_op jit(solution)/shard_map/ppermute | solution.py:32
  49.4 1.8 %collective-permute-start.16 = (f32[4,16,256]{2,1,0:T(8,128)S(1)}, f32[4,16,256]{2,1,0:T(8,128)S(1)}, u32[]{:S(2)}, u32[]{:S(2)}) collective-permute-start(f32[4,16,256]{2,1,0:T(8,128)S(1)} %get-tuple-element.74), channel_id=1, source_target_pairs={{0,16},{16,0},{1,17},{17,1},{2,18},{18,2},{3,19},{19,3},{4,20},{20... | collective-permute-start | bytes 196616 | tf_op jit(solution)/shard_map/ppermute | solution.py:32
  51.2 5.0 %collective-permute-start.17 = (f32[2,32,128]{2,1,0:T(8,128)S(1)}, f32[2,32,128]{2,1,0:T(8,128)S(1)}, u32[]{:S(2)}, u32[]{:S(2)}) collective-permute-start(f32[2,32,128]{2,1,0:T(8,128)S(1)} %bitcast.71), channel_id=1, source_target_pairs={{0,8},{4,12},{8,0},{12,4},{1,9},{5,13},{9,1},{13,5},{2,10},{6,14},... | collective-permute-start | bytes 98312 | tf_op jit(solution)/shard_map/ppermute | solution.py:47
  54.3 1.9 %collective-permute-start.18 = (f32[16,128]{1,0:T(8,128)S(1)}, f32[16,128]{1,0:T(8,128)S(1)}, u32[]{:S(2)}, u32[]{:S(2)}) collective-permute-start(f32[16,128]{1,0:T(8,128)S(1)} %get-tuple-element.76), channel_id=1, source_target_pairs={{0,16},{4,8},{8,4},{12,28},{16,0},{20,24},{24,20},{28,12},{1,17},{... | collective-permute-start | bytes 24584 | tf_op jit(solution)/shard_map/ppermute | solution.py:42
  56.3 6.7 %collective-permute-start.19 = (f32[128,128]{0,1:T(8,128)S(1)}, f32[128,128]{0,1:T(8,128)S(1)}, u32[]{:S(2)}, u32[]{:S(2)}) collective-permute-start(f32[128,128]{0,1:T(8,128)S(1)} %copy.11), channel_id=1, source_target_pairs={{0,2},{1,3},{2,0},{3,1},{4,6},{5,7},{6,4},{7,5},{8,10},{9,11},{10,... | collective-permute-start | bytes 196616 | tf_op jit(solution)/shard_map/ppermute | solution.py:47
  63.0 1.2 %collective-permute-start.20 = (f32[1,128,32]{1,2,0:T(8,128)S(1)}, f32[1,128,32]{1,2,0:T(8,128)S(1)}, u32[]{:S(2)}, u32[]{:S(2)}) collective-permute-start(f32[1,128,32]{1,2,0:T(8,128)S(1)} %dynamic-slice_bitcast_fusion), channel_id=1, source_target_pairs={{0,16},{16,0},{1,17},{17,1},{2,18},{18,2},{3,19},{19,3},{4,20},{20... | collective-permute-start | bytes 49160 | tf_op jit(solution)/shard_map/ppermute | solution.py:47

commit v14 on v13

--- a/solution.py
+++ b/solution.py
@@ -392,12 +392,12 @@
     faces = pl.pallas_call(
         functools.partial(faces_body, shape=shape),
         out_shape=forms,
-        in_specs=[pl.BlockSpec(memory_space=pl.ANY)],
+        in_specs=[pl.BlockSpec(memory_space=pltpu.HBM)],
         out_specs=vmem_specs(len(forms)),
         scratch_shapes=[pltpu.VMEM(q.shape, jnp.float32), pltpu.SemaphoreType.DMA((4,))],
         compiler_params=params,
         name="faces",
-    )(q)
+    )(pltpu.with_memory_space_constraint(q, pltpu.HBM))
     table, faces = barrier((table, list(faces)))
     za, zb, ya, yb = faces[:4]
     za = masked(swap(za, "gz", 0), "gz", 0)

time: 65.4 us -> 65.7 us (level)
  local copies, waits for them, and re-layouts: 3.17 us -> 1.73 us
  Pallas kernels: 15.8 us -> 16.8 us
    unnamed x10 -> x8, local copies, waits for them, and re-layouts: 2.33 us -> 0.88 us
    pallas_call x1, Pallas kernels: 1.09 us -> 1.97 us  [shards(): pl.pallas_call(functools.partial(faces_body, shape=shape), out_shape=form...]
    ppermute x9, waiting for transfers between devices: 11.8 us -> 11.1 us  [swap(): return lax.ppermute(value, axis, pairs)]
    ppermute x7, waiting for transfers between devices: 6.56 us -> 7.26 us  [from_distance(): return lax.ppermute(value, axis, [(i, i ^ distance) for i in range(count)])]
  transfers between devices with their start and end apart: 21 -> 21, of which waited for: 11 -> 11; matrix products, arithmetic and copies ran while one was open for 0% -> 0% of each run, Pallas kernels for 9% -> 10%
where the time goes in v14:
time: 65.7 us; the launch traced here: 65.4 us
  starting transfers between devices  27.2 us (41%)
  waiting for transfers between devices  18.4 us (28%)
  Pallas kernels  16.8 us (26%)
  local copies, waits for them, and re-layouts  1.73 us (3%)
  between operations  0.93 us (1%)
    pallas_call x3, Pallas kernels, shards(): pl.pallas_call(functools.partial(step_body, shape=shape, points=points, c...  14.9 us
    ppermute x7, starting transfers between devices, from_distance(): return lax.ppermute(value, axis, [(i, i ^ distance) for i in range(count)])  13.9 us
    ppermute x9, starting transfers between devices, swap(): return lax.ppermute(value, axis, pairs)  13.3 us
    ppermute x9, waiting for transfers between devices, swap(): return lax.ppermute(value, axis, pairs)  11.1 us
    ppermute x7, waiting for transfers between devices, from_distance(): return lax.ppermute(value, axis, [(i, i ^ distance) for i in range(count)])  7.26 us
    pallas_call x1, Pallas kernels, shards(): pl.pallas_call(functools.partial(faces_body, shape=shape), out_shape=form...  1.97 us
  transfers between devices with their start and end apart: 21, of which 11 were waited for; matrix products, arithmetic and copies ran while one was open for 0% of the time, Pallas kernels for 10%

profile of v14, /device:TPU:0, one launch (start us, length us, event | category | flops | bytes accessed | tf_op | source)
XLA Modules:
  0.0 65.4 jit_solution(1634458478225389004)
XLA Ops:
  0.7 0.9 %copy_bitcast_fusion = (f32[3,3,32]{2,1,0:T(4,128)S(1)}, f32[3,3,32]{2,1,0:T(4,128)S(1)}) fusion(f32[3,3,1,32]{3,2,1,0:T(1,128)} %param.6, f32[3,3,1,32]{3,2,1,0:T(1,128)} %param.5), kind=kLoop, calls=%fused_computation.35 | loop fusion | bytes 4608
  1.5 3.1 %collective-permute-start = (f32[1,24,32]{2,1,0:T(8,128)S(1)}, f32[1,24,32]{2,1,0:T(8,128)S(1)}, u32[]{:S(2)}, u32[]{:S(2)}) collective-permute-start(f32[1,24,32]{2,1,0:T(8,128)S(1)} %fusion.5), channel_id=1, source_target_pairs={{0,1},{1,0},{2,3},{3,2},{4,5},{5,4},{6,7},{7,6},{8,9},{9,8},{10,11... | collective-permute-start | bytes 9224 | tf_op jit(solution)/shard_map/ppermute | solution.py:47
  4.6 2.0 %faces.1 = (f32[128,256]{1,0:T(8,128)S(1)}, f32[128,256]{1,0:T(8,128)S(1)}, f32[16,128]{1,0:T(8,128)S(1)}, f32[16,128]{1,0:T(8,128)S(1)}, f32[4,16,256]{2,1,0:T(8,128)S(1)}) custom-call(f32[4,32,16,256]{3,2,1,0:T(8,128)} %refs_2_.1), custom_call_target="tpu_custom_call" | custom-call | tf_op jit(solution)/shard_map/faces/pallas_call | solution.py:392
  6.6 1.7 %collective-permute-start.2 = (f32[128,256]{1,0:T(8,128)S(1)}, f32[128,256]{1,0:T(8,128)S(1)}, u32[]{:S(2)}, u32[]{:S(2)}) collective-permute-start(f32[128,256]{1,0:T(8,128)S(1)} %get-tuple-element.51), channel_id=1, source_target_pairs={{0,1},{1,0},{2,3},{3,2},{4,5},{5,4},{6,7},{7,6},{8,9},{9,8},{10,11... | collective-permute-start | bytes 393224 | tf_op jit(solution)/shard_map/ppermute | solution.py:32
  8.3 2.6 %collective-permute-start.1 = (f32[2,24,32]{2,1,0:T(8,128)S(1)}, f32[2,24,32]{2,1,0:T(8,128)S(1)}, u32[]{:S(2)}, u32[]{:S(2)}) collective-permute-start(f32[2,24,32]{2,1,0:T(8,128)S(1)} %pad_maximum_fusion.5), channel_id=1, source_target_pairs={{0,2},{1,3},{2,0},{3,1},{4,6},{5,7},{6,4},{7,5},{8,10},{9,11},{10,... | collective-permute-start | bytes 18440 | tf_op jit(solution)/shard_map/ppermute | solution.py:47
  10.9 1.0 %collective-permute-done.2 = f32[128,256]{1,0:T(8,128)S(1)} collective-permute-done((f32[128,256]{1,0:T(8,128)S(1)}, f32[128,256]{1,0:T(8,128)S(1)}, u32[]{:S(2)}, u32[]{:S(2)}) %collective-permute-start.2) | collective-permute-done | bytes 131104 | tf_op jit(solution)/shard_map/ppermute | solution.py:32
  11.9 1.1 %collective-permute-done.1 = f32[2,24,32]{2,1,0:T(8,128)S(1)} collective-permute-done((f32[2,24,32]{2,1,0:T(8,128)S(1)}, f32[2,24,32]{2,1,0:T(8,128)S(1)}, u32[]{:S(2)}, u32[]{:S(2)}) %collective-permute-start.1) | collective-permute-done | bytes 6176 | tf_op jit(solution)/shard_map/ppermute | solution.py:47
  13.2 1.6 %collective-permute-start.3 = (f32[40,128]{1,0:T(8,128)S(1)}, f32[40,128]{1,0:T(8,128)S(1)}, u32[]{:S(2)}, u32[]{:S(2)}) collective-permute-start(f32[40,128]{1,0:T(8,128)S(1)} %pad_maximum_fusion.7), channel_id=1, source_target_pairs={{0,4},{4,0},{8,12},{12,8},{1,5},{5,1},{9,13},{13,9},{2,6},{6,2},{1... | collective-permute-start | bytes 61448 | tf_op jit(solution)/shard_map/ppermute | solution.py:32
  14.8 2.3 %collective-permute-done.3.refs_5_ = f32[40,128]{1,0:T(8,128)S(1)} collective-permute-done((f32[40,128]{1,0:T(8,128)S(1)}, f32[40,128]{1,0:T(8,128)S(1)}, u32[]{:S(2)}, u32[]{:S(2)}) %collective-permute-start.3) | collective-permute-done | bytes 20512 | tf_op jit(solution)/shard_map/ppermute | solution.py:32
  17.1 2.4 %collective-permute-start.5 = (f32[64,128]{1,0:T(8,128)S(1)}, f32[64,128]{1,0:T(8,128)S(1)}, u32[]{:S(2)}, u32[]{:S(2)}) collective-permute-start(f32[64,128]{1,0:T(8,128)S(1)} %pad_maximum_fusion.2), channel_id=1, source_target_pairs={{0,12},{4,8},{8,4},{12,0},{1,13},{5,9},{9,5},{13,1},{2,14},{6,10},... | collective-permute-start | bytes 98312 | tf_op jit(solution)/shard_map/ppermute | solution.py:47
  19.5 2.4 %collective-permute-done.5.refs_6_ = f32[64,128]{1,0:T(8,128)S(1)} collective-permute-done((f32[64,128]{1,0:T(8,128)S(1)}, f32[64,128]{1,0:T(8,128)S(1)}, u32[]{:S(2)}, u32[]{:S(2)}) %collective-permute-start.5) | collective-permute-done | bytes 32800 | tf_op jit(solution)/shard_map/ppermute | solution.py:47
  22.0 0.5 collective-permute-start.7
  22.5 0.7 %collective-permute-done.6 = f32[1,96,128]{2,1,0:T(8,128)S(1)} collective-permute-done((f32[1,96,128]{2,1,0:T(8,128)S(1)}, f32[1,96,128]{2,1,0:T(8,128)S(1)}, u32[]{:S(2)}, u32[]{:S(2)}) %collective-permute-start.6) | collective-permute-done | bytes 49184 | tf_op jit(solution)/shard_map/ppermute | solution.py:47
  23.2 0.2 collective-permute-done.7.refs_7_
  23.4 5.2 %step.3 = (f32[4,32,16,256]{3,2,1,0:T(8,128)S(1)}, f32[128,256]{1,0:T(8,128)S(1)}, f32[128,256]{1,0:T(8,128)S(1)}, f32[16,128]{1,0:T(8,128)S(1)}, f32[16,128]{1,...) custom-call(s32[2]{0:T(128)S(1)} %bitcast.62, f32[8,24,128]{2,1,0:T(8,128)S(1)} %bitcast.59, ...), custom_call_target="tpu_custom_call" | custom-call | tf_op jit(solution)/shard_map/step/pallas_call | solution.py:441
  28.6 3.1 %collective-permute-start.8 = (f32[128,256]{1,0:T(8,128)S(1)}, f32[128,256]{1,0:T(8,128)S(1)}, u32[]{:S(2)}, u32[]{:S(2)}) collective-permute-start(f32[128,256]{1,0:T(8,128)S(1)} %get-tuple-element.62), channel_id=1, source_target_pairs={{0,1},{1,0},{2,3},{3,2},{4,5},{5,4},{6,7},{7,6},{8,9},{9,8},{10,11... | collective-permute-start | bytes 393224 | tf_op jit(solution)/shard_map/ppermute | solution.py:32
  31.8 0.4 collective-permute-start.12
  32.2 1.5 %collective-permute-start.10 = (f32[16,128]{1,0:T(8,128)S(1)}, f32[16,128]{1,0:T(8,128)S(1)}, u32[]{:S(2)}, u32[]{:S(2)}) collective-permute-start(f32[16,128]{1,0:T(8,128)S(1)} %get-tuple-element.64), channel_id=1, source_target_pairs={{0,4},{4,0},{8,12},{12,8},{1,5},{5,1},{9,13},{13,9},{2,6},{6,2},{1... | collective-permute-start | bytes 24584 | tf_op jit(solution)/shard_map/ppermute | solution.py:32
  33.7 2.2 %collective-permute-done.10.refs_5_ = f32[16,128]{1,0:T(8,128)S(1)} collective-permute-done((f32[16,128]{1,0:T(8,128)S(1)}, f32[16,128]{1,0:T(8,128)S(1)}, u32[]{:S(2)}, u32[]{:S(2)}) %collective-permute-start.10) | collective-permute-done | bytes 8224 | tf_op jit(solution)/shard_map/ppermute | solution.py:32
  35.9 4.9 %step.4 = (f32[4,32,16,256]{3,2,1,0:T(8,128)S(1)}, f32[144,256]{1,0:T(8,128)S(1)}, f32[128,256]{1,0:T(8,128)S(1)}, f32[16,128]{1,0:T(8,128)S(1)}, f32[16,128]{1,0:T(8,128)S(1)}, /*index=5*/f32[4,16,256]{2,1,0:T(8,128)S(1)}) custom-call(s32[2]{0:T(128)S(1)} %bitcast.63, f32[8,24,128]{2,1,0:T(8,128)S(1)} %bitcast.60, ...), custom_call_target="tpu_custom_call" | custom-call | tf_op jit(solution)/shard_map/step/pallas_call | solution.py:441
  40.8 1.7 %collective-permute-start.13 = (f32[144,256]{1,0:T(8,128)S(1)}, f32[144,256]{1,0:T(8,128)S(1)}, u32[]{:S(2)}, u32[]{:S(2)}) collective-permute-start(f32[144,256]{1,0:T(8,128)S(1)} %get-tuple-element.68), channel_id=1, source_target_pairs={{0,1},{1,0},{2,3},{3,2},{4,5},{5,4},{6,7},{7,6},{8,9},{9,8},{10,11... | collective-permute-start | bytes 442376 | tf_op jit(solution)/shard_map/ppermute | solution.py:32
  42.5 3.7 %collective-permute-done.13.refs_3_ = f32[144,256]{1,0:T(8,128)S(1)} collective-permute-done((f32[144,256]{1,0:T(8,128)S(1)}, f32[144,256]{1,0:T(8,128)S(1)}, u32[]{:S(2)}, u32[]{:S(2)}) %collective-permute-start.13) | collective-permute-done | bytes 147488 | tf_op jit(solution)/shard_map/ppermute | solution.py:32
  46.2 2.8 %collective-permute-start.15 = (f32[48,128]{1,0:T(8,128)S(1)}, f32[48,128]{1,0:T(8,128)S(1)}, u32[]{:S(2)}, u32[]{:S(2)}) collective-permute-start(f32[48,128]{1,0:T(8,128)S(1)} %pad_maximum_fusion.6), channel_id=1, source_target_pairs={{0,4},{4,0},{8,12},{12,8},{1,5},{5,1},{9,13},{13,9},{2,6},{6,2},{1... | collective-permute-start | bytes 73736 | tf_op jit(solution)/shard_map/ppermute | solution.py:32
  49.0 1.8 %collective-permute-done.15.refs_5_ = f32[48,128]{1,0:T(8,128)S(1)} collective-permute-done((f32[48,128]{1,0:T(8,128)S(1)}, f32[48,128]{1,0:T(8,128)S(1)}, u32[]{:S(2)}, u32[]{:S(2)}) %collective-permute-start.15) | collective-permute-done | bytes 24608 | tf_op jit(solution)/shard_map/ppermute | solution.py:32
  50.8 3.2 %collective-permute-start.17 = (f32[2,32,128]{2,1,0:T(8,128)S(1)}, f32[2,32,128]{2,1,0:T(8,128)S(1)}, u32[]{:S(2)}, u32[]{:S(2)}) collective-permute-start(f32[2,32,128]{2,1,0:T(8,128)S(1)} %bitcast.71), channel_id=1, source_target_pairs={{0,8},{4,12},{8,0},{12,4},{1,9},{5,13},{9,1},{13,5},{2,10},{6,14},... | collective-permute-start | bytes 98312 | tf_op jit(solution)/shard_map/ppermute | solution.py:47
  54.0 1.9 %collective-permute-done.17 = f32[2,32,128]{2,1,0:T(8,128)S(1)} collective-permute-done((f32[2,32,128]{2,1,0:T(8,128)S(1)}, f32[2,32,128]{2,1,0:T(8,128)S(1)}, u32[]{:S(2)}, u32[]{:S(2)}) %collective-permute-start.17) | collective-permute-done | bytes 32800 | tf_op jit(solution)/shard_map/ppermute | solution.py:47
  55.9 0.1 copy.11
  56.0 2.4 %collective-permute-start.19 = (f32[128,128]{0,1:T(8,128)S(1)}, f32[128,128]{0,1:T(8,128)S(1)}, u32[]{:S(2)}, u32[]{:S(2)}) collective-permute-start(f32[128,128]{0,1:T(8,128)S(1)} %copy.11), channel_id=1, source_target_pairs={{0,2},{1,3},{2,0},{3,1},{4,6},{5,7},{6,4},{7,5},{8,10},{9,11},{10,... | collective-permute-start | bytes 196616 | tf_op jit(solution)/shard_map/ppermute | solution.py:47
  58.4 4.8 %step.5 = f32[4,32,16,256]{3,2,1,0:T(8,128)} custom-call(s32[2]{0:T(128)S(1)} %bitcast.64, f32[8,24,128]{2,1,0:T(8,128)S(1)} %bitcast.61, f32[4,32,16,256]{3,2,1,0:T(8,128)S(1)} %get-tuple-element.78.refs_2_, f32[144,256]{1,0:T(8,128)S(1)} %collective-permute-done.13.refs_3_, f32[128,256]{1,0:T(8,128)S(1)} %collective-permute-done.14.refs_4_, ...), custom_call_target="tpu_custom_call" | custom-call | tf_op jit(solution)/shard_map/step/pallas_call | solution.py:441
  63.4 1.2 %collective-permute-done.20 = f32[1,128,32]{1,2,0:T(8,128)S(1)} collective-permute-done((f32[1,128,32]{1,2,0:T(8,128)S(1)}, f32[1,128,32]{1,2,0:T(8,128)S(1)}, u32[]{:S(2)}, u32[]{:S(2)}) %collective-permute-start.20) | collective-permute-done | bytes 16416 | tf_op jit(solution)/shard_map/ppermute | solution.py:47
  64.6 0.1 copy.12
  64.8 0.6 add.42
  (57 shorter events, 0.6 us)
Async XLA Ops:
  0.6 22.8 %copy-start = (f32[4,32,16,256]{3,2,1,0:T(8,128)S(1)}, f32[4,32,16,256]{3,2,1,0:T(8,128)}, u32[]{:S(2)}) copy-start(f32[4,32,16,256]{3,2,1,0:T(8,128)} %refs_2_.1) | copy-start | bytes 6291460
  0.6 22.8 %copy-start.1 = (s32[1,1,1,2]{3,2,1,0:T(1,128)S(1)}, s32[1,1,1,2]{3,2,1,0:T(1,128)}, u32[]{:S(2)}) copy-start(s32[1,1,1,2]{3,2,1,0:T(1,128)} %param.7) | copy-start | bytes 28
  1.5 5.1 %collective-permute-start = (f32[1,24,32]{2,1,0:T(8,128)S(1)}, f32[1,24,32]{2,1,0:T(8,128)S(1)}, u32[]{:S(2)}, u32[]{:S(2)}) collective-permute-start(f32[1,24,32]{2,1,0:T(8,128)S(1)} %fusion.5), channel_id=1, source_target_pairs={{0,1},{1,0},{2,3},{3,2},{4,5},{5,4},{6,7},{7,6},{8,9},{9,8},{10,11... | collective-permute-start | bytes 9224 | tf_op jit(solution)/shard_map/ppermute | solution.py:47
  6.6 5.3 %collective-permute-start.2 = (f32[128,256]{1,0:T(8,128)S(1)}, f32[128,256]{1,0:T(8,128)S(1)}, u32[]{:S(2)}, u32[]{:S(2)}) collective-permute-start(f32[128,256]{1,0:T(8,128)S(1)} %get-tuple-element.51), channel_id=1, source_target_pairs={{0,1},{1,0},{2,3},{3,2},{4,5},{5,4},{6,7},{7,6},{8,9},{9,8},{10,11... | collective-permute-start | bytes 393224 | tf_op jit(solution)/shard_map/ppermute | solution.py:32
  8.3 4.7 %collective-permute-start.1 = (f32[2,24,32]{2,1,0:T(8,128)S(1)}, f32[2,24,32]{2,1,0:T(8,128)S(1)}, u32[]{:S(2)}, u32[]{:S(2)}) collective-permute-start(f32[2,24,32]{2,1,0:T(8,128)S(1)} %pad_maximum_fusion.5), channel_id=1, source_target_pairs={{0,2},{1,3},{2,0},{3,1},{4,6},{5,7},{6,4},{7,5},{8,10},{9,11},{10,... | collective-permute-start | bytes 18440 | tf_op jit(solution)/shard_map/ppermute | solution.py:47
  13.2 1.6 %collective-permute-start.4 = (f32[128,256]{1,0:T(8,128)S(1)}, f32[128,256]{1,0:T(8,128)S(1)}, u32[]{:S(2)}, u32[]{:S(2)}) collective-permute-start(f32[128,256]{1,0:T(8,128)S(1)} %get-tuple-element.55), channel_id=1, source_target_pairs={{0,16},{1,2},{2,1},{3,19},{16,0},{17,18},{18,17},{19,3},{4,20},{5,... | collective-permute-start | bytes 393224 | tf_op jit(solution)/shard_map/ppermute | solution.py:42
  13.2 3.8 %collective-permute-start.3 = (f32[40,128]{1,0:T(8,128)S(1)}, f32[40,128]{1,0:T(8,128)S(1)}, u32[]{:S(2)}, u32[]{:S(2)}) collective-permute-start(f32[40,128]{1,0:T(8,128)S(1)} %pad_maximum_fusion.7), channel_id=1, source_target_pairs={{0,4},{4,0},{8,12},{12,8},{1,5},{5,1},{9,13},{13,9},{2,6},{6,2},{1... | collective-permute-start | bytes 61448 | tf_op jit(solution)/shard_map/ppermute | solution.py:32
  17.1 4.8 %collective-permute-start.5 = (f32[64,128]{1,0:T(8,128)S(1)}, f32[64,128]{1,0:T(8,128)S(1)}, u32[]{:S(2)}, u32[]{:S(2)}) collective-permute-start(f32[64,128]{1,0:T(8,128)S(1)} %pad_maximum_fusion.2), channel_id=1, source_target_pairs={{0,12},{4,8},{8,4},{12,0},{1,13},{5,9},{9,5},{13,1},{2,14},{6,10},... | collective-permute-start | bytes 98312 | tf_op jit(solution)/shard_map/ppermute | solution.py:47
  21.9 1.3 %collective-permute-start.6 = (f32[1,96,128]{2,1,0:T(8,128)S(1)}, f32[1,96,128]{2,1,0:T(8,128)S(1)}, u32[]{:S(2)}, u32[]{:S(2)}) collective-permute-start(f32[1,96,128]{2,1,0:T(8,128)S(1)} %maximum_bitcast_fusion), channel_id=1, source_target_pairs={{0,16},{16,0},{1,17},{17,1},{2,18},{18,2},{3,19},{19,3},{4,20},{20... | collective-permute-start | bytes 147464 | tf_op jit(solution)/shard_map/ppermute | solution.py:47
  22.0 1.4 %collective-permute-start.7 = (f32[4,16,256]{2,1,0:T(8,128)S(1)}, f32[4,16,256]{2,1,0:T(8,128)S(1)}, u32[]{:S(2)}, u32[]{:S(2)}) collective-permute-start(f32[4,16,256]{2,1,0:T(8,128)S(1)} %get-tuple-element.60), channel_id=1, source_target_pairs={{0,16},{16,0},{1,17},{17,1},{2,18},{18,2},{3,19},{19,3},{4,20},{20... | collective-permute-start | bytes 196616 | tf_op jit(solution)/shard_map/ppermute | solution.py:32
  28.6 7.3 %collective-permute-start.8 = (f32[128,256]{1,0:T(8,128)S(1)}, f32[128,256]{1,0:T(8,128)S(1)}, u32[]{:S(2)}, u32[]{:S(2)}) collective-permute-start(f32[128,256]{1,0:T(8,128)S(1)} %get-tuple-element.62), channel_id=1, source_target_pairs={{0,1},{1,0},{2,3},{3,2},{4,5},{5,4},{6,7},{7,6},{8,9},{9,8},{10,11... | collective-permute-start | bytes 393224 | tf_op jit(solution)/shard_map/ppermute | solution.py:32
  31.7 4.2 %collective-permute-start.9 = (f32[128,256]{1,0:T(8,128)S(1)}, f32[128,256]{1,0:T(8,128)S(1)}, u32[]{:S(2)}, u32[]{:S(2)}) collective-permute-start(f32[128,256]{1,0:T(8,128)S(1)} %get-tuple-element.63), channel_id=1, source_target_pairs={{0,16},{1,2},{2,1},{3,19},{16,0},{17,18},{18,17},{19,3},{4,20},{5,... | collective-permute-start | bytes 393224 | tf_op jit(solution)/shard_map/ppermute | solution.py:42
  31.8 4.1 %collective-permute-start.12 = (f32[4,16,256]{2,1,0:T(8,128)S(1)}, f32[4,16,256]{2,1,0:T(8,128)S(1)}, u32[]{:S(2)}, u32[]{:S(2)}) collective-permute-start(f32[4,16,256]{2,1,0:T(8,128)S(1)} %get-tuple-element.66), channel_id=1, source_target_pairs={{0,16},{16,0},{1,17},{17,1},{2,18},{18,2},{3,19},{19,3},{4,20},{20... | collective-permute-start | bytes 196616 | tf_op jit(solution)/shard_map/ppermute | solution.py:32
  32.2 3.7 %collective-permute-start.10 = (f32[16,128]{1,0:T(8,128)S(1)}, f32[16,128]{1,0:T(8,128)S(1)}, u32[]{:S(2)}, u32[]{:S(2)}) collective-permute-start(f32[16,128]{1,0:T(8,128)S(1)} %get-tuple-element.64), channel_id=1, source_target_pairs={{0,4},{4,0},{8,12},{12,8},{1,5},{5,1},{9,13},{13,9},{2,6},{6,2},{1... | collective-permute-start | bytes 24584 | tf_op jit(solution)/shard_map/ppermute | solution.py:32
  33.7 2.2 %collective-permute-start.11 = (f32[16,128]{1,0:T(8,128)S(1)}, f32[16,128]{1,0:T(8,128)S(1)}, u32[]{:S(2)}, u32[]{:S(2)}) collective-permute-start(f32[16,128]{1,0:T(8,128)S(1)} %get-tuple-element.65), channel_id=1, source_target_pairs={{0,16},{4,8},{8,4},{12,28},{16,0},{20,24},{24,20},{28,12},{1,17},{... | collective-permute-start | bytes 24584 | tf_op jit(solution)/shard_map/ppermute | solution.py:42
  40.8 5.4 %collective-permute-start.13 = (f32[144,256]{1,0:T(8,128)S(1)}, f32[144,256]{1,0:T(8,128)S(1)}, u32[]{:S(2)}, u32[]{:S(2)}) collective-permute-start(f32[144,256]{1,0:T(8,128)S(1)} %get-tuple-element.68), channel_id=1, source_target_pairs={{0,1},{1,0},{2,3},{3,2},{4,5},{5,4},{6,7},{7,6},{8,9},{9,8},{10,11... | collective-permute-start | bytes 442376 | tf_op jit(solution)/shard_map/ppermute | solution.py:32
  42.5 3.7 %collective-permute-start.14 = (f32[128,256]{1,0:T(8,128)S(1)}, f32[128,256]{1,0:T(8,128)S(1)}, u32[]{:S(2)}, u32[]{:S(2)}) collective-permute-start(f32[128,256]{1,0:T(8,128)S(1)} %get-tuple-element.70), channel_id=1, source_target_pairs={{0,16},{1,2},{2,1},{3,19},{16,0},{17,18},{18,17},{19,3},{4,20},{5,... | collective-permute-start | bytes 393224 | tf_op jit(solution)/shard_map/ppermute | solution.py:42
  46.2 4.6 %collective-permute-start.15 = (f32[48,128]{1,0:T(8,128)S(1)}, f32[48,128]{1,0:T(8,128)S(1)}, u32[]{:S(2)}, u32[]{:S(2)}) collective-permute-start(f32[48,128]{1,0:T(8,128)S(1)} %pad_maximum_fusion.6), channel_id=1, source_target_pairs={{0,4},{4,0},{8,12},{12,8},{1,5},{5,1},{9,13},{13,9},{2,6},{6,2},{1... | collective-permute-start | bytes 73736 | tf_op jit(solution)/shard_map/ppermute | solution.py:32
  49.0 1.8 %collective-permute-start.16 = (f32[4,16,256]{2,1,0:T(8,128)S(1)}, f32[4,16,256]{2,1,0:T(8,128)S(1)}, u32[]{:S(2)}, u32[]{:S(2)}) collective-permute-start(f32[4,16,256]{2,1,0:T(8,128)S(1)} %get-tuple-element.74), channel_id=1, source_target_pairs={{0,16},{16,0},{1,17},{17,1},{2,18},{18,2},{3,19},{19,3},{4,20},{20... | collective-permute-start | bytes 196616 | tf_op jit(solution)/shard_map/ppermute | solution.py:32
  50.8 5.1 %collective-permute-start.17 = (f32[2,32,128]{2,1,0:T(8,128)S(1)}, f32[2,32,128]{2,1,0:T(8,128)S(1)}, u32[]{:S(2)}, u32[]{:S(2)}) collective-permute-start(f32[2,32,128]{2,1,0:T(8,128)S(1)} %bitcast.71), channel_id=1, source_target_pairs={{0,8},{4,12},{8,0},{12,4},{1,9},{5,13},{9,1},{13,5},{2,10},{6,14},... | collective-permute-start | bytes 98312 | tf_op jit(solution)/shard_map/ppermute | solution.py:47
  54.0 1.9 %collective-permute-start.18 = (f32[16,128]{1,0:T(8,128)S(1)}, f32[16,128]{1,0:T(8,128)S(1)}, u32[]{:S(2)}, u32[]{:S(2)}) collective-permute-start(f32[16,128]{1,0:T(8,128)S(1)} %get-tuple-element.76), channel_id=1, source_target_pairs={{0,16},{4,8},{8,4},{12,28},{16,0},{20,24},{24,20},{28,12},{1,17},{... | collective-permute-start | bytes 24584 | tf_op jit(solution)/shard_map/ppermute | solution.py:42
  56.0 7.3 %collective-permute-start.19 = (f32[128,128]{0,1:T(8,128)S(1)}, f32[128,128]{0,1:T(8,128)S(1)}, u32[]{:S(2)}, u32[]{:S(2)}) collective-permute-start(f32[128,128]{0,1:T(8,128)S(1)} %copy.11), channel_id=1, source_target_pairs={{0,2},{1,3},{2,0},{3,1},{4,6},{5,7},{6,4},{7,5},{8,10},{9,11},{10,... | collective-permute-start | bytes 196616 | tf_op jit(solution)/shard_map/ppermute | solution.py:47
  63.3 1.2 %collective-permute-start.20 = (f32[1,128,32]{1,2,0:T(8,128)S(1)}, f32[1,128,32]{1,2,0:T(8,128)S(1)}, u32[]{:S(2)}, u32[]{:S(2)}) collective-permute-start(f32[1,128,32]{1,2,0:T(8,128)S(1)} %dynamic-slice_bitcast_fusion), channel_id=1, source_target_pairs={{0,16},{16,0},{1,17},{17,1},{2,18},{18,2},{3,19},{19,3},{4,20},{20... | collective-permute-start | bytes 49160 | tf_op jit(solution)/shard_map/ppermute | solution.py:47

commit v15 on v12

--- a/solution.py
+++ b/solution.py
@@ -458,9 +458,11 @@
             halos = swap_faces(faces)
             continue
         za, zb, ya, yb = faces[:4]
-        za_in, zb_in = swap(za, "gz", 0), swap_inner(zb, "gz")
+        zb_in = swap_inner(zb, "gz")
+        za_in = swap(za, "gz", 0)
         sums = za[4 * count_x :] + za_in[4 * count_x :]
         pieces = jnp.concatenate([sums[:, h * 128 : h * 128 + 128] for h in range(2)], axis=0)
+        zb_in = masked(zb_in, "gz", 1)
         pieces, ya, zb_in = barrier((pieces, ya, zb_in))
         ya_in = swap(jnp.concatenate([ya, pieces], axis=0), "gy", 0)
         x_faces = [swap(face, "gx", first) for first, face in enumerate(faces[4:])]

time: 65.3 us -> 65.4 us (level)
    ppermute x9, starting transfers between devices: 13 us -> 14.2 us  [swap(): return lax.ppermute(value, axis, pairs)]
    ppermute x7, starting transfers between devices: 13.7 us -> 12.5 us  [from_distance(): return lax.ppermute(value, axis, [(i, i ^ distance) for i in range(count)])]
  transfers between devices with their start and end apart: 21 -> 21, of which waited for: 11 -> 12; matrix products, arithmetic and copies ran while one was open for 0% -> 0% of each run, Pallas kernels for 8% -> 8%
where the time goes in v15:
time: 65.4 us; the launch traced here: 65.1 us
  starting transfers between devices  26.8 us (41%)
  waiting for transfers between devices  18.5 us (28%)
  Pallas kernels  15.4 us (24%)
  local copies, waits for them, and re-layouts  3.17 us (5%)
  between operations  0.91 us (1%)
    pallas_call x3, Pallas kernels, shards(): pl.pallas_call(functools.partial(step_body, shape=shape, points=points, c...  14.7 us
    ppermute x9, starting transfers between devices, swap(): return lax.ppermute(value, axis, pairs)  14.2 us
    ppermute x7, starting transfers between devices, from_distance(): return lax.ppermute(value, axis, [(i, i ^ distance) for i in range(count)])  12.5 us
    ppermute x9, waiting for transfers between devices, swap(): return lax.ppermute(value, axis, pairs)  11.3 us
    ppermute x7, waiting for transfers between devices, from_distance(): return lax.ppermute(value, axis, [(i, i ^ distance) for i in range(count)])  7.2 us
    unnamed x10, local copies, waits for them, and re-layouts  2.33 us
  transfers between devices with their start and end apart: 21, of which 12 were waited for; matrix products, arithmetic and copies ran while one was open for 0% of the time, Pallas kernels for 8%

profile of v15, /device:TPU:0, one launch (start us, length us, event | category | flops | bytes accessed | tf_op | source)
XLA Modules:
  0.0 65.1 jit_solution(15671099609130198428)
XLA Ops:
  0.6 0.7 %copy_bitcast_fusion = (f32[3,3,32]{2,1,0:T(4,128)S(1)}, f32[3,3,32]{2,1,0:T(4,128)S(1)}) fusion(f32[3,3,1,32]{3,2,1,0:T(1,128)} %param.6, f32[3,3,1,32]{3,2,1,0:T(1,128)} %param.5), kind=kLoop, calls=%fused_computation.36 | loop fusion | bytes 4608
  1.4 3.1 %collective-permute-start = (f32[1,24,32]{2,1,0:T(8,128)S(1)}, f32[1,24,32]{2,1,0:T(8,128)S(1)}, u32[]{:S(2)}, u32[]{:S(2)}) collective-permute-start(f32[1,24,32]{2,1,0:T(8,128)S(1)} %fusion.5), channel_id=1, source_target_pairs={{0,1},{1,0},{2,3},{3,2},{4,5},{5,4},{6,7},{7,6},{8,9},{9,8},{10,11... | collective-permute-start | bytes 9224 | tf_op jit(solution)/shard_map/ppermute | solution.py:47
  4.5 1.6 %copy-done = f32[4,32,16,256]{3,2,1,0:T(8,128)S(1)} copy-done((f32[4,32,16,256]{3,2,1,0:T(8,128)S(1)}, f32[4,32,16,256]{3,2,1,0:T(8,128)}, u32[]{:S(2)}) %copy-start) | copy-done | bytes 2097176
  6.0 0.7 %faces.1 = (f32[128,256]{1,0:T(8,128)S(1)}, f32[128,256]{1,0:T(8,128)S(1)}, f32[16,128]{1,0:T(8,128)S(1)}, f32[16,128]{1,0:T(8,128)S(1)}, f32[4,16,256]{2,1,0:T(8,128)S(1)}) custom-call(f32[4,32,16,256]{3,2,1,0:T(8,128)S(1)} %copy-done), custom_call_target="tpu_custom_call" | custom-call | tf_op jit(solution)/shard_map/faces/pallas_call | solution.py:387
  6.8 1.3 %collective-permute-start.2 = (f32[128,256]{1,0:T(8,128)S(1)}, f32[128,256]{1,0:T(8,128)S(1)}, u32[]{:S(2)}, u32[]{:S(2)}) collective-permute-start(f32[128,256]{1,0:T(8,128)S(1)} %get-tuple-element.51), channel_id=1, source_target_pairs={{0,1},{1,0},{2,3},{3,2},{4,5},{5,4},{6,7},{7,6},{8,9},{9,8},{10,11... | collective-permute-start | bytes 393224 | tf_op jit(solution)/shard_map/ppermute | solution.py:32
  8.2 2.6 %collective-permute-start.1 = (f32[2,24,32]{2,1,0:T(8,128)S(1)}, f32[2,24,32]{2,1,0:T(8,128)S(1)}, u32[]{:S(2)}, u32[]{:S(2)}) collective-permute-start(f32[2,24,32]{2,1,0:T(8,128)S(1)} %pad_maximum_fusion.5), channel_id=1, source_target_pairs={{0,2},{1,3},{2,0},{3,1},{4,6},{5,7},{6,4},{7,5},{8,10},{9,11},{10,... | collective-permute-start | bytes 18440 | tf_op jit(solution)/shard_map/ppermute | solution.py:47
  10.7 1.3 %collective-permute-done.2 = f32[128,256]{1,0:T(8,128)S(1)} collective-permute-done((f32[128,256]{1,0:T(8,128)S(1)}, f32[128,256]{1,0:T(8,128)S(1)}, u32[]{:S(2)}, u32[]{:S(2)}) %collective-permute-start.2) | collective-permute-done | bytes 131104 | tf_op jit(solution)/shard_map/ppermute | solution.py:32
  12.1 0.9 %collective-permute-done.1 = f32[2,24,32]{2,1,0:T(8,128)S(1)} collective-permute-done((f32[2,24,32]{2,1,0:T(8,128)S(1)}, f32[2,24,32]{2,1,0:T(8,128)S(1)}, u32[]{:S(2)}, u32[]{:S(2)}) %collective-permute-start.1) | collective-permute-done | bytes 6176 | tf_op jit(solution)/shard_map/ppermute | solution.py:47
  13.2 1.6 %collective-permute-start.3 = (f32[40,128]{1,0:T(8,128)S(1)}, f32[40,128]{1,0:T(8,128)S(1)}, u32[]{:S(2)}, u32[]{:S(2)}) collective-permute-start(f32[40,128]{1,0:T(8,128)S(1)} %pad_maximum_fusion.7), channel_id=1, source_target_pairs={{0,4},{4,0},{8,12},{12,8},{1,5},{5,1},{9,13},{13,9},{2,6},{6,2},{1... | collective-permute-start | bytes 61448 | tf_op jit(solution)/shard_map/ppermute | solution.py:32
  14.8 2.3 %collective-permute-done.3.refs_5_ = f32[40,128]{1,0:T(8,128)S(1)} collective-permute-done((f32[40,128]{1,0:T(8,128)S(1)}, f32[40,128]{1,0:T(8,128)S(1)}, u32[]{:S(2)}, u32[]{:S(2)}) %collective-permute-start.3) | collective-permute-done | bytes 20512 | tf_op jit(solution)/shard_map/ppermute | solution.py:32
  17.1 2.4 %collective-permute-start.5 = (f32[64,128]{1,0:T(8,128)S(1)}, f32[64,128]{1,0:T(8,128)S(1)}, u32[]{:S(2)}, u32[]{:S(2)}) collective-permute-start(f32[64,128]{1,0:T(8,128)S(1)} %pad_maximum_fusion.2), channel_id=1, source_target_pairs={{0,12},{4,8},{8,4},{12,0},{1,13},{5,9},{9,5},{13,1},{2,14},{6,10},... | collective-permute-start | bytes 98312 | tf_op jit(solution)/shard_map/ppermute | solution.py:47
  19.5 2.4 %collective-permute-done.5.refs_6_ = f32[64,128]{1,0:T(8,128)S(1)} collective-permute-done((f32[64,128]{1,0:T(8,128)S(1)}, f32[64,128]{1,0:T(8,128)S(1)}, u32[]{:S(2)}, u32[]{:S(2)}) %collective-permute-start.5) | collective-permute-done | bytes 32800 | tf_op jit(solution)/shard_map/ppermute | solution.py:47
  22.0 0.5 collective-permute-start.7
  22.5 0.7 %collective-permute-done.6 = f32[1,96,128]{2,1,0:T(8,128)S(1)} collective-permute-done((f32[1,96,128]{2,1,0:T(8,128)S(1)}, f32[1,96,128]{2,1,0:T(8,128)S(1)}, u32[]{:S(2)}, u32[]{:S(2)}) %collective-permute-start.6) | collective-permute-done | bytes 49184 | tf_op jit(solution)/shard_map/ppermute | solution.py:47
  23.2 0.2 collective-permute-done.7.refs_7_
  23.4 5.2 %step.3 = (f32[4,32,16,256]{3,2,1,0:T(8,128)S(1)}, f32[128,256]{1,0:T(8,128)S(1)}, f32[128,256]{1,0:T(8,128)S(1)}, f32[16,128]{1,0:T(8,128)S(1)}, f32[16,128]{1,...) custom-call(s32[2]{0:T(128)S(1)} %bitcast.62, f32[8,24,128]{2,1,0:T(8,128)S(1)} %bitcast.59, ...), custom_call_target="tpu_custom_call" | custom-call | tf_op jit(solution)/shard_map/step/pallas_call | solution.py:435
  28.6 3.2 %collective-permute-start.8 = (f32[128,256]{1,0:T(8,128)S(1)}, f32[128,256]{1,0:T(8,128)S(1)}, u32[]{:S(2)}, u32[]{:S(2)}) collective-permute-start(f32[128,256]{1,0:T(8,128)S(1)} %get-tuple-element.62), channel_id=1, source_target_pairs={{0,1},{1,0},{2,3},{3,2},{4,5},{5,4},{6,7},{7,6},{8,9},{9,8},{10,11... | collective-permute-start | bytes 393224 | tf_op jit(solution)/shard_map/ppermute | solution.py:32
  31.8 0.4 collective-permute-start.12
  32.3 1.5 %collective-permute-start.10 = (f32[16,128]{1,0:T(8,128)S(1)}, f32[16,128]{1,0:T(8,128)S(1)}, u32[]{:S(2)}, u32[]{:S(2)}) collective-permute-start(f32[16,128]{1,0:T(8,128)S(1)} %get-tuple-element.64), channel_id=1, source_target_pairs={{0,4},{4,0},{8,12},{12,8},{1,5},{5,1},{9,13},{13,9},{2,6},{6,2},{1... | collective-permute-start | bytes 24584 | tf_op jit(solution)/shard_map/ppermute | solution.py:32
  33.8 2.1 %collective-permute-done.10.refs_5_ = f32[16,128]{1,0:T(8,128)S(1)} collective-permute-done((f32[16,128]{1,0:T(8,128)S(1)}, f32[16,128]{1,0:T(8,128)S(1)}, u32[]{:S(2)}, u32[]{:S(2)}) %collective-permute-start.10) | collective-permute-done | bytes 8224 | tf_op jit(solution)/shard_map/ppermute | solution.py:32
  36.0 4.9 %step.4 = (f32[4,32,16,256]{3,2,1,0:T(8,128)S(1)}, f32[144,256]{1,0:T(8,128)S(1)}, f32[128,256]{1,0:T(8,128)S(1)}, f32[16,128]{1,0:T(8,128)S(1)}, f32[16,128]{1,0:T(8,128)S(1)}, /*index=5*/f32[4,16,256]{2,1,0:T(8,128)S(1)}) custom-call(s32[2]{0:T(128)S(1)} %bitcast.63, f32[8,24,128]{2,1,0:T(8,128)S(1)} %bitcast.60, ...), custom_call_target="tpu_custom_call" | custom-call | tf_op jit(solution)/shard_map/step/pallas_call | solution.py:435
  40.9 2.7 %collective-permute-start.13 = (f32[144,256]{1,0:T(8,128)S(1)}, f32[144,256]{1,0:T(8,128)S(1)}, u32[]{:S(2)}, u32[]{:S(2)}) collective-permute-start(f32[144,256]{1,0:T(8,128)S(1)} %get-tuple-element.68), channel_id=1, source_target_pairs={{0,1},{1,0},{2,3},{3,2},{4,5},{5,4},{6,7},{7,6},{8,9},{9,8},{10,11... | collective-permute-start | bytes 442376 | tf_op jit(solution)/shard_map/ppermute | solution.py:32
  43.6 3.5 %collective-permute-done.13.refs_3_ = f32[144,256]{1,0:T(8,128)S(1)} collective-permute-done((f32[144,256]{1,0:T(8,128)S(1)}, f32[144,256]{1,0:T(8,128)S(1)}, u32[]{:S(2)}, u32[]{:S(2)}) %collective-permute-start.13) | collective-permute-done | bytes 147488 | tf_op jit(solution)/shard_map/ppermute | solution.py:32
  47.2 3.0 %collective-permute-start.15 = (f32[48,128]{1,0:T(8,128)S(1)}, f32[48,128]{1,0:T(8,128)S(1)}, u32[]{:S(2)}, u32[]{:S(2)}) collective-permute-start(f32[48,128]{1,0:T(8,128)S(1)} %pad_maximum_fusion.6), channel_id=1, source_target_pairs={{0,4},{4,0},{8,12},{12,8},{1,5},{5,1},{9,13},{13,9},{2,6},{6,2},{1... | collective-permute-start | bytes 73736 | tf_op jit(solution)/shard_map/ppermute | solution.py:32
  50.2 1.8 %collective-permute-done.15.refs_5_ = f32[48,128]{1,0:T(8,128)S(1)} collective-permute-done((f32[48,128]{1,0:T(8,128)S(1)}, f32[48,128]{1,0:T(8,128)S(1)}, u32[]{:S(2)}, u32[]{:S(2)}) %collective-permute-start.15) | collective-permute-done | bytes 24608 | tf_op jit(solution)/shard_map/ppermute | solution.py:32
  52.0 3.1 %collective-permute-start.17 = (f32[2,32,128]{2,1,0:T(8,128)S(1)}, f32[2,32,128]{2,1,0:T(8,128)S(1)}, u32[]{:S(2)}, u32[]{:S(2)}) collective-permute-start(f32[2,32,128]{2,1,0:T(8,128)S(1)} %bitcast.71), channel_id=1, source_target_pairs={{0,8},{4,12},{8,0},{12,4},{1,9},{5,13},{9,1},{13,5},{2,10},{6,14},... | collective-permute-start | bytes 98312 | tf_op jit(solution)/shard_map/ppermute | solution.py:47
  55.1 1.9 %collective-permute-done.17 = f32[2,32,128]{2,1,0:T(8,128)S(1)} collective-permute-done((f32[2,32,128]{2,1,0:T(8,128)S(1)}, f32[2,32,128]{2,1,0:T(8,128)S(1)}, u32[]{:S(2)}, u32[]{:S(2)}) %collective-permute-start.17) | collective-permute-done | bytes 32800 | tf_op jit(solution)/shard_map/ppermute | solution.py:47
  57.1 1.1 %collective-permute-start.19 = (f32[128,128]{0,1:T(8,128)S(1)}, f32[128,128]{0,1:T(8,128)S(1)}, u32[]{:S(2)}, u32[]{:S(2)}) collective-permute-start(f32[128,128]{0,1:T(8,128)S(1)} %copy.11), channel_id=1, source_target_pairs={{0,2},{1,3},{2,0},{3,1},{4,6},{5,7},{6,4},{7,5},{8,10},{9,11},{10,... | collective-permute-start | bytes 196616 | tf_op jit(solution)/shard_map/ppermute | solution.py:47
  58.2 4.6 %step.5 = f32[4,32,16,256]{3,2,1,0:T(8,128)} custom-call(s32[2]{0:T(128)S(1)} %bitcast.64, f32[8,24,128]{2,1,0:T(8,128)S(1)} %bitcast.61, f32[4,32,16,256]{3,2,1,0:T(8,128)S(1)} %get-tuple-element.78.refs_2_, f32[144,256]{1,0:T(8,128)S(1)} %collective-permute-done.13.refs_3_, f32[128,256]{1,0:T(8,128)S(1)} %broadcast_select_fusion.refs_4_, ...), custom_call_target="tpu_custom_call" | custom-call | tf_op jit(solution)/shard_map/step/pallas_call | solution.py:435
  62.8 0.1 collective-permute-done.19
  63.1 1.2 %collective-permute-done.20 = f32[1,128,32]{1,2,0:T(8,128)S(1)} collective-permute-done((f32[1,128,32]{1,2,0:T(8,128)S(1)}, f32[1,128,32]{1,2,0:T(8,128)S(1)}, u32[]{:S(2)}, u32[]{:S(2)}) %collective-permute-start.20) | collective-permute-done | bytes 16416 | tf_op jit(solution)/shard_map/ppermute | solution.py:47
  64.5 0.6 add.44
  (60 shorter events, 0.9 us)
Async XLA Ops:
  0.6 22.8 %copy-start.2 = (s32[1,1,1,2]{3,2,1,0:T(1,128)S(1)}, s32[1,1,1,2]{3,2,1,0:T(1,128)}, u32[]{:S(2)}) copy-start(s32[1,1,1,2]{3,2,1,0:T(1,128)} %param.7) | copy-start | bytes 28
  1.4 5.4 %collective-permute-start = (f32[1,24,32]{2,1,0:T(8,128)S(1)}, f32[1,24,32]{2,1,0:T(8,128)S(1)}, u32[]{:S(2)}, u32[]{:S(2)}) collective-permute-start(f32[1,24,32]{2,1,0:T(8,128)S(1)} %fusion.5), channel_id=1, source_target_pairs={{0,1},{1,0},{2,3},{3,2},{4,5},{5,4},{6,7},{7,6},{8,9},{9,8},{10,11... | collective-permute-start | bytes 9224 | tf_op jit(solution)/shard_map/ppermute | solution.py:47
  4.5 1.6 %copy-start = (f32[4,32,16,256]{3,2,1,0:T(8,128)S(1)}, f32[4,32,16,256]{3,2,1,0:T(8,128)}, u32[]{:S(2)}) copy-start(f32[4,32,16,256]{3,2,1,0:T(8,128)} %refs_2_.1) | copy-start | bytes 6291460
  6.0 17.4 %copy-start.1 = (f32[4,32,16,256]{3,2,1,0:T(8,128)S(1)}, f32[4,32,16,256]{3,2,1,0:T(8,128)}, u32[]{:S(2)}) copy-start(f32[4,32,16,256]{3,2,1,0:T(8,128)} %refs_2_.1) | copy-start | bytes 6291460
  6.8 5.3 %collective-permute-start.2 = (f32[128,256]{1,0:T(8,128)S(1)}, f32[128,256]{1,0:T(8,128)S(1)}, u32[]{:S(2)}, u32[]{:S(2)}) collective-permute-start(f32[128,256]{1,0:T(8,128)S(1)} %get-tuple-element.51), channel_id=1, source_target_pairs={{0,1},{1,0},{2,3},{3,2},{4,5},{5,4},{6,7},{7,6},{8,9},{9,8},{10,11... | collective-permute-start | bytes 393224 | tf_op jit(solution)/shard_map/ppermute | solution.py:32
  8.2 4.9 %collective-permute-start.1 = (f32[2,24,32]{2,1,0:T(8,128)S(1)}, f32[2,24,32]{2,1,0:T(8,128)S(1)}, u32[]{:S(2)}, u32[]{:S(2)}) collective-permute-start(f32[2,24,32]{2,1,0:T(8,128)S(1)} %pad_maximum_fusion.5), channel_id=1, source_target_pairs={{0,2},{1,3},{2,0},{3,1},{4,6},{5,7},{6,4},{7,5},{8,10},{9,11},{10,... | collective-permute-start | bytes 18440 | tf_op jit(solution)/shard_map/ppermute | solution.py:47
  13.2 1.6 %collective-permute-start.4 = (f32[128,256]{1,0:T(8,128)S(1)}, f32[128,256]{1,0:T(8,128)S(1)}, u32[]{:S(2)}, u32[]{:S(2)}) collective-permute-start(f32[128,256]{1,0:T(8,128)S(1)} %get-tuple-element.55), channel_id=1, source_target_pairs={{0,16},{1,2},{2,1},{3,19},{16,0},{17,18},{18,17},{19,3},{4,20},{5,... | collective-permute-start | bytes 393224 | tf_op jit(solution)/shard_map/ppermute | solution.py:42
  13.2 3.8 %collective-permute-start.3 = (f32[40,128]{1,0:T(8,128)S(1)}, f32[40,128]{1,0:T(8,128)S(1)}, u32[]{:S(2)}, u32[]{:S(2)}) collective-permute-start(f32[40,128]{1,0:T(8,128)S(1)} %pad_maximum_fusion.7), channel_id=1, source_target_pairs={{0,4},{4,0},{8,12},{12,8},{1,5},{5,1},{9,13},{13,9},{2,6},{6,2},{1... | collective-permute-start | bytes 61448 | tf_op jit(solution)/shard_map/ppermute | solution.py:32
  17.1 4.8 %collective-permute-start.5 = (f32[64,128]{1,0:T(8,128)S(1)}, f32[64,128]{1,0:T(8,128)S(1)}, u32[]{:S(2)}, u32[]{:S(2)}) collective-permute-start(f32[64,128]{1,0:T(8,128)S(1)} %pad_maximum_fusion.2), channel_id=1, source_target_pairs={{0,12},{4,8},{8,4},{12,0},{1,13},{5,9},{9,5},{13,1},{2,14},{6,10},... | collective-permute-start | bytes 98312 | tf_op jit(solution)/shard_map/ppermute | solution.py:47
  21.9 1.3 %collective-permute-start.6 = (f32[1,96,128]{2,1,0:T(8,128)S(1)}, f32[1,96,128]{2,1,0:T(8,128)S(1)}, u32[]{:S(2)}, u32[]{:S(2)}) collective-permute-start(f32[1,96,128]{2,1,0:T(8,128)S(1)} %maximum_bitcast_fusion), channel_id=1, source_target_pairs={{0,16},{16,0},{1,17},{17,1},{2,18},{18,2},{3,19},{19,3},{4,20},{20... | collective-permute-start | bytes 147464 | tf_op jit(solution)/shard_map/ppermute | solution.py:47
  22.0 1.4 %collective-permute-start.7 = (f32[4,16,256]{2,1,0:T(8,128)S(1)}, f32[4,16,256]{2,1,0:T(8,128)S(1)}, u32[]{:S(2)}, u32[]{:S(2)}) collective-permute-start(f32[4,16,256]{2,1,0:T(8,128)S(1)} %get-tuple-element.60), channel_id=1, source_target_pairs={{0,16},{16,0},{1,17},{17,1},{2,18},{18,2},{3,19},{19,3},{4,20},{20... | collective-permute-start | bytes 196616 | tf_op jit(solution)/shard_map/ppermute | solution.py:32
  28.6 7.3 %collective-permute-start.8 = (f32[128,256]{1,0:T(8,128)S(1)}, f32[128,256]{1,0:T(8,128)S(1)}, u32[]{:S(2)}, u32[]{:S(2)}) collective-permute-start(f32[128,256]{1,0:T(8,128)S(1)} %get-tuple-element.62), channel_id=1, source_target_pairs={{0,1},{1,0},{2,3},{3,2},{4,5},{5,4},{6,7},{7,6},{8,9},{9,8},{10,11... | collective-permute-start | bytes 393224 | tf_op jit(solution)/shard_map/ppermute | solution.py:32
  31.8 4.2 %collective-permute-start.9 = (f32[128,256]{1,0:T(8,128)S(1)}, f32[128,256]{1,0:T(8,128)S(1)}, u32[]{:S(2)}, u32[]{:S(2)}) collective-permute-start(f32[128,256]{1,0:T(8,128)S(1)} %get-tuple-element.63), channel_id=1, source_target_pairs={{0,16},{1,2},{2,1},{3,19},{16,0},{17,18},{18,17},{19,3},{4,20},{5,... | collective-permute-start | bytes 393224 | tf_op jit(solution)/shard_map/ppermute | solution.py:42
  31.8 4.1 %collective-permute-start.12 = (f32[4,16,256]{2,1,0:T(8,128)S(1)}, f32[4,16,256]{2,1,0:T(8,128)S(1)}, u32[]{:S(2)}, u32[]{:S(2)}) collective-permute-start(f32[4,16,256]{2,1,0:T(8,128)S(1)} %get-tuple-element.66), channel_id=1, source_target_pairs={{0,16},{16,0},{1,17},{17,1},{2,18},{18,2},{3,19},{19,3},{4,20},{20... | collective-permute-start | bytes 196616 | tf_op jit(solution)/shard_map/ppermute | solution.py:32
  32.3 3.7 %collective-permute-start.10 = (f32[16,128]{1,0:T(8,128)S(1)}, f32[16,128]{1,0:T(8,128)S(1)}, u32[]{:S(2)}, u32[]{:S(2)}) collective-permute-start(f32[16,128]{1,0:T(8,128)S(1)} %get-tuple-element.64), channel_id=1, source_target_pairs={{0,4},{4,0},{8,12},{12,8},{1,5},{5,1},{9,13},{13,9},{2,6},{6,2},{1... | collective-permute-start | bytes 24584 | tf_op jit(solution)/shard_map/ppermute | solution.py:32
  33.8 2.2 %collective-permute-start.11 = (f32[16,128]{1,0:T(8,128)S(1)}, f32[16,128]{1,0:T(8,128)S(1)}, u32[]{:S(2)}, u32[]{:S(2)}) collective-permute-start(f32[16,128]{1,0:T(8,128)S(1)} %get-tuple-element.65), channel_id=1, source_target_pairs={{0,16},{4,8},{8,4},{12,28},{16,0},{20,24},{24,20},{28,12},{1,17},{... | collective-permute-start | bytes 24584 | tf_op jit(solution)/shard_map/ppermute | solution.py:42
  40.8 2.8 %collective-permute-start.14 = (f32[128,256]{1,0:T(8,128)S(1)}, f32[128,256]{1,0:T(8,128)S(1)}, u32[]{:S(2)}, u32[]{:S(2)}) collective-permute-start(f32[128,256]{1,0:T(8,128)S(1)} %get-tuple-element.70), channel_id=1, source_target_pairs={{0,16},{1,2},{2,1},{3,19},{16,0},{17,18},{18,17},{19,3},{4,20},{5,... | collective-permute-start | bytes 393224 | tf_op jit(solution)/shard_map/ppermute | solution.py:42
  40.9 6.3 %collective-permute-start.13 = (f32[144,256]{1,0:T(8,128)S(1)}, f32[144,256]{1,0:T(8,128)S(1)}, u32[]{:S(2)}, u32[]{:S(2)}) collective-permute-start(f32[144,256]{1,0:T(8,128)S(1)} %get-tuple-element.68), channel_id=1, source_target_pairs={{0,1},{1,0},{2,3},{3,2},{4,5},{5,4},{6,7},{7,6},{8,9},{9,8},{10,11... | collective-permute-start | bytes 442376 | tf_op jit(solution)/shard_map/ppermute | solution.py:32
  47.2 4.8 %collective-permute-start.15 = (f32[48,128]{1,0:T(8,128)S(1)}, f32[48,128]{1,0:T(8,128)S(1)}, u32[]{:S(2)}, u32[]{:S(2)}) collective-permute-start(f32[48,128]{1,0:T(8,128)S(1)} %pad_maximum_fusion.6), channel_id=1, source_target_pairs={{0,4},{4,0},{8,12},{12,8},{1,5},{5,1},{9,13},{13,9},{2,6},{6,2},{1... | collective-permute-start | bytes 73736 | tf_op jit(solution)/shard_map/ppermute | solution.py:32
  50.2 1.8 %collective-permute-start.16 = (f32[4,16,256]{2,1,0:T(8,128)S(1)}, f32[4,16,256]{2,1,0:T(8,128)S(1)}, u32[]{:S(2)}, u32[]{:S(2)}) collective-permute-start(f32[4,16,256]{2,1,0:T(8,128)S(1)} %get-tuple-element.74), channel_id=1, source_target_pairs={{0,16},{16,0},{1,17},{17,1},{2,18},{18,2},{3,19},{19,3},{4,20},{20... | collective-permute-start | bytes 196616 | tf_op jit(solution)/shard_map/ppermute | solution.py:32
  52.0 5.0 %collective-permute-start.17 = (f32[2,32,128]{2,1,0:T(8,128)S(1)}, f32[2,32,128]{2,1,0:T(8,128)S(1)}, u32[]{:S(2)}, u32[]{:S(2)}) collective-permute-start(f32[2,32,128]{2,1,0:T(8,128)S(1)} %bitcast.71), channel_id=1, source_target_pairs={{0,8},{4,12},{8,0},{12,4},{1,9},{5,13},{9,1},{13,5},{2,10},{6,14},... | collective-permute-start | bytes 98312 | tf_op jit(solution)/shard_map/ppermute | solution.py:47
  55.1 1.9 %collective-permute-start.18 = (f32[16,128]{1,0:T(8,128)S(1)}, f32[16,128]{1,0:T(8,128)S(1)}, u32[]{:S(2)}, u32[]{:S(2)}) collective-permute-start(f32[16,128]{1,0:T(8,128)S(1)} %get-tuple-element.76), channel_id=1, source_target_pairs={{0,16},{4,8},{8,4},{12,28},{16,0},{20,24},{24,20},{28,12},{1,17},{... | collective-permute-start | bytes 24584 | tf_op jit(solution)/shard_map/ppermute | solution.py:42
  57.1 5.9 %collective-permute-start.19 = (f32[128,128]{0,1:T(8,128)S(1)}, f32[128,128]{0,1:T(8,128)S(1)}, u32[]{:S(2)}, u32[]{:S(2)}) collective-permute-start(f32[128,128]{0,1:T(8,128)S(1)} %copy.11), channel_id=1, source_target_pairs={{0,2},{1,3},{2,0},{3,1},{4,6},{5,7},{6,4},{7,5},{8,10},{9,11},{10,... | collective-permute-start | bytes 196616 | tf_op jit(solution)/shard_map/ppermute | solution.py:47
  63.0 1.2 %collective-permute-start.20 = (f32[1,128,32]{1,2,0:T(8,128)S(1)}, f32[1,128,32]{1,2,0:T(8,128)S(1)}, u32[]{:S(2)}, u32[]{:S(2)}) collective-permute-start(f32[1,128,32]{1,2,0:T(8,128)S(1)} %dynamic-slice_bitcast_fusion), channel_id=1, source_target_pairs={{0,16},{16,0},{1,17},{17,1},{2,18},{18,2},{3,19},{19,3},{4,20},{20... | collective-permute-start | bytes 49160 | tf_op jit(solution)/shard_map/ppermute | solution.py:47
